TPU v7x, 256 devices: a whole 4x4x8 slice. The times are simulated.
256 devices in a mesh: req: 16 (over z, y_lo), blk: 16 (over x, y_hi, core).
Axes of the slice: x: 4, y: 4 (y_hi: 2, y_lo: 2; y = y_hi * 2 + y_lo), z: 8, core: 2. Of those that a mesh axis runs over, the one named last changes fastest.
Arguments:
- step_inputs: bfloat16 [2, 1024, 2560], P(None, 'req', 'blk'), may hold values from -6 to 6
- attention_gain: float32 [2560], replicated, may hold values from 0.25 to 1.75
- query_weight: bfloat16 [2560, 2560], P(None, 'blk'), may hold values from -0.3125 to 0.3125
- key_value_weight: bfloat16 [2560, 1024], P(None, 'blk'), may hold values from -0.125 to 0.125
- output_weight: bfloat16 [2560, 2560], P(None, 'blk'), may hold values from -0.125 to 0.125
- prompt_cache: bfloat16 [16, 48, 128, 1024], P('req', 'blk'), may hold values from -102 to 102
- page_table: int32 [16, 16, 3], P(None, 'blk'), may hold values from 0 to 2, each once within a row
- cache_lengths: int32 [16], replicated, may hold values from 1 to 6144, 49152 in all
- migration: int32 [16], replicated, may hold values from 0 to 15, each once
- parents: int32 [1, 1024], P(None, 'req'), may hold values from 0 to 7
- routes: int32 [2, 1024, 6], P(None, 'req'), may hold values from 0 to 63, all different within a row; in each aligned block of 64 rows (0 to 63, 64 to 127, ..., all dimensions but the last counted through in order) at most 16 rows name the same one
- feedforward_gain: float32 [2560], replicated, may hold values from 0.25 to 1.75
- router_weight: bfloat16 [2560, 64], replicated, may hold values from -0.125 to 0.125
- expert_gate: bfloat16 [256, 2560, 384], P(('req', 'blk')), may hold values from -0.125 to 0.125
- expert_up: bfloat16 [256, 2560, 384], P(('req', 'blk')), may hold values from -0.125 to 0.125
- expert_down: bfloat16 [256, 384, 2560], P(('req', 'blk')), may hold values from -0.15625 to 0.15625
- shared_gate: bfloat16 [2560, 3072], P(None, 'blk'), may hold values from -0.125 to 0.125
- shared_up: bfloat16 [2560, 3072], P(None, 'blk'), may hold values from -0.125 to 0.125
- shared_down: bfloat16 [3072, 2560], P('blk'), may hold values from -0.15625 to 0.15625
Outputs:
- layer_outputs: bfloat16 [2, 1024, 2560], P(None, 'req', 'blk')
Inputs may be any that keep to these rules, and one draw needn't show every extreme that they name: `routes`: in each step the 64 rows of one device along req name any one expert at most 16 times. `migration`: A permutation of the slots. Each page_table[g, c] is a permutation.
All inputs are finite; a program needn't handle non-finite values.
Results may differ from a plain program's by a relative error of at most 0.018.
The roundings to bfloat16 on the way count: a program that leaves them out, or rounds other values in their place, can miss the bound.
Values may be sent and summed in bfloat16 or wider, within the bound.
No kernel may reach another device: no remote copies, remote signals or barrier semaphores. Data moves between devices by JAX's collectives and lax.ppermute only.
A program may use at most 128 MiB of HBM per device.

v0:
```python
import jax
import jax.numpy as jnp
from jax import lax
from jax.experimental import pallas as pl
from jax.experimental.pallas import tpu as pltpu
from jax.sharding import PartitionSpec as P

QUERY_HEADS = 20
KEY_VALUE_HEADS = 4
HEAD_WIDTH = 128
E = 64
TOPK = 6
BEAMS = 8
CAP = 16
PAGE = 128

epsilon = 1e-05
rope_base = 500000.0
masked_floor = -1e30

bf16 = jnp.bfloat16
f32 = jnp.float32

SIDE = 4
QUAD = [[SIDE * i + k for k in range(SIDE)] for i in range(SIDE)]


def dot(a, b):
    return jnp.dot(a, b, preferred_element_type=f32)


def to_all(piece, axis):
    count = lax.axis_size(axis)
    copies = jnp.broadcast_to(piece[None], (count,) + piece.shape)
    return lax.all_to_all(copies, axis, 0, 0, tiled=True)


def partners(distance):
    return [(d, d ^ distance) for d in range(SIDE * SIDE)]


def group_parts(piece_for, stride):
    return [piece_for(0)] + [
        lax.ppermute(piece_for(d), "blk", partners(d * stride)) for d in range(1, SIDE)
    ]


def in_order(parts, index):
    odd = index % 2 == 1
    upper = index // 2 == 1
    a, b, c, d = parts
    a, b = jnp.where(odd, b, a), jnp.where(odd, a, b)
    c, d = jnp.where(odd, d, c), jnp.where(odd, c, d)
    return [
        jnp.where(upper, c, a),
        jnp.where(upper, d, b),
        jnp.where(upper, a, c),
        jnp.where(upper, b, d),
    ]


def norm_rows(rows, gain, axis):
    wide = rows.astype(f32)
    inverse = lax.rsqrt(jnp.mean(wide * wide, axis=axis, keepdims=True) + epsilon)
    return (wide * inverse * gain).astype(bf16)


def three_parts(value):
    high = value.astype(bf16)
    rest = value - high.astype(f32)
    middle = rest.astype(bf16)
    low = (rest - middle.astype(f32)).astype(bf16)
    return high, middle, low


def rotated(vectors, cosine, sine):
    half = vectors.shape[0] // 2
    a = vectors[:half].astype(f32)
    b = vectors[half:].astype(f32)
    return jnp.concatenate([a * cosine - b * sine, b * cosine + a * sine], axis=0)


def across(a, b):
    return lax.dot_general(a, b, (((0,), (0,)), ((), ())), preferred_element_type=f32)


def attention_kernel(
    scalars, parent, cosine, sine, p0, p1, p2, p3, c0, c1, c2, c3,
    o0, o1, o2, o3, query_rows, key_rows, value_rows, bias, scores, stats, joined,
):
    length = scalars[0]
    q_index = scalars[1]
    x_index = scalars[2]
    features, total = p0.shape
    span = query_rows.shape[0]
    share = span // SIDE
    half = HEAD_WIDTH // SIDE
    for d, piece in enumerate((p0, p1, p2, p3)):
        source = q_index ^ d
        query_rows[pl.ds(pl.multiple_of(source * share, half), share), :] = piece[:share, :]
        key_rows[pl.ds(pl.multiple_of(source * half, half), half), :] = piece[
            share : share + half, :
        ]
        value_rows[pl.ds(pl.multiple_of(source * half, half), half), :] = piece[
            share + half :, :
        ]
    cos = cosine[...]
    sin = sine[...]
    new_keys = rotated(key_rows[...], cos, sin).T.astype(bf16)
    new_values = value_rows[...]
    caches = (c0, c1, c2, c3)
    held = c0.shape[0]
    line = lax.broadcasted_iota(jnp.int32, (held, total), 0)
    spread = line + (line // PAGE) * (SIDE * SIDE - 1) * PAGE
    for d in range(SIDE):
        column = (x_index ^ d) * SIDE + q_index
        bias[d * held : (d + 1) * held, :] = jnp.where(
            spread + column * PAGE < length, 0.0, masked_floor
        )
    key_id = lax.broadcasted_iota(jnp.int32, (total, total), 0)
    row_id = lax.broadcasted_iota(jnp.int32, (total, total), 1)
    near = ((key_id == row_id) | (key_id == parent[...])) & (
        key_id // (total // SIDE) == q_index
    )
    bias[SIDE * held :, :] = jnp.where(near, 0.0, masked_floor)
    stats[...] = jnp.zeros(stats.shape, f32)
    scale = HEAD_WIDTH ** (-0.5)
    heads_here = span // HEAD_WIDTH
    for h in range(heads_here):
        query = rotated(
            query_rows[h * HEAD_WIDTH : (h + 1) * HEAD_WIDTH, :], cos, sin
        ).astype(bf16)
        for d, cache in enumerate(caches):
            scores[d * held : (d + 1) * held, :] = (
                dot(cache[:, :HEAD_WIDTH], query) * scale
                + bias[d * held : (d + 1) * held, :]
            )
        scores[SIDE * held :, :] = dot(new_keys, query) * scale + bias[SIDE * held :, :]
        peak = jnp.max(scores[...], axis=0, keepdims=True)
        mass = jnp.zeros((1, total), f32)
        weighted = jnp.zeros((HEAD_WIDTH, total), f32)
        for d, cache in enumerate(caches):
            raised = jnp.exp(scores[d * held : (d + 1) * held, :] - peak)
            mass = mass + jnp.sum(raised, axis=0, keepdims=True)
            weighted = weighted + across(cache[:, HEAD_WIDTH:], raised.astype(bf16))
        raised = jnp.exp(scores[SIDE * held :, :] - peak)
        mass = mass + jnp.sum(raised, axis=0, keepdims=True)
        weighted = weighted + dot(new_values, raised.astype(bf16))
        joined[:, h * HEAD_WIDTH : (h + 1) * HEAD_WIDTH] = (weighted / mass).T.astype(bf16)
        level = jnp.where(peak > 0.5 * masked_floor, peak + jnp.log(mass), masked_floor)
        for i, part in enumerate(three_parts(level)):
            place = i * heads_here + h
            stats[place : place + 1, :] = part.astype(f32)
    joined[:, span:] = stats[...].T.astype(bf16)
    subset = total // SIDE
    for d, out in enumerate((o0, o1, o2, o3)):
        out[...] = joined[pl.ds(pl.multiple_of((q_index ^ d) * subset, subset), subset), :]


def attend(scalars, parent, cosine, sine, pieces, caches):
    total = pieces[0].shape[1]
    subset = total // SIDE
    span = QUERY_HEADS // KEY_VALUE_HEADS * HEAD_WIDTH
    keys = SIDE * caches[0].shape[0] + total
    vmem = pl.BlockSpec(memory_space=pltpu.VMEM)
    return pl.pallas_call(
        attention_kernel,
        out_shape=[jax.ShapeDtypeStruct((subset, span + HEAD_WIDTH), bf16)] * SIDE,
        in_specs=[pl.BlockSpec(memory_space=pltpu.SMEM)] + [vmem] * (3 + 2 * SIDE),
        out_specs=[vmem] * SIDE,
        scratch_shapes=[
            pltpu.VMEM((span, total), bf16),
            pltpu.VMEM((HEAD_WIDTH, total), bf16),
            pltpu.VMEM((HEAD_WIDTH, total), bf16),
            pltpu.VMEM((keys, total), f32),
            pltpu.VMEM((keys, total), f32),
            pltpu.VMEM((HEAD_WIDTH, total), f32),
            pltpu.VMEM((total, span + HEAD_WIDTH), bf16),
        ],
        compiler_params=pltpu.CompilerParams(vmem_limit_bytes=24 << 20),
        name="attention",
    )(scalars, parent, cosine, sine, *pieces, *caches)


def expert_kernel(rows, g0, u0, d0, g1, u1, d1, out, gate_w, up_w, down_w, sems):
    copies = []
    for i, (g, u, d) in enumerate(((g0, u0, d0), (g1, u1, d1))):
        copies.append(
            [
                pltpu.make_async_copy(src, dst.at[i], sems.at[3 * i + k])
                for k, (src, dst) in enumerate(((g, gate_w), (u, up_w), (d, down_w)))
            ]
        )
    order = [(0, 0), (0, 1), (1, 0), (1, 1), (0, 2), (1, 2)]
    for i, k in order:
        copies[i][k].start()
    width = down_w.shape[2]
    hidden = []
    for i in (0, 1):
        copies[i][0].wait()
        gated = dot(rows[:, :width], gate_w[i])
        copies[i][1].wait()
        lifted = dot(rows[:, :width], up_w[i])
        hidden.append((gated / (1.0 + jnp.exp(-gated)) * lifted).astype(bf16))
    weight = (
        rows[:, width : width + 1].astype(f32)
        + rows[:, width + 1 : width + 2].astype(f32)
        + rows[:, width + 2 : width + 3].astype(f32)
    )
    copies[0][2].wait()
    copies[1][2].wait()
    step = 512
    for n in range(width // step):
        part = dot(hidden[0], down_w[0, :, n * step : (n + 1) * step]) + dot(
            hidden[1], down_w[1, :, n * step : (n + 1) * step]
        )
        out[n * step : (n + 1) * step, :] = (part * weight).T.astype(bf16)


def expert_rows(rows, blocks):
    count, wide = rows.shape
    width, units = blocks[0].shape
    vmem = pl.BlockSpec(memory_space=pltpu.VMEM)
    return pl.pallas_call(
        expert_kernel,
        out_shape=jax.ShapeDtypeStruct((width, count), bf16),
        in_specs=[vmem] + [pl.BlockSpec(memory_space=pl.ANY)] * 6,
        out_specs=vmem,
        scratch_shapes=[
            pltpu.VMEM((2, width, units), bf16),
            pltpu.VMEM((2, width, units), bf16),
            pltpu.VMEM((2, units, width), bf16),
            pltpu.SemaphoreType.DMA((6,)),
        ],
        compiler_params=pltpu.CompilerParams(vmem_limit_bytes=40 << 20),
        name="experts",
    )(rows, *blocks)


def collect_kernel(slot, returned, codes, shared, own, out, sums):
    groups, width, count = returned.shape
    slots, _, total = out.shape
    rows = total // 2
    lines = lax.broadcasted_iota(jnp.int32, (count, slots * rows), 0)
    by_step = []
    for c in (0, 1):
        acc = jnp.zeros((2 * width, slots * rows), f32)
        for x in range(SIDE):
            pick = jnp.where(
                lines == codes[2 * x + c : 2 * x + c + 1, :], 1.0, 0.0
            ).astype(bf16)
            pair = jnp.concatenate(
                [returned[SIDE * x + c], returned[SIDE * x + 2 + c]], axis=0
            )
            acc = acc + dot(pair, pick)
        by_step.append(acc[:width] + acc[width:])
    lane = lax.broadcasted_iota(jnp.int32, (width, total), 1)
    for pair in range(slots // 2):
        a = by_step[0][:, pair * total : (pair + 1) * total]
        b = by_step[1][:, pair * total : (pair + 1) * total]
        sums[2 * pair] = jnp.where(lane < rows, a, pltpu.roll(b, rows, 1))
        sums[2 * pair + 1] = jnp.where(lane < rows, pltpu.roll(a, rows, 1), b)
    mine = own[...].astype(f32)
    for g in range(groups):
        mine = mine + shared[g].astype(f32)
    sums[slot[0]] = sums[slot[0]] + mine
    out[...] = sums[...].astype(bf16)


def collect(slot, returned, codes, shared, own):
    vmem = pl.BlockSpec(memory_space=pltpu.VMEM)
    return pl.pallas_call(
        collect_kernel,
        out_shape=jax.ShapeDtypeStruct(shared.shape, bf16),
        in_specs=[pl.BlockSpec(memory_space=pltpu.SMEM)] + [vmem] * 4,
        out_specs=vmem,
        scratch_shapes=[pltpu.VMEM(shared.shape, f32)],
        compiler_params=pltpu.CompilerParams(vmem_limit_bytes=32 << 20),
        name="collect",
    )(slot, returned, codes, shared, own)


def ranks_of(named):
    rows = named.shape[-2]
    lower = (
        jnp.arange(rows, dtype=jnp.int32)[:, None] > jnp.arange(rows, dtype=jnp.int32)[None, :]
    ).astype(bf16)
    return jnp.einsum("ij,...je->...ie", lower, named.astype(bf16), preferred_element_type=f32)


def per_device(
    step_inputs,
    attention_gain,
    query_weight,
    key_value_weight,
    output_weight,
    prompt_cache,
    page_table,
    cache_lengths,
    migration,
    parents,
    routes,
    feedforward_gain,
    router_weight,
    expert_gate,
    expert_up,
    expert_down,
    shared_gate,
    shared_up,
    shared_down,
):
    req_count = lax.axis_size("req")
    blk_count = lax.axis_size("blk")
    req_index = lax.axis_index("req")
    blk_index = lax.axis_index("blk")
    x_index = blk_index // SIDE
    q_index = blk_index % SIDE
    core = blk_index % 2
    steps, rows, width_local = step_inputs.shape
    total = steps * rows
    width = width_local * blk_count
    heads_here = QUERY_HEADS // KEY_VALUE_HEADS
    span = heads_here * HEAD_WIDTH
    subset = total // SIDE

    beam = jnp.concatenate([jnp.zeros((rows,), jnp.int32), parents.reshape(-1)])
    payload = jnp.concatenate(
        [
            step_inputs.reshape(total, width_local).T,
            routes.reshape(total, TOPK).T.astype(bf16),
            beam.astype(bf16)[None],
            jnp.zeros((1, total), bf16),
        ],
        axis=0,
    )
    key_value_weight, payload = lax.optimization_barrier((key_value_weight, payload))
    by_slot = to_all(payload, "req")
    slot = migration[req_index]
    mine = lax.dynamic_index_in_dim(by_slot, slot, 0, False)
    routes_all = by_slot[:, width_local : width_local + TOPK].astype(jnp.int32)
    routes_mine = mine[width_local : width_local + TOPK].astype(jnp.int32).T
    beam_mine = mine[width_local + TOPK, rows:].astype(jnp.int32)
    inputs = to_all(mine[:width_local], "blk").reshape(width, total)

    half = key_value_weight.shape[1] // 2
    left, right = key_value_weight[:, :half], key_value_weight[:, half:]
    prompt, _ = lax.optimization_barrier((prompt_cache[0], by_slot))
    low_side = blk_index < blk_count // 2
    groups = blk_count // 2
    straight = [(d, 2 * d) for d in range(groups)] + [
        (groups + d, 2 * d + 1) for d in range(groups)
    ]
    crossed = [(d, 2 * d + 1) for d in range(groups)] + [
        (groups + d, 2 * d) for d in range(groups)
    ]
    first = lax.ppermute(jnp.where(low_side, left, right), "blk", straight)
    second = lax.ppermute(jnp.where(low_side, right, left), "blk", crossed)
    key_columns = jnp.where(core == 0, first, second)
    value_columns = jnp.where(core == 0, second, first)
    projection = jnp.concatenate([query_weight, key_columns, value_columns], axis=1)

    output_columns = lax.all_gather(
        output_weight, "blk", axis=1, tiled=True, axis_index_groups=QUAD
    )

    order = lax.dynamic_index_in_dim(page_table, req_index, 0, False)[0]
    pages = prompt[order]
    pages_local = pages.shape[0]
    by_head = (
        pages.reshape(pages_local * PAGE, 2, KEY_VALUE_HEADS, HEAD_WIDTH)
        .transpose(2, 0, 1, 3)
        .reshape(KEY_VALUE_HEADS, pages_local * PAGE, 2 * HEAD_WIDTH)
    )
    caches = group_parts(
        lambda d: lax.dynamic_index_in_dim(by_head, x_index ^ d, 0, False), SIDE
    )

    normed = norm_rows(inputs, attention_gain[:, None], 0)
    projected = across(projection, normed).astype(bf16)
    length = cache_lengths[req_index]
    frequency = rope_base ** (
        -2.0 * jnp.arange(HEAD_WIDTH // 2, dtype=f32) / HEAD_WIDTH
    )
    position = length + jnp.arange(steps, dtype=jnp.int32)
    angles = position.astype(f32)[:, None] * frequency
    cosine = jnp.repeat(jnp.cos(angles).T, rows, axis=1)
    sine = jnp.repeat(jnp.sin(angles).T, rows, axis=1)

    parent = jnp.concatenate(
        [
            jnp.full((rows,), -1, jnp.int32),
            jnp.arange(rows, dtype=jnp.int32) // BEAMS * BEAMS + beam_mine,
        ]
    )[None]
    parts = attend(
        jnp.stack([length, q_index, x_index]).astype(jnp.int32),
        parent,
        cosine,
        sine,
        group_parts(lambda d: projected, 1),
        caches,
    )
    met = jnp.stack(group_parts(lambda d: parts[d], 1))
    levels = sum(
        met[:, :, span + i * heads_here : span + (i + 1) * heads_here].astype(f32)
        for i in range(3)
    )
    shares = jnp.exp(levels - jnp.max(levels, axis=0, keepdims=True))
    shares = shares / jnp.sum(shares, axis=0, keepdims=True)
    heads = (
        jnp.sum(
            shares[..., None]
            * met[:, :, :span].reshape(SIDE, subset, heads_here, HEAD_WIDTH).astype(f32),
            axis=0,
        )
        .astype(bf16)
        .reshape(subset, span)
    )

    all_heads = jnp.concatenate(
        in_order(group_parts(lambda d: heads, SIDE), x_index), axis=1
    )
    residual = lax.dynamic_slice(
        inputs, (x_index * span, q_index * subset), (span, subset)
    ).T
    attended_part = (residual.astype(f32) + dot(all_heads, output_columns)).astype(bf16)
    gate_here, up_here, down_here, attended_part = lax.optimization_barrier(
        (expert_gate[0], expert_up[0], expert_down[0], attended_part)
    )
    blocks = [gate_here, up_here, down_here]
    expert_blocks = blocks + [lax.ppermute(b, "blk", partners(1)) for b in blocks]
    attended = (
        to_all(attended_part, "blk")
        .reshape(SIDE, SIDE, subset, span)
        .transpose(1, 2, 0, 3)
        .reshape(total, width)
    )
    normed_h = norm_rows(attended, feedforward_gain, 1)

    experts = jnp.arange(E, dtype=jnp.int32)
    named = jnp.any(routes_mine[:, :, None] == experts, axis=1)
    raised_gate = jnp.where(named, jnp.exp(dot(normed_h, router_weight)), 0.0)
    gates = raised_gate / jnp.sum(raised_gate, axis=1, keepdims=True)
    per_req = E // req_count

    def of_step(a):
        return lax.dynamic_slice_in_dim(a, core * rows, rows, 0)

    def of_expert(a):
        return lax.dynamic_index_in_dim(a.reshape(rows, req_count, per_req), x_index, 2, False).T

    named_step = of_step(named)
    rank_step = of_expert(ranks_of(named_step))
    named_here = of_expert(named_step.astype(f32)) > 0.0
    slots = jnp.arange(CAP, dtype=f32)
    dispatch = (
        named_here[:, None, :] & (rank_step[:, None, :] == slots[None, :, None])
    ).reshape(req_count * CAP, rows)
    gate_here = jnp.broadcast_to(
        of_expert(of_step(gates))[:, None, :], (req_count, CAP, rows)
    ).reshape(req_count * CAP, rows)
    slot_gate = jnp.sum(jnp.where(dispatch, gate_here, 0.0), axis=1, keepdims=True)
    sent = jnp.concatenate(
        [
            dot(dispatch.astype(bf16), of_step(normed_h)).astype(bf16),
            *three_parts(slot_gate),
            jnp.zeros((req_count * CAP, HEAD_WIDTH - 3), bf16),
        ],
        axis=1,
    ).reshape(req_count, CAP, width + HEAD_WIDTH)
    arrived = lax.all_to_all(sent, "req", 0, 0, tiled=True).reshape(
        req_count * CAP, width + HEAD_WIDTH
    )

    returned = lax.all_to_all(
        expert_rows(arrived, expert_blocks).reshape(blk_count, width_local, req_count * CAP),
        "blk",
        0,
        0,
        tiled=True,
    )

    act = (jax.nn.silu(dot(normed_h, shared_gate)) * dot(normed_h, shared_up)).astype(bf16)
    shared_part = lax.dot_general(
        shared_down, act, (((0,), (1,)), ((), ())), preferred_element_type=f32
    ).astype(bf16)
    shared = lax.all_to_all(
        shared_part.reshape(blk_count, width_local, total), "blk", 0, 0, tiled=True
    )

    slot_ids = jnp.arange(req_count, dtype=jnp.int32)
    holder = jnp.sum(
        jnp.where(migration[None, :] == slot_ids[:, None], slot_ids[None, :], 0), axis=1
    )
    owned = jnp.arange(per_req, dtype=jnp.int32) + req_index * per_req
    named_all = jnp.any(
        routes_all.reshape(1, req_count, TOPK, steps, rows) == owned[:, None, None, None, None],
        axis=2,
    )
    before = (
        jnp.arange(rows, dtype=jnp.int32)[:, None] < jnp.arange(rows, dtype=jnp.int32)[None, :]
    ).astype(bf16)
    rank_all = dot(named_all.astype(bf16).reshape(-1, rows), before).reshape(named_all.shape)
    codes = (
        jnp.where(
            named_all,
            holder[None, :, None, None] * CAP + rank_all.astype(jnp.int32),
            -1,
        )
        .transpose(0, 2, 1, 3)
        .reshape(per_req * steps, req_count * rows)
    )
    own = lax.dynamic_slice_in_dim(attended, blk_index * width_local, width_local, 1).T
    outgoing = collect(slot[None], returned, codes, shared, own)
    final = lax.all_to_all(outgoing, "req", 0, 0, tiled=True)
    return (
        jnp.sum(final.astype(f32), axis=0).T.astype(bf16).reshape(steps, rows, width_local)
    )


def solution(mesh):
    in_specs = (
        P(None, "req", "blk"),
        P(),
        P(None, "blk"),
        P(None, "blk"),
        P(None, "blk"),
        P("req", "blk", None, None),
        P(None, "blk", None),
        P(),
        P(),
        P(None, "req"),
        P(None, "req", None),
        P(),
        P(),
        P(("req", "blk"), None, None),
        P(("req", "blk"), None, None),
        P(("req", "blk"), None, None),
        P(None, "blk"),
        P(None, "blk"),
        P("blk", None),
    )
    out_specs = P(None, "req", "blk")
    return jax.shard_map(
        per_device, mesh=mesh, in_specs=in_specs, out_specs=out_specs, check_vma=False
    )
```

profile of v0, /device:TPU:1, one launch (start us, length us, event | category | flops | bytes accessed | tf_op | source)
XLA Modules:
  0.0 237.1 jit_solution(18002515232911362848)
XLA Ops:
  6.5 0.7 all-gather.2.cloned.1.call-update
  7.3 0.7 convert_bitcast_fusion.1
  8.0 0.7 convert_element_type.183
  8.8 0.9 copy.113
  10.0 0.9 broadcast_in_dim.44
  10.9 10.1 %all-to-all-start = ((bf16[16,168,128]{2,1,0:T(8,128)(2,1)}), bf16[16,168,128]{2,1,0:T(8,128)(2,1)S(1)}, u32[]{:S(2)}, u32[]{:S(2)}) async-start(bf16[16,168,128]{2,1,0:T(8,128)(2,1)} %broadcast_in_dim.44), calls=%async_computation | async-start | bytes 1376256 | tf_op jit(solution)/shard_map/all_to_all | solution.py:35
  21.1 0.7 broadcast_select_fusion.1
  21.8 5.4 %collective-permute-start = (bf16[2560,32]{0,1:T(8,128)(2,1)}, bf16[2560,32]{0,1:T(8,128)(2,1)}, u32[]{:S(2)}, u32[]{:S(2)}) collective-permute-start(bf16[2560,32]{0,1:T(8,128)(2,1)} %get-tuple-element.35), channel_id=1, source_target_pairs={{0,0},{1,2},{2,4},{3,6},{4,8},{5,10},{6,12},{7,14},{8,1},{9,3},{10... | collective-permute-start | bytes 491528 | tf_op jit(solution)/shard_map/ppermute | solution.py:356
  27.2 1.3 collective-permute-start.1
  28.5 0.6 dynamic_slice.58
  29.3 0.7 add_convert_fusion
  30.1 0.7 pad_add_fusion.scalars
  30.8 0.6 dynamic_slice.52.slot
  34.1 5.9 %all-to-all-done = bf16[16,168,128]{2,1,0:T(8,128)(2,1)S(1)} async-done(((bf16[16,168,128]{2,1,0:T(8,128)(2,1)}), bf16[16,168,128]{2,1,0:T(8,128)(2,1)S(1)}, u32[]{:S(2)}, u32[]{:S(2)}) %all-to-all-start) | async-done | bytes 688160 | tf_op jit(solution)/shard_map/all_to_all | solution.py:35
  39.9 0.9 broadcast_in_dim.47
  40.9 9.6 %all-to-all-start.1 = ((bf16[16,160,128]{2,1,0:T(8,128)(2,1)}), bf16[16,160,128]{2,1,0:T(8,128)(2,1)S(1)}, u32[]{:S(2)}, u32[]{:S(2)}) async-start(bf16[16,160,128]{2,1,0:T(8,128)(2,1)} %broadcast_in_dim.47), calls=%async_computation.1 | async-start | bytes 1310720 | tf_op jit(solution)/shard_map/all_to_all | solution.py:35
  50.5 1.8 broadcast_select_fusion.3
  52.3 0.6 gather_fusion
  52.9 0.6 reshape.234
  53.4 0.6 copy.119
  54.6 0.8 dynamic-slice_bitcast_fusion
  55.4 2.6 %collective-permute-start.7 = (bf16[384,256]{1,0:T(8,128)(2,1)}, bf16[384,256]{1,0:T(8,128)(2,1)S(1)}, u32[]{:S(2)}, u32[]{:S(2)}) collective-permute-start(bf16[384,256]{1,0:T(8,128)(2,1)} %get-tuple-element.29), channel_id=1, source_target_pairs={{0,12},{1,13},{2,14},{3,15},{4,8},{5,9},{6,10},{7,11},{8,4},{9,5},... | collective-permute-start | bytes 589832 | tf_op jit(solution)/shard_map/ppermute | solution.py:44
  58.0 0.6 collective-permute-start.6
  58.8 4.0 %all-to-all-done.1 = bf16[16,160,128]{2,1,0:T(8,128)(2,1)S(1)} async-done(((bf16[16,160,128]{2,1,0:T(8,128)(2,1)}), bf16[16,160,128]{2,1,0:T(8,128)(2,1)S(1)}, u32[]{:S(2)}, u32[]{:S(2)}) %all-to-all-start.1) | async-done | bytes 655392 | tf_op jit(solution)/shard_map/all_to_all | solution.py:35
  63.2 2.0 fusion.7.p0
  65.2 1.7 collective-permute-start.4
  66.8 3.3 %collective-permute-start.3 = (bf16[224,128]{1,0:T(8,128)(2,1)S(1)}, bf16[224,128]{1,0:T(8,128)(2,1)S(1)}, u32[]{:S(2)}, u32[]{:S(2)}) collective-permute-start(bf16[224,128]{1,0:T(8,128)(2,1)S(1)} %fusion.7.p0), channel_id=1, source_target_pairs={{0,2},{1,3},{2,0},{3,1},{4,6},{5,7},{6,4},{7,5},{8,10},{9,11},{10,... | collective-permute-start | bytes 172040 | tf_op jit(solution)/shard_map/ppermute | solution.py:44
  70.5 2.7 %collective-permute-done.3.p2 = bf16[224,128]{1,0:T(8,128)(2,1)S(1)} collective-permute-done((bf16[224,128]{1,0:T(8,128)(2,1)S(1)}, bf16[224,128]{1,0:T(8,128)(2,1)S(1)}, u32[]{:S(2)}, u32[]{:S(2)}) %collective-permute-start.3) | collective-permute-done | bytes 57376 | tf_op jit(solution)/shard_map/ppermute | solution.py:44
  73.2 3.7 %attention.1 = (bf16[32,768]{1,0:T(8,128)(2,1)S(1)}, bf16[32,768]{1,0:T(8,128)(2,1)S(1)}, bf16[32,768]{1,0:T(8,128)(2,1)S(1)}, bf16[32,768]{1,0:T(8,128)(2,1)S(1)}) custom-call(s32[3]{0:T(128)S(1)} %pad_add_fusion.scalars, s32[1,128]{1,0:T(1,128)S(1)} %pad_bitcast_fusion.parent, f32[64,128]{1,0:T(8,128)S(1)} %reshape.232.cosine, ...), custom_call_target="tpu_custom_call" | custom-call | tf_op jit(solution)/shard_map/attention/pallas_call | solution.py:166
  76.9 0.7 collective-permute-start.8
  77.6 1.2 collective-permute-start.9
  78.8 2.1 collective-permute-start.10
  81.0 1.1 collective-permute-done.9
  82.1 2.5 %collective-permute-done.10 = bf16[32,768]{1,0:T(8,128)(2,1)S(1)} collective-permute-done((bf16[32,768]{1,0:T(8,128)(2,1)S(1)}, bf16[32,768]{1,0:T(8,128)(2,1)S(1)}, u32[]{:S(2)}, u32[]{:S(2)}) %collective-permute-start.10) | collective-permute-done | bytes 49184 | tf_op jit(solution)/shard_map/ppermute | solution.py:44
  85.1 1.4 collective-permute-start.13
  86.5 2.1 collective-permute-start.12
  89.1 0.7 convert_bitcast_fusion
  90.0 1.3 collective-permute-done.12
  91.3 1.4 collective-permute-done.11
  92.8 3.0 %fusion.14 = bf16[32,640]{1,0:T(8,128)(2,1)S(1)} fusion(bf16[2560,640]{0,1:T(8,128)(2,1)} %all-gather.2.cloned.1.call-done, bf16[32,640]{1,0:T(8,128)(2,1)S(1)} %get-tuple-element.40, bf16[32,640]{1,0:T(8,128)(2,1)S(1)} %get-tuple-element.39, bf16[32,640]{1,0:T(8,128)(2,1)S(1)} %get-tuple-element.38, bf16[32,640]{1,0:T(8,128)(2,1)S(1)} %get-tuple-element.37, ...), kind=kOutput, calls=%fused_computation.22 | convolution fusion | flops 105574400 | bytes 3522560 | tf_op jit(solution)/shard_map/dot_general | solution.py:29
  95.8 0.9 broadcast_in_dim.52
  96.7 5.4 %all-to-all-start.2 = ((bf16[16,32,640]{2,1,0:T(8,128)(2,1)}), bf16[16,32,640]{2,1,0:T(8,128)(2,1)S(1)}, u32[]{:S(2)}, u32[]{:S(2)}) async-start(bf16[16,32,640]{2,1,0:T(8,128)(2,1)} %broadcast_in_dim.52), calls=%async_computation.2 | async-start | bytes 1310720 | tf_op jit(solution)/shard_map/all_to_all | solution.py:35
  102.6 12.0 %all-to-all-done.2 = bf16[16,32,640]{2,1,0:T(8,128)(2,1)S(1)} async-done(((bf16[16,32,640]{2,1,0:T(8,128)(2,1)}), bf16[16,32,640]{2,1,0:T(8,128)(2,1)S(1)}, u32[]{:S(2)}, u32[]{:S(2)}) %all-to-all-start.2) | async-done | bytes 655392 | tf_op jit(solution)/shard_map/all_to_all | solution.py:35
  115.7 0.5 copy-done.9
  118.0 2.1 concatenate.27
  120.1 4.9 %all-to-all-start.3 = ((bf16[16,16,2688]{2,1,0:T(8,128)(2,1)}), bf16[16,16,2688]{2,1,0:T(8,128)(2,1)S(1)}, u32[]{:S(2)}, u32[]{:S(2)}) async-start(bf16[16,16,2688]{2,1,0:T(8,128)(2,1)} %concatenate.27), calls=%async_computation.3 | async-start | bytes 2752512 | tf_op jit(solution)/shard_map/all_to_all | solution.py:471
  125.1 1.9 collective-permute-start.14
  127.4 1.6 fusion.55
  129.1 3.1 %fusion = bf16[2560,128]{0,1:T(8,128)(2,1)} fusion(bf16[192,2560]{1,0:T(8,128)(2,1)S(1)} %copy-done, bf16[128,2560]{1,0:T(8,128)(2,1)S(1)} %multiply_convert_fusion, bf16[2560,192]{0,1:T(8,128)(2,1)} %param.36, f32[128,192]{0,1:T(8,128)S(1)} %fusion.55), kind=kOutput, calls=%fused_computation.3 | convolution fusion | flops 252133376 | bytes 3375104 | tf_op jit(solution)/shard_map/dot_general | solution.py:484
  132.2 2.2 copy.126
  134.4 21.8 %all-to-all-done.3 = bf16[16,16,2688]{2,1,0:T(8,128)(2,1)S(1)} async-done(((bf16[16,16,2688]{2,1,0:T(8,128)(2,1)}), bf16[16,16,2688]{2,1,0:T(8,128)(2,1)S(1)}, u32[]{:S(2)}, u32[]{:S(2)}) %all-to-all-start.3) | async-done | bytes 1376288 | tf_op jit(solution)/shard_map/all_to_all | solution.py:471
  156.3 9.6 %all-to-all-start.5 = ((bf16[16,160,128]{2,1,0:T(8,128)(2,1)}), bf16[16,160,128]{2,1,0:T(8,128)(2,1)S(1)}, u32[]{:S(2)}, u32[]{:S(2)}) async-start(bf16[16,160,128]{2,1,0:T(8,128)(2,1)} %bitcast.146), calls=%async_computation.5 | async-start | bytes 1310720 | tf_op jit(solution)/shard_map/all_to_all | solution.py:487
  165.9 1.5 copy-done.2
  167.4 1.5 copy-done.3
  169.0 1.5 copy-done.4
  170.5 5.9 %experts.1 = bf16[2560,256]{1,0:T(8,128)(2,1)S(1)} custom-call(bf16[256,2688]{1,0:T(8,128)(2,1)S(1)} %bitcast.127, bf16[2560,384]{1,0:T(8,128)(2,1)S(1)} %bitcast.130, bf16[2560,384]{1,0:T(8,128)(2,1)S(1)} %bitcast.132, bf16[384,2560]{1,0:T(8,128)(2,1)S(1)} %bitcast.134, bf16[2560,384]{1,0:T(8,128)(2,1)} %collective-permute-done.14.g1, ...), custom_call_target="tpu_custom_call" | custom-call | tf_op jit(solution)/shard_map/experts/pallas_call | solution.py:224
  176.5 1.1 copy-done.1
  177.5 0.7 all-to-all-done.5.shared
  178.2 6.7 %all-to-all-start.4 = ((bf16[16,160,256]{2,1,0:T(8,128)(2,1)}), bf16[16,160,256]{2,1,0:T(8,128)(2,1)S(1)}, u32[]{:S(2)}, u32[]{:S(2)}) async-start(bf16[16,160,256]{2,1,0:T(8,128)(2,1)} %bitcast.128), calls=%async_computation.4 | async-start | bytes 2621440 | tf_op jit(solution)/shard_map/all_to_all | solution.py:475
  185.5 1.0 constant_dynamic-slice_fusion.1
  186.6 18.3 %all-to-all-done.4.returned = bf16[16,160,256]{2,1,0:T(8,128)(2,1)S(1)} async-done(((bf16[16,160,256]{2,1,0:T(8,128)(2,1)}), bf16[16,160,256]{2,1,0:T(8,128)(2,1)S(1)}, u32[]{:S(2)}, u32[]{:S(2)}) %all-to-all-start.4) | async-done | bytes 1310752 | tf_op jit(solution)/shard_map/all_to_all | solution.py:475
  204.9 2.4 %collect.1 = bf16[16,160,128]{2,1,0:T(8,128)(2,1)S(1)} custom-call(s32[1]{0:T(128)} %dynamic_slice.52.slot, bf16[16,160,256]{2,1,0:T(8,128)(2,1)S(1)} %all-to-all-done.4.returned, s32[8,1024]{1,0:T(8,128)S(1)} %reshape.241.codes, bf16[16,160,128]{2,1,0:T(8,128)(2,1)S(1)} %all-to-all-done.5.shared, bf16[160,128]{1,0:T(8,128)(2,1)S(1)} %bitcast.137), custom_call_target="tpu_custom_call" | custom-call | tf_op jit(solution)/shard_map/collect/pallas_call | solution.py:272
  207.3 22.1 %all_to_all.35 = bf16[16,160,128]{2,1,0:T(8,128)(2,1)S(1)} all-to-all(bf16[16,160,128]{2,1,0:T(8,128)(2,1)S(1)} %collect.1), channel_id=1, replica_groups=mesh['req'=16,'blk'=16] {'req'}, dimensions={0} | all-to-all | bytes 1310720 | tf_op jit(solution)/shard_map/all_to_all | solution.py:515
  229.5 0.7 copy.128
  (116 shorter events, 8.6 us)
Async XLA Ops:
  6.5 122.5 %copy-start = (bf16[192,2560]{1,0:T(8,128)(2,1)S(1)}, bf16[192,2560]{1,0:T(8,128)(2,1)}, u32[]{:S(2)}) copy-start(bf16[192,2560]{1,0:T(8,128)(2,1)} %param.37) | copy-start | bytes 2949124
  6.5 86.2 %all-gather.2.cloned.1.call-start = ((), (), s32[]{:S(2)}) async-start(), calls=%async_computation.7 | async-start | bytes 4096000 | tf_op jit(solution)/shard_map/all_gather | solution.py:362
  7.3 13.8 %copy-start.10 = (bf16[2560,64]{0,1:T(8,128)(2,1)S(1)}, bf16[2560,64]{0,1:T(8,128)(2,1)}, u32[]{:S(2)}) copy-start(bf16[2560,64]{0,1:T(8,128)(2,1)} %param.22) | copy-start | bytes 983044
  10.0 18.5 %copy-start.14 = (s32[16]{0:T(128)S(1)}, s32[16]{0:T(128)}, u32[]{:S(2)}) copy-start(s32[16]{0:T(128)} %param.26) | copy-start | bytes 196
  10.0 19.1 %copy-start.12 = (s32[16,1,3]{0,1,2:T(1,128)S(1)}, s32[16,1,3]{0,1,2:T(1,128)}, u32[]{:S(2)}) copy-start(s32[16,1,3]{0,1,2:T(1,128)} %param.25) | copy-start | bytes 580
  10.0 20.9 %copy-start.15 = (s32[16]{0:T(128)S(1)}, s32[16]{0:T(128)}, u32[]{:S(2)}) copy-start(s32[16]{0:T(128)} %param.27) | copy-start | bytes 196
  10.9 29.0 %all-to-all-start = ((bf16[16,168,128]{2,1,0:T(8,128)(2,1)}), bf16[16,168,128]{2,1,0:T(8,128)(2,1)S(1)}, u32[]{:S(2)}, u32[]{:S(2)}) async-start(bf16[16,168,128]{2,1,0:T(8,128)(2,1)} %broadcast_in_dim.44), calls=%async_computation | async-start | bytes 1376256 | tf_op jit(solution)/shard_map/all_to_all | solution.py:35
  21.8 28.7 %collective-permute-start = (bf16[2560,32]{0,1:T(8,128)(2,1)}, bf16[2560,32]{0,1:T(8,128)(2,1)}, u32[]{:S(2)}, u32[]{:S(2)}) collective-permute-start(bf16[2560,32]{0,1:T(8,128)(2,1)} %get-tuple-element.35), channel_id=1, source_target_pairs={{0,0},{1,2},{2,4},{3,6},{4,8},{5,10},{6,12},{7,14},{8,1},{9,3},{10... | collective-permute-start | bytes 491528 | tf_op jit(solution)/shard_map/ppermute | solution.py:356
  27.2 23.3 %collective-permute-start.1 = (bf16[2560,32]{0,1:T(8,128)(2,1)}, bf16[2560,32]{0,1:T(8,128)(2,1)}, u32[]{:S(2)}, u32[]{:S(2)}) collective-permute-start(bf16[2560,32]{0,1:T(8,128)(2,1)} %get-tuple-element.36), channel_id=1, source_target_pairs={{0,1},{1,3},{2,5},{3,7},{4,9},{5,11},{6,13},{7,15},{8,0},{9,2},{10... | collective-permute-start | bytes 491528 | tf_op jit(solution)/shard_map/ppermute | solution.py:357
  39.9 12.3 %copy-start.6 = (bf16[16,168,128]{2,1,0:T(8,128)(2,1)}, bf16[16,168,128]{2,1,0:T(8,128)(2,1)S(1)}, u32[]{:S(2)}) copy-start(bf16[16,168,128]{2,1,0:T(8,128)(2,1)S(1)} %all-to-all-done) | copy-start | bytes 2064388
  39.9 12.3 %copy-start.8 = (bf16[1,3,128,1024]{3,2,1,0:T(8,128)(2,1)S(1)}, bf16[1,3,128,1024]{3,2,1,0:T(8,128)(2,1)}, u32[]{:S(2)}) copy-start(bf16[1,3,128,1024]{3,2,1,0:T(8,128)(2,1)} %param.24) | copy-start | bytes 2359300
  40.9 22.0 %all-to-all-start.1 = ((bf16[16,160,128]{2,1,0:T(8,128)(2,1)}), bf16[16,160,128]{2,1,0:T(8,128)(2,1)S(1)}, u32[]{:S(2)}, u32[]{:S(2)}) async-start(bf16[16,160,128]{2,1,0:T(8,128)(2,1)} %broadcast_in_dim.47), calls=%async_computation.1 | async-start | bytes 1310720 | tf_op jit(solution)/shard_map/all_to_all | solution.py:35
  54.6 4.2 %copy-start.7 = (bf16[16,168,128]{2,1,0:T(8,128)(2,1)S(1)}, bf16[16,168,128]{2,1,0:T(8,128)(2,1)}, u32[]{:S(2)}) copy-start(bf16[16,168,128]{2,1,0:T(8,128)(2,1)} %copy-done.6) | copy-start | bytes 2064388
  54.6 8.6 %copy-start.13 = (f32[2560]{0:T(1024)S(1)}, f32[2560]{0:T(1024)}, u32[]{:S(2)}) copy-start(f32[2560]{0:T(1024)} %param.20) | copy-start | bytes 30724
  55.4 14.7 %collective-permute-start.7 = (bf16[384,256]{1,0:T(8,128)(2,1)}, bf16[384,256]{1,0:T(8,128)(2,1)S(1)}, u32[]{:S(2)}, u32[]{:S(2)}) collective-permute-start(bf16[384,256]{1,0:T(8,128)(2,1)} %get-tuple-element.29), channel_id=1, source_target_pairs={{0,12},{1,13},{2,14},{3,15},{4,8},{5,9},{6,10},{7,11},{8,4},{9,5},... | collective-permute-start | bytes 589832 | tf_op jit(solution)/shard_map/ppermute | solution.py:44
  58.0 12.4 %collective-permute-start.6 = (bf16[384,256]{1,0:T(8,128)(2,1)}, bf16[384,256]{1,0:T(8,128)(2,1)S(1)}, u32[]{:S(2)}, u32[]{:S(2)}) collective-permute-start(bf16[384,256]{1,0:T(8,128)(2,1)} %get-tuple-element.30), channel_id=1, source_target_pairs={{0,8},{1,9},{2,10},{3,11},{4,12},{5,13},{6,14},{7,15},{8,0},{9,1},... | collective-permute-start | bytes 589832 | tf_op jit(solution)/shard_map/ppermute | solution.py:44
  58.6 11.8 %collective-permute-start.5 = (bf16[384,256]{1,0:T(8,128)(2,1)}, bf16[384,256]{1,0:T(8,128)(2,1)S(1)}, u32[]{:S(2)}, u32[]{:S(2)}) collective-permute-start(bf16[384,256]{1,0:T(8,128)(2,1)} %get-tuple-element.31), channel_id=1, source_target_pairs={{0,4},{1,5},{2,6},{3,7},{4,0},{5,1},{6,2},{7,3},{8,12},{9,13},{10,... | collective-permute-start | bytes 589832 | tf_op jit(solution)/shard_map/ppermute | solution.py:44
  65.2 5.3 %collective-permute-start.4 = (bf16[224,128]{1,0:T(8,128)(2,1)S(1)}, bf16[224,128]{1,0:T(8,128)(2,1)S(1)}, u32[]{:S(2)}, u32[]{:S(2)}) collective-permute-start(bf16[224,128]{1,0:T(8,128)(2,1)S(1)} %fusion.7.p0), channel_id=1, source_target_pairs={{0,3},{1,2},{2,1},{3,0},{4,7},{5,6},{6,5},{7,4},{8,11},{9,10},{10,... | collective-permute-start | bytes 172040 | tf_op jit(solution)/shard_map/ppermute | solution.py:44
  66.8 6.4 %collective-permute-start.3 = (bf16[224,128]{1,0:T(8,128)(2,1)S(1)}, bf16[224,128]{1,0:T(8,128)(2,1)S(1)}, u32[]{:S(2)}, u32[]{:S(2)}) collective-permute-start(bf16[224,128]{1,0:T(8,128)(2,1)S(1)} %fusion.7.p0), channel_id=1, source_target_pairs={{0,2},{1,3},{2,0},{3,1},{4,6},{5,7},{6,4},{7,5},{8,10},{9,11},{10,... | collective-permute-start | bytes 172040 | tf_op jit(solution)/shard_map/ppermute | solution.py:44
  70.1 3.1 %collective-permute-start.2 = (bf16[224,128]{1,0:T(8,128)(2,1)S(1)}, bf16[224,128]{1,0:T(8,128)(2,1)S(1)}, u32[]{:S(2)}, u32[]{:S(2)}) collective-permute-start(bf16[224,128]{1,0:T(8,128)(2,1)S(1)} %fusion.7.p0), channel_id=1, source_target_pairs={{0,1},{1,0},{2,3},{3,2},{4,5},{5,4},{6,7},{7,6},{8,9},{9,8},{10,11... | collective-permute-start | bytes 172040 | tf_op jit(solution)/shard_map/ppermute | solution.py:44
  76.9 4.0 %collective-permute-start.8 = (bf16[32,768]{1,0:T(8,128)(2,1)S(1)}, bf16[32,768]{1,0:T(8,128)(2,1)S(1)}, u32[]{:S(2)}, u32[]{:S(2)}) collective-permute-start(bf16[32,768]{1,0:T(8,128)(2,1)S(1)} %get-tuple-element.20), channel_id=1, source_target_pairs={{0,1},{1,0},{2,3},{3,2},{4,5},{5,4},{6,7},{7,6},{8,9},{9,8},{10,11... | collective-permute-start | bytes 147464 | tf_op jit(solution)/shard_map/ppermute | solution.py:44
  77.6 4.5 %collective-permute-start.9 = (bf16[32,768]{1,0:T(8,128)(2,1)S(1)}, bf16[32,768]{1,0:T(8,128)(2,1)S(1)}, u32[]{:S(2)}, u32[]{:S(2)}) collective-permute-start(bf16[32,768]{1,0:T(8,128)(2,1)S(1)} %get-tuple-element.21), channel_id=1, source_target_pairs={{0,2},{1,3},{2,0},{3,1},{4,6},{5,7},{6,4},{7,5},{8,10},{9,11},{10,... | collective-permute-start | bytes 147464 | tf_op jit(solution)/shard_map/ppermute | solution.py:44
  78.8 5.8 %collective-permute-start.10 = (bf16[32,768]{1,0:T(8,128)(2,1)S(1)}, bf16[32,768]{1,0:T(8,128)(2,1)S(1)}, u32[]{:S(2)}, u32[]{:S(2)}) collective-permute-start(bf16[32,768]{1,0:T(8,128)(2,1)S(1)} %get-tuple-element.22), channel_id=1, source_target_pairs={{0,3},{1,2},{2,1},{3,0},{4,7},{5,6},{6,5},{7,4},{8,11},{9,10},{10,... | collective-permute-start | bytes 147464 | tf_op jit(solution)/shard_map/ppermute | solution.py:44
  85.1 4.9 %collective-permute-start.13 = (bf16[32,640]{1,0:T(8,128)(2,1)S(1)}, bf16[32,640]{1,0:T(8,128)(2,1)S(1)}, u32[]{:S(2)}, u32[]{:S(2)}) collective-permute-start(bf16[32,640]{1,0:T(8,128)(2,1)S(1)} %multiply_reduce_fusion.2), channel_id=1, source_target_pairs={{0,4},{1,5},{2,6},{3,7},{4,0},{5,1},{6,2},{7,3},{8,12},{9,13},{10,... | collective-permute-start | bytes 122888 | tf_op jit(solution)/shard_map/ppermute | solution.py:44
  86.5 4.7 %collective-permute-start.12 = (bf16[32,640]{1,0:T(8,128)(2,1)S(1)}, bf16[32,640]{1,0:T(8,128)(2,1)S(1)}, u32[]{:S(2)}, u32[]{:S(2)}) collective-permute-start(bf16[32,640]{1,0:T(8,128)(2,1)S(1)} %multiply_reduce_fusion.2), channel_id=1, source_target_pairs={{0,8},{1,9},{2,10},{3,11},{4,12},{5,13},{6,14},{7,15},{8,0},{9,1},... | collective-permute-start | bytes 122888 | tf_op jit(solution)/shard_map/ppermute | solution.py:44
  88.6 4.1 %collective-permute-start.11 = (bf16[32,640]{1,0:T(8,128)(2,1)S(1)}, bf16[32,640]{1,0:T(8,128)(2,1)S(1)}, u32[]{:S(2)}, u32[]{:S(2)}) collective-permute-start(bf16[32,640]{1,0:T(8,128)(2,1)S(1)} %multiply_reduce_fusion.2), channel_id=1, source_target_pairs={{0,12},{1,13},{2,14},{3,15},{4,8},{5,9},{6,10},{7,11},{8,4},{9,5},... | collective-permute-start | bytes 122888 | tf_op jit(solution)/shard_map/ppermute | solution.py:44
  96.7 17.9 %all-to-all-start.2 = ((bf16[16,32,640]{2,1,0:T(8,128)(2,1)}), bf16[16,32,640]{2,1,0:T(8,128)(2,1)S(1)}, u32[]{:S(2)}, u32[]{:S(2)}) async-start(bf16[16,32,640]{2,1,0:T(8,128)(2,1)} %broadcast_in_dim.52), calls=%async_computation.2 | async-start | bytes 1310720 | tf_op jit(solution)/shard_map/all_to_all | solution.py:35
  114.8 0.7 copy-start.11
  115.3 1.0 copy-start.9
  115.4 1.9 copy-start.5
  120.1 36.1 %all-to-all-start.3 = ((bf16[16,16,2688]{2,1,0:T(8,128)(2,1)}), bf16[16,16,2688]{2,1,0:T(8,128)(2,1)S(1)}, u32[]{:S(2)}, u32[]{:S(2)}) async-start(bf16[16,16,2688]{2,1,0:T(8,128)(2,1)} %concatenate.27), calls=%async_computation.3 | async-start | bytes 2752512 | tf_op jit(solution)/shard_map/all_to_all | solution.py:471
  125.1 40.8 %collective-permute-start.14 = (bf16[2560,384]{1,0:T(8,128)(2,1)}, bf16[2560,384]{1,0:T(8,128)(2,1)}, u32[]{:S(2)}, u32[]{:S(2)}) collective-permute-start(bf16[2560,384]{1,0:T(8,128)(2,1)} %bitcast.129), channel_id=1, source_target_pairs={{0,1},{1,0},{2,3},{3,2},{4,5},{5,4},{6,7},{7,6},{8,9},{9,8},{10,11... | collective-permute-start | bytes 5898248 | tf_op jit(solution)/shard_map/ppermute | solution.py:431
  126.9 38.9 %collective-permute-start.15 = (bf16[2560,384]{1,0:T(8,128)(2,1)}, bf16[2560,384]{1,0:T(8,128)(2,1)}, u32[]{:S(2)}, u32[]{:S(2)}) collective-permute-start(bf16[2560,384]{1,0:T(8,128)(2,1)} %bitcast.131), channel_id=1, source_target_pairs={{0,1},{1,0},{2,3},{3,2},{4,5},{5,4},{6,7},{7,6},{8,9},{9,8},{10,11... | collective-permute-start | bytes 5898248 | tf_op jit(solution)/shard_map/ppermute | solution.py:431
  127.0 38.8 %collective-permute-start.16 = (bf16[384,2560]{1,0:T(8,128)(2,1)}, bf16[384,2560]{1,0:T(8,128)(2,1)}, u32[]{:S(2)}, u32[]{:S(2)}) collective-permute-start(bf16[384,2560]{1,0:T(8,128)(2,1)} %bitcast.133), channel_id=1, source_target_pairs={{0,1},{1,0},{2,3},{3,2},{4,5},{5,4},{6,7},{7,6},{8,9},{9,8},{10,11... | collective-permute-start | bytes 5898248 | tf_op jit(solution)/shard_map/ppermute | solution.py:431
  156.3 21.9 %all-to-all-start.5 = ((bf16[16,160,128]{2,1,0:T(8,128)(2,1)}), bf16[16,160,128]{2,1,0:T(8,128)(2,1)S(1)}, u32[]{:S(2)}, u32[]{:S(2)}) async-start(bf16[16,160,128]{2,1,0:T(8,128)(2,1)} %bitcast.146), calls=%async_computation.5 | async-start | bytes 1310720 | tf_op jit(solution)/shard_map/all_to_all | solution.py:487
  165.9 1.5 copy-start.2
  167.4 1.5 copy-start.3
  169.0 1.5 copy-start.4
  176.5 1.1 copy-start.1
  178.2 6.8 %slice-start = ((bf16[16,168,128]{2,1,0:T(8,128)(2,1)}), bf16[16,6,128]{2,1,0:T(8,128)(2,1)S(1)}, s32[]{:S(2)}) async-start(bf16[16,168,128]{2,1,0:T(8,128)(2,1)} %copy-done.6), calls=%async_computation.8 | async-start | bytes 65536 | tf_op jit(solution)/shard_map/slice | solution.py:340
  178.2 26.7 %all-to-all-start.4 = ((bf16[16,160,256]{2,1,0:T(8,128)(2,1)}), bf16[16,160,256]{2,1,0:T(8,128)(2,1)S(1)}, u32[]{:S(2)}, u32[]{:S(2)}) async-start(bf16[16,160,256]{2,1,0:T(8,128)(2,1)} %bitcast.128), calls=%async_computation.4 | async-start | bytes 2621440 | tf_op jit(solution)/shard_map/all_to_all | solution.py:475
Sparse Core Ops, SparseCore 0:
  9.2 54.2 all-gather.1
where the time goes:
time: 239 us; the launch traced here: 237 us
  waiting for transfers between devices  72.5 us (30%)
  starting transfers between devices  71.8 us (30%)
  local copies, waits for them, and re-layouts  23.8 us (10%)
  blocking collectives  22.1 us (9%)
  between operations  15.9 us (7%)
  Pallas kernels  12 us (5%)
  matrix products  10.9 us (5%)
  other arithmetic  8.05 us (3%)
    all_to_all x3, starting transfers between devices, to_all(): return lax.all_to_all(copies, axis, 0, 0, tiled=True)  25.2 us
    all_to_all x1, blocking collectives, per_device(): final = lax.all_to_all(outgoing, 'req', 0, 0, tiled=True)  22.1 us
    all_to_all x3, waiting for transfers between devices, to_all(): return lax.all_to_all(copies, axis, 0, 0, tiled=True)  21.9 us
    all_to_all x1, waiting for transfers between devices, per_device(): lax.all_to_all(sent, 'req', 0, 0, tiled=True)  21.8 us
    all_to_all x1, waiting for transfers between devices, per_device(): lax.all_to_all(expert_rows(arrived, expert_blocks).reshape(blk_count, wid...  18.3 us
    ppermute x12, starting transfers between devices, group_parts(): lax.ppermute(piece_for(d), 'blk', partners(d * stride))  16.3 us
    all_to_all x1, starting transfers between devices, per_device(): lax.all_to_all(shared_part.reshape(blk_count, width_local, total), 'blk',...  9.59 us
    ppermute x12, waiting for transfers between devices, group_parts(): lax.ppermute(piece_for(d), 'blk', partners(d * stride))  9.12 us
  transfers between devices with their start and end apart: 24, of which 11 were waited for; matrix products, arithmetic and copies ran while one was open for 11% of the time, Pallas kernels for 4%

commit v1 on v0

--- a/solution.py
+++ b/solution.py
@@ -182,7 +182,10 @@
     )(scalars, parent, cosine, sine, *pieces, *caches)
 
 
-def expert_kernel(rows, g0, u0, d0, g1, u1, d1, out, gate_w, up_w, down_w, sems):
+def expert_kernel(
+    expert, rows, router, named, g0, u0, d0, g1, u1, d1, out,
+    gate_w, up_w, down_w, result, sems, out_sems,
+):
     copies = []
     for i, (g, u, d) in enumerate(((g0, u0, d0), (g1, u1, d1))):
         copies.append(
@@ -198,46 +201,60 @@
     hidden = []
     for i in (0, 1):
         copies[i][0].wait()
-        gated = dot(rows[:, :width], gate_w[i])
+        gated = dot(rows[...], gate_w[i])
         copies[i][1].wait()
-        lifted = dot(rows[:, :width], up_w[i])
+        lifted = dot(rows[...], up_w[i])
         hidden.append((gated / (1.0 + jnp.exp(-gated)) * lifted).astype(bf16))
-    weight = (
-        rows[:, width : width + 1].astype(f32)
-        + rows[:, width + 1 : width + 2].astype(f32)
-        + rows[:, width + 2 : width + 3].astype(f32)
-    )
+    logits = lax.dot_general(
+        rows[...], router[...], (((1,), (1,)), ((), ())), preferred_element_type=f32
+    )
+    raised = jnp.where(named[...] > 0.0, jnp.exp(logits), 0.0)
+    column = lax.broadcasted_iota(jnp.int32, raised.shape, 1)
+    total = jnp.sum(raised, axis=1, keepdims=True)
+    picked = jnp.sum(jnp.where(column == expert[0], raised, 0.0), axis=1, keepdims=True)
+    weight = picked / jnp.where(total > 0.0, total, 1.0)
     copies[0][2].wait()
     copies[1][2].wait()
-    step = 512
+    step = width // out_sems.shape[0]
+    stores = []
     for n in range(width // step):
         part = dot(hidden[0], down_w[0, :, n * step : (n + 1) * step]) + dot(
             hidden[1], down_w[1, :, n * step : (n + 1) * step]
         )
-        out[n * step : (n + 1) * step, :] = (part * weight).T.astype(bf16)
-
-
-def expert_rows(rows, blocks):
-    count, wide = rows.shape
-    width, units = blocks[0].shape
+        span = slice(n * step, (n + 1) * step)
+        result[span, :] = (part * weight).T.astype(bf16)
+        stores.append(
+            pltpu.make_async_copy(result.at[span, :], out.at[span, :], out_sems.at[n])
+        )
+        stores[-1].start()
+    for store in stores:
+        store.wait()
+
+
+def expert_rows(expert, rows, router, named, blocks):
+    count, width = rows.shape
+    units = blocks[0].shape[1]
     vmem = pl.BlockSpec(memory_space=pltpu.VMEM)
+    hbm = pl.BlockSpec(memory_space=pltpu.HBM)
     return pl.pallas_call(
         expert_kernel,
         out_shape=jax.ShapeDtypeStruct((width, count), bf16),
-        in_specs=[vmem] + [pl.BlockSpec(memory_space=pl.ANY)] * 6,
-        out_specs=vmem,
+        in_specs=[pl.BlockSpec(memory_space=pltpu.SMEM)] + [vmem] * 3 + [hbm] * 6,
+        out_specs=hbm,
         scratch_shapes=[
             pltpu.VMEM((2, width, units), bf16),
             pltpu.VMEM((2, width, units), bf16),
             pltpu.VMEM((2, units, width), bf16),
+            pltpu.VMEM((width, count), bf16),
             pltpu.SemaphoreType.DMA((6,)),
+            pltpu.SemaphoreType.DMA((5,)),
         ],
         compiler_params=pltpu.CompilerParams(vmem_limit_bytes=40 << 20),
         name="experts",
-    )(rows, *blocks)
-
-
-def collect_kernel(slot, returned, codes, shared, own, out, sums):
+    )(expert, rows, router, named, *blocks)
+
+
+def collect_kernel(slot, returned, codes, own, out, sums):
     groups, width, count = returned.shape
     slots, _, total = out.shape
     rows = total // 2
@@ -260,24 +277,23 @@
         b = by_step[1][:, pair * total : (pair + 1) * total]
         sums[2 * pair] = jnp.where(lane < rows, a, pltpu.roll(b, rows, 1))
         sums[2 * pair + 1] = jnp.where(lane < rows, pltpu.roll(a, rows, 1), b)
-    mine = own[...].astype(f32)
-    for g in range(groups):
-        mine = mine + shared[g].astype(f32)
-    sums[slot[0]] = sums[slot[0]] + mine
+    sums[slot[0]] = sums[slot[0]] + own[...]
     out[...] = sums[...].astype(bf16)
 
 
-def collect(slot, returned, codes, shared, own):
+def collect(slot, returned, codes, own):
+    groups, width, _ = returned.shape
+    shape = (groups, width, own.shape[1])
     vmem = pl.BlockSpec(memory_space=pltpu.VMEM)
     return pl.pallas_call(
         collect_kernel,
-        out_shape=jax.ShapeDtypeStruct(shared.shape, bf16),
-        in_specs=[pl.BlockSpec(memory_space=pltpu.SMEM)] + [vmem] * 4,
+        out_shape=jax.ShapeDtypeStruct(shape, bf16),
+        in_specs=[pl.BlockSpec(memory_space=pltpu.SMEM)] + [vmem] * 3,
         out_specs=vmem,
-        scratch_shapes=[pltpu.VMEM(shared.shape, f32)],
+        scratch_shapes=[pltpu.VMEM(shape, f32)],
         compiler_params=pltpu.CompilerParams(vmem_limit_bytes=32 << 20),
         name="collect",
-    )(slot, returned, codes, shared, own)
+    )(slot, returned, codes, own)
 
 
 def ranks_of(named):
@@ -333,7 +349,9 @@
         ],
         axis=0,
     )
-    key_value_weight, payload = lax.optimization_barrier((key_value_weight, payload))
+    key_value_weight, prompt, payload = lax.optimization_barrier(
+        (key_value_weight, prompt_cache[0], payload)
+    )
     by_slot = to_all(payload, "req")
     slot = migration[req_index]
     mine = lax.dynamic_index_in_dim(by_slot, slot, 0, False)
@@ -344,7 +362,6 @@
 
     half = key_value_weight.shape[1] // 2
     left, right = key_value_weight[:, :half], key_value_weight[:, half:]
-    prompt, _ = lax.optimization_barrier((prompt_cache[0], by_slot))
     low_side = blk_index < blk_count // 2
     groups = blk_count // 2
     straight = [(d, 2 * d) for d in range(groups)] + [
@@ -371,6 +388,7 @@
         .transpose(2, 0, 1, 3)
         .reshape(KEY_VALUE_HEADS, pages_local * PAGE, 2 * HEAD_WIDTH)
     )
+    by_head, by_slot = lax.optimization_barrier((by_head, by_slot))
     caches = group_parts(
         lambda d: lax.dynamic_index_in_dim(by_head, x_index ^ d, 0, False), SIDE
     )
@@ -437,57 +455,7 @@
     )
     normed_h = norm_rows(attended, feedforward_gain, 1)
 
-    experts = jnp.arange(E, dtype=jnp.int32)
-    named = jnp.any(routes_mine[:, :, None] == experts, axis=1)
-    raised_gate = jnp.where(named, jnp.exp(dot(normed_h, router_weight)), 0.0)
-    gates = raised_gate / jnp.sum(raised_gate, axis=1, keepdims=True)
     per_req = E // req_count
-
-    def of_step(a):
-        return lax.dynamic_slice_in_dim(a, core * rows, rows, 0)
-
-    def of_expert(a):
-        return lax.dynamic_index_in_dim(a.reshape(rows, req_count, per_req), x_index, 2, False).T
-
-    named_step = of_step(named)
-    rank_step = of_expert(ranks_of(named_step))
-    named_here = of_expert(named_step.astype(f32)) > 0.0
-    slots = jnp.arange(CAP, dtype=f32)
-    dispatch = (
-        named_here[:, None, :] & (rank_step[:, None, :] == slots[None, :, None])
-    ).reshape(req_count * CAP, rows)
-    gate_here = jnp.broadcast_to(
-        of_expert(of_step(gates))[:, None, :], (req_count, CAP, rows)
-    ).reshape(req_count * CAP, rows)
-    slot_gate = jnp.sum(jnp.where(dispatch, gate_here, 0.0), axis=1, keepdims=True)
-    sent = jnp.concatenate(
-        [
-            dot(dispatch.astype(bf16), of_step(normed_h)).astype(bf16),
-            *three_parts(slot_gate),
-            jnp.zeros((req_count * CAP, HEAD_WIDTH - 3), bf16),
-        ],
-        axis=1,
-    ).reshape(req_count, CAP, width + HEAD_WIDTH)
-    arrived = lax.all_to_all(sent, "req", 0, 0, tiled=True).reshape(
-        req_count * CAP, width + HEAD_WIDTH
-    )
-
-    returned = lax.all_to_all(
-        expert_rows(arrived, expert_blocks).reshape(blk_count, width_local, req_count * CAP),
-        "blk",
-        0,
-        0,
-        tiled=True,
-    )
-
-    act = (jax.nn.silu(dot(normed_h, shared_gate)) * dot(normed_h, shared_up)).astype(bf16)
-    shared_part = lax.dot_general(
-        shared_down, act, (((0,), (1,)), ((), ())), preferred_element_type=f32
-    ).astype(bf16)
-    shared = lax.all_to_all(
-        shared_part.reshape(blk_count, width_local, total), "blk", 0, 0, tiled=True
-    )
-
     slot_ids = jnp.arange(req_count, dtype=jnp.int32)
     holder = jnp.sum(
         jnp.where(migration[None, :] == slot_ids[:, None], slot_ids[None, :], 0), axis=1
@@ -510,8 +478,75 @@
         .transpose(0, 2, 1, 3)
         .reshape(per_req * steps, req_count * rows)
     )
-    own = lax.dynamic_slice_in_dim(attended, blk_index * width_local, width_local, 1).T
-    outgoing = collect(slot[None], returned, codes, shared, own)
+
+    experts = jnp.arange(E, dtype=jnp.int32)
+    code = lax.dynamic_index_in_dim(codes, x_index * steps + core, 0, False)
+    slot_of = (
+        code[None, :] == jnp.arange(req_count * CAP, dtype=jnp.int32)[:, None]
+    ).astype(bf16)
+    routes_step = lax.dynamic_slice_in_dim(routes_all, core * rows, rows, 2)
+    named_rows = (
+        jnp.any(routes_step.transpose(0, 2, 1)[..., None] == experts, axis=2)
+        .astype(bf16)
+        .reshape(req_count * rows, E)
+    )
+    named_slots = dot(slot_of, named_rows)
+
+    def of_step(a):
+        return lax.dynamic_slice_in_dim(a, core * rows, rows, 0)
+
+    def of_expert(a):
+        return lax.dynamic_index_in_dim(a.reshape(rows, req_count, per_req), x_index, 2, False).T
+
+    named_step = jnp.any(of_step(routes_mine)[:, :, None] == experts, axis=1)
+    rank_step = of_expert(ranks_of(named_step))
+    named_here = of_expert(named_step.astype(f32)) > 0.0
+    slots = jnp.arange(CAP, dtype=f32)
+    dispatch = (
+        (named_here[:, None, :] & (rank_step[:, None, :] == slots[None, :, None]))
+        .reshape(req_count * CAP, rows)
+        .astype(bf16)
+    )
+    sent = dot(dispatch, of_step(normed_h)).astype(bf16).reshape(req_count, CAP, width)
+    arrived = lax.all_to_all(sent, "req", 0, 0, tiled=True).reshape(req_count * CAP, width)
+
+    returned = lax.all_to_all(
+        expert_rows(
+            (req_index * per_req + x_index)[None].astype(jnp.int32),
+            arrived,
+            router_weight.T,
+            named_slots,
+            expert_blocks,
+        ).reshape(blk_count, width_local, req_count * CAP),
+        "blk",
+        0,
+        0,
+        tiled=True,
+    )
+
+    act = (jax.nn.silu(dot(normed_h, shared_gate)) * dot(normed_h, shared_up)).astype(bf16)
+    shared_part = lax.dot_general(
+        shared_down, act, (((0,), (1,)), ((), ())), preferred_element_type=f32
+    ).astype(bf16)
+    shared_pieces = shared_part.reshape(SIDE, SIDE, width_local, total)
+    over_q = sum(
+        p.astype(f32)
+        for p in group_parts(
+            lambda d: lax.dynamic_index_in_dim(shared_pieces, q_index ^ d, 1, False), 1
+        )
+    ).astype(bf16)
+    shared = sum(
+        p.astype(f32)
+        for p in group_parts(
+            lambda d: lax.dynamic_index_in_dim(over_q, x_index ^ d, 0, False), SIDE
+        )
+    )
+    own = (
+        lax.dynamic_slice_in_dim(attended, blk_index * width_local, width_local, 1)
+        .T.astype(f32)
+        + shared
+    )
+    outgoing = collect(slot[None], returned, codes, own)
     final = lax.all_to_all(outgoing, "req", 0, 0, tiled=True)
     return (
         jnp.sum(final.astype(f32), axis=0).T.astype(bf16).reshape(steps, rows, width_local)

time: 239 us -> 246 us (1.029)
  starting transfers between devices: 71.8 us -> 77.4 us
  other arithmetic: 8.05 us -> 11 us
  local copies, waits for them, and re-layouts: 23.8 us -> 21.2 us
    all_to_all x2 -> x1, waiting for transfers between devices: 18.9 us -> 0.01 us  [per_device(): lax.all_to_all(expert_rows((req_index * per_req + x_index)[None].astype(j...]
    ppermute x12 -> x18, waiting for transfers between devices: 9.12 us -> 26.7 us  [group_parts(): lax.ppermute(piece_for(d), 'blk', partners(d * stride))]
    ppermute x12 -> x18, starting transfers between devices: 16.3 us -> 26.9 us  [group_parts(): lax.ppermute(piece_for(d), 'blk', partners(d * stride))]
    all_to_all x2 -> x1, starting transfers between devices: 16.3 us -> 9.72 us  [per_device(): lax.all_to_all(expert_rows((req_index * per_req + x_index)[None].astype(j...]
    ppermute x3, waiting for transfers between devices: 0.01 us -> 4.42 us  [per_device(): lax.ppermute(b, 'blk', partners(1))]
    all_to_all x1, waiting for transfers between devices: 21.8 us -> 18.4 us  [per_device(): lax.all_to_all(sent, 'req', 0, 0, tiled=True)]
    convert_element_type x2 -> x4, other arithmetic: 0.01 us -> 2.54 us  [the longest x1 1.09 us: per_device(): over_q = sum((p.astype(f32) for p in group_parts(lambda d: lax.dynamic_in...]
    unnamed x35 -> x30, local copies, waits for them, and re-layouts: 6.59 us -> 5 us
  transfers between devices with their start and end apart: 24 -> 29, of which waited for: 11 -> 14; matrix products, arithmetic and copies ran while one was open for 11% -> 13% of each run, Pallas kernels for 4% -> 2%
where the time goes in v1:
time: 246 us; the launch traced here: 242 us
  starting transfers between devices  77.4 us (31%)
  waiting for transfers between devices  71.1 us (29%)
  local copies, waits for them, and re-layouts  21.2 us (9%)
  blocking collectives  20.1 us (8%)
  between operations  15.9 us (6%)
  Pallas kernels  13.9 us (6%)
  matrix products  11.9 us (5%)
  other arithmetic  11 us (4%)
    ppermute x18, starting transfers between devices, group_parts(): lax.ppermute(piece_for(d), 'blk', partners(d * stride))  26.9 us
    all_to_all x3, starting transfers between devices, to_all(): return lax.all_to_all(copies, axis, 0, 0, tiled=True)  26.8 us
    ppermute x18, waiting for transfers between devices, group_parts(): lax.ppermute(piece_for(d), 'blk', partners(d * stride))  26.7 us
    all_to_all x3, waiting for transfers between devices, to_all(): return lax.all_to_all(copies, axis, 0, 0, tiled=True)  20.8 us
    all_to_all x1, blocking collectives, per_device(): final = lax.all_to_all(outgoing, 'req', 0, 0, tiled=True)  20.1 us
    all_to_all x1, waiting for transfers between devices, per_device(): lax.all_to_all(sent, 'req', 0, 0, tiled=True)  18.4 us
    all_to_all x1, starting transfers between devices, per_device(): lax.all_to_all(expert_rows((req_index * per_req + x_index)[None].astype(j...  9.72 us
    pallas_call x1, Pallas kernels, expert_rows(): pl.pallas_call(expert_kernel, out_shape=jax.ShapeDtypeStruct((width, coun...  7.75 us
  transfers between devices with their start and end apart: 29, of which 14 were waited for; matrix products, arithmetic and copies ran while one was open for 13% of the time, Pallas kernels for 2%

profile of v1, /device:TPU:1, one launch (start us, length us, event | category | flops | bytes accessed | tf_op | source)
XLA Modules:
  0.0 242.4 jit_solution(9356964592658370954)
XLA Ops:
  6.5 0.7 all-gather.2.cloned.1.call-update
  7.3 0.7 convert_bitcast_fusion
  8.0 0.7 convert_element_type.152
  8.8 0.9 copy.82
  10.0 0.9 broadcast_in_dim.40
  10.9 10.3 %all-to-all-start = ((bf16[16,168,128]{2,1,0:T(8,128)(2,1)}), bf16[16,168,128]{2,1,0:T(8,128)(2,1)}, u32[]{:S(2)}, u32[]{:S(2)}) async-start(bf16[16,168,128]{2,1,0:T(8,128)(2,1)} %broadcast_in_dim.40), calls=%async_computation | async-start | bytes 1376256 | tf_op jit(solution)/shard_map/all_to_all | solution.py:35
  21.3 0.8 broadcast_select_fusion.1
  22.0 5.4 %collective-permute-start = (bf16[2560,32]{0,1:T(8,128)(2,1)}, bf16[2560,32]{0,1:T(8,128)(2,1)}, u32[]{:S(2)}, u32[]{:S(2)}) collective-permute-start(bf16[2560,32]{0,1:T(8,128)(2,1)} %get-tuple-element.40), channel_id=1, source_target_pairs={{0,0},{1,2},{2,4},{3,6},{4,8},{5,10},{6,12},{7,14},{8,1},{9,3},{10... | collective-permute-start | bytes 491528 | tf_op jit(solution)/shard_map/ppermute | solution.py:373
  27.4 1.3 collective-permute-start.1
  30.3 0.7 pad_add_fusion.scalars
  36.6 3.6 %all-to-all-done = bf16[16,168,128]{2,1,0:T(8,128)(2,1)} async-done(((bf16[16,168,128]{2,1,0:T(8,128)(2,1)}), bf16[16,168,128]{2,1,0:T(8,128)(2,1)}, u32[]{:S(2)}, u32[]{:S(2)}) %all-to-all-start) | async-done | bytes 688160 | tf_op jit(solution)/shard_map/all_to_all | solution.py:35
  40.2 0.8 dynamic-slice_bitcast_fusion.9
  41.0 0.9 broadcast_in_dim.42
  41.9 9.6 %all-to-all-start.1 = ((bf16[16,160,128]{2,1,0:T(8,128)(2,1)}), bf16[16,160,128]{2,1,0:T(8,128)(2,1)S(1)}, u32[]{:S(2)}, u32[]{:S(2)}) async-start(bf16[16,160,128]{2,1,0:T(8,128)(2,1)} %broadcast_in_dim.42), calls=%async_computation.1 | async-start | bytes 1310720 | tf_op jit(solution)/shard_map/all_to_all | solution.py:35
  51.5 1.8 broadcast_select_fusion.3
  53.3 0.8 dynamic-slice_bitcast_fusion
  54.1 2.6 %collective-permute-start.7 = (bf16[384,256]{1,0:T(8,128)(2,1)}, bf16[384,256]{1,0:T(8,128)(2,1)S(1)}, u32[]{:S(2)}, u32[]{:S(2)}) collective-permute-start(bf16[384,256]{1,0:T(8,128)(2,1)} %get-tuple-element.31), channel_id=1, source_target_pairs={{0,12},{1,13},{2,14},{3,15},{4,8},{5,9},{6,10},{7,11},{8,4},{9,5},... | collective-permute-start | bytes 589832 | tf_op jit(solution)/shard_map/ppermute | solution.py:44
  57.4 0.8 dynamic-slice_bitcast_fusion.8
  58.3 5.6 %all-to-all-done.1 = bf16[16,160,128]{2,1,0:T(8,128)(2,1)S(1)} async-done(((bf16[16,160,128]{2,1,0:T(8,128)(2,1)}), bf16[16,160,128]{2,1,0:T(8,128)(2,1)S(1)}, u32[]{:S(2)}, u32[]{:S(2)}) %all-to-all-start.1) | async-done | bytes 655392 | tf_op jit(solution)/shard_map/all_to_all | solution.py:35
  64.2 2.0 fusion.8.p0
  66.2 1.6 collective-permute-start.4
  67.8 7.2 %collective-permute-start.3 = (bf16[224,128]{1,0:T(8,128)(2,1)S(1)}, bf16[224,128]{1,0:T(8,128)(2,1)S(1)}, u32[]{:S(2)}, u32[]{:S(2)}) collective-permute-start(bf16[224,128]{1,0:T(8,128)(2,1)S(1)} %fusion.8.p0), channel_id=1, source_target_pairs={{0,2},{1,3},{2,0},{3,1},{4,6},{5,7},{6,4},{7,5},{8,10},{9,11},{10,... | collective-permute-start | bytes 172040 | tf_op jit(solution)/shard_map/ppermute | solution.py:44
  75.2 3.0 %collective-permute-done.3.p2 = bf16[224,128]{1,0:T(8,128)(2,1)S(1)} collective-permute-done((bf16[224,128]{1,0:T(8,128)(2,1)S(1)}, bf16[224,128]{1,0:T(8,128)(2,1)S(1)}, u32[]{:S(2)}, u32[]{:S(2)}) %collective-permute-start.3) | collective-permute-done | bytes 57376 | tf_op jit(solution)/shard_map/ppermute | solution.py:44
  78.1 3.8 %attention.1 = (bf16[32,768]{1,0:T(8,128)(2,1)S(1)}, bf16[32,768]{1,0:T(8,128)(2,1)S(1)}, bf16[32,768]{1,0:T(8,128)(2,1)S(1)}, bf16[32,768]{1,0:T(8,128)(2,1)S(1)}) custom-call(s32[3]{0:T(128)S(1)} %pad_add_fusion.scalars, s32[1,128]{1,0:T(1,128)S(1)} %pad_bitcast_fusion.parent, f32[64,128]{1,0:T(8,128)S(1)} %reshape.176.cosine, ...), custom_call_target="tpu_custom_call" | custom-call | tf_op jit(solution)/shard_map/attention/pallas_call | solution.py:166
  82.6 1.2 collective-permute-start.9
  83.8 2.1 collective-permute-start.10
  85.9 1.1 collective-permute-done.9
  87.1 2.5 %collective-permute-done.10 = bf16[32,768]{1,0:T(8,128)(2,1)S(1)} collective-permute-done((bf16[32,768]{1,0:T(8,128)(2,1)S(1)}, bf16[32,768]{1,0:T(8,128)(2,1)S(1)}, u32[]{:S(2)}, u32[]{:S(2)}) %collective-permute-start.10) | collective-permute-done | bytes 49184 | tf_op jit(solution)/shard_map/ppermute | solution.py:44
  90.2 0.9 collective-permute-start.12
  91.1 2.9 %collective-permute-start.11 = (bf16[32,640]{1,0:T(8,128)(2,1)S(1)}, bf16[32,640]{1,0:T(8,128)(2,1)S(1)}, u32[]{:S(2)}, u32[]{:S(2)}) collective-permute-start(bf16[32,640]{1,0:T(8,128)(2,1)S(1)} %multiply_reduce_fusion.2), channel_id=1, source_target_pairs={{0,12},{1,13},{2,14},{3,15},{4,8},{5,9},{6,10},{7,11},{8,4},{9,5},... | collective-permute-start | bytes 122888 | tf_op jit(solution)/shard_map/ppermute | solution.py:44
  95.0 0.9 collective-permute-done.11
  95.9 3.0 %fusion.15 = bf16[32,640]{1,0:T(8,128)(2,1)S(1)} fusion(bf16[2560,640]{0,1:T(8,128)(2,1)} %all-gather.2.cloned.1.call-done, bf16[32,640]{1,0:T(8,128)(2,1)S(1)} %get-tuple-element.48, bf16[32,640]{1,0:T(8,128)(2,1)S(1)} %get-tuple-element.47, bf16[32,640]{1,0:T(8,128)(2,1)S(1)} %get-tuple-element.46, bf16[32,640]{1,0:T(8,128)(2,1)S(1)} %get-tuple-element.45, ...), kind=kOutput, calls=%fused_computation.24 | convolution fusion | flops 105574400 | bytes 3522560 | tf_op jit(solution)/shard_map/dot_general | solution.py:29
  98.9 0.9 broadcast_in_dim.48
  99.8 6.8 %all-to-all-start.2 = ((bf16[16,32,640]{2,1,0:T(8,128)(2,1)}), bf16[16,32,640]{2,1,0:T(8,128)(2,1)S(1)}, u32[]{:S(2)}, u32[]{:S(2)}) async-start(bf16[16,32,640]{2,1,0:T(8,128)(2,1)} %broadcast_in_dim.48), calls=%async_computation.2 | async-start | bytes 1310720 | tf_op jit(solution)/shard_map/all_to_all | solution.py:35
  107.4 11.6 %all-to-all-done.2 = bf16[16,32,640]{2,1,0:T(8,128)(2,1)S(1)} async-done(((bf16[16,32,640]{2,1,0:T(8,128)(2,1)}), bf16[16,32,640]{2,1,0:T(8,128)(2,1)S(1)}, u32[]{:S(2)}, u32[]{:S(2)}) %all-to-all-start.2) | async-done | bytes 655392 | tf_op jit(solution)/shard_map/all_to_all | solution.py:35
  120.1 1.6 convolution_convert_fusion
  121.7 4.9 %all-to-all-start.3 = ((bf16[16,16,2560]{2,1,0:T(8,128)(2,1)}), bf16[16,16,2560]{2,1,0:T(8,128)(2,1)S(1)}, u32[]{:S(2)}, u32[]{:S(2)}) async-start(bf16[16,16,2560]{2,1,0:T(8,128)(2,1)} %bitcast.148), calls=%async_computation.3 | async-start | bytes 2621440 | tf_op jit(solution)/shard_map/all_to_all | solution.py:511
  126.6 1.9 collective-permute-start.14
  129.2 0.8 slice_convert_fusion
  130.5 1.2 fusion.1
  132.0 1.6 fusion.62
  133.7 1.6 collective-permute-done.15.u1
  135.3 2.8 %collective-permute-done.16.d1 = bf16[384,2560]{1,0:T(8,128)(2,1)} collective-permute-done((bf16[384,2560]{1,0:T(8,128)(2,1)}, bf16[384,2560]{1,0:T(8,128)(2,1)}, u32[]{:S(2)}, u32[]{:S(2)}) %collective-permute-start.16) | collective-permute-done | bytes 1966112 | tf_op jit(solution)/shard_map/ppermute | solution.py:449
  138.1 18.4 %all-to-all-done.3 = bf16[16,16,2560]{2,1,0:T(8,128)(2,1)S(1)} async-done(((bf16[16,16,2560]{2,1,0:T(8,128)(2,1)}), bf16[16,16,2560]{2,1,0:T(8,128)(2,1)S(1)}, u32[]{:S(2)}, u32[]{:S(2)}) %all-to-all-start.3) | async-done | bytes 1310752 | tf_op jit(solution)/shard_map/all_to_all | solution.py:511
  156.5 1.5 copy-done.1
  158.0 1.5 copy-done.2
  159.6 1.5 copy-done.3
  161.1 7.8 %experts.1 = bf16[2560,256]{1,0:T(8,128)(2,1)} custom-call(s32[1]{0:T(128)} %bitcast.expert, bf16[256,2560]{1,0:T(8,128)(2,1)S(1)} %bitcast.136, bf16[64,2560]{1,0:T(8,128)(2,1)S(1)} %bitcast.143, f32[256,64]{1,0:T(8,128)S(1)} %fusion.16.named, bf16[2560,384]{1,0:T(8,128)(2,1)S(1)} %bitcast.138, bf16[2560,384]{1,0:T(8,128)(2,1)S(1)} %bitcast.140, ...), custom_call_target="tpu_custom_call" | custom-call | tf_op jit(solution)/shard_map/experts/pallas_call | solution.py:239
  168.9 9.7 %all-to-all-start.4 = ((bf16[16,160,256]{2,1,0:T(8,128)(2,1)}), bf16[16,160,256]{2,1,0:T(8,128)(2,1)S(1)}, u32[]{:S(2)}, u32[]{:S(2)}) async-start(bf16[16,160,256]{2,1,0:T(8,128)(2,1)} %bitcast.53), calls=%async_computation.4 | async-start | bytes 2621440 | tf_op jit(solution)/shard_map/all_to_all | solution.py:513
  178.6 3.1 %fusion = bf16[2560,128]{0,1:T(8,128)(2,1)} fusion(bf16[192,2560]{1,0:T(8,128)(2,1)S(1)} %copy-done, bf16[128,2560]{1,0:T(8,128)(2,1)S(1)} %multiply_convert_fusion, bf16[2560,192]{0,1:T(8,128)(2,1)} %param.36, f32[128,192]{0,1:T(8,128)S(1)} %fusion.62), kind=kOutput, calls=%fused_computation.3 | convolution fusion | flops 252133376 | bytes 3375104 | tf_op jit(solution)/shard_map/dot_general | solution.py:528
  181.7 1.4 copy.95
  183.1 0.7 dynamic-slice_bitcast_fusion.6
  183.9 3.2 %collective-permute-start.19 = (bf16[4,160,128]{2,1,0:T(8,128)(2,1)S(1)}, bf16[4,160,128]{2,1,0:T(8,128)(2,1)}, u32[]{:S(2)}, u32[]{:S(2)}) collective-permute-start(bf16[4,160,128]{2,1,0:T(8,128)(2,1)S(1)} %get-tuple-element.36), channel_id=1, source_target_pairs={{0,3},{1,2},{2,1},{3,0},{4,7},{5,6},{6,5},{7,4},{8,11},{9,10},{10,... | collective-permute-start | bytes 491528 | tf_op jit(solution)/shard_map/ppermute | solution.py:44
  187.2 13.4 %collective-permute-done.19 = bf16[4,160,128]{2,1,0:T(8,128)(2,1)} collective-permute-done((bf16[4,160,128]{2,1,0:T(8,128)(2,1)S(1)}, bf16[4,160,128]{2,1,0:T(8,128)(2,1)}, u32[]{:S(2)}, u32[]{:S(2)}) %collective-permute-start.19) | collective-permute-done | bytes 163872 | tf_op jit(solution)/shard_map/ppermute | solution.py:44
  200.7 3.5 %collective-permute-done.18 = bf16[4,160,128]{2,1,0:T(8,128)(2,1)} collective-permute-done((bf16[4,160,128]{2,1,0:T(8,128)(2,1)S(1)}, bf16[4,160,128]{2,1,0:T(8,128)(2,1)}, u32[]{:S(2)}, u32[]{:S(2)}) %collective-permute-start.18) | collective-permute-done | bytes 163872 | tf_op jit(solution)/shard_map/ppermute | solution.py:44
  204.2 1.1 fusion.22
  205.3 0.7 collective-permute-start.20
  206.0 1.8 collective-permute-start.22
  207.8 1.0 collective-permute-start.21
  208.8 1.0 constant_dynamic-slice_fusion.1
  210.1 2.1 collective-permute-done.21
  212.2 2.4 collect.1
  214.6 20.1 %all_to_all.30 = bf16[16,160,128]{2,1,0:T(8,128)(2,1)S(1)} all-to-all(bf16[16,160,128]{2,1,0:T(8,128)(2,1)S(1)} %collect.1), channel_id=1, replica_groups=mesh['req'=16,'blk'=16] {'req'}, dimensions={0} | all-to-all | bytes 1310720 | tf_op jit(solution)/shard_map/all_to_all | solution.py:550
  234.8 0.7 copy.97
  (118 shorter events, 12.8 us)
Async XLA Ops:
  6.5 172.1 %copy-start = (bf16[192,2560]{1,0:T(8,128)(2,1)S(1)}, bf16[192,2560]{1,0:T(8,128)(2,1)}, u32[]{:S(2)}) copy-start(bf16[192,2560]{1,0:T(8,128)(2,1)} %param.37) | copy-start | bytes 2949124
  6.5 89.4 %all-gather.2.cloned.1.call-start = ((), (), s32[]{:S(2)}) async-start(), calls=%async_computation.6 | async-start | bytes 4096000 | tf_op jit(solution)/shard_map/all_gather | solution.py:379
  7.3 14.0 %copy-start.7 = (bf16[2560,64]{0,1:T(8,128)(2,1)S(1)}, bf16[2560,64]{0,1:T(8,128)(2,1)}, u32[]{:S(2)}) copy-start(bf16[2560,64]{0,1:T(8,128)(2,1)} %param.22) | copy-start | bytes 983044
  10.0 18.7 %copy-start.11 = (s32[16]{0:T(128)S(1)}, s32[16]{0:T(128)}, u32[]{:S(2)}) copy-start(s32[16]{0:T(128)} %param.26) | copy-start | bytes 196
  10.0 19.3 %copy-start.9 = (s32[16,1,3]{0,1,2:T(1,128)S(1)}, s32[16,1,3]{0,1,2:T(1,128)}, u32[]{:S(2)}) copy-start(s32[16,1,3]{0,1,2:T(1,128)} %param.25) | copy-start | bytes 580
  10.0 21.1 %copy-start.12 = (s32[16]{0:T(128)S(1)}, s32[16]{0:T(128)}, u32[]{:S(2)}) copy-start(s32[16]{0:T(128)} %param.27) | copy-start | bytes 196
  10.9 22.7 %copy-start.6 = (bf16[1,3,128,1024]{3,2,1,0:T(8,128)(2,1)S(1)}, bf16[1,3,128,1024]{3,2,1,0:T(8,128)(2,1)}, u32[]{:S(2)}) copy-start(bf16[1,3,128,1024]{3,2,1,0:T(8,128)(2,1)} %param.24) | copy-start | bytes 2359300
  10.9 29.2 %all-to-all-start = ((bf16[16,168,128]{2,1,0:T(8,128)(2,1)}), bf16[16,168,128]{2,1,0:T(8,128)(2,1)}, u32[]{:S(2)}, u32[]{:S(2)}) async-start(bf16[16,168,128]{2,1,0:T(8,128)(2,1)} %broadcast_in_dim.40), calls=%async_computation | async-start | bytes 1376256 | tf_op jit(solution)/shard_map/all_to_all | solution.py:35
  22.0 29.5 %collective-permute-start = (bf16[2560,32]{0,1:T(8,128)(2,1)}, bf16[2560,32]{0,1:T(8,128)(2,1)}, u32[]{:S(2)}, u32[]{:S(2)}) collective-permute-start(bf16[2560,32]{0,1:T(8,128)(2,1)} %get-tuple-element.40), channel_id=1, source_target_pairs={{0,0},{1,2},{2,4},{3,6},{4,8},{5,10},{6,12},{7,14},{8,1},{9,3},{10... | collective-permute-start | bytes 491528 | tf_op jit(solution)/shard_map/ppermute | solution.py:373
  27.4 24.1 %collective-permute-start.1 = (bf16[2560,32]{0,1:T(8,128)(2,1)}, bf16[2560,32]{0,1:T(8,128)(2,1)}, u32[]{:S(2)}, u32[]{:S(2)}) collective-permute-start(bf16[2560,32]{0,1:T(8,128)(2,1)} %get-tuple-element.41), channel_id=1, source_target_pairs={{0,1},{1,3},{2,5},{3,7},{4,9},{5,11},{6,13},{7,15},{8,0},{9,2},{10... | collective-permute-start | bytes 491528 | tf_op jit(solution)/shard_map/ppermute | solution.py:374
  41.9 22.0 %all-to-all-start.1 = ((bf16[16,160,128]{2,1,0:T(8,128)(2,1)}), bf16[16,160,128]{2,1,0:T(8,128)(2,1)S(1)}, u32[]{:S(2)}, u32[]{:S(2)}) async-start(bf16[16,160,128]{2,1,0:T(8,128)(2,1)} %broadcast_in_dim.42), calls=%async_computation.1 | async-start | bytes 1310720 | tf_op jit(solution)/shard_map/all_to_all | solution.py:35
  53.3 10.9 %copy-start.10 = (f32[2560]{0:T(1024)S(1)}, f32[2560]{0:T(1024)}, u32[]{:S(2)}) copy-start(f32[2560]{0:T(1024)} %param.20) | copy-start | bytes 30724
  54.1 21.0 %collective-permute-start.7 = (bf16[384,256]{1,0:T(8,128)(2,1)}, bf16[384,256]{1,0:T(8,128)(2,1)S(1)}, u32[]{:S(2)}, u32[]{:S(2)}) collective-permute-start(bf16[384,256]{1,0:T(8,128)(2,1)} %get-tuple-element.31), channel_id=1, source_target_pairs={{0,12},{1,13},{2,14},{3,15},{4,8},{5,9},{6,10},{7,11},{8,4},{9,5},... | collective-permute-start | bytes 589832 | tf_op jit(solution)/shard_map/ppermute | solution.py:44
  56.7 18.4 %collective-permute-start.6 = (bf16[384,256]{1,0:T(8,128)(2,1)}, bf16[384,256]{1,0:T(8,128)(2,1)S(1)}, u32[]{:S(2)}, u32[]{:S(2)}) collective-permute-start(bf16[384,256]{1,0:T(8,128)(2,1)} %get-tuple-element.32), channel_id=1, source_target_pairs={{0,8},{1,9},{2,10},{3,11},{4,12},{5,13},{6,14},{7,15},{8,0},{9,1},... | collective-permute-start | bytes 589832 | tf_op jit(solution)/shard_map/ppermute | solution.py:44
  57.3 17.9 %collective-permute-start.5 = (bf16[384,256]{1,0:T(8,128)(2,1)}, bf16[384,256]{1,0:T(8,128)(2,1)S(1)}, u32[]{:S(2)}, u32[]{:S(2)}) collective-permute-start(bf16[384,256]{1,0:T(8,128)(2,1)} %get-tuple-element.33), channel_id=1, source_target_pairs={{0,4},{1,5},{2,6},{3,7},{4,0},{5,1},{6,2},{7,3},{8,12},{9,13},{10,... | collective-permute-start | bytes 589832 | tf_op jit(solution)/shard_map/ppermute | solution.py:44
  66.2 9.0 %collective-permute-start.4 = (bf16[224,128]{1,0:T(8,128)(2,1)S(1)}, bf16[224,128]{1,0:T(8,128)(2,1)S(1)}, u32[]{:S(2)}, u32[]{:S(2)}) collective-permute-start(bf16[224,128]{1,0:T(8,128)(2,1)S(1)} %fusion.8.p0), channel_id=1, source_target_pairs={{0,3},{1,2},{2,1},{3,0},{4,7},{5,6},{6,5},{7,4},{8,11},{9,10},{10,... | collective-permute-start | bytes 172040 | tf_op jit(solution)/shard_map/ppermute | solution.py:44
  67.8 10.3 %collective-permute-start.3 = (bf16[224,128]{1,0:T(8,128)(2,1)S(1)}, bf16[224,128]{1,0:T(8,128)(2,1)S(1)}, u32[]{:S(2)}, u32[]{:S(2)}) collective-permute-start(bf16[224,128]{1,0:T(8,128)(2,1)S(1)} %fusion.8.p0), channel_id=1, source_target_pairs={{0,2},{1,3},{2,0},{3,1},{4,6},{5,7},{6,4},{7,5},{8,10},{9,11},{10,... | collective-permute-start | bytes 172040 | tf_op jit(solution)/shard_map/ppermute | solution.py:44
  75.1 3.1 %collective-permute-start.2 = (bf16[224,128]{1,0:T(8,128)(2,1)S(1)}, bf16[224,128]{1,0:T(8,128)(2,1)S(1)}, u32[]{:S(2)}, u32[]{:S(2)}) collective-permute-start(bf16[224,128]{1,0:T(8,128)(2,1)S(1)} %fusion.8.p0), channel_id=1, source_target_pairs={{0,1},{1,0},{2,3},{3,2},{4,5},{5,4},{6,7},{7,6},{8,9},{9,8},{10,11... | collective-permute-start | bytes 172040 | tf_op jit(solution)/shard_map/ppermute | solution.py:44
  81.9 4.0 %collective-permute-start.8 = (bf16[32,768]{1,0:T(8,128)(2,1)S(1)}, bf16[32,768]{1,0:T(8,128)(2,1)S(1)}, u32[]{:S(2)}, u32[]{:S(2)}) collective-permute-start(bf16[32,768]{1,0:T(8,128)(2,1)S(1)} %get-tuple-element.22), channel_id=1, source_target_pairs={{0,1},{1,0},{2,3},{3,2},{4,5},{5,4},{6,7},{7,6},{8,9},{9,8},{10,11... | collective-permute-start | bytes 147464 | tf_op jit(solution)/shard_map/ppermute | solution.py:44
  82.6 4.5 %collective-permute-start.9 = (bf16[32,768]{1,0:T(8,128)(2,1)S(1)}, bf16[32,768]{1,0:T(8,128)(2,1)S(1)}, u32[]{:S(2)}, u32[]{:S(2)}) collective-permute-start(bf16[32,768]{1,0:T(8,128)(2,1)S(1)} %get-tuple-element.23), channel_id=1, source_target_pairs={{0,2},{1,3},{2,0},{3,1},{4,6},{5,7},{6,4},{7,5},{8,10},{9,11},{10,... | collective-permute-start | bytes 147464 | tf_op jit(solution)/shard_map/ppermute | solution.py:44
  83.8 5.8 %collective-permute-start.10 = (bf16[32,768]{1,0:T(8,128)(2,1)S(1)}, bf16[32,768]{1,0:T(8,128)(2,1)S(1)}, u32[]{:S(2)}, u32[]{:S(2)}) collective-permute-start(bf16[32,768]{1,0:T(8,128)(2,1)S(1)} %get-tuple-element.24), channel_id=1, source_target_pairs={{0,3},{1,2},{2,1},{3,0},{4,7},{5,6},{6,5},{7,4},{8,11},{9,10},{10,... | collective-permute-start | bytes 147464 | tf_op jit(solution)/shard_map/ppermute | solution.py:44
  90.1 4.9 %collective-permute-start.13 = (bf16[32,640]{1,0:T(8,128)(2,1)S(1)}, bf16[32,640]{1,0:T(8,128)(2,1)S(1)}, u32[]{:S(2)}, u32[]{:S(2)}) collective-permute-start(bf16[32,640]{1,0:T(8,128)(2,1)S(1)} %multiply_reduce_fusion.2), channel_id=1, source_target_pairs={{0,4},{1,5},{2,6},{3,7},{4,0},{5,1},{6,2},{7,3},{8,12},{9,13},{10,... | collective-permute-start | bytes 122888 | tf_op jit(solution)/shard_map/ppermute | solution.py:44
  90.2 4.8 %collective-permute-start.12 = (bf16[32,640]{1,0:T(8,128)(2,1)S(1)}, bf16[32,640]{1,0:T(8,128)(2,1)S(1)}, u32[]{:S(2)}, u32[]{:S(2)}) collective-permute-start(bf16[32,640]{1,0:T(8,128)(2,1)S(1)} %multiply_reduce_fusion.2), channel_id=1, source_target_pairs={{0,8},{1,9},{2,10},{3,11},{4,12},{5,13},{6,14},{7,15},{8,0},{9,1},... | collective-permute-start | bytes 122888 | tf_op jit(solution)/shard_map/ppermute | solution.py:44
  91.1 4.7 %collective-permute-start.11 = (bf16[32,640]{1,0:T(8,128)(2,1)S(1)}, bf16[32,640]{1,0:T(8,128)(2,1)S(1)}, u32[]{:S(2)}, u32[]{:S(2)}) collective-permute-start(bf16[32,640]{1,0:T(8,128)(2,1)S(1)} %multiply_reduce_fusion.2), channel_id=1, source_target_pairs={{0,12},{1,13},{2,14},{3,15},{4,8},{5,9},{6,10},{7,11},{8,4},{9,5},... | collective-permute-start | bytes 122888 | tf_op jit(solution)/shard_map/ppermute | solution.py:44
  99.8 19.1 %all-to-all-start.2 = ((bf16[16,32,640]{2,1,0:T(8,128)(2,1)}), bf16[16,32,640]{2,1,0:T(8,128)(2,1)S(1)}, u32[]{:S(2)}, u32[]{:S(2)}) async-start(bf16[16,32,640]{2,1,0:T(8,128)(2,1)} %broadcast_in_dim.48), calls=%async_computation.2 | async-start | bytes 1310720 | tf_op jit(solution)/shard_map/all_to_all | solution.py:35
  119.2 0.7 copy-start.8
  119.8 1.9 copy-start.5
  121.7 34.8 %all-to-all-start.3 = ((bf16[16,16,2560]{2,1,0:T(8,128)(2,1)}), bf16[16,16,2560]{2,1,0:T(8,128)(2,1)S(1)}, u32[]{:S(2)}, u32[]{:S(2)}) async-start(bf16[16,16,2560]{2,1,0:T(8,128)(2,1)} %bitcast.148), calls=%async_computation.3 | async-start | bytes 2621440 | tf_op jit(solution)/shard_map/all_to_all | solution.py:511
  126.6 7.0 %collective-permute-start.14 = (bf16[2560,384]{1,0:T(8,128)(2,1)}, bf16[2560,384]{1,0:T(8,128)(2,1)}, u32[]{:S(2)}, u32[]{:S(2)}) collective-permute-start(bf16[2560,384]{1,0:T(8,128)(2,1)} %bitcast.137), channel_id=1, source_target_pairs={{0,1},{1,0},{2,3},{3,2},{4,5},{5,4},{6,7},{7,6},{8,9},{9,8},{10,11... | collective-permute-start | bytes 5898248 | tf_op jit(solution)/shard_map/ppermute | solution.py:449
  128.5 6.8 %collective-permute-start.15 = (bf16[2560,384]{1,0:T(8,128)(2,1)}, bf16[2560,384]{1,0:T(8,128)(2,1)}, u32[]{:S(2)}, u32[]{:S(2)}) collective-permute-start(bf16[2560,384]{1,0:T(8,128)(2,1)} %bitcast.139), channel_id=1, source_target_pairs={{0,1},{1,0},{2,3},{3,2},{4,5},{5,4},{6,7},{7,6},{8,9},{9,8},{10,11... | collective-permute-start | bytes 5898248 | tf_op jit(solution)/shard_map/ppermute | solution.py:449
  128.6 9.5 %collective-permute-start.16 = (bf16[384,2560]{1,0:T(8,128)(2,1)}, bf16[384,2560]{1,0:T(8,128)(2,1)}, u32[]{:S(2)}, u32[]{:S(2)}) collective-permute-start(bf16[384,2560]{1,0:T(8,128)(2,1)} %bitcast.141), channel_id=1, source_target_pairs={{0,1},{1,0},{2,3},{3,2},{4,5},{5,4},{6,7},{7,6},{8,9},{9,8},{10,11... | collective-permute-start | bytes 5898248 | tf_op jit(solution)/shard_map/ppermute | solution.py:449
  130.5 26.0 %copy-start.4 = (bf16[2560,64]{0,1:T(8,128)(2,1)S(1)}, bf16[2560,64]{0,1:T(8,128)(2,1)}, u32[]{:S(2)}) copy-start(bf16[2560,64]{0,1:T(8,128)(2,1)} %param.31) | copy-start | bytes 983044
  156.5 1.5 copy-start.1
  158.0 1.5 copy-start.2
  159.6 1.5 copy-start.3
  168.9 43.3 %all-to-all-start.4 = ((bf16[16,160,256]{2,1,0:T(8,128)(2,1)}), bf16[16,160,256]{2,1,0:T(8,128)(2,1)S(1)}, u32[]{:S(2)}, u32[]{:S(2)}) async-start(bf16[16,160,256]{2,1,0:T(8,128)(2,1)} %bitcast.53), calls=%async_computation.4 | async-start | bytes 2621440 | tf_op jit(solution)/shard_map/all_to_all | solution.py:513
  183.8 3.4 %collective-permute-start.17 = (bf16[4,160,128]{2,1,0:T(8,128)(2,1)}, bf16[4,160,128]{2,1,0:T(8,128)(2,1)S(1)}, u32[]{:S(2)}, u32[]{:S(2)}) collective-permute-start(bf16[4,160,128]{2,1,0:T(8,128)(2,1)} %get-tuple-element.35), channel_id=1, source_target_pairs={{0,1},{1,0},{2,3},{3,2},{4,5},{5,4},{6,7},{7,6},{8,9},{9,8},{10,11... | collective-permute-start | bytes 491528 | tf_op jit(solution)/shard_map/ppermute | solution.py:44
  183.9 16.7 %collective-permute-start.19 = (bf16[4,160,128]{2,1,0:T(8,128)(2,1)S(1)}, bf16[4,160,128]{2,1,0:T(8,128)(2,1)}, u32[]{:S(2)}, u32[]{:S(2)}) collective-permute-start(bf16[4,160,128]{2,1,0:T(8,128)(2,1)S(1)} %get-tuple-element.36), channel_id=1, source_target_pairs={{0,3},{1,2},{2,1},{3,0},{4,7},{5,6},{6,5},{7,4},{8,11},{9,10},{10,... | collective-permute-start | bytes 491528 | tf_op jit(solution)/shard_map/ppermute | solution.py:44
  187.1 17.0 %collective-permute-start.18 = (bf16[4,160,128]{2,1,0:T(8,128)(2,1)S(1)}, bf16[4,160,128]{2,1,0:T(8,128)(2,1)}, u32[]{:S(2)}, u32[]{:S(2)}) collective-permute-start(bf16[4,160,128]{2,1,0:T(8,128)(2,1)S(1)} %get-tuple-element.37), channel_id=1, source_target_pairs={{0,2},{1,3},{2,0},{3,1},{4,6},{5,7},{6,4},{7,5},{8,10},{9,11},{10,... | collective-permute-start | bytes 491528 | tf_op jit(solution)/shard_map/ppermute | solution.py:44
  205.3 4.6 %collective-permute-start.20 = (bf16[160,128]{1,0:T(8,128)(2,1)S(1)}, bf16[160,128]{1,0:T(8,128)(2,1)S(1)}, u32[]{:S(2)}, u32[]{:S(2)}) collective-permute-start(bf16[160,128]{1,0:T(8,128)(2,1)S(1)} %get-tuple-element.42), channel_id=1, source_target_pairs={{0,4},{1,5},{2,6},{3,7},{4,0},{5,1},{6,2},{7,3},{8,12},{9,13},{10,... | collective-permute-start | bytes 122888 | tf_op jit(solution)/shard_map/ppermute | solution.py:44
  206.0 4.1 %collective-permute-start.22 = (bf16[160,128]{1,0:T(8,128)(2,1)S(1)}, bf16[160,128]{1,0:T(8,128)(2,1)S(1)}, u32[]{:S(2)}, u32[]{:S(2)}) collective-permute-start(bf16[160,128]{1,0:T(8,128)(2,1)S(1)} %get-tuple-element.43), channel_id=1, source_target_pairs={{0,12},{1,13},{2,14},{3,15},{4,8},{5,9},{6,10},{7,11},{8,4},{9,5},... | collective-permute-start | bytes 122888 | tf_op jit(solution)/shard_map/ppermute | solution.py:44
  207.8 4.4 %collective-permute-start.21 = (bf16[160,128]{1,0:T(8,128)(2,1)S(1)}, bf16[160,128]{1,0:T(8,128)(2,1)S(1)}, u32[]{:S(2)}, u32[]{:S(2)}) collective-permute-start(bf16[160,128]{1,0:T(8,128)(2,1)S(1)} %get-tuple-element.44), channel_id=1, source_target_pairs={{0,8},{1,9},{2,10},{3,11},{4,12},{5,13},{6,14},{7,15},{8,0},{9,1},... | collective-permute-start | bytes 122888 | tf_op jit(solution)/shard_map/ppermute | solution.py:44
Sparse Core Ops, SparseCore 0:
  9.2 54.3 all-gather.1

commit v2 on v1

--- a/solution.py
+++ b/solution.py
@@ -251,7 +251,13 @@
         ],
         compiler_params=pltpu.CompilerParams(vmem_limit_bytes=40 << 20),
         name="experts",
-    )(expert, rows, router, named, *blocks)
+    )(
+        expert,
+        rows,
+        router,
+        named,
+        *[pltpu.with_memory_space_constraint(b, pltpu.HBM) for b in blocks],
+    )
 
 
 def collect_kernel(slot, returned, codes, own, out, sums):
@@ -349,9 +355,7 @@
         ],
         axis=0,
     )
-    key_value_weight, prompt, payload = lax.optimization_barrier(
-        (key_value_weight, prompt_cache[0], payload)
-    )
+    prompt, payload = lax.optimization_barrier((prompt_cache[0], payload))
     by_slot = to_all(payload, "req")
     slot = migration[req_index]
     mine = lax.dynamic_index_in_dim(by_slot, slot, 0, False)
@@ -359,6 +363,23 @@
     routes_mine = mine[width_local : width_local + TOPK].astype(jnp.int32).T
     beam_mine = mine[width_local + TOPK, rows:].astype(jnp.int32)
     inputs = to_all(mine[:width_local], "blk").reshape(width, total)
+
+    output_columns = lax.all_gather(
+        output_weight, "blk", axis=1, tiled=True, axis_index_groups=QUAD
+    )
+
+    order = lax.dynamic_index_in_dim(page_table, req_index, 0, False)[0]
+    pages = prompt[order]
+    pages_local = pages.shape[0]
+    by_head = (
+        pages.reshape(pages_local * PAGE, 2, KEY_VALUE_HEADS, HEAD_WIDTH)
+        .transpose(2, 0, 1, 3)
+        .reshape(KEY_VALUE_HEADS, pages_local * PAGE, 2 * HEAD_WIDTH)
+    )
+    key_value_weight, by_head = lax.optimization_barrier((key_value_weight, by_head))
+    caches = group_parts(
+        lambda d: lax.dynamic_index_in_dim(by_head, x_index ^ d, 0, False), SIDE
+    )
 
     half = key_value_weight.shape[1] // 2
     left, right = key_value_weight[:, :half], key_value_weight[:, half:]
@@ -376,23 +397,6 @@
     value_columns = jnp.where(core == 0, second, first)
     projection = jnp.concatenate([query_weight, key_columns, value_columns], axis=1)
 
-    output_columns = lax.all_gather(
-        output_weight, "blk", axis=1, tiled=True, axis_index_groups=QUAD
-    )
-
-    order = lax.dynamic_index_in_dim(page_table, req_index, 0, False)[0]
-    pages = prompt[order]
-    pages_local = pages.shape[0]
-    by_head = (
-        pages.reshape(pages_local * PAGE, 2, KEY_VALUE_HEADS, HEAD_WIDTH)
-        .transpose(2, 0, 1, 3)
-        .reshape(KEY_VALUE_HEADS, pages_local * PAGE, 2 * HEAD_WIDTH)
-    )
-    by_head, by_slot = lax.optimization_barrier((by_head, by_slot))
-    caches = group_parts(
-        lambda d: lax.dynamic_index_in_dim(by_head, x_index ^ d, 0, False), SIDE
-    )
-
     normed = norm_rows(inputs, attention_gain[:, None], 0)
     projected = across(projection, normed).astype(bf16)
     length = cache_lengths[req_index]
@@ -510,6 +514,30 @@
     sent = dot(dispatch, of_step(normed_h)).astype(bf16).reshape(req_count, CAP, width)
     arrived = lax.all_to_all(sent, "req", 0, 0, tiled=True).reshape(req_count * CAP, width)
 
+    act = (jax.nn.silu(dot(normed_h, shared_gate)) * dot(normed_h, shared_up)).astype(bf16)
+    shared_part = lax.dot_general(
+        shared_down, act, (((0,), (1,)), ((), ())), preferred_element_type=f32
+    ).astype(bf16)
+    shared_pieces = shared_part.reshape(SIDE, SIDE, width_local, total)
+    over_q = sum(
+        p.astype(f32)
+        for p in group_parts(
+            lambda d: lax.dynamic_index_in_dim(shared_pieces, q_index ^ d, 1, False), 1
+        )
+    ).astype(bf16)
+    shared = sum(
+        p.astype(f32)
+        for p in group_parts(
+            lambda d: lax.dynamic_index_in_dim(over_q, x_index ^ d, 0, False), SIDE
+        )
+    )
+    own = (
+        lax.dynamic_slice_in_dim(attended, blk_index * width_local, width_local, 1)
+        .T.astype(f32)
+        + shared
+    )
+    arrived, own = lax.optimization_barrier((arrived, own))
+
     returned = lax.all_to_all(
         expert_rows(
             (req_index * per_req + x_index)[None].astype(jnp.int32),
@@ -524,28 +552,6 @@
         tiled=True,
     )
 
-    act = (jax.nn.silu(dot(normed_h, shared_gate)) * dot(normed_h, shared_up)).astype(bf16)
-    shared_part = lax.dot_general(
-        shared_down, act, (((0,), (1,)), ((), ())), preferred_element_type=f32
-    ).astype(bf16)
-    shared_pieces = shared_part.reshape(SIDE, SIDE, width_local, total)
-    over_q = sum(
-        p.astype(f32)
-        for p in group_parts(
-            lambda d: lax.dynamic_index_in_dim(shared_pieces, q_index ^ d, 1, False), 1
-        )
-    ).astype(bf16)
-    shared = sum(
-        p.astype(f32)
-        for p in group_parts(
-            lambda d: lax.dynamic_index_in_dim(over_q, x_index ^ d, 0, False), SIDE
-        )
-    )
-    own = (
-        lax.dynamic_slice_in_dim(attended, blk_index * width_local, width_local, 1)
-        .T.astype(f32)
-        + shared
-    )
     outgoing = collect(slot[None], returned, codes, own)
     final = lax.all_to_all(outgoing, "req", 0, 0, tiled=True)
     return (

time: 246 us -> 239 us (0.972); the launches traced: 242 us -> 238 us
  blocking collectives: 20.1 us -> 55.7 us
  waiting for transfers between devices: 71.1 us -> 47.2 us
  starting transfers between devices: 77.4 us -> 64.8 us
  local copies, waits for them, and re-layouts: 21.2 us -> 16.4 us
    all_to_all x0 -> x1, blocking collectives: none -> 27.6 us  [per_device(): lax.all_to_all(expert_rows((req_index * per_req + x_index)[None].astype(j...]
    all_to_all x1, waiting for transfers between devices: 18.4 us -> 0.01 us  [per_device(): lax.all_to_all(sent, 'req', 0, 0, tiled=True)]
    all_to_all x1 -> x0, starting transfers between devices: 9.72 us -> none  [per_device(): lax.all_to_all(expert_rows((req_index * per_req + x_index)[None].astype(j...]
    all_to_all x1, blocking collectives: 20.1 us -> 28.1 us  [per_device(): final = lax.all_to_all(outgoing, 'req', 0, 0, tiled=True)]
    ppermute x3, waiting for transfers between devices: 4.42 us -> 0.01 us  [per_device(): lax.ppermute(b, 'blk', partners(1))]
    unnamed x30 -> x26, local copies, waits for them, and re-layouts: 5 us -> 0.79 us
  transfers between devices with their start and end apart: 29 -> 28, of which waited for: 14 -> 13; matrix products, arithmetic and copies ran while one was open for 13% -> 13% of each run, Pallas kernels for 2% -> 2%
where the time goes in v2:
time: 239 us; the launch traced here: 238 us
  starting transfers between devices  64.8 us (27%)
  blocking collectives  55.7 us (23%)
  waiting for transfers between devices  47.2 us (20%)
  local copies, waits for them, and re-layouts  16.4 us (7%)
  between operations  15.9 us (7%)
  Pallas kernels  14.8 us (6%)
  matrix products  11.9 us (5%)
  other arithmetic  11.4 us (5%)
    all_to_all x1, blocking collectives, per_device(): final = lax.all_to_all(outgoing, 'req', 0, 0, tiled=True)  28.1 us
    all_to_all x1, blocking collectives, per_device(): lax.all_to_all(expert_rows((req_index * per_req + x_index)[None].astype(j...  27.6 us
    ppermute x18, starting transfers between devices, group_parts(): lax.ppermute(piece_for(d), 'blk', partners(d * stride))  26.4 us
    ppermute x18, waiting for transfers between devices, group_parts(): lax.ppermute(piece_for(d), 'blk', partners(d * stride))  24.8 us
    all_to_all x3, starting transfers between devices, to_all(): return lax.all_to_all(copies, axis, 0, 0, tiled=True)  24.6 us
    all_to_all x3, waiting for transfers between devices, to_all(): return lax.all_to_all(copies, axis, 0, 0, tiled=True)  21.6 us
    pallas_call x1, Pallas kernels, expert_rows(): pl.pallas_call(expert_kernel, out_shape=jax.ShapeDtypeStruct((width, coun...  8.74 us
    dot_general x5, matrix products, dot(): return jnp.dot(a, b, preferred_element_type=f32)  6.64 us
  transfers between devices with their start and end apart: 28, of which 13 were waited for; matrix products, arithmetic and copies ran while one was open for 13% of the time, Pallas kernels for 2%

profile of v2, /device:TPU:1, one launch (start us, length us, event | category | flops | bytes accessed | tf_op | source)
XLA Modules:
  0.0 238.1 jit_solution(17935318916894525776)
XLA Ops:
  6.5 0.7 all-gather.2.cloned.1.call-update
  7.3 0.7 convert_bitcast_fusion
  8.1 0.7 convert_element_type.152
  8.9 0.9 copy.82
  10.0 0.9 broadcast_in_dim.40
  10.9 10.2 %all-to-all-start = ((bf16[16,168,128]{2,1,0:T(8,128)(2,1)}), bf16[16,168,128]{2,1,0:T(8,128)(2,1)}, u32[]{:S(2)}, u32[]{:S(2)}) async-start(bf16[16,168,128]{2,1,0:T(8,128)(2,1)} %broadcast_in_dim.40), calls=%async_computation | async-start | bytes 1376256 | tf_op jit(solution)/shard_map/all_to_all | solution.py:35
  22.6 0.6 copy.89
  24.2 0.8 broadcast_select_fusion.1
  24.9 5.4 %collective-permute-start = (bf16[2560,32]{0,1:T(8,128)(2,1)}, bf16[2560,32]{0,1:T(8,128)(2,1)S(1)}, u32[]{:S(2)}, u32[]{:S(2)}) collective-permute-start(bf16[2560,32]{0,1:T(8,128)(2,1)} %get-tuple-element.44), channel_id=1, source_target_pairs={{0,0},{1,2},{2,4},{3,6},{4,8},{5,10},{6,12},{7,14},{8,1},{9,3},{10... | collective-permute-start | bytes 491528 | tf_op jit(solution)/shard_map/ppermute | solution.py:394
  30.3 1.3 collective-permute-start.1
  31.7 1.6 collective-permute-start.7
  33.3 1.6 collective-permute-start.6
  35.6 0.7 add_convert_fusion
  37.1 0.7 pad_add_fusion.scalars
  41.1 0.8 dynamic-slice_bitcast_fusion.9
  41.9 0.9 broadcast_in_dim.42
  42.8 9.0 %all-to-all-start.1 = ((bf16[16,160,128]{2,1,0:T(8,128)(2,1)}), bf16[16,160,128]{2,1,0:T(8,128)(2,1)S(1)}, u32[]{:S(2)}, u32[]{:S(2)}) async-start(bf16[16,160,128]{2,1,0:T(8,128)(2,1)} %broadcast_in_dim.42), calls=%async_computation.1 | async-start | bytes 1310720 | tf_op jit(solution)/shard_map/all_to_all | solution.py:35
  51.8 1.7 broadcast_select_fusion.3
  53.5 0.8 dynamic-slice_bitcast_fusion.8
  54.4 9.8 %all-to-all-done.1 = bf16[16,160,128]{2,1,0:T(8,128)(2,1)S(1)} async-done(((bf16[16,160,128]{2,1,0:T(8,128)(2,1)}), bf16[16,160,128]{2,1,0:T(8,128)(2,1)S(1)}, u32[]{:S(2)}, u32[]{:S(2)}) %all-to-all-start.1) | async-done | bytes 655392 | tf_op jit(solution)/shard_map/all_to_all | solution.py:35
  64.5 2.0 fusion.8.p0
  66.5 1.6 collective-permute-start.4
  68.1 2.9 %collective-permute-start.3 = (bf16[224,128]{1,0:T(8,128)(2,1)S(1)}, bf16[224,128]{1,0:T(8,128)(2,1)S(1)}, u32[]{:S(2)}, u32[]{:S(2)}) collective-permute-start(bf16[224,128]{1,0:T(8,128)(2,1)S(1)} %fusion.8.p0), channel_id=1, source_target_pairs={{0,2},{1,3},{2,0},{3,1},{4,6},{5,7},{6,4},{7,5},{8,10},{9,11},{10,... | collective-permute-start | bytes 172040 | tf_op jit(solution)/shard_map/ppermute | solution.py:44
  71.0 0.6 collective-permute-done.4.p3
  71.7 2.2 collective-permute-done.3.p2
  73.8 3.7 %attention.1 = (bf16[32,768]{1,0:T(8,128)(2,1)S(1)}, bf16[32,768]{1,0:T(8,128)(2,1)S(1)}, bf16[32,768]{1,0:T(8,128)(2,1)S(1)}, bf16[32,768]{1,0:T(8,128)(2,1)S(1)}) custom-call(s32[3]{0:T(128)S(1)} %pad_add_fusion.scalars, s32[1,128]{1,0:T(1,128)S(1)} %pad_bitcast_fusion.parent, f32[64,128]{1,0:T(8,128)S(1)} %reshape.176.cosine, ...), custom_call_target="tpu_custom_call" | custom-call | tf_op jit(solution)/shard_map/attention/pallas_call | solution.py:166
  77.6 0.9 collective-permute-start.8
  78.4 1.3 collective-permute-start.9
  79.7 2.0 collective-permute-start.10
  81.8 1.1 collective-permute-done.9
  82.9 2.5 %collective-permute-done.10 = bf16[32,768]{1,0:T(8,128)(2,1)S(1)} collective-permute-done((bf16[32,768]{1,0:T(8,128)(2,1)S(1)}, bf16[32,768]{1,0:T(8,128)(2,1)S(1)}, u32[]{:S(2)}, u32[]{:S(2)}) %collective-permute-start.10) | collective-permute-done | bytes 49184 | tf_op jit(solution)/shard_map/ppermute | solution.py:44
  85.9 2.0 collective-permute-start.13
  87.9 2.1 collective-permute-start.12
  90.4 0.7 fusion.52
  91.3 1.3 collective-permute-done.12
  92.6 1.4 collective-permute-done.11
  94.1 3.0 %fusion.15 = bf16[32,640]{1,0:T(8,128)(2,1)S(1)} fusion(bf16[2560,640]{0,1:T(8,128)(2,1)} %all-gather.2.cloned.1.call-done, bf16[32,640]{1,0:T(8,128)(2,1)S(1)} %get-tuple-element.52, bf16[32,640]{1,0:T(8,128)(2,1)S(1)} %get-tuple-element.51, bf16[32,640]{1,0:T(8,128)(2,1)S(1)} %get-tuple-element.50, bf16[32,640]{1,0:T(8,128)(2,1)S(1)} %get-tuple-element.49, ...), kind=kOutput, calls=%fused_computation.24 | convolution fusion | flops 105574400 | bytes 3522560 | tf_op jit(solution)/shard_map/dot_general | solution.py:29
  97.1 0.9 broadcast_in_dim.48
  98.0 5.4 %all-to-all-start.2 = ((bf16[16,32,640]{2,1,0:T(8,128)(2,1)}), bf16[16,32,640]{2,1,0:T(8,128)(2,1)S(1)}, u32[]{:S(2)}, u32[]{:S(2)}) async-start(bf16[16,32,640]{2,1,0:T(8,128)(2,1)} %broadcast_in_dim.48), calls=%async_computation.2 | async-start | bytes 1310720 | tf_op jit(solution)/shard_map/all_to_all | solution.py:35
  104.2 11.7 %all-to-all-done.2 = bf16[16,32,640]{2,1,0:T(8,128)(2,1)S(1)} async-done(((bf16[16,32,640]{2,1,0:T(8,128)(2,1)}), bf16[16,32,640]{2,1,0:T(8,128)(2,1)S(1)}, u32[]{:S(2)}, u32[]{:S(2)}) %all-to-all-start.2) | async-done | bytes 655392 | tf_op jit(solution)/shard_map/all_to_all | solution.py:35
  117.1 1.6 convolution_convert_fusion
  118.6 4.7 %all-to-all-start.3 = ((bf16[16,16,2560]{2,1,0:T(8,128)(2,1)}), bf16[16,16,2560]{2,1,0:T(8,128)(2,1)S(1)}, u32[]{:S(2)}, u32[]{:S(2)}) async-start(bf16[16,16,2560]{2,1,0:T(8,128)(2,1)} %bitcast.143), calls=%async_computation.3 | async-start | bytes 2621440 | tf_op jit(solution)/shard_map/all_to_all | solution.py:515
  123.4 0.8 slice_convert_fusion
  124.4 1.9 collective-permute-start.20
  126.8 1.6 fusion.62
  128.4 3.2 %fusion = bf16[2560,128]{0,1:T(8,128)(2,1)} fusion(bf16[192,2560]{1,0:T(8,128)(2,1)S(1)} %copy-done, bf16[128,2560]{1,0:T(8,128)(2,1)S(1)} %multiply_convert_fusion, bf16[2560,192]{0,1:T(8,128)(2,1)} %param.36, f32[128,192]{0,1:T(8,128)S(1)} %fusion.62), kind=kOutput, calls=%fused_computation.3 | convolution fusion | flops 252133376 | bytes 3375104 | tf_op jit(solution)/shard_map/dot_general | solution.py:518
  131.6 1.4 copy.92
  133.0 0.8 dynamic-slice_bitcast_fusion.6
  134.3 1.0 collective-permute-start.16
  135.3 0.8 collective-permute-done.14
  136.1 1.5 collective-permute-start.15
  137.6 1.2 fusion.1
  138.8 5.4 %collective-permute-done.16 = bf16[4,160,128]{2,1,0:T(8,128)(2,1)S(1)} collective-permute-done((bf16[4,160,128]{2,1,0:T(8,128)(2,1)}, bf16[4,160,128]{2,1,0:T(8,128)(2,1)S(1)}, u32[]{:S(2)}, u32[]{:S(2)}) %collective-permute-start.16) | collective-permute-done | bytes 163872 | tf_op jit(solution)/shard_map/ppermute | solution.py:44
  144.2 8.4 %collective-permute-done.15 = bf16[4,160,128]{2,1,0:T(8,128)(2,1)S(1)} collective-permute-done((bf16[4,160,128]{2,1,0:T(8,128)(2,1)S(1)}, bf16[4,160,128]{2,1,0:T(8,128)(2,1)S(1)}, u32[]{:S(2)}, u32[]{:S(2)}) %collective-permute-start.15) | collective-permute-done | bytes 163872 | tf_op jit(solution)/shard_map/ppermute | solution.py:44
  152.6 1.0 fusion.22
  154.3 4.9 %collective-permute-start.19 = (bf16[160,128]{1,0:T(8,128)(2,1)S(1)}, bf16[160,128]{1,0:T(8,128)(2,1)S(1)}, u32[]{:S(2)}, u32[]{:S(2)}) collective-permute-start(bf16[160,128]{1,0:T(8,128)(2,1)S(1)} %get-tuple-element.47), channel_id=1, source_target_pairs={{0,12},{1,13},{2,14},{3,15},{4,8},{5,9},{6,10},{7,11},{8,4},{9,5},... | collective-permute-start | bytes 122888 | tf_op jit(solution)/shard_map/ppermute | solution.py:44
  159.2 2.1 collective-permute-start.18
  161.3 1.0 constant_dynamic-slice_fusion.2
  162.4 1.1 collective-permute-done.18
  163.6 8.7 %experts.1 = bf16[2560,256]{1,0:T(8,128)(2,1)S(1)} custom-call(s32[1]{0:T(128)} %bitcast.expert, bf16[256,2560]{1,0:T(8,128)(2,1)S(1)} %bitcast.136, bf16[64,2560]{1,0:T(8,128)(2,1)S(1)} %bitcast.138, f32[256,64]{1,0:T(8,128)S(1)} %fusion.16.named, bf16[2560,384]{1,0:T(8,128)(2,1)} %bitcast.153, bf16[2560,384]{1,0:T(8,128)(2,1)} %bitcast.155, ...), custom_call_target="tpu_custom_call" | custom-call | tf_op jit(solution)/shard_map/experts/pallas_call | solution.py:239
  172.3 27.6 %all_to_all.30.returned = bf16[16,160,256]{2,1,0:T(8,128)(2,1)S(1)} all-to-all(bf16[16,160,256]{2,1,0:T(8,128)(2,1)S(1)} %bitcast.137), channel_id=1, replica_groups=mesh['req'=16,'blk'=16] {'blk'}, dimensions={0} | all-to-all | bytes 2621440 | tf_op jit(solution)/shard_map/all_to_all | solution.py:541
  199.9 2.4 collect.1
  202.3 28.1 %all_to_all.31 = bf16[16,160,128]{2,1,0:T(8,128)(2,1)S(1)} all-to-all(bf16[16,160,128]{2,1,0:T(8,128)(2,1)S(1)} %collect.1), channel_id=1, replica_groups=mesh['req'=16,'blk'=16] {'req'}, dimensions={0} | all-to-all | bytes 1310720 | tf_op jit(solution)/shard_map/all_to_all | solution.py:556
  230.5 0.7 copy.97
  (113 shorter events, 11.2 us)
Async XLA Ops:
  6.5 121.9 %copy-start = (bf16[192,2560]{1,0:T(8,128)(2,1)S(1)}, bf16[192,2560]{1,0:T(8,128)(2,1)}, u32[]{:S(2)}) copy-start(bf16[192,2560]{1,0:T(8,128)(2,1)} %param.37) | copy-start | bytes 2949124
  6.5 87.5 %all-gather.2.cloned.1.call-start = ((), (), s32[]{:S(2)}) async-start(), calls=%async_computation.6 | async-start | bytes 4096000 | tf_op jit(solution)/shard_map/all_gather | solution.py:367
  7.3 13.9 %copy-start.6 = (s32[16,1,3]{0,1,2:T(1,128)S(1)}, s32[16,1,3]{0,1,2:T(1,128)}, u32[]{:S(2)}) copy-start(s32[16,1,3]{0,1,2:T(1,128)} %param.25) | copy-start | bytes 580
  7.3 14.1 %copy-start.3 = (bf16[1,3,128,1024]{3,2,1,0:T(8,128)(2,1)S(1)}, bf16[1,3,128,1024]{3,2,1,0:T(8,128)(2,1)}, u32[]{:S(2)}) copy-start(bf16[1,3,128,1024]{3,2,1,0:T(8,128)(2,1)} %param.24) | copy-start | bytes 2359300
  10.9 30.2 %all-to-all-start = ((bf16[16,168,128]{2,1,0:T(8,128)(2,1)}), bf16[16,168,128]{2,1,0:T(8,128)(2,1)}, u32[]{:S(2)}, u32[]{:S(2)}) async-start(bf16[16,168,128]{2,1,0:T(8,128)(2,1)} %broadcast_in_dim.40), calls=%async_computation | async-start | bytes 1376256 | tf_op jit(solution)/shard_map/all_to_all | solution.py:35
  23.2 1.0 copy-start.4
  23.7 11.3 %copy-start.8 = (s32[16]{0:T(128)S(1)}, s32[16]{0:T(128)}, u32[]{:S(2)}) copy-start(s32[16]{0:T(128)} %param.26) | copy-start | bytes 196
  23.7 12.5 %copy-start.9 = (s32[16]{0:T(128)S(1)}, s32[16]{0:T(128)}, u32[]{:S(2)}) copy-start(s32[16]{0:T(128)} %param.27) | copy-start | bytes 196
  24.9 26.9 %collective-permute-start = (bf16[2560,32]{0,1:T(8,128)(2,1)}, bf16[2560,32]{0,1:T(8,128)(2,1)S(1)}, u32[]{:S(2)}, u32[]{:S(2)}) collective-permute-start(bf16[2560,32]{0,1:T(8,128)(2,1)} %get-tuple-element.44), channel_id=1, source_target_pairs={{0,0},{1,2},{2,4},{3,6},{4,8},{5,10},{6,12},{7,14},{8,1},{9,3},{10... | collective-permute-start | bytes 491528 | tf_op jit(solution)/shard_map/ppermute | solution.py:394
  30.3 21.5 %collective-permute-start.1 = (bf16[2560,32]{0,1:T(8,128)(2,1)}, bf16[2560,32]{0,1:T(8,128)(2,1)}, u32[]{:S(2)}, u32[]{:S(2)}) collective-permute-start(bf16[2560,32]{0,1:T(8,128)(2,1)} %get-tuple-element.45), channel_id=1, source_target_pairs={{0,1},{1,3},{2,5},{3,7},{4,9},{5,11},{6,13},{7,15},{8,0},{9,2},{10... | collective-permute-start | bytes 491528 | tf_op jit(solution)/shard_map/ppermute | solution.py:395
  31.7 39.3 %collective-permute-start.7 = (bf16[384,256]{1,0:T(8,128)(2,1)S(1)}, bf16[384,256]{1,0:T(8,128)(2,1)S(1)}, u32[]{:S(2)}, u32[]{:S(2)}) collective-permute-start(bf16[384,256]{1,0:T(8,128)(2,1)S(1)} %get-tuple-element.35), channel_id=1, source_target_pairs={{0,12},{1,13},{2,14},{3,15},{4,8},{5,9},{6,10},{7,11},{8,4},{9,5},... | collective-permute-start | bytes 589832 | tf_op jit(solution)/shard_map/ppermute | solution.py:44
  33.3 37.7 %collective-permute-start.6 = (bf16[384,256]{1,0:T(8,128)(2,1)S(1)}, bf16[384,256]{1,0:T(8,128)(2,1)S(1)}, u32[]{:S(2)}, u32[]{:S(2)}) collective-permute-start(bf16[384,256]{1,0:T(8,128)(2,1)S(1)} %get-tuple-element.36), channel_id=1, source_target_pairs={{0,8},{1,9},{2,10},{3,11},{4,12},{5,13},{6,14},{7,15},{8,0},{9,1},... | collective-permute-start | bytes 589832 | tf_op jit(solution)/shard_map/ppermute | solution.py:44
  34.9 36.2 %collective-permute-start.5 = (bf16[384,256]{1,0:T(8,128)(2,1)S(1)}, bf16[384,256]{1,0:T(8,128)(2,1)S(1)}, u32[]{:S(2)}, u32[]{:S(2)}) collective-permute-start(bf16[384,256]{1,0:T(8,128)(2,1)S(1)} %get-tuple-element.37), channel_id=1, source_target_pairs={{0,4},{1,5},{2,6},{3,7},{4,0},{5,1},{6,2},{7,3},{8,12},{9,13},{10,... | collective-permute-start | bytes 589832 | tf_op jit(solution)/shard_map/ppermute | solution.py:44
  42.8 21.7 %copy-start.7 = (f32[2560]{0:T(1024)S(1)}, f32[2560]{0:T(1024)}, u32[]{:S(2)}) copy-start(f32[2560]{0:T(1024)} %param.20) | copy-start | bytes 30724
  42.8 21.3 %all-to-all-start.1 = ((bf16[16,160,128]{2,1,0:T(8,128)(2,1)}), bf16[16,160,128]{2,1,0:T(8,128)(2,1)S(1)}, u32[]{:S(2)}, u32[]{:S(2)}) async-start(bf16[16,160,128]{2,1,0:T(8,128)(2,1)} %broadcast_in_dim.42), calls=%async_computation.1 | async-start | bytes 1310720 | tf_op jit(solution)/shard_map/all_to_all | solution.py:35
  66.5 5.2 %collective-permute-start.4 = (bf16[224,128]{1,0:T(8,128)(2,1)S(1)}, bf16[224,128]{1,0:T(8,128)(2,1)S(1)}, u32[]{:S(2)}, u32[]{:S(2)}) collective-permute-start(bf16[224,128]{1,0:T(8,128)(2,1)S(1)} %fusion.8.p0), channel_id=1, source_target_pairs={{0,3},{1,2},{2,1},{3,0},{4,7},{5,6},{6,5},{7,4},{8,11},{9,10},{10,... | collective-permute-start | bytes 172040 | tf_op jit(solution)/shard_map/ppermute | solution.py:44
  68.1 5.7 %collective-permute-start.3 = (bf16[224,128]{1,0:T(8,128)(2,1)S(1)}, bf16[224,128]{1,0:T(8,128)(2,1)S(1)}, u32[]{:S(2)}, u32[]{:S(2)}) collective-permute-start(bf16[224,128]{1,0:T(8,128)(2,1)S(1)} %fusion.8.p0), channel_id=1, source_target_pairs={{0,2},{1,3},{2,0},{3,1},{4,6},{5,7},{6,4},{7,5},{8,10},{9,11},{10,... | collective-permute-start | bytes 172040 | tf_op jit(solution)/shard_map/ppermute | solution.py:44
  71.0 2.9 %collective-permute-start.2 = (bf16[224,128]{1,0:T(8,128)(2,1)S(1)}, bf16[224,128]{1,0:T(8,128)(2,1)S(1)}, u32[]{:S(2)}, u32[]{:S(2)}) collective-permute-start(bf16[224,128]{1,0:T(8,128)(2,1)S(1)} %fusion.8.p0), channel_id=1, source_target_pairs={{0,1},{1,0},{2,3},{3,2},{4,5},{5,4},{6,7},{7,6},{8,9},{9,8},{10,11... | collective-permute-start | bytes 172040 | tf_op jit(solution)/shard_map/ppermute | solution.py:44
  77.6 4.2 %collective-permute-start.8 = (bf16[32,768]{1,0:T(8,128)(2,1)S(1)}, bf16[32,768]{1,0:T(8,128)(2,1)S(1)}, u32[]{:S(2)}, u32[]{:S(2)}) collective-permute-start(bf16[32,768]{1,0:T(8,128)(2,1)S(1)} %get-tuple-element.24), channel_id=1, source_target_pairs={{0,1},{1,0},{2,3},{3,2},{4,5},{5,4},{6,7},{7,6},{8,9},{9,8},{10,11... | collective-permute-start | bytes 147464 | tf_op jit(solution)/shard_map/ppermute | solution.py:44
  78.4 4.5 %collective-permute-start.9 = (bf16[32,768]{1,0:T(8,128)(2,1)S(1)}, bf16[32,768]{1,0:T(8,128)(2,1)S(1)}, u32[]{:S(2)}, u32[]{:S(2)}) collective-permute-start(bf16[32,768]{1,0:T(8,128)(2,1)S(1)} %get-tuple-element.25), channel_id=1, source_target_pairs={{0,2},{1,3},{2,0},{3,1},{4,6},{5,7},{6,4},{7,5},{8,10},{9,11},{10,... | collective-permute-start | bytes 147464 | tf_op jit(solution)/shard_map/ppermute | solution.py:44
  79.7 5.7 %collective-permute-start.10 = (bf16[32,768]{1,0:T(8,128)(2,1)S(1)}, bf16[32,768]{1,0:T(8,128)(2,1)S(1)}, u32[]{:S(2)}, u32[]{:S(2)}) collective-permute-start(bf16[32,768]{1,0:T(8,128)(2,1)S(1)} %get-tuple-element.26), channel_id=1, source_target_pairs={{0,3},{1,2},{2,1},{3,0},{4,7},{5,6},{6,5},{7,4},{8,11},{9,10},{10,... | collective-permute-start | bytes 147464 | tf_op jit(solution)/shard_map/ppermute | solution.py:44
  85.9 5.4 %collective-permute-start.13 = (bf16[32,640]{1,0:T(8,128)(2,1)S(1)}, bf16[32,640]{1,0:T(8,128)(2,1)S(1)}, u32[]{:S(2)}, u32[]{:S(2)}) collective-permute-start(bf16[32,640]{1,0:T(8,128)(2,1)S(1)} %multiply_reduce_fusion.2), channel_id=1, source_target_pairs={{0,4},{1,5},{2,6},{3,7},{4,0},{5,1},{6,2},{7,3},{8,12},{9,13},{10,... | collective-permute-start | bytes 122888 | tf_op jit(solution)/shard_map/ppermute | solution.py:44
  87.9 4.7 %collective-permute-start.12 = (bf16[32,640]{1,0:T(8,128)(2,1)S(1)}, bf16[32,640]{1,0:T(8,128)(2,1)S(1)}, u32[]{:S(2)}, u32[]{:S(2)}) collective-permute-start(bf16[32,640]{1,0:T(8,128)(2,1)S(1)} %multiply_reduce_fusion.2), channel_id=1, source_target_pairs={{0,8},{1,9},{2,10},{3,11},{4,12},{5,13},{6,14},{7,15},{8,0},{9,1},... | collective-permute-start | bytes 122888 | tf_op jit(solution)/shard_map/ppermute | solution.py:44
  90.0 4.1 %collective-permute-start.11 = (bf16[32,640]{1,0:T(8,128)(2,1)S(1)}, bf16[32,640]{1,0:T(8,128)(2,1)S(1)}, u32[]{:S(2)}, u32[]{:S(2)}) collective-permute-start(bf16[32,640]{1,0:T(8,128)(2,1)S(1)} %multiply_reduce_fusion.2), channel_id=1, source_target_pairs={{0,12},{1,13},{2,14},{3,15},{4,8},{5,9},{6,10},{7,11},{8,4},{9,5},... | collective-permute-start | bytes 122888 | tf_op jit(solution)/shard_map/ppermute | solution.py:44
  98.0 17.9 %all-to-all-start.2 = ((bf16[16,32,640]{2,1,0:T(8,128)(2,1)}), bf16[16,32,640]{2,1,0:T(8,128)(2,1)S(1)}, u32[]{:S(2)}, u32[]{:S(2)}) async-start(bf16[16,32,640]{2,1,0:T(8,128)(2,1)} %broadcast_in_dim.48), calls=%async_computation.2 | async-start | bytes 1310720 | tf_op jit(solution)/shard_map/all_to_all | solution.py:35
  116.1 0.7 copy-start.5
  116.7 1.9 copy-start.2
  118.6 44.9 %all-to-all-start.3 = ((bf16[16,16,2560]{2,1,0:T(8,128)(2,1)}), bf16[16,16,2560]{2,1,0:T(8,128)(2,1)S(1)}, u32[]{:S(2)}, u32[]{:S(2)}) async-start(bf16[16,16,2560]{2,1,0:T(8,128)(2,1)} %bitcast.143), calls=%async_computation.3 | async-start | bytes 2621440 | tf_op jit(solution)/shard_map/all_to_all | solution.py:515
  124.4 39.1 %collective-permute-start.20 = (bf16[2560,384]{1,0:T(8,128)(2,1)}, bf16[2560,384]{1,0:T(8,128)(2,1)}, u32[]{:S(2)}, u32[]{:S(2)}) collective-permute-start(bf16[2560,384]{1,0:T(8,128)(2,1)} %bitcast.152), channel_id=1, source_target_pairs={{0,1},{1,0},{2,3},{3,2},{4,5},{5,4},{6,7},{7,6},{8,9},{9,8},{10,11... | collective-permute-start | bytes 5898248 | tf_op jit(solution)/shard_map/ppermute | solution.py:453
  126.3 37.3 %collective-permute-start.21 = (bf16[2560,384]{1,0:T(8,128)(2,1)}, bf16[2560,384]{1,0:T(8,128)(2,1)}, u32[]{:S(2)}, u32[]{:S(2)}) collective-permute-start(bf16[2560,384]{1,0:T(8,128)(2,1)} %bitcast.154), channel_id=1, source_target_pairs={{0,1},{1,0},{2,3},{3,2},{4,5},{5,4},{6,7},{7,6},{8,9},{9,8},{10,11... | collective-permute-start | bytes 5898248 | tf_op jit(solution)/shard_map/ppermute | solution.py:453
  126.4 37.2 %collective-permute-start.22 = (bf16[384,2560]{1,0:T(8,128)(2,1)}, bf16[384,2560]{1,0:T(8,128)(2,1)}, u32[]{:S(2)}, u32[]{:S(2)}) collective-permute-start(bf16[384,2560]{1,0:T(8,128)(2,1)} %bitcast.156), channel_id=1, source_target_pairs={{0,1},{1,0},{2,3},{3,2},{4,5},{5,4},{6,7},{7,6},{8,9},{9,8},{10,11... | collective-permute-start | bytes 5898248 | tf_op jit(solution)/shard_map/ppermute | solution.py:453
  131.6 2.3 copy-start.10
  133.9 2.2 collective-permute-start.14
  134.2 29.4 %copy-start.1 = (bf16[2560,64]{0,1:T(8,128)(2,1)S(1)}, bf16[2560,64]{0,1:T(8,128)(2,1)}, u32[]{:S(2)}) copy-start(bf16[2560,64]{0,1:T(8,128)(2,1)} %param.31) | copy-start | bytes 983044
  134.3 9.9 %collective-permute-start.16 = (bf16[4,160,128]{2,1,0:T(8,128)(2,1)}, bf16[4,160,128]{2,1,0:T(8,128)(2,1)S(1)}, u32[]{:S(2)}, u32[]{:S(2)}) collective-permute-start(bf16[4,160,128]{2,1,0:T(8,128)(2,1)} %get-tuple-element.40), channel_id=1, source_target_pairs={{0,3},{1,2},{2,1},{3,0},{4,7},{5,6},{6,5},{7,4},{8,11},{9,10},{10,... | collective-permute-start | bytes 491528 | tf_op jit(solution)/shard_map/ppermute | solution.py:44
  136.1 16.5 %collective-permute-start.15 = (bf16[4,160,128]{2,1,0:T(8,128)(2,1)S(1)}, bf16[4,160,128]{2,1,0:T(8,128)(2,1)S(1)}, u32[]{:S(2)}, u32[]{:S(2)}) collective-permute-start(bf16[4,160,128]{2,1,0:T(8,128)(2,1)S(1)} %get-tuple-element.41), channel_id=1, source_target_pairs={{0,2},{1,3},{2,0},{3,1},{4,6},{5,7},{6,4},{7,5},{8,10},{9,11},{10,... | collective-permute-start | bytes 491528 | tf_op jit(solution)/shard_map/ppermute | solution.py:44
  153.6 5.5 %collective-permute-start.17 = (bf16[160,128]{1,0:T(8,128)(2,1)S(1)}, bf16[160,128]{1,0:T(8,128)(2,1)S(1)}, u32[]{:S(2)}, u32[]{:S(2)}) collective-permute-start(bf16[160,128]{1,0:T(8,128)(2,1)S(1)} %get-tuple-element.46), channel_id=1, source_target_pairs={{0,4},{1,5},{2,6},{3,7},{4,0},{5,1},{6,2},{7,3},{8,12},{9,13},{10,... | collective-permute-start | bytes 122888 | tf_op jit(solution)/shard_map/ppermute | solution.py:44
  154.3 8.1 %collective-permute-start.19 = (bf16[160,128]{1,0:T(8,128)(2,1)S(1)}, bf16[160,128]{1,0:T(8,128)(2,1)S(1)}, u32[]{:S(2)}, u32[]{:S(2)}) collective-permute-start(bf16[160,128]{1,0:T(8,128)(2,1)S(1)} %get-tuple-element.47), channel_id=1, source_target_pairs={{0,12},{1,13},{2,14},{3,15},{4,8},{5,9},{6,10},{7,11},{8,4},{9,5},... | collective-permute-start | bytes 122888 | tf_op jit(solution)/shard_map/ppermute | solution.py:44
  159.2 4.4 %collective-permute-start.18 = (bf16[160,128]{1,0:T(8,128)(2,1)S(1)}, bf16[160,128]{1,0:T(8,128)(2,1)S(1)}, u32[]{:S(2)}, u32[]{:S(2)}) collective-permute-start(bf16[160,128]{1,0:T(8,128)(2,1)S(1)} %get-tuple-element.48), channel_id=1, source_target_pairs={{0,8},{1,9},{2,10},{3,11},{4,12},{5,13},{6,14},{7,15},{8,0},{9,1},... | collective-permute-start | bytes 122888 | tf_op jit(solution)/shard_map/ppermute | solution.py:44
Sparse Core Ops, SparseCore 0:
  9.2 54.2 all-gather.1

commit v3 on v2

--- a/solution.py
+++ b/solution.py
@@ -82,6 +82,38 @@
 
 def across(a, b):
     return lax.dot_general(a, b, (((0,), (0,)), ((), ())), preferred_element_type=f32)
+
+
+def payload_kernel(x, routes, beams, out, lines):
+    total, width = x.shape
+    rows = total // 2
+    main = width // 128 * 128
+    lines[:main, :] = x[:, :main].astype(f32).T.astype(bf16)
+    rest = jnp.concatenate(
+        [x[:, main:].astype(f32), jnp.zeros((total, 128 - width + main), f32)], axis=1
+    )
+    lines[main:width, :] = rest.T[: width - main].astype(bf16)
+    named = [
+        jnp.concatenate([routes[k, 0:1, :], routes[k, 1:2, :]], axis=1) for k in range(TOPK)
+    ]
+    beam = jnp.concatenate([jnp.zeros((1, rows), jnp.int32), beams[...]], axis=1)
+    extra = jnp.concatenate(named + [beam, jnp.zeros((1, total), jnp.int32)], axis=0)
+    lines[width:, :] = extra.astype(f32).astype(bf16)
+    for i in range(out.shape[0]):
+        out[i] = lines[...]
+
+
+def payloads(count, x, routes, beams):
+    total, width = x.shape
+    vmem = pl.BlockSpec(memory_space=pltpu.VMEM)
+    return pl.pallas_call(
+        payload_kernel,
+        out_shape=jax.ShapeDtypeStruct((count, width + TOPK + 2, total), bf16),
+        in_specs=[vmem] * 3,
+        out_specs=vmem,
+        scratch_shapes=[pltpu.VMEM((width + TOPK + 2, total), bf16)],
+        name="payload",
+    )(x, routes, beams)
 
 
 def attention_kernel(
@@ -198,6 +230,14 @@
     for i, k in order:
         copies[i][k].start()
     width = down_w.shape[2]
+    logits = lax.dot_general(
+        rows[...], router[...], (((1,), (1,)), ((), ())), preferred_element_type=f32
+    )
+    raised = jnp.where(named[...] > 0.0, jnp.exp(logits), 0.0)
+    column = lax.broadcasted_iota(jnp.int32, raised.shape, 1)
+    total = jnp.sum(raised, axis=1, keepdims=True)
+    picked = jnp.sum(jnp.where(column == expert[0], raised, 0.0), axis=1, keepdims=True)
+    weight = picked / jnp.where(total > 0.0, total, 1.0)
     hidden = []
     for i in (0, 1):
         copies[i][0].wait()
@@ -205,14 +245,6 @@
         copies[i][1].wait()
         lifted = dot(rows[...], up_w[i])
         hidden.append((gated / (1.0 + jnp.exp(-gated)) * lifted).astype(bf16))
-    logits = lax.dot_general(
-        rows[...], router[...], (((1,), (1,)), ((), ())), preferred_element_type=f32
-    )
-    raised = jnp.where(named[...] > 0.0, jnp.exp(logits), 0.0)
-    column = lax.broadcasted_iota(jnp.int32, raised.shape, 1)
-    total = jnp.sum(raised, axis=1, keepdims=True)
-    picked = jnp.sum(jnp.where(column == expert[0], raised, 0.0), axis=1, keepdims=True)
-    weight = picked / jnp.where(total > 0.0, total, 1.0)
     copies[0][2].wait()
     copies[1][2].wait()
     step = width // out_sems.shape[0]
@@ -345,18 +377,14 @@
     span = heads_here * HEAD_WIDTH
     subset = total // SIDE
 
-    beam = jnp.concatenate([jnp.zeros((rows,), jnp.int32), parents.reshape(-1)])
-    payload = jnp.concatenate(
-        [
-            step_inputs.reshape(total, width_local).T,
-            routes.reshape(total, TOPK).T.astype(bf16),
-            beam.astype(bf16)[None],
-            jnp.zeros((1, total), bf16),
-        ],
-        axis=0,
+    payload = payloads(
+        req_count,
+        step_inputs.reshape(total, width_local),
+        routes.transpose(2, 0, 1),
+        parents,
     )
     prompt, payload = lax.optimization_barrier((prompt_cache[0], payload))
-    by_slot = to_all(payload, "req")
+    by_slot = lax.all_to_all(payload, "req", 0, 0, tiled=True)
     slot = migration[req_index]
     mine = lax.dynamic_index_in_dim(by_slot, slot, 0, False)
     routes_all = by_slot[:, width_local : width_local + TOPK].astype(jnp.int32)
@@ -518,12 +546,17 @@
     shared_part = lax.dot_general(
         shared_down, act, (((0,), (1,)), ((), ())), preferred_element_type=f32
     ).astype(bf16)
-    shared_pieces = shared_part.reshape(SIDE, SIDE, width_local, total)
-    over_q = sum(
-        p.astype(f32)
-        for p in group_parts(
-            lambda d: lax.dynamic_index_in_dim(shared_pieces, q_index ^ d, 1, False), 1
-        )
+    q_high = q_index // 2
+    halves = shared_part.reshape(SIDE, 2, 2, width_local, total)
+    pair = lax.dynamic_index_in_dim(halves, core, 2, False).astype(f32) + lax.ppermute(
+        lax.dynamic_index_in_dim(halves, 1 - core, 2, False), "blk", partners(1)
+    ).astype(f32)
+    quads = pair.astype(bf16)
+    over_q = (
+        lax.dynamic_index_in_dim(pair, q_high, 1, False)
+        + lax.ppermute(
+            lax.dynamic_index_in_dim(quads, 1 - q_high, 1, False), "blk", partners(2)
+        ).astype(f32)
     ).astype(bf16)
     shared = sum(
         p.astype(f32)

time: 239 us -> 230 us (0.962)
  starting transfers between devices: 64.8 us -> 58.3 us
  local copies, waits for them, and re-layouts: 16.4 us -> 12.4 us
  blocking collectives: 55.7 us -> 58.7 us
    ppermute x18 -> x15, waiting for transfers between devices: 24.8 us -> 13.2 us  [group_parts(): lax.ppermute(piece_for(d), 'blk', partners(d * stride))]
    all_to_all x3 -> x2, starting transfers between devices: 24.6 us -> 13.8 us  [to_all(): return lax.all_to_all(copies, axis, 0, 0, tiled=True)]
    all_to_all x0 -> x1, starting transfers between devices: none -> 10.1 us  [per_device(): by_slot = lax.all_to_all(payload, 'req', 0, 0, tiled=True)]
    ppermute x18 -> x15, starting transfers between devices: 26.4 us -> 18.8 us  [group_parts(): lax.ppermute(piece_for(d), 'blk', partners(d * stride))]
    ppermute x0 -> x2, waiting for transfers between devices: none -> 7.04 us  [the longest x1 5.95 us: per_device(): lax.ppermute(lax.dynamic_index_in_dim(quads, 1 - q_high, 1, False), 'blk'...]
    all_to_all x1, waiting for transfers between devices: 0.01 us -> 3.59 us  [per_device(): lax.all_to_all(sent, 'req', 0, 0, tiled=True)]
    ppermute x0 -> x2, starting transfers between devices: none -> 2.64 us  [the longest x1 1.9 us: per_device(): lax.ppermute(lax.dynamic_index_in_dim(halves, 1 - core, 2, False), 'blk',...]
    all_to_all x3 -> x2, waiting for transfers between devices: 21.6 us -> 20.8 us  [to_all(): return lax.all_to_all(copies, axis, 0, 0, tiled=True)]
  transfers between devices with their start and end apart: 28 -> 27, of which waited for: 13 -> 13; matrix products, arithmetic and copies ran while one was open for 13% -> 13% of each run, Pallas kernels for 2% -> 2%
where the time goes in v3:
time: 230 us; the launch traced here: 229 us
  blocking collectives  58.7 us (26%)
  starting transfers between devices  58.3 us (25%)
  waiting for transfers between devices  45.3 us (20%)
  Pallas kernels  16.8 us (7%)
  between operations  16 us (7%)
  local copies, waits for them, and re-layouts  12.4 us (5%)
  matrix products  11.9 us (5%)
  other arithmetic  9.63 us (4%)
    all_to_all x1, blocking collectives, per_device(): lax.all_to_all(expert_rows((req_index * per_req + x_index)[None].astype(j...  29.7 us
    all_to_all x1, blocking collectives, per_device(): final = lax.all_to_all(outgoing, 'req', 0, 0, tiled=True)  29 us
    all_to_all x2, waiting for transfers between devices, to_all(): return lax.all_to_all(copies, axis, 0, 0, tiled=True)  20.8 us
    ppermute x15, starting transfers between devices, group_parts(): lax.ppermute(piece_for(d), 'blk', partners(d * stride))  18.8 us
    all_to_all x2, starting transfers between devices, to_all(): return lax.all_to_all(copies, axis, 0, 0, tiled=True)  13.8 us
    ppermute x15, waiting for transfers between devices, group_parts(): lax.ppermute(piece_for(d), 'blk', partners(d * stride))  13.2 us
    all_to_all x1, starting transfers between devices, per_device(): by_slot = lax.all_to_all(payload, 'req', 0, 0, tiled=True)  10.1 us
    pallas_call x1, Pallas kernels, expert_rows(): pl.pallas_call(expert_kernel, out_shape=jax.ShapeDtypeStruct((width, coun...  8.85 us
  transfers between devices with their start and end apart: 27, of which 13 were waited for; matrix products, arithmetic and copies ran while one was open for 13% of the time, Pallas kernels for 2%

profile of v3, /device:TPU:1, one launch (start us, length us, event | category | flops | bytes accessed | tf_op | source)
XLA Modules:
  0.0 229.1 jit_solution(13693547464473930058)
XLA Ops:
  6.5 0.7 all-gather.2.cloned.1.call-update
  7.3 1.9 payload.1
  9.2 10.1 %all-to-all-start = ((bf16[16,168,128]{2,1,0:T(8,128)(2,1)}), bf16[16,168,128]{2,1,0:T(8,128)(2,1)S(1)}, u32[]{:S(2)}, u32[]{:S(2)}) async-start(bf16[16,168,128]{2,1,0:T(8,128)(2,1)} %payload.1), calls=%async_computation | async-start | bytes 1376256 | tf_op jit(solution)/shard_map/all_to_all | solution.py:387
  19.6 0.6 gather_fusion
  20.2 0.6 reshape.170
  20.7 0.6 copy.80
  21.4 0.5 reshape.171
  21.9 1.8 broadcast_select_fusion.1
  23.7 5.4 %collective-permute-start = (bf16[2560,32]{0,1:T(8,128)(2,1)}, bf16[2560,32]{0,1:T(8,128)(2,1)S(1)}, u32[]{:S(2)}, u32[]{:S(2)}) collective-permute-start(bf16[2560,32]{0,1:T(8,128)(2,1)} %get-tuple-element.41), channel_id=1, source_target_pairs={{0,0},{1,2},{2,4},{3,6},{4,8},{5,10},{6,12},{7,14},{8,1},{9,3},{10... | collective-permute-start | bytes 491528 | tf_op jit(solution)/shard_map/ppermute | solution.py:422
  29.0 1.3 collective-permute-start.1
  30.3 0.8 dynamic-slice_bitcast_fusion.1
  31.2 1.5 collective-permute-start.7
  32.7 1.5 collective-permute-start.6
  34.4 0.6 dynamic_slice.87
  35.1 0.6 add_convert_fusion
  35.9 0.7 pad_add_fusion.scalars
  36.6 0.6 dynamic_slice.81.slot
  40.0 1.0 broadcast_in_dim.27
  41.0 8.4 %all-to-all-start.1 = ((bf16[16,160,128]{2,1,0:T(8,128)(2,1)}), bf16[16,160,128]{2,1,0:T(8,128)(2,1)S(1)}, u32[]{:S(2)}, u32[]{:S(2)}) async-start(bf16[16,160,128]{2,1,0:T(8,128)(2,1)} %broadcast_in_dim.27), calls=%async_computation.1 | async-start | bytes 1310720 | tf_op jit(solution)/shard_map/all_to_all | solution.py:35
  49.4 1.7 broadcast_select_fusion.3
  51.3 10.5 %all-to-all-done.1 = bf16[16,160,128]{2,1,0:T(8,128)(2,1)S(1)} async-done(((bf16[16,160,128]{2,1,0:T(8,128)(2,1)}), bf16[16,160,128]{2,1,0:T(8,128)(2,1)S(1)}, u32[]{:S(2)}, u32[]{:S(2)}) %all-to-all-start.1) | async-done | bytes 655392 | tf_op jit(solution)/shard_map/all_to_all | solution.py:35
  62.1 2.0 fusion.8.p0
  64.1 1.6 collective-permute-start.4
  65.7 2.9 %collective-permute-start.3 = (bf16[224,128]{1,0:T(8,128)(2,1)S(1)}, bf16[224,128]{1,0:T(8,128)(2,1)S(1)}, u32[]{:S(2)}, u32[]{:S(2)}) collective-permute-start(bf16[224,128]{1,0:T(8,128)(2,1)S(1)} %fusion.8.p0), channel_id=1, source_target_pairs={{0,2},{1,3},{2,0},{3,1},{4,6},{5,7},{6,4},{7,5},{8,10},{9,11},{10,... | collective-permute-start | bytes 172040 | tf_op jit(solution)/shard_map/ppermute | solution.py:44
  68.7 0.6 collective-permute-done.4.p3
  69.3 2.2 collective-permute-done.3.p2
  71.4 3.7 %attention.1 = (bf16[32,768]{1,0:T(8,128)(2,1)S(1)}, bf16[32,768]{1,0:T(8,128)(2,1)S(1)}, bf16[32,768]{1,0:T(8,128)(2,1)S(1)}, bf16[32,768]{1,0:T(8,128)(2,1)S(1)}) custom-call(s32[3]{0:T(128)S(1)} %pad_add_fusion.scalars, s32[1,128]{1,0:T(1,128)S(1)} %pad_bitcast_fusion.parent, f32[64,128]{1,0:T(8,128)S(1)} %reshape.168.cosine, ...), custom_call_target="tpu_custom_call" | custom-call | tf_op jit(solution)/shard_map/attention/pallas_call | solution.py:198
  75.2 0.9 collective-permute-start.8
  76.1 1.3 collective-permute-start.9
  77.3 2.0 collective-permute-start.10
  79.5 1.0 collective-permute-done.9
  80.5 2.5 %collective-permute-done.10 = bf16[32,768]{1,0:T(8,128)(2,1)S(1)} collective-permute-done((bf16[32,768]{1,0:T(8,128)(2,1)S(1)}, bf16[32,768]{1,0:T(8,128)(2,1)S(1)}, u32[]{:S(2)}, u32[]{:S(2)}) %collective-permute-start.10) | collective-permute-done | bytes 49184 | tf_op jit(solution)/shard_map/ppermute | solution.py:44
  83.5 2.0 collective-permute-start.13
  85.5 2.1 collective-permute-start.12
  88.4 1.8 collective-permute-done.12
  90.2 1.4 collective-permute-done.11
  91.7 3.0 %fusion.15 = bf16[32,640]{1,0:T(8,128)(2,1)S(1)} fusion(bf16[2560,640]{0,1:T(8,128)(2,1)} %all-gather.2.cloned.1.call-done, bf16[32,640]{1,0:T(8,128)(2,1)S(1)} %get-tuple-element.49, bf16[32,640]{1,0:T(8,128)(2,1)S(1)} %get-tuple-element.48, bf16[32,640]{1,0:T(8,128)(2,1)S(1)} %get-tuple-element.47, bf16[32,640]{1,0:T(8,128)(2,1)S(1)} %get-tuple-element.46, ...), kind=kOutput, calls=%fused_computation.24 | convolution fusion | flops 105574400 | bytes 3522560 | tf_op jit(solution)/shard_map/dot_general | solution.py:29
  94.7 0.9 broadcast_in_dim.35
  95.6 5.4 %all-to-all-start.2 = ((bf16[16,32,640]{2,1,0:T(8,128)(2,1)}), bf16[16,32,640]{2,1,0:T(8,128)(2,1)S(1)}, u32[]{:S(2)}, u32[]{:S(2)}) async-start(bf16[16,32,640]{2,1,0:T(8,128)(2,1)} %broadcast_in_dim.35), calls=%async_computation.2 | async-start | bytes 1310720 | tf_op jit(solution)/shard_map/all_to_all | solution.py:35
  101.1 0.8 slice_convert_fusion
  103.2 10.3 %all-to-all-done.2 = bf16[16,32,640]{2,1,0:T(8,128)(2,1)S(1)} async-done(((bf16[16,32,640]{2,1,0:T(8,128)(2,1)}), bf16[16,32,640]{2,1,0:T(8,128)(2,1)S(1)}, u32[]{:S(2)}, u32[]{:S(2)}) %all-to-all-start.2) | async-done | bytes 655392 | tf_op jit(solution)/shard_map/all_to_all | solution.py:35
  113.7 0.5 copy.81
  114.6 1.6 convolution_convert_fusion
  116.2 5.5 %all-to-all-start.3 = ((bf16[16,16,2560]{2,1,0:T(8,128)(2,1)}), bf16[16,16,2560]{2,1,0:T(8,128)(2,1)S(1)}, u32[]{:S(2)}, u32[]{:S(2)}) async-start(bf16[16,16,2560]{2,1,0:T(8,128)(2,1)} %bitcast.135), calls=%async_computation.3 | async-start | bytes 2621440 | tf_op jit(solution)/shard_map/all_to_all | solution.py:543
  121.7 1.6 fusion.61
  123.3 3.2 %fusion = bf16[2560,128]{0,1:T(8,128)(2,1)} fusion(bf16[192,2560]{1,0:T(8,128)(2,1)S(1)} %copy-done, bf16[128,2560]{1,0:T(8,128)(2,1)S(1)} %multiply_convert_fusion, bf16[2560,192]{0,1:T(8,128)(2,1)} %param.36, f32[128,192]{0,1:T(8,128)S(1)} %fusion.61), kind=kOutput, calls=%fused_computation.3 | convolution fusion | flops 252133376 | bytes 3375104 | tf_op jit(solution)/shard_map/dot_general | solution.py:546
  126.5 1.4 copy.83
  127.9 1.9 collective-permute-start.14
  130.1 1.1 collective-permute-done.14
  131.2 1.0 convert_add_fusion
  132.3 0.7 collective-permute-start.15
  133.1 1.2 fusion.1
  134.3 6.0 %collective-permute-done.15 = bf16[4,160,128]{2,1,0:T(8,128)(2,1)S(1)} collective-permute-done((bf16[4,160,128]{2,1,0:T(8,128)(2,1)S(1)}, bf16[4,160,128]{2,1,0:T(8,128)(2,1)S(1)}, u32[]{:S(2)}, u32[]{:S(2)}) %collective-permute-start.15) | collective-permute-done | bytes 163872 | tf_op jit(solution)/shard_map/ppermute | solution.py:557
  140.7 1.4 collective-permute-start.18
  142.1 1.1 collective-permute-done.16
  143.2 1.0 collective-permute-start.17
  144.3 1.0 constant_dynamic-slice_fusion.2
  145.4 2.5 %collective-permute-done.17 = bf16[160,128]{1,0:T(8,128)(2,1)S(1)} collective-permute-done((bf16[160,128]{1,0:T(8,128)(2,1)S(1)}, bf16[160,128]{1,0:T(8,128)(2,1)S(1)}, u32[]{:S(2)}, u32[]{:S(2)}) %collective-permute-start.17) | collective-permute-done | bytes 40992 | tf_op jit(solution)/shard_map/ppermute | solution.py:44
  147.9 3.6 %all-to-all-done.3 = bf16[16,16,2560]{2,1,0:T(8,128)(2,1)S(1)} async-done(((bf16[16,16,2560]{2,1,0:T(8,128)(2,1)}), bf16[16,16,2560]{2,1,0:T(8,128)(2,1)S(1)}, u32[]{:S(2)}, u32[]{:S(2)}) %all-to-all-start.3) | async-done | bytes 1310752 | tf_op jit(solution)/shard_map/all_to_all | solution.py:543
  151.5 8.9 %experts.1 = bf16[2560,256]{1,0:T(8,128)(2,1)S(1)} custom-call(s32[1]{0:T(128)} %bitcast.expert, bf16[256,2560]{1,0:T(8,128)(2,1)S(1)} %bitcast.128, bf16[64,2560]{1,0:T(8,128)(2,1)S(1)} %bitcast.130, f32[256,64]{1,0:T(8,128)S(1)} %fusion.16.named, bf16[2560,384]{1,0:T(8,128)(2,1)} %bitcast.145, bf16[2560,384]{1,0:T(8,128)(2,1)} %bitcast.147, ...), custom_call_target="tpu_custom_call" | custom-call | tf_op jit(solution)/shard_map/experts/pallas_call | solution.py:271
  160.4 29.7 %all_to_all.30.returned = bf16[16,160,256]{2,1,0:T(8,128)(2,1)S(1)} all-to-all(bf16[16,160,256]{2,1,0:T(8,128)(2,1)S(1)} %bitcast.129), channel_id=1, replica_groups=mesh['req'=16,'blk'=16] {'blk'}, dimensions={0} | all-to-all | bytes 2621440 | tf_op jit(solution)/shard_map/all_to_all | solution.py:574
  190.1 2.4 %collect.1 = bf16[16,160,128]{2,1,0:T(8,128)(2,1)S(1)} custom-call(s32[1]{0:T(128)} %dynamic_slice.81.slot, bf16[16,160,256]{2,1,0:T(8,128)(2,1)S(1)} %all_to_all.30.returned, s32[8,1024]{1,0:T(8,128)S(1)} %reshape.177.codes, f32[160,128]{1,0:T(8,128)S(1)} %fusion.39.own), custom_call_target="tpu_custom_call" | custom-call | tf_op jit(solution)/shard_map/collect/pallas_call | solution.py:326
  192.5 29.0 %all_to_all.31 = bf16[16,160,128]{2,1,0:T(8,128)(2,1)S(1)} all-to-all(bf16[16,160,128]{2,1,0:T(8,128)(2,1)S(1)} %collect.1), channel_id=1, replica_groups=mesh['req'=16,'blk'=16] {'req'}, dimensions={0} | all-to-all | bytes 1310720 | tf_op jit(solution)/shard_map/all_to_all | solution.py:589
  221.5 0.7 copy.87
  (104 shorter events, 6.6 us)
Async XLA Ops:
  6.5 116.7 %copy-start = (bf16[192,2560]{1,0:T(8,128)(2,1)S(1)}, bf16[192,2560]{1,0:T(8,128)(2,1)}, u32[]{:S(2)}) copy-start(bf16[192,2560]{1,0:T(8,128)(2,1)} %param.37) | copy-start | bytes 2949124
  6.5 13.0 %copy-start.4 = (bf16[1,3,128,1024]{3,2,1,0:T(8,128)(2,1)S(1)}, bf16[1,3,128,1024]{3,2,1,0:T(8,128)(2,1)}, u32[]{:S(2)}) copy-start(bf16[1,3,128,1024]{3,2,1,0:T(8,128)(2,1)} %param.24) | copy-start | bytes 2359300
  6.5 12.8 %copy-start.6 = (s32[16,1,3]{0,1,2:T(1,128)S(1)}, s32[16,1,3]{0,1,2:T(1,128)}, u32[]{:S(2)}) copy-start(s32[16,1,3]{0,1,2:T(1,128)} %param.25) | copy-start | bytes 580
  6.5 85.1 %all-gather.2.cloned.1.call-start = ((), (), s32[]{:S(2)}) async-start(), calls=%async_computation.6 | async-start | bytes 4096000 | tf_op jit(solution)/shard_map/all_gather | solution.py:395
  9.2 30.8 %all-to-all-start = ((bf16[16,168,128]{2,1,0:T(8,128)(2,1)}), bf16[16,168,128]{2,1,0:T(8,128)(2,1)S(1)}, u32[]{:S(2)}, u32[]{:S(2)}) async-start(bf16[16,168,128]{2,1,0:T(8,128)(2,1)} %payload.1), calls=%async_computation | async-start | bytes 1376256 | tf_op jit(solution)/shard_map/all_to_all | solution.py:387
  21.9 12.6 %copy-start.8 = (s32[16]{0:T(128)S(1)}, s32[16]{0:T(128)}, u32[]{:S(2)}) copy-start(s32[16]{0:T(128)} %param.26) | copy-start | bytes 196
  21.9 13.8 %copy-start.9 = (s32[16]{0:T(128)S(1)}, s32[16]{0:T(128)}, u32[]{:S(2)}) copy-start(s32[16]{0:T(128)} %param.27) | copy-start | bytes 196
  23.7 25.8 %collective-permute-start = (bf16[2560,32]{0,1:T(8,128)(2,1)}, bf16[2560,32]{0,1:T(8,128)(2,1)S(1)}, u32[]{:S(2)}, u32[]{:S(2)}) collective-permute-start(bf16[2560,32]{0,1:T(8,128)(2,1)} %get-tuple-element.41), channel_id=1, source_target_pairs={{0,0},{1,2},{2,4},{3,6},{4,8},{5,10},{6,12},{7,14},{8,1},{9,3},{10... | collective-permute-start | bytes 491528 | tf_op jit(solution)/shard_map/ppermute | solution.py:422
  29.0 20.4 %collective-permute-start.1 = (bf16[2560,32]{0,1:T(8,128)(2,1)}, bf16[2560,32]{0,1:T(8,128)(2,1)}, u32[]{:S(2)}, u32[]{:S(2)}) collective-permute-start(bf16[2560,32]{0,1:T(8,128)(2,1)} %get-tuple-element.42), channel_id=1, source_target_pairs={{0,1},{1,3},{2,5},{3,7},{4,9},{5,11},{6,13},{7,15},{8,0},{9,2},{10... | collective-permute-start | bytes 491528 | tf_op jit(solution)/shard_map/ppermute | solution.py:423
  31.2 37.4 %collective-permute-start.7 = (bf16[384,256]{1,0:T(8,128)(2,1)}, bf16[384,256]{1,0:T(8,128)(2,1)S(1)}, u32[]{:S(2)}, u32[]{:S(2)}) collective-permute-start(bf16[384,256]{1,0:T(8,128)(2,1)} %get-tuple-element.35), channel_id=1, source_target_pairs={{0,12},{1,13},{2,14},{3,15},{4,8},{5,9},{6,10},{7,11},{8,4},{9,5},... | collective-permute-start | bytes 589832 | tf_op jit(solution)/shard_map/ppermute | solution.py:44
  32.7 35.9 %collective-permute-start.6 = (bf16[384,256]{1,0:T(8,128)(2,1)}, bf16[384,256]{1,0:T(8,128)(2,1)S(1)}, u32[]{:S(2)}, u32[]{:S(2)}) collective-permute-start(bf16[384,256]{1,0:T(8,128)(2,1)} %get-tuple-element.36), channel_id=1, source_target_pairs={{0,8},{1,9},{2,10},{3,11},{4,12},{5,13},{6,14},{7,15},{8,0},{9,1},... | collective-permute-start | bytes 589832 | tf_op jit(solution)/shard_map/ppermute | solution.py:44
  34.2 34.5 %collective-permute-start.5 = (bf16[384,256]{1,0:T(8,128)(2,1)}, bf16[384,256]{1,0:T(8,128)(2,1)S(1)}, u32[]{:S(2)}, u32[]{:S(2)}) collective-permute-start(bf16[384,256]{1,0:T(8,128)(2,1)} %get-tuple-element.37), channel_id=1, source_target_pairs={{0,4},{1,5},{2,6},{3,7},{4,0},{5,1},{6,2},{7,3},{8,12},{9,13},{10,... | collective-permute-start | bytes 589832 | tf_op jit(solution)/shard_map/ppermute | solution.py:44
  40.0 11.2 %copy-start.3 = (bf16[16,168,128]{2,1,0:T(8,128)(2,1)}, bf16[16,168,128]{2,1,0:T(8,128)(2,1)S(1)}, u32[]{:S(2)}) copy-start(bf16[16,168,128]{2,1,0:T(8,128)(2,1)S(1)} %all-to-all-done) | copy-start | bytes 2064388
  41.0 21.1 %copy-start.7 = (f32[2560]{0:T(1024)S(1)}, f32[2560]{0:T(1024)}, u32[]{:S(2)}) copy-start(f32[2560]{0:T(1024)} %param.20) | copy-start | bytes 30724
  41.0 20.7 %all-to-all-start.1 = ((bf16[16,160,128]{2,1,0:T(8,128)(2,1)}), bf16[16,160,128]{2,1,0:T(8,128)(2,1)S(1)}, u32[]{:S(2)}, u32[]{:S(2)}) async-start(bf16[16,160,128]{2,1,0:T(8,128)(2,1)} %broadcast_in_dim.27), calls=%async_computation.1 | async-start | bytes 1310720 | tf_op jit(solution)/shard_map/all_to_all | solution.py:35
  64.1 5.2 %collective-permute-start.4 = (bf16[224,128]{1,0:T(8,128)(2,1)S(1)}, bf16[224,128]{1,0:T(8,128)(2,1)S(1)}, u32[]{:S(2)}, u32[]{:S(2)}) collective-permute-start(bf16[224,128]{1,0:T(8,128)(2,1)S(1)} %fusion.8.p0), channel_id=1, source_target_pairs={{0,3},{1,2},{2,1},{3,0},{4,7},{5,6},{6,5},{7,4},{8,11},{9,10},{10,... | collective-permute-start | bytes 172040 | tf_op jit(solution)/shard_map/ppermute | solution.py:44
  65.7 5.7 %collective-permute-start.3 = (bf16[224,128]{1,0:T(8,128)(2,1)S(1)}, bf16[224,128]{1,0:T(8,128)(2,1)S(1)}, u32[]{:S(2)}, u32[]{:S(2)}) collective-permute-start(bf16[224,128]{1,0:T(8,128)(2,1)S(1)} %fusion.8.p0), channel_id=1, source_target_pairs={{0,2},{1,3},{2,0},{3,1},{4,6},{5,7},{6,4},{7,5},{8,10},{9,11},{10,... | collective-permute-start | bytes 172040 | tf_op jit(solution)/shard_map/ppermute | solution.py:44
  68.6 2.9 %collective-permute-start.2 = (bf16[224,128]{1,0:T(8,128)(2,1)S(1)}, bf16[224,128]{1,0:T(8,128)(2,1)S(1)}, u32[]{:S(2)}, u32[]{:S(2)}) collective-permute-start(bf16[224,128]{1,0:T(8,128)(2,1)S(1)} %fusion.8.p0), channel_id=1, source_target_pairs={{0,1},{1,0},{2,3},{3,2},{4,5},{5,4},{6,7},{7,6},{8,9},{9,8},{10,11... | collective-permute-start | bytes 172040 | tf_op jit(solution)/shard_map/ppermute | solution.py:44
  75.2 4.3 %collective-permute-start.8 = (bf16[32,768]{1,0:T(8,128)(2,1)S(1)}, bf16[32,768]{1,0:T(8,128)(2,1)S(1)}, u32[]{:S(2)}, u32[]{:S(2)}) collective-permute-start(bf16[32,768]{1,0:T(8,128)(2,1)S(1)} %get-tuple-element.24), channel_id=1, source_target_pairs={{0,1},{1,0},{2,3},{3,2},{4,5},{5,4},{6,7},{7,6},{8,9},{9,8},{10,11... | collective-permute-start | bytes 147464 | tf_op jit(solution)/shard_map/ppermute | solution.py:44
  76.1 4.5 %collective-permute-start.9 = (bf16[32,768]{1,0:T(8,128)(2,1)S(1)}, bf16[32,768]{1,0:T(8,128)(2,1)S(1)}, u32[]{:S(2)}, u32[]{:S(2)}) collective-permute-start(bf16[32,768]{1,0:T(8,128)(2,1)S(1)} %get-tuple-element.25), channel_id=1, source_target_pairs={{0,2},{1,3},{2,0},{3,1},{4,6},{5,7},{6,4},{7,5},{8,10},{9,11},{10,... | collective-permute-start | bytes 147464 | tf_op jit(solution)/shard_map/ppermute | solution.py:44
  77.3 5.7 %collective-permute-start.10 = (bf16[32,768]{1,0:T(8,128)(2,1)S(1)}, bf16[32,768]{1,0:T(8,128)(2,1)S(1)}, u32[]{:S(2)}, u32[]{:S(2)}) collective-permute-start(bf16[32,768]{1,0:T(8,128)(2,1)S(1)} %get-tuple-element.26), channel_id=1, source_target_pairs={{0,3},{1,2},{2,1},{3,0},{4,7},{5,6},{6,5},{7,4},{8,11},{9,10},{10,... | collective-permute-start | bytes 147464 | tf_op jit(solution)/shard_map/ppermute | solution.py:44
  83.5 4.9 %collective-permute-start.13 = (bf16[32,640]{1,0:T(8,128)(2,1)S(1)}, bf16[32,640]{1,0:T(8,128)(2,1)S(1)}, u32[]{:S(2)}, u32[]{:S(2)}) collective-permute-start(bf16[32,640]{1,0:T(8,128)(2,1)S(1)} %multiply_reduce_fusion.2), channel_id=1, source_target_pairs={{0,4},{1,5},{2,6},{3,7},{4,0},{5,1},{6,2},{7,3},{8,12},{9,13},{10,... | collective-permute-start | bytes 122888 | tf_op jit(solution)/shard_map/ppermute | solution.py:44
  85.5 4.7 %collective-permute-start.12 = (bf16[32,640]{1,0:T(8,128)(2,1)S(1)}, bf16[32,640]{1,0:T(8,128)(2,1)S(1)}, u32[]{:S(2)}, u32[]{:S(2)}) collective-permute-start(bf16[32,640]{1,0:T(8,128)(2,1)S(1)} %multiply_reduce_fusion.2), channel_id=1, source_target_pairs={{0,8},{1,9},{2,10},{3,11},{4,12},{5,13},{6,14},{7,15},{8,0},{9,1},... | collective-permute-start | bytes 122888 | tf_op jit(solution)/shard_map/ppermute | solution.py:44
  87.6 4.1 %collective-permute-start.11 = (bf16[32,640]{1,0:T(8,128)(2,1)S(1)}, bf16[32,640]{1,0:T(8,128)(2,1)S(1)}, u32[]{:S(2)}, u32[]{:S(2)}) collective-permute-start(bf16[32,640]{1,0:T(8,128)(2,1)S(1)} %multiply_reduce_fusion.2), channel_id=1, source_target_pairs={{0,12},{1,13},{2,14},{3,15},{4,8},{5,9},{6,10},{7,11},{8,4},{9,5},... | collective-permute-start | bytes 122888 | tf_op jit(solution)/shard_map/ppermute | solution.py:44
  95.6 17.9 %all-to-all-start.2 = ((bf16[16,32,640]{2,1,0:T(8,128)(2,1)}), bf16[16,32,640]{2,1,0:T(8,128)(2,1)S(1)}, u32[]{:S(2)}, u32[]{:S(2)}) async-start(bf16[16,32,640]{2,1,0:T(8,128)(2,1)} %broadcast_in_dim.35), calls=%async_computation.2 | async-start | bytes 1310720 | tf_op jit(solution)/shard_map/all_to_all | solution.py:35
  102.3 49.2 %collective-permute-start.19 = (bf16[2560,384]{1,0:T(8,128)(2,1)}, bf16[2560,384]{1,0:T(8,128)(2,1)}, u32[]{:S(2)}, u32[]{:S(2)}) collective-permute-start(bf16[2560,384]{1,0:T(8,128)(2,1)} %bitcast.144), channel_id=1, source_target_pairs={{0,1},{1,0},{2,3},{3,2},{4,5},{5,4},{6,7},{7,6},{8,9},{9,8},{10,11... | collective-permute-start | bytes 5898248 | tf_op jit(solution)/shard_map/ppermute | solution.py:481
  102.6 48.9 %collective-permute-start.20 = (bf16[2560,384]{1,0:T(8,128)(2,1)}, bf16[2560,384]{1,0:T(8,128)(2,1)}, u32[]{:S(2)}, u32[]{:S(2)}) collective-permute-start(bf16[2560,384]{1,0:T(8,128)(2,1)} %bitcast.146), channel_id=1, source_target_pairs={{0,1},{1,0},{2,3},{3,2},{4,5},{5,4},{6,7},{7,6},{8,9},{9,8},{10,11... | collective-permute-start | bytes 5898248 | tf_op jit(solution)/shard_map/ppermute | solution.py:481
  102.9 48.6 %collective-permute-start.21 = (bf16[384,2560]{1,0:T(8,128)(2,1)}, bf16[384,2560]{1,0:T(8,128)(2,1)}, u32[]{:S(2)}, u32[]{:S(2)}) collective-permute-start(bf16[384,2560]{1,0:T(8,128)(2,1)} %bitcast.148), channel_id=1, source_target_pairs={{0,1},{1,0},{2,3},{3,2},{4,5},{5,4},{6,7},{7,6},{8,9},{9,8},{10,11... | collective-permute-start | bytes 5898248 | tf_op jit(solution)/shard_map/ppermute | solution.py:481
  113.7 0.7 copy-start.5
  114.3 1.9 copy-start.2
  116.2 35.3 %all-to-all-start.3 = ((bf16[16,16,2560]{2,1,0:T(8,128)(2,1)}), bf16[16,16,2560]{2,1,0:T(8,128)(2,1)S(1)}, u32[]{:S(2)}, u32[]{:S(2)}) async-start(bf16[16,16,2560]{2,1,0:T(8,128)(2,1)} %bitcast.135), calls=%async_computation.3 | async-start | bytes 2621440 | tf_op jit(solution)/shard_map/all_to_all | solution.py:543
  127.9 3.3 %collective-permute-start.14 = (bf16[4,2,160,128]{3,2,1,0:T(8,128)(2,1)S(1)}, bf16[4,2,160,128]{3,2,1,0:T(8,128)(2,1)}, u32[]{:S(2)}, u32[]{:S(2)}) collective-permute-start(bf16[4,2,160,128]{3,2,1,0:T(8,128)(2,1)S(1)} %dynamic-slice_bitcast_fusion), channel_id=1, source_target_pairs={{0,1},{1,0},{2,3},{3,2},{4,5},{5,4},{6,7},{7,6},{8,9},{9,8},{10,11... | collective-permute-start | bytes 983048 | tf_op jit(solution)/shard_map/ppermute | solution.py:551
  132.3 19.2 %copy-start.1 = (bf16[2560,64]{0,1:T(8,128)(2,1)S(1)}, bf16[2560,64]{0,1:T(8,128)(2,1)}, u32[]{:S(2)}) copy-start(bf16[2560,64]{0,1:T(8,128)(2,1)} %param.31) | copy-start | bytes 983044
  132.3 7.9 %collective-permute-start.15 = (bf16[4,160,128]{2,1,0:T(8,128)(2,1)S(1)}, bf16[4,160,128]{2,1,0:T(8,128)(2,1)S(1)}, u32[]{:S(2)}, u32[]{:S(2)}) collective-permute-start(bf16[4,160,128]{2,1,0:T(8,128)(2,1)S(1)} %fusion.23), channel_id=1, source_target_pairs={{0,2},{1,3},{2,0},{3,1},{4,6},{5,7},{6,4},{7,5},{8,10},{9,11},{10,... | collective-permute-start | bytes 491528 | tf_op jit(solution)/shard_map/ppermute | solution.py:557
  140.3 2.9 %collective-permute-start.16 = (bf16[160,128]{1,0:T(8,128)(2,1)S(1)}, bf16[160,128]{1,0:T(8,128)(2,1)S(1)}, u32[]{:S(2)}, u32[]{:S(2)}) collective-permute-start(bf16[160,128]{1,0:T(8,128)(2,1)S(1)} %get-tuple-element.43), channel_id=1, source_target_pairs={{0,4},{1,5},{2,6},{3,7},{4,0},{5,1},{6,2},{7,3},{8,12},{9,13},{10,... | collective-permute-start | bytes 122888 | tf_op jit(solution)/shard_map/ppermute | solution.py:44
  140.7 4.7 %collective-permute-start.18 = (bf16[160,128]{1,0:T(8,128)(2,1)S(1)}, bf16[160,128]{1,0:T(8,128)(2,1)S(1)}, u32[]{:S(2)}, u32[]{:S(2)}) collective-permute-start(bf16[160,128]{1,0:T(8,128)(2,1)S(1)} %get-tuple-element.44), channel_id=1, source_target_pairs={{0,12},{1,13},{2,14},{3,15},{4,8},{5,9},{6,10},{7,11},{8,4},{9,5},... | collective-permute-start | bytes 122888 | tf_op jit(solution)/shard_map/ppermute | solution.py:44
  143.2 4.7 %collective-permute-start.17 = (bf16[160,128]{1,0:T(8,128)(2,1)S(1)}, bf16[160,128]{1,0:T(8,128)(2,1)S(1)}, u32[]{:S(2)}, u32[]{:S(2)}) collective-permute-start(bf16[160,128]{1,0:T(8,128)(2,1)S(1)} %get-tuple-element.45), channel_id=1, source_target_pairs={{0,8},{1,9},{2,10},{3,11},{4,12},{5,13},{6,14},{7,15},{8,0},{9,1},... | collective-permute-start | bytes 122888 | tf_op jit(solution)/shard_map/ppermute | solution.py:44
Sparse Core Ops, SparseCore 0:
  9.2 53.9 all-gather.1

commit v4 on v3

--- a/solution.py
+++ b/solution.py
@@ -87,17 +87,34 @@
 def payload_kernel(x, routes, beams, out, lines):
     total, width = x.shape
     rows = total // 2
+    part = rows // SIDE
     main = width // 128 * 128
-    lines[:main, :] = x[:, :main].astype(f32).T.astype(bf16)
+    ordered = jnp.concatenate(
+        [
+            x[t * rows + q * part : t * rows + (q + 1) * part, :]
+            for q in range(SIDE)
+            for t in (0, 1)
+        ],
+        axis=0,
+    ).astype(f32)
+    lines[:main, :] = ordered[:, :main].T.astype(bf16)
     rest = jnp.concatenate(
-        [x[:, main:].astype(f32), jnp.zeros((total, 128 - width + main), f32)], axis=1
+        [ordered[:, main:], jnp.zeros((total, 128 - width + main), f32)], axis=1
     )
     lines[main:width, :] = rest.T[: width - main].astype(bf16)
-    named = [
-        jnp.concatenate([routes[k, 0:1, :], routes[k, 1:2, :]], axis=1) for k in range(TOPK)
+    none = jnp.zeros((1, rows), jnp.int32)
+    by_step = [
+        jnp.concatenate([routes[k, t : t + 1, :] for k in range(TOPK)] + [last, none], axis=0)
+        for t, last in ((0, none), (1, beams[...]))
     ]
-    beam = jnp.concatenate([jnp.zeros((1, rows), jnp.int32), beams[...]], axis=1)
-    extra = jnp.concatenate(named + [beam, jnp.zeros((1, total), jnp.int32)], axis=0)
+    extra = jnp.concatenate(
+        [
+            by_step[t][:, q * part : (q + 1) * part]
+            for q in range(SIDE)
+            for t in (0, 1)
+        ],
+        axis=1,
+    )
     lines[width:, :] = extra.astype(f32).astype(bf16)
     for i in range(out.shape[0]):
         out[i] = lines[...]
@@ -212,6 +229,34 @@
         compiler_params=pltpu.CompilerParams(vmem_limit_bytes=24 << 20),
         name="attention",
     )(scalars, parent, cosine, sine, *pieces, *caches)
+
+
+def spread_kernel(pieces, gain, dispatch, attended, normed, sent):
+    count, part, span = pieces.shape
+    for x in range(count // SIDE):
+        for q in range(SIDE):
+            attended[q * part : (q + 1) * part, x * span : (x + 1) * span] = pieces[
+                SIDE * x + q
+            ]
+    normed[...] = norm_rows(attended[...], gain[...], 1)
+    sent[...] = dot(dispatch[...], normed[...]).astype(bf16)
+
+
+def spread(pieces, gain, dispatch):
+    count, part, span = pieces.shape
+    width = count // SIDE * span
+    vmem = pl.BlockSpec(memory_space=pltpu.VMEM)
+    return pl.pallas_call(
+        spread_kernel,
+        out_shape=[
+            jax.ShapeDtypeStruct((SIDE * part, width), bf16),
+            jax.ShapeDtypeStruct((SIDE * part, width), bf16),
+            jax.ShapeDtypeStruct((dispatch.shape[0], width), bf16),
+        ],
+        in_specs=[vmem] * 3,
+        out_specs=[vmem] * 3,
+        name="spread",
+    )(pieces, gain, dispatch)
 
 
 def expert_kernel(
@@ -387,9 +432,16 @@
     by_slot = lax.all_to_all(payload, "req", 0, 0, tiled=True)
     slot = migration[req_index]
     mine = lax.dynamic_index_in_dim(by_slot, slot, 0, False)
-    routes_all = by_slot[:, width_local : width_local + TOPK].astype(jnp.int32)
-    routes_mine = mine[width_local : width_local + TOPK].astype(jnp.int32).T
-    beam_mine = mine[width_local + TOPK, rows:].astype(jnp.int32)
+    part = rows // SIDE
+    routes_all = (
+        by_slot[:, width_local : width_local + TOPK]
+        .astype(jnp.int32)
+        .reshape(req_count, TOPK, SIDE, steps, part)
+        .transpose(0, 1, 3, 2, 4)
+        .reshape(req_count, TOPK, total)
+    )
+    routes_mine = lax.dynamic_index_in_dim(routes_all, slot, 0, False).T
+    beam_mine = mine[width_local + TOPK].astype(jnp.int32)
     inputs = to_all(mine[:width_local], "blk").reshape(width, total)
 
     output_columns = lax.all_gather(
@@ -433,14 +485,14 @@
     )
     position = length + jnp.arange(steps, dtype=jnp.int32)
     angles = position.astype(f32)[:, None] * frequency
-    cosine = jnp.repeat(jnp.cos(angles).T, rows, axis=1)
-    sine = jnp.repeat(jnp.sin(angles).T, rows, axis=1)
-
-    parent = jnp.concatenate(
-        [
-            jnp.full((rows,), -1, jnp.int32),
-            jnp.arange(rows, dtype=jnp.int32) // BEAMS * BEAMS + beam_mine,
-        ]
+    cosine = jnp.tile(jnp.repeat(jnp.cos(angles).T, part, axis=1), (1, SIDE))
+    sine = jnp.tile(jnp.repeat(jnp.sin(angles).T, part, axis=1), (1, SIDE))
+
+    line = jnp.arange(total, dtype=jnp.int32)
+    parent = jnp.where(
+        line // part % steps == 1,
+        line // subset * subset + line % part // BEAMS * BEAMS + beam_mine,
+        -1,
     )[None]
     parts = attend(
         jnp.stack([length, q_index, x_index]).astype(jnp.int32),
@@ -479,13 +531,10 @@
     )
     blocks = [gate_here, up_here, down_here]
     expert_blocks = blocks + [lax.ppermute(b, "blk", partners(1)) for b in blocks]
-    attended = (
-        to_all(attended_part, "blk")
-        .reshape(SIDE, SIDE, subset, span)
-        .transpose(1, 2, 0, 3)
-        .reshape(total, width)
-    )
-    normed_h = norm_rows(attended, feedforward_gain, 1)
+    to_core = jnp.broadcast_to(
+        attended_part.reshape(1, steps, part, span), (blk_count // 2, steps, part, span)
+    ).reshape(blk_count, part, span)
+    attended_pieces = lax.all_to_all(to_core, "blk", 0, 0, tiled=True)
 
     per_req = E // req_count
     slot_ids = jnp.arange(req_count, dtype=jnp.int32)
@@ -539,34 +588,54 @@
         .reshape(req_count * CAP, rows)
         .astype(bf16)
     )
-    sent = dot(dispatch, of_step(normed_h)).astype(bf16).reshape(req_count, CAP, width)
-    arrived = lax.all_to_all(sent, "req", 0, 0, tiled=True).reshape(req_count * CAP, width)
-
-    act = (jax.nn.silu(dot(normed_h, shared_gate)) * dot(normed_h, shared_up)).astype(bf16)
+    attended, normed_h, sent = spread(attended_pieces, feedforward_gain[None], dispatch)
+    arrived = lax.all_to_all(
+        sent.reshape(req_count, CAP, width), "req", 0, 0, tiled=True
+    ).reshape(req_count * CAP, width)
+
+    other = lax.ppermute(normed_h, "blk", partners(1))
+    act = [
+        (jax.nn.silu(dot(h, shared_gate)) * dot(h, shared_up)).astype(bf16)
+        for h in (normed_h, other)
+    ]
+
+    def by_step(here, there):
+        return jnp.concatenate(
+            [jnp.where(core == 0, here, there), jnp.where(core == 0, there, here)], axis=0
+        )
+
+    act = by_step(*act)
     shared_part = lax.dot_general(
         shared_down, act, (((0,), (1,)), ((), ())), preferred_element_type=f32
     ).astype(bf16)
     q_high = q_index // 2
     halves = shared_part.reshape(SIDE, 2, 2, width_local, total)
-    pair = lax.dynamic_index_in_dim(halves, core, 2, False).astype(f32) + lax.ppermute(
-        lax.dynamic_index_in_dim(halves, 1 - core, 2, False), "blk", partners(1)
-    ).astype(f32)
-    quads = pair.astype(bf16)
-    over_q = (
-        lax.dynamic_index_in_dim(pair, q_high, 1, False)
+    pair = (
+        lax.dynamic_index_in_dim(halves, core, 2, False).astype(f32)
         + lax.ppermute(
-            lax.dynamic_index_in_dim(quads, 1 - q_high, 1, False), "blk", partners(2)
+            lax.dynamic_index_in_dim(halves, 1 - core, 2, False), "blk", partners(1)
         ).astype(f32)
     ).astype(bf16)
-    shared = sum(
+    over_x = sum(
         p.astype(f32)
         for p in group_parts(
-            lambda d: lax.dynamic_index_in_dim(over_q, x_index ^ d, 0, False), SIDE
-        )
-    )
+            lambda d: lax.dynamic_index_in_dim(pair, x_index ^ d, 0, False), SIDE
+        )
+    )
+    shared = lax.dynamic_index_in_dim(over_x, q_high, 0, False) + lax.ppermute(
+        lax.dynamic_index_in_dim(over_x, 1 - q_high, 0, False).astype(bf16),
+        "blk",
+        partners(2),
+    ).astype(f32)
+
+    def columns_of(b):
+        return lax.dynamic_slice_in_dim(attended, b * width_local, width_local, 1)
+
     own = (
-        lax.dynamic_slice_in_dim(attended, blk_index * width_local, width_local, 1)
-        .T.astype(f32)
+        by_step(
+            columns_of(blk_index),
+            lax.ppermute(columns_of(blk_index ^ 1), "blk", partners(1)),
+        ).T.astype(f32)
         + shared
     )
     arrived, own = lax.optimization_barrier((arrived, own))

time: 230 us -> 229 us (level)
  blocking collectives: 58.7 us -> 53 us
  local copies, waits for them, and re-layouts: 12.4 us -> 16.5 us
  Pallas kernels: 16.8 us -> 19.6 us
    all_to_all x2 -> x1, waiting for transfers between devices: 20.8 us -> 10.2 us  [to_all(): return lax.all_to_all(copies, axis, 0, 0, tiled=True)]
    all_to_all x2 -> x1, starting transfers between devices: 13.8 us -> 5.62 us  [to_all(): return lax.all_to_all(copies, axis, 0, 0, tiled=True)]
    all_to_all x1 -> x2, starting transfers between devices: 5.45 us -> 13.5 us  [the longest x1 6.97 us: per_device(): lax.all_to_all(sent.reshape(req_count, CAP, width), 'req', 0, 0, tiled=True)]
    all_to_all x1 -> x2, waiting for transfers between devices: 3.59 us -> 10.9 us  [the longest x1 8.53 us: per_device(): attended_pieces = lax.all_to_all(to_core, 'blk', 0, 0, tiled=True)]
    ppermute x1, waiting for transfers between devices: 0.01 us -> 5.27 us  [per_device(): second = lax.ppermute(jnp.where(low_side, right, left), 'blk', crossed)]
    all_to_all x1, blocking collectives: 29 us -> 24.5 us  [per_device(): final = lax.all_to_all(outgoing, 'req', 0, 0, tiled=True)]
    pallas_call x0 -> x1, Pallas kernels: none -> 2.7 us  [spread(): pl.pallas_call(spread_kernel, out_shape=[jax.ShapeDtypeStruct((SIDE * par...]
    ppermute x1 -> x3, waiting for transfers between devices: 5.95 us -> 4.1 us  [the longest x1 4.09 us: per_device(): lax.ppermute(lax.dynamic_index_in_dim(over_x, 1 - q_high, 0, False).astyp...]
  transfers between devices with their start and end apart: 27 -> 29, of which waited for: 13 -> 14; matrix products, arithmetic and copies ran while one was open for 13% -> 14% of each run, Pallas kernels for 2% -> 4%
where the time goes in v4:
time: 229 us; the launch traced here: 228 us
  starting transfers between devices  57.3 us (25%)
  blocking collectives  53 us (23%)
  waiting for transfers between devices  44.9 us (20%)
  Pallas kernels  19.6 us (9%)
  local copies, waits for them, and re-layouts  16.5 us (7%)
  between operations  16.1 us (7%)
  matrix products  10.8 us (5%)
  other arithmetic  9.87 us (4%)
    all_to_all x1, blocking collectives, per_device(): lax.all_to_all(expert_rows((req_index * per_req + x_index)[None].astype(j...  28.6 us
    all_to_all x1, blocking collectives, per_device(): final = lax.all_to_all(outgoing, 'req', 0, 0, tiled=True)  24.5 us
    ppermute x15, starting transfers between devices, group_parts(): lax.ppermute(piece_for(d), 'blk', partners(d * stride))  17.8 us
    ppermute x15, waiting for transfers between devices, group_parts(): lax.ppermute(piece_for(d), 'blk', partners(d * stride))  11.2 us
    all_to_all x1, starting transfers between devices, per_device(): by_slot = lax.all_to_all(payload, 'req', 0, 0, tiled=True)  10.2 us
    all_to_all x1, waiting for transfers between devices, to_all(): return lax.all_to_all(copies, axis, 0, 0, tiled=True)  10.2 us
    pallas_call x1, Pallas kernels, expert_rows(): pl.pallas_call(expert_kernel, out_shape=jax.ShapeDtypeStruct((width, coun...  8.84 us
    all_to_all x1, waiting for transfers between devices, per_device(): attended_pieces = lax.all_to_all(to_core, 'blk', 0, 0, tiled=True)  8.53 us
  transfers between devices with their start and end apart: 29, of which 14 were waited for; matrix products, arithmetic and copies ran while one was open for 14% of the time, Pallas kernels for 4%

profile of v4, /device:TPU:1, one launch (start us, length us, event | category | flops | bytes accessed | tf_op | source)
XLA Modules:
  0.0 228.0 jit_solution(1014893105155814121)
XLA Ops:
  6.5 0.7 all-gather.2.cloned.1.call-update
  7.3 1.9 payload.1
  9.2 10.2 %all-to-all-start = ((bf16[16,168,128]{2,1,0:T(8,128)(2,1)}), bf16[16,168,128]{2,1,0:T(8,128)(2,1)}, u32[]{:S(2)}, u32[]{:S(2)}) async-start(bf16[16,168,128]{2,1,0:T(8,128)(2,1)} %payload.1), calls=%async_computation | async-start | bytes 1376256 | tf_op jit(solution)/shard_map/all_to_all | solution.py:432
  22.0 5.4 %collective-permute-start = (bf16[2560,32]{0,1:T(8,128)(2,1)S(1)}, bf16[2560,32]{0,1:T(8,128)(2,1)S(1)}, u32[]{:S(2)}, u32[]{:S(2)}) collective-permute-start(bf16[2560,32]{0,1:T(8,128)(2,1)S(1)} %get-tuple-element.54), channel_id=1, source_target_pairs={{0,0},{1,2},{2,4},{3,6},{4,8},{5,10},{6,12},{7,14},{8,1},{9,3},{10... | collective-permute-start | bytes 491528 | tf_op jit(solution)/shard_map/ppermute | solution.py:474
  27.4 1.3 collective-permute-start.1
  28.7 0.8 dynamic-slice_bitcast_fusion.1
  29.5 1.5 collective-permute-start.7
  31.1 1.5 collective-permute-start.6
  39.6 0.7 pad_add_fusion.scalars
  40.3 1.9 collective-permute-done
  42.2 5.3 %collective-permute-done.1 = bf16[2560,32]{0,1:T(8,128)(2,1)S(1)} collective-permute-done((bf16[2560,32]{0,1:T(8,128)(2,1)S(1)}, bf16[2560,32]{0,1:T(8,128)(2,1)S(1)}, u32[]{:S(2)}, u32[]{:S(2)}) %collective-permute-start.1) | collective-permute-done | bytes 163872 | tf_op jit(solution)/shard_map/ppermute | solution.py:475
  47.4 0.8 broadcast_select_fusion.3
  48.2 0.8 dynamic-slice_bitcast_fusion.9
  49.0 0.9 broadcast_in_dim.35
  49.9 5.6 %all-to-all-start.1 = ((bf16[16,160,128]{2,1,0:T(8,128)(2,1)}), bf16[16,160,128]{2,1,0:T(8,128)(2,1)S(1)}, u32[]{:S(2)}, u32[]{:S(2)}) async-start(bf16[16,160,128]{2,1,0:T(8,128)(2,1)} %broadcast_in_dim.35), calls=%async_computation.1 | async-start | bytes 1310720 | tf_op jit(solution)/shard_map/all_to_all | solution.py:35
  55.6 0.8 slice_convert_fusion
  57.7 10.2 %all-to-all-done.1 = bf16[16,160,128]{2,1,0:T(8,128)(2,1)S(1)} async-done(((bf16[16,160,128]{2,1,0:T(8,128)(2,1)}), bf16[16,160,128]{2,1,0:T(8,128)(2,1)S(1)}, u32[]{:S(2)}, u32[]{:S(2)}) %all-to-all-start.1) | async-done | bytes 655392 | tf_op jit(solution)/shard_map/all_to_all | solution.py:35
  68.2 2.0 fusion.8.p0
  70.2 1.6 collective-permute-start.4
  71.8 2.9 %collective-permute-start.3 = (bf16[224,128]{1,0:T(8,128)(2,1)S(1)}, bf16[224,128]{1,0:T(8,128)(2,1)S(1)}, u32[]{:S(2)}, u32[]{:S(2)}) collective-permute-start(bf16[224,128]{1,0:T(8,128)(2,1)S(1)} %fusion.8.p0), channel_id=1, source_target_pairs={{0,2},{1,3},{2,0},{3,1},{4,6},{5,7},{6,4},{7,5},{8,10},{9,11},{10,... | collective-permute-start | bytes 172040 | tf_op jit(solution)/shard_map/ppermute | solution.py:44
  74.7 0.7 compare_select_fusion.3.parent
  75.4 2.1 collective-permute-done.3.p2
  77.6 3.7 %attention.1 = (bf16[32,768]{1,0:T(8,128)(2,1)S(1)}, bf16[32,768]{1,0:T(8,128)(2,1)S(1)}, bf16[32,768]{1,0:T(8,128)(2,1)S(1)}, bf16[32,768]{1,0:T(8,128)(2,1)S(1)}) custom-call(s32[3]{0:T(128)S(1)} %pad_add_fusion.scalars, s32[1,128]{1,0:T(1,128)S(1)} %compare_select_fusion.3.parent, f32[64,128]{1,0:T(8,128)S(1)} %copy.111.cosine, ...), custom_call_target="tpu_custom_call" | custom-call | tf_op jit(solution)/shard_map/attention/pallas_call | solution.py:215
  81.3 0.7 collective-permute-start.8
  82.0 1.3 collective-permute-start.9
  83.3 2.0 collective-permute-start.10
  85.4 1.1 collective-permute-done.9
  86.5 2.5 %collective-permute-done.10 = bf16[32,768]{1,0:T(8,128)(2,1)S(1)} collective-permute-done((bf16[32,768]{1,0:T(8,128)(2,1)S(1)}, bf16[32,768]{1,0:T(8,128)(2,1)S(1)}, u32[]{:S(2)}, u32[]{:S(2)}) %collective-permute-start.10) | collective-permute-done | bytes 49184 | tf_op jit(solution)/shard_map/ppermute | solution.py:44
  89.7 1.9 collective-permute-start.12
  91.6 1.8 collective-permute-start.11
  93.8 0.7 fusion.32.dispatch
  94.8 0.9 collective-permute-done.11
  95.8 3.0 %fusion.14 = bf16[32,640]{1,0:T(8,128)(2,1)S(1)} fusion(bf16[2560,640]{0,1:T(8,128)(2,1)} %all-gather.2.cloned.1.call-done, bf16[32,640]{1,0:T(8,128)(2,1)S(1)} %get-tuple-element.59, bf16[32,640]{1,0:T(8,128)(2,1)S(1)} %get-tuple-element.58, bf16[32,640]{1,0:T(8,128)(2,1)S(1)} %get-tuple-element.57, bf16[32,640]{1,0:T(8,128)(2,1)S(1)} %get-tuple-element.56, ...), kind=kOutput, calls=%fused_computation.20 | convolution fusion | flops 105574400 | bytes 3522560 | tf_op jit(solution)/shard_map/dot_general | solution.py:29
  98.8 0.8 broadcast_in_dim.40
  99.5 6.5 %all-to-all-start.2 = ((bf16[16,16,640]{2,1,0:T(8,128)(2,1)}), bf16[16,16,640]{2,1,0:T(8,128)(2,1)S(1)}, u32[]{:S(2)}, u32[]{:S(2)}) async-start(bf16[16,16,640]{2,1,0:T(8,128)(2,1)} %bitcast.30), calls=%async_computation.2 | async-start | bytes 655360 | tf_op jit(solution)/shard_map/all_to_all | solution.py:537
  107.1 8.5 %all-to-all-done.2.pieces = bf16[16,16,640]{2,1,0:T(8,128)(2,1)S(1)} async-done(((bf16[16,16,640]{2,1,0:T(8,128)(2,1)}), bf16[16,16,640]{2,1,0:T(8,128)(2,1)S(1)}, u32[]{:S(2)}, u32[]{:S(2)}) %all-to-all-start.2) | async-done | bytes 327712 | tf_op jit(solution)/shard_map/all_to_all | solution.py:537
  115.6 0.7 copy-done.5
  116.3 2.7 %spread.1 = (bf16[64,2560]{1,0:T(8,128)(2,1)}, bf16[64,2560]{1,0:T(8,128)(2,1)}, bf16[256,2560]{1,0:T(8,128)(2,1)}) custom-call(bf16[16,16,640]{2,1,0:T(8,128)(2,1)} %copy-done.5, f32[1,2560]{1,0:T(1,128)} %broadcast_in_dim.41.gain, bf16[256,64]{1,0:T(8,128)(2,1)} %fusion.32.dispatch), custom_call_target="tpu_custom_call" | custom-call | tf_op jit(solution)/shard_map/spread/pallas_call | solution.py:249
  119.0 7.0 %all-to-all-start.3 = ((bf16[16,16,2560]{2,1,0:T(8,128)(2,1)}), bf16[16,16,2560]{2,1,0:T(8,128)(2,1)S(1)}, u32[]{:S(2)}, u32[]{:S(2)}) async-start(bf16[16,16,2560]{2,1,0:T(8,128)(2,1)} %bitcast.157), calls=%async_computation.3 | async-start | bytes 2621440 | tf_op jit(solution)/shard_map/all_to_all | solution.py:592
  126.0 1.1 collective-permute-start.15
  127.1 1.4 fusion.58
  128.5 1.7 fusion.15
  131.2 1.2 fusion
  132.4 1.4 copy.120
  133.8 0.8 dynamic-slice_bitcast_fusion
  134.8 1.2 fusion.1
  136.5 1.1 fusion.17
  137.6 0.7 dynamic-slice_bitcast_fusion.7
  138.7 1.3 copy.118
  140.0 1.2 collective-permute-start.19
  141.3 1.3 collective-permute-done.17
  142.6 0.9 collective-permute-start.18
  143.5 1.9 collective-permute-done.19
  145.4 0.9 collective-permute-start.14
  146.4 1.3 collective-permute-done.18
  147.7 1.0 fusion.30
  148.7 0.8 collective-permute-start.20
  149.5 4.1 %collective-permute-done.20 = bf16[160,128]{1,0:T(8,128)(2,1)S(1)} collective-permute-done((bf16[160,128]{1,0:T(8,128)(2,1)S(1)}, bf16[160,128]{1,0:T(8,128)(2,1)S(1)}, u32[]{:S(2)}, u32[]{:S(2)}) %collective-permute-start.20) | collective-permute-done | bytes 40992 | tf_op jit(solution)/shard_map/ppermute | solution.py:625
  153.7 2.4 %all-to-all-done.3 = bf16[16,16,2560]{2,1,0:T(8,128)(2,1)S(1)} async-done(((bf16[16,16,2560]{2,1,0:T(8,128)(2,1)}), bf16[16,16,2560]{2,1,0:T(8,128)(2,1)S(1)}, u32[]{:S(2)}, u32[]{:S(2)}) %all-to-all-start.3) | async-done | bytes 1310752 | tf_op jit(solution)/shard_map/all_to_all | solution.py:592
  156.1 8.8 %experts.1 = bf16[2560,256]{1,0:T(8,128)(2,1)S(1)} custom-call(s32[1]{0:T(128)} %bitcast.expert, bf16[256,2560]{1,0:T(8,128)(2,1)S(1)} %bitcast.139, bf16[64,2560]{1,0:T(8,128)(2,1)S(1)} %bitcast.141, f32[256,64]{1,0:T(8,128)S(1)} %fusion.16.named, bf16[2560,384]{1,0:T(8,128)(2,1)} %bitcast.152, bf16[2560,384]{1,0:T(8,128)(2,1)} %bitcast.154, ...), custom_call_target="tpu_custom_call" | custom-call | tf_op jit(solution)/shard_map/experts/pallas_call | solution.py:316
  164.9 28.6 %all_to_all.30.returned = bf16[16,160,256]{2,1,0:T(8,128)(2,1)S(1)} all-to-all(bf16[16,160,256]{2,1,0:T(8,128)(2,1)S(1)} %bitcast.140), channel_id=1, replica_groups=mesh['req'=16,'blk'=16] {'blk'}, dimensions={0} | all-to-all | bytes 2621440 | tf_op jit(solution)/shard_map/all_to_all | solution.py:643
  193.5 2.4 %collect.1 = bf16[16,160,128]{2,1,0:T(8,128)(2,1)S(1)} custom-call(s32[1]{0:T(128)} %dynamic_slice.82.slot, bf16[16,160,256]{2,1,0:T(8,128)(2,1)S(1)} %all_to_all.30.returned, s32[8,1024]{1,0:T(8,128)S(1)} %reshape.344.codes, f32[160,128]{1,0:T(8,128)S(1)} %fusion.33.own), custom_call_target="tpu_custom_call" | custom-call | tf_op jit(solution)/shard_map/collect/pallas_call | solution.py:371
  195.9 24.5 %all_to_all.31 = bf16[16,160,128]{2,1,0:T(8,128)(2,1)S(1)} all-to-all(bf16[16,160,128]{2,1,0:T(8,128)(2,1)S(1)} %collect.1), channel_id=1, replica_groups=mesh['req'=16,'blk'=16] {'req'}, dimensions={0} | all-to-all | bytes 1310720 | tf_op jit(solution)/shard_map/all_to_all | solution.py:658
  220.5 0.7 copy.125
  (123 shorter events, 13.8 us)
Async XLA Ops:
  6.5 124.6 %copy-start = (bf16[192,2560]{1,0:T(8,128)(2,1)S(1)}, bf16[192,2560]{1,0:T(8,128)(2,1)}, u32[]{:S(2)}) copy-start(bf16[192,2560]{1,0:T(8,128)(2,1)} %param.37) | copy-start | bytes 2949124
  6.5 13.1 %copy-start.6 = (bf16[1,3,128,1024]{3,2,1,0:T(8,128)(2,1)S(1)}, bf16[1,3,128,1024]{3,2,1,0:T(8,128)(2,1)}, u32[]{:S(2)}) copy-start(bf16[1,3,128,1024]{3,2,1,0:T(8,128)(2,1)} %param.24) | copy-start | bytes 2359300
  6.5 12.8 %copy-start.10 = (s32[16,1,3]{0,1,2:T(1,128)S(1)}, s32[16,1,3]{0,1,2:T(1,128)}, u32[]{:S(2)}) copy-start(s32[16,1,3]{0,1,2:T(1,128)} %param.25) | copy-start | bytes 580
  6.5 89.2 %all-gather.2.cloned.1.call-start = ((), (), s32[]{:S(2)}) async-start(), calls=%async_computation.6 | async-start | bytes 4096000 | tf_op jit(solution)/shard_map/all_gather | solution.py:447
  9.2 39.0 %all-to-all-start = ((bf16[16,168,128]{2,1,0:T(8,128)(2,1)}), bf16[16,168,128]{2,1,0:T(8,128)(2,1)}, u32[]{:S(2)}, u32[]{:S(2)}) async-start(bf16[16,168,128]{2,1,0:T(8,128)(2,1)} %payload.1), calls=%async_computation | async-start | bytes 1376256 | tf_op jit(solution)/shard_map/all_to_all | solution.py:432
  20.8 1.2 copy-start.7
  21.4 11.3 %copy-start.14 = (s32[16]{0:T(128)S(1)}, s32[16]{0:T(128)}, u32[]{:S(2)}) copy-start(s32[16]{0:T(128)} %param.27) | copy-start | bytes 196
  21.4 12.0 %copy-start.13 = (s32[16]{0:T(128)S(1)}, s32[16]{0:T(128)}, u32[]{:S(2)}) copy-start(s32[16]{0:T(128)} %param.26) | copy-start | bytes 196
  21.5 16.6 %copy-start.8 = (f32[2560]{0:T(1024)S(1)}, f32[2560]{0:T(1024)}, u32[]{:S(2)}) copy-start(f32[2560]{0:T(1024)} %param.30) | copy-start | bytes 30724
  22.0 20.1 %collective-permute-start = (bf16[2560,32]{0,1:T(8,128)(2,1)S(1)}, bf16[2560,32]{0,1:T(8,128)(2,1)S(1)}, u32[]{:S(2)}, u32[]{:S(2)}) collective-permute-start(bf16[2560,32]{0,1:T(8,128)(2,1)S(1)} %get-tuple-element.54), channel_id=1, source_target_pairs={{0,0},{1,2},{2,4},{3,6},{4,8},{5,10},{6,12},{7,14},{8,1},{9,3},{10... | collective-permute-start | bytes 491528 | tf_op jit(solution)/shard_map/ppermute | solution.py:474
  27.4 20.0 %collective-permute-start.1 = (bf16[2560,32]{0,1:T(8,128)(2,1)S(1)}, bf16[2560,32]{0,1:T(8,128)(2,1)S(1)}, u32[]{:S(2)}, u32[]{:S(2)}) collective-permute-start(bf16[2560,32]{0,1:T(8,128)(2,1)S(1)} %get-tuple-element.55), channel_id=1, source_target_pairs={{0,1},{1,3},{2,5},{3,7},{4,9},{5,11},{6,13},{7,15},{8,0},{9,2},{10... | collective-permute-start | bytes 491528 | tf_op jit(solution)/shard_map/ppermute | solution.py:475
  29.5 45.2 %collective-permute-start.7 = (bf16[384,256]{1,0:T(8,128)(2,1)}, bf16[384,256]{1,0:T(8,128)(2,1)S(1)}, u32[]{:S(2)}, u32[]{:S(2)}) collective-permute-start(bf16[384,256]{1,0:T(8,128)(2,1)} %get-tuple-element.43), channel_id=1, source_target_pairs={{0,12},{1,13},{2,14},{3,15},{4,8},{5,9},{6,10},{7,11},{8,4},{9,5},... | collective-permute-start | bytes 589832 | tf_op jit(solution)/shard_map/ppermute | solution.py:44
  31.1 44.3 %collective-permute-start.6 = (bf16[384,256]{1,0:T(8,128)(2,1)}, bf16[384,256]{1,0:T(8,128)(2,1)S(1)}, u32[]{:S(2)}, u32[]{:S(2)}) collective-permute-start(bf16[384,256]{1,0:T(8,128)(2,1)} %get-tuple-element.44), channel_id=1, source_target_pairs={{0,8},{1,9},{2,10},{3,11},{4,12},{5,13},{6,14},{7,15},{8,0},{9,1},... | collective-permute-start | bytes 589832 | tf_op jit(solution)/shard_map/ppermute | solution.py:44
  32.6 42.9 %collective-permute-start.5 = (bf16[384,256]{1,0:T(8,128)(2,1)S(1)}, bf16[384,256]{1,0:T(8,128)(2,1)S(1)}, u32[]{:S(2)}, u32[]{:S(2)}) collective-permute-start(bf16[384,256]{1,0:T(8,128)(2,1)S(1)} %get-tuple-element.45), channel_id=1, source_target_pairs={{0,4},{1,5},{2,6},{3,7},{4,0},{5,1},{6,2},{7,3},{8,12},{9,13},{10,... | collective-permute-start | bytes 589832 | tf_op jit(solution)/shard_map/ppermute | solution.py:44
  49.9 18.3 %copy-start.12 = (f32[2560]{0:T(1024)S(1)}, f32[2560]{0:T(1024)}, u32[]{:S(2)}) copy-start(f32[2560]{0:T(1024)} %param.20) | copy-start | bytes 30724
  49.9 18.0 %all-to-all-start.1 = ((bf16[16,160,128]{2,1,0:T(8,128)(2,1)}), bf16[16,160,128]{2,1,0:T(8,128)(2,1)S(1)}, u32[]{:S(2)}, u32[]{:S(2)}) async-start(bf16[16,160,128]{2,1,0:T(8,128)(2,1)} %broadcast_in_dim.35), calls=%async_computation.1 | async-start | bytes 1310720 | tf_op jit(solution)/shard_map/all_to_all | solution.py:35
  70.2 5.2 %collective-permute-start.4 = (bf16[224,128]{1,0:T(8,128)(2,1)S(1)}, bf16[224,128]{1,0:T(8,128)(2,1)S(1)}, u32[]{:S(2)}, u32[]{:S(2)}) collective-permute-start(bf16[224,128]{1,0:T(8,128)(2,1)S(1)} %fusion.8.p0), channel_id=1, source_target_pairs={{0,3},{1,2},{2,1},{3,0},{4,7},{5,6},{6,5},{7,4},{8,11},{9,10},{10,... | collective-permute-start | bytes 172040 | tf_op jit(solution)/shard_map/ppermute | solution.py:44
  71.8 5.7 %collective-permute-start.3 = (bf16[224,128]{1,0:T(8,128)(2,1)S(1)}, bf16[224,128]{1,0:T(8,128)(2,1)S(1)}, u32[]{:S(2)}, u32[]{:S(2)}) collective-permute-start(bf16[224,128]{1,0:T(8,128)(2,1)S(1)} %fusion.8.p0), channel_id=1, source_target_pairs={{0,2},{1,3},{2,0},{3,1},{4,6},{5,7},{6,4},{7,5},{8,10},{9,11},{10,... | collective-permute-start | bytes 172040 | tf_op jit(solution)/shard_map/ppermute | solution.py:44
  74.7 2.9 %collective-permute-start.2 = (bf16[224,128]{1,0:T(8,128)(2,1)S(1)}, bf16[224,128]{1,0:T(8,128)(2,1)S(1)}, u32[]{:S(2)}, u32[]{:S(2)}) collective-permute-start(bf16[224,128]{1,0:T(8,128)(2,1)S(1)} %fusion.8.p0), channel_id=1, source_target_pairs={{0,1},{1,0},{2,3},{3,2},{4,5},{5,4},{6,7},{7,6},{8,9},{9,8},{10,11... | collective-permute-start | bytes 172040 | tf_op jit(solution)/shard_map/ppermute | solution.py:44
  81.3 4.0 %collective-permute-start.8 = (bf16[32,768]{1,0:T(8,128)(2,1)S(1)}, bf16[32,768]{1,0:T(8,128)(2,1)S(1)}, u32[]{:S(2)}, u32[]{:S(2)}) collective-permute-start(bf16[32,768]{1,0:T(8,128)(2,1)S(1)} %get-tuple-element.27), channel_id=1, source_target_pairs={{0,1},{1,0},{2,3},{3,2},{4,5},{5,4},{6,7},{7,6},{8,9},{9,8},{10,11... | collective-permute-start | bytes 147464 | tf_op jit(solution)/shard_map/ppermute | solution.py:44
  82.0 4.5 %collective-permute-start.9 = (bf16[32,768]{1,0:T(8,128)(2,1)S(1)}, bf16[32,768]{1,0:T(8,128)(2,1)S(1)}, u32[]{:S(2)}, u32[]{:S(2)}) collective-permute-start(bf16[32,768]{1,0:T(8,128)(2,1)S(1)} %get-tuple-element.28), channel_id=1, source_target_pairs={{0,2},{1,3},{2,0},{3,1},{4,6},{5,7},{6,4},{7,5},{8,10},{9,11},{10,... | collective-permute-start | bytes 147464 | tf_op jit(solution)/shard_map/ppermute | solution.py:44
  83.3 5.7 %collective-permute-start.10 = (bf16[32,768]{1,0:T(8,128)(2,1)S(1)}, bf16[32,768]{1,0:T(8,128)(2,1)S(1)}, u32[]{:S(2)}, u32[]{:S(2)}) collective-permute-start(bf16[32,768]{1,0:T(8,128)(2,1)S(1)} %get-tuple-element.29), channel_id=1, source_target_pairs={{0,3},{1,2},{2,1},{3,0},{4,7},{5,6},{6,5},{7,4},{8,11},{9,10},{10,... | collective-permute-start | bytes 147464 | tf_op jit(solution)/shard_map/ppermute | solution.py:44
  85.3 8.5 %copy-start.9 = (f32[256]{0:T(256)S(1)}, f32[256]{0:T(256)}, u32[]{:S(2)}) copy-start(f32[256]{0:T(256)} %eq.131) | copy-start | bytes 3076
  89.5 5.3 %collective-permute-start.13 = (bf16[32,640]{1,0:T(8,128)(2,1)S(1)}, bf16[32,640]{1,0:T(8,128)(2,1)S(1)}, u32[]{:S(2)}, u32[]{:S(2)}) collective-permute-start(bf16[32,640]{1,0:T(8,128)(2,1)S(1)} %multiply_reduce_fusion.1), channel_id=1, source_target_pairs={{0,4},{1,5},{2,6},{3,7},{4,0},{5,1},{6,2},{7,3},{8,12},{9,13},{10,... | collective-permute-start | bytes 122888 | tf_op jit(solution)/shard_map/ppermute | solution.py:44
  89.7 5.1 %collective-permute-start.12 = (bf16[32,640]{1,0:T(8,128)(2,1)S(1)}, bf16[32,640]{1,0:T(8,128)(2,1)S(1)}, u32[]{:S(2)}, u32[]{:S(2)}) collective-permute-start(bf16[32,640]{1,0:T(8,128)(2,1)S(1)} %multiply_reduce_fusion.1), channel_id=1, source_target_pairs={{0,8},{1,9},{2,10},{3,11},{4,12},{5,13},{6,14},{7,15},{8,0},{9,1},... | collective-permute-start | bytes 122888 | tf_op jit(solution)/shard_map/ppermute | solution.py:44
  91.6 4.1 %collective-permute-start.11 = (bf16[32,640]{1,0:T(8,128)(2,1)S(1)}, bf16[32,640]{1,0:T(8,128)(2,1)S(1)}, u32[]{:S(2)}, u32[]{:S(2)}) collective-permute-start(bf16[32,640]{1,0:T(8,128)(2,1)S(1)} %multiply_reduce_fusion.1), channel_id=1, source_target_pairs={{0,12},{1,13},{2,14},{3,15},{4,8},{5,9},{6,10},{7,11},{8,4},{9,5},... | collective-permute-start | bytes 122888 | tf_op jit(solution)/shard_map/ppermute | solution.py:44
  95.8 10.3 %copy-start.11 = (s32[4]{0:T(128)S(1)}, s32[4]{0:T(128)}, u32[]{:S(2)}) copy-start(s32[4]{0:T(128)} %iota_add_fusion) | copy-start | bytes 52
  95.8 10.5 %copy-start.15 = (s32[16]{0:T(128)S(1)}, s32[16]{0:T(128)}, u32[]{:S(2)}) copy-start(s32[16]{0:T(128)} %broadcast_multiply_fusion) | copy-start | bytes 196
  99.5 27.6 %copy-start.2 = (bf16[2560,192]{0,1:T(8,128)(2,1)S(1)}, bf16[2560,192]{0,1:T(8,128)(2,1)}, u32[]{:S(2)}) copy-start(bf16[2560,192]{0,1:T(8,128)(2,1)} %param.35) | copy-start | bytes 2949124
  99.5 16.1 %all-to-all-start.2 = ((bf16[16,16,640]{2,1,0:T(8,128)(2,1)}), bf16[16,16,640]{2,1,0:T(8,128)(2,1)S(1)}, u32[]{:S(2)}, u32[]{:S(2)}) async-start(bf16[16,16,640]{2,1,0:T(8,128)(2,1)} %bitcast.30), calls=%async_computation.2 | async-start | bytes 655360 | tf_op jit(solution)/shard_map/all_to_all | solution.py:537
  106.4 49.7 %collective-permute-start.21 = (bf16[2560,384]{1,0:T(8,128)(2,1)}, bf16[2560,384]{1,0:T(8,128)(2,1)}, u32[]{:S(2)}, u32[]{:S(2)}) collective-permute-start(bf16[2560,384]{1,0:T(8,128)(2,1)} %bitcast.151), channel_id=1, source_target_pairs={{0,1},{1,0},{2,3},{3,2},{4,5},{5,4},{6,7},{7,6},{8,9},{9,8},{10,11... | collective-permute-start | bytes 5898248 | tf_op jit(solution)/shard_map/ppermute | solution.py:533
  106.6 49.5 %collective-permute-start.22 = (bf16[2560,384]{1,0:T(8,128)(2,1)}, bf16[2560,384]{1,0:T(8,128)(2,1)}, u32[]{:S(2)}, u32[]{:S(2)}) collective-permute-start(bf16[2560,384]{1,0:T(8,128)(2,1)} %bitcast.153), channel_id=1, source_target_pairs={{0,1},{1,0},{2,3},{3,2},{4,5},{5,4},{6,7},{7,6},{8,9},{9,8},{10,11... | collective-permute-start | bytes 5898248 | tf_op jit(solution)/shard_map/ppermute | solution.py:533
  107.0 49.1 %collective-permute-start.23 = (bf16[384,2560]{1,0:T(8,128)(2,1)}, bf16[384,2560]{1,0:T(8,128)(2,1)}, u32[]{:S(2)}, u32[]{:S(2)}) collective-permute-start(bf16[384,2560]{1,0:T(8,128)(2,1)} %bitcast.155), channel_id=1, source_target_pairs={{0,1},{1,0},{2,3},{3,2},{4,5},{5,4},{6,7},{7,6},{8,9},{9,8},{10,11... | collective-permute-start | bytes 5898248 | tf_op jit(solution)/shard_map/ppermute | solution.py:533
  115.6 0.7 copy-start.5
  119.0 37.0 %all-to-all-start.3 = ((bf16[16,16,2560]{2,1,0:T(8,128)(2,1)}), bf16[16,16,2560]{2,1,0:T(8,128)(2,1)S(1)}, u32[]{:S(2)}, u32[]{:S(2)}) async-start(bf16[16,16,2560]{2,1,0:T(8,128)(2,1)} %bitcast.157), calls=%async_computation.3 | async-start | bytes 2621440 | tf_op jit(solution)/shard_map/all_to_all | solution.py:592
  126.0 4.7 %copy-start.3 = (bf16[2560,192]{0,1:T(8,128)(2,1)S(1)}, bf16[2560,192]{0,1:T(8,128)(2,1)}, u32[]{:S(2)}) copy-start(bf16[2560,192]{0,1:T(8,128)(2,1)} %param.36) | copy-start | bytes 2949124
  126.0 4.2 %collective-permute-start.15 = (bf16[64,2560]{1,0:T(8,128)(2,1)}, bf16[64,2560]{1,0:T(8,128)(2,1)S(1)}, u32[]{:S(2)}, u32[]{:S(2)}) collective-permute-start(bf16[64,2560]{1,0:T(8,128)(2,1)} %get-tuple-element.33), channel_id=1, source_target_pairs={{0,1},{1,0},{2,3},{3,2},{4,5},{5,4},{6,7},{7,6},{8,9},{9,8},{10,11... | collective-permute-start | bytes 983048 | tf_op jit(solution)/shard_map/ppermute | solution.py:596
  134.6 2.0 collective-permute-start.16
  136.0 20.1 %copy-start.1 = (bf16[2560,64]{0,1:T(8,128)(2,1)S(1)}, bf16[2560,64]{0,1:T(8,128)(2,1)}, u32[]{:S(2)}) copy-start(bf16[2560,64]{0,1:T(8,128)(2,1)} %param.31) | copy-start | bytes 983044
  137.6 0.8 copy-start.4
  138.4 4.2 %collective-permute-start.17 = (bf16[2,160,128]{2,1,0:T(8,128)(2,1)}, bf16[2,160,128]{2,1,0:T(8,128)(2,1)}, u32[]{:S(2)}, u32[]{:S(2)}) collective-permute-start(bf16[2,160,128]{2,1,0:T(8,128)(2,1)} %get-tuple-element.49), channel_id=1, source_target_pairs={{0,4},{1,5},{2,6},{3,7},{4,0},{5,1},{6,2},{7,3},{8,12},{9,13},{10,... | collective-permute-start | bytes 245768 | tf_op jit(solution)/shard_map/ppermute | solution.py:44
  140.0 5.4 %collective-permute-start.19 = (bf16[2,160,128]{2,1,0:T(8,128)(2,1)}, bf16[2,160,128]{2,1,0:T(8,128)(2,1)S(1)}, u32[]{:S(2)}, u32[]{:S(2)}) collective-permute-start(bf16[2,160,128]{2,1,0:T(8,128)(2,1)} %get-tuple-element.50), channel_id=1, source_target_pairs={{0,12},{1,13},{2,14},{3,15},{4,8},{5,9},{6,10},{7,11},{8,4},{9,5},... | collective-permute-start | bytes 245768 | tf_op jit(solution)/shard_map/ppermute | solution.py:44
  142.6 5.1 %collective-permute-start.18 = (bf16[2,160,128]{2,1,0:T(8,128)(2,1)S(1)}, bf16[2,160,128]{2,1,0:T(8,128)(2,1)S(1)}, u32[]{:S(2)}, u32[]{:S(2)}) collective-permute-start(bf16[2,160,128]{2,1,0:T(8,128)(2,1)S(1)} %get-tuple-element.51), channel_id=1, source_target_pairs={{0,8},{1,9},{2,10},{3,11},{4,12},{5,13},{6,14},{7,15},{8,0},{9,1},... | collective-permute-start | bytes 245768 | tf_op jit(solution)/shard_map/ppermute | solution.py:44
  145.4 4.0 %collective-permute-start.14 = (bf16[64,160]{0,1:T(8,128)(2,1)S(1)}, bf16[64,160]{0,1:T(8,128)(2,1)S(1)}, u32[]{:S(2)}, u32[]{:S(2)}) collective-permute-start(bf16[64,160]{0,1:T(8,128)(2,1)S(1)} %constant_dynamic-slice_fusion.1), channel_id=1, source_target_pairs={{0,1},{1,0},{2,3},{3,2},{4,5},{5,4},{6,7},{7,6},{8,9},{9,8},{10,11... | collective-permute-start | bytes 61448 | tf_op jit(solution)/shard_map/ppermute | solution.py:637
  148.7 4.9 %collective-permute-start.20 = (bf16[160,128]{1,0:T(8,128)(2,1)S(1)}, bf16[160,128]{1,0:T(8,128)(2,1)S(1)}, u32[]{:S(2)}, u32[]{:S(2)}) collective-permute-start(bf16[160,128]{1,0:T(8,128)(2,1)S(1)} %fusion.39), channel_id=1, source_target_pairs={{0,2},{1,3},{2,0},{3,1},{4,6},{5,7},{6,4},{7,5},{8,10},{9,11},{10,... | collective-permute-start | bytes 122888 | tf_op jit(solution)/shard_map/ppermute | solution.py:625
Sparse Core Ops, SparseCore 0:
  9.2 46.9 all-gather.1

commit v5 on v4

--- a/solution.py
+++ b/solution.py
@@ -129,8 +129,43 @@
         in_specs=[vmem] * 3,
         out_specs=vmem,
         scratch_shapes=[pltpu.VMEM((width + TOPK + 2, total), bf16)],
+        compiler_params=pltpu.CompilerParams(vmem_limit_bytes=4 << 20),
         name="payload",
     )(x, routes, beams)
+
+
+def project_kernel(core, x, gain, query, first, second, out, normed):
+    width = x.shape[0]
+    wide = x[...].astype(f32)
+    inverse = lax.rsqrt(jnp.sum(wide * wide, axis=0, keepdims=True) / width + epsilon)
+    gains = gain[...].T
+    for i in range(width // 128):
+        rows = slice(i * 128, (i + 1) * 128)
+        normed[rows, :] = (
+            x[rows, :].astype(f32) * inverse * gains[:, i : i + 1]
+        ).astype(bf16)
+    share = query.shape[0]
+    half = first.shape[0]
+    out[:share, :] = dot(query[...], normed[...]).astype(bf16)
+    a = dot(first[...], normed[...])
+    b = dot(second[...], normed[...])
+    even = core[0] == 0
+    out[share : share + half, :] = jnp.where(even, a, b).astype(bf16)
+    out[share + half :, :] = jnp.where(even, b, a).astype(bf16)
+
+
+def project(core, x, gain, query, first, second):
+    vmem = pl.BlockSpec(memory_space=pltpu.VMEM)
+    share = query.shape[0] + 2 * first.shape[0]
+    return pl.pallas_call(
+        project_kernel,
+        out_shape=jax.ShapeDtypeStruct((share, x.shape[1]), bf16),
+        in_specs=[pl.BlockSpec(memory_space=pltpu.SMEM)] + [vmem] * 5,
+        out_specs=vmem,
+        scratch_shapes=[pltpu.VMEM(x.shape, bf16)],
+        compiler_params=pltpu.CompilerParams(vmem_limit_bytes=10 << 20),
+        name="project",
+    )(core, x, gain, query, first, second)
 
 
 def attention_kernel(
@@ -226,7 +261,7 @@
             pltpu.VMEM((HEAD_WIDTH, total), f32),
             pltpu.VMEM((total, span + HEAD_WIDTH), bf16),
         ],
-        compiler_params=pltpu.CompilerParams(vmem_limit_bytes=24 << 20),
+        compiler_params=pltpu.CompilerParams(vmem_limit_bytes=12 << 20),
         name="attention",
     )(scalars, parent, cosine, sine, *pieces, *caches)
 
@@ -326,7 +361,7 @@
             pltpu.SemaphoreType.DMA((6,)),
             pltpu.SemaphoreType.DMA((5,)),
         ],
-        compiler_params=pltpu.CompilerParams(vmem_limit_bytes=40 << 20),
+        compiler_params=pltpu.CompilerParams(vmem_limit_bytes=28 << 20),
         name="experts",
     )(
         expert,
@@ -374,7 +409,7 @@
         in_specs=[pl.BlockSpec(memory_space=pltpu.SMEM)] + [vmem] * 3,
         out_specs=vmem,
         scratch_shapes=[pltpu.VMEM(shape, f32)],
-        compiler_params=pltpu.CompilerParams(vmem_limit_bytes=32 << 20),
+        compiler_params=pltpu.CompilerParams(vmem_limit_bytes=16 << 20),
         name="collect",
     )(slot, returned, codes, own)
 
@@ -462,7 +497,8 @@
     )
 
     half = key_value_weight.shape[1] // 2
-    left, right = key_value_weight[:, :half], key_value_weight[:, half:]
+    turned = key_value_weight.T
+    left, right = turned[:half], turned[half:]
     low_side = blk_index < blk_count // 2
     groups = blk_count // 2
     straight = [(d, 2 * d) for d in range(groups)] + [
@@ -473,12 +509,14 @@
     ]
     first = lax.ppermute(jnp.where(low_side, left, right), "blk", straight)
     second = lax.ppermute(jnp.where(low_side, right, left), "blk", crossed)
-    key_columns = jnp.where(core == 0, first, second)
-    value_columns = jnp.where(core == 0, second, first)
-    projection = jnp.concatenate([query_weight, key_columns, value_columns], axis=1)
-
-    normed = norm_rows(inputs, attention_gain[:, None], 0)
-    projected = across(projection, normed).astype(bf16)
+    projected = project(
+        core[None].astype(jnp.int32),
+        inputs,
+        attention_gain.reshape(-1, 128),
+        query_weight.T,
+        first,
+        second,
+    )
     length = cache_lengths[req_index]
     frequency = rope_base ** (
         -2.0 * jnp.arange(HEAD_WIDTH // 2, dtype=f32) / HEAD_WIDTH

time: 229 us -> 226 us (0.987)
  waiting for transfers between devices: 44.9 us -> 34.6 us
  local copies, waits for them, and re-layouts: 16.5 us -> 22.8 us
    ppermute x1, waiting for transfers between devices: 5.27 us -> 0.01 us  [per_device(): second = lax.ppermute(jnp.where(low_side, right, left), 'blk', crossed)]
    all_to_all x1, waiting for transfers between devices: 10.2 us -> 6.03 us  [to_all(): return lax.all_to_all(copies, axis, 0, 0, tiled=True)]
    transpose x4, local copies, waits for them, and re-layouts: 0.76 us -> 3.29 us  [per_device(): routes_all = by_slot[:, width_local:width_local + TOPK].astype(jnp.int32)...]
  transfers between devices with their start and end apart: 29 -> 29, of which waited for: 14 -> 13; matrix products, arithmetic and copies ran while one was open for 14% -> 15% of each run, Pallas kernels for 4% -> 4%
where the time goes in v5:
time: 226 us; the launch traced here: 224 us
  starting transfers between devices  58.3 us (26%)
  blocking collectives  53.1 us (23%)
  waiting for transfers between devices  34.6 us (15%)
  local copies, waits for them, and re-layouts  22.8 us (10%)
  Pallas kernels  20.8 us (9%)
  between operations  16 us (7%)
  other arithmetic  9.59 us (4%)
  matrix products  9.38 us (4%)
    all_to_all x1, blocking collectives, per_device(): lax.all_to_all(expert_rows((req_index * per_req + x_index)[None].astype(j...  28.6 us
    all_to_all x1, blocking collectives, per_device(): final = lax.all_to_all(outgoing, 'req', 0, 0, tiled=True)  24.4 us
    ppermute x15, starting transfers between devices, group_parts(): lax.ppermute(piece_for(d), 'blk', partners(d * stride))  18.7 us
    ppermute x15, waiting for transfers between devices, group_parts(): lax.ppermute(piece_for(d), 'blk', partners(d * stride))  12.4 us
    all_to_all x1, starting transfers between devices, per_device(): by_slot = lax.all_to_all(payload, 'req', 0, 0, tiled=True)  10.2 us
    pallas_call x1, Pallas kernels, expert_rows(): pl.pallas_call(expert_kernel, out_shape=jax.ShapeDtypeStruct((width, coun...  8.84 us
    all_to_all x1, waiting for transfers between devices, per_device(): attended_pieces = lax.all_to_all(to_core, 'blk', 0, 0, tiled=True)  8.47 us
    dot_general x7, matrix products, dot(): return jnp.dot(a, b, preferred_element_type=f32)  7.39 us
  transfers between devices with their start and end apart: 29, of which 13 were waited for; matrix products, arithmetic and copies ran while one was open for 15% of the time, Pallas kernels for 4%

profile of v5, /device:TPU:1, one launch (start us, length us, event | category | flops | bytes accessed | tf_op | source)
XLA Modules:
  0.0 224.5 jit_solution(3362987907286926444)
XLA Ops:
  6.5 0.7 all-gather.2.cloned.1.call-update
  7.3 0.8 copy-done.3
  9.5 1.1 payload.1
  10.5 10.2 %all-to-all-start = ((bf16[16,168,128]{2,1,0:T(8,128)(2,1)}), bf16[16,168,128]{2,1,0:T(8,128)(2,1)}, u32[]{:S(2)}, u32[]{:S(2)}) async-start(bf16[16,168,128]{2,1,0:T(8,128)(2,1)} %payload.1), calls=%async_computation | async-start | bytes 1376256 | tf_op jit(solution)/shard_map/all_to_all | solution.py:467
  23.3 0.8 broadcast_select_fusion
  24.1 2.6 %collective-permute-start.1 = (bf16[32,2560]{1,0:T(8,128)(2,1)}, bf16[32,2560]{1,0:T(8,128)(2,1)S(1)}, u32[]{:S(2)}, u32[]{:S(2)}) collective-permute-start(bf16[32,2560]{1,0:T(8,128)(2,1)} %get-tuple-element.52), channel_id=1, source_target_pairs={{0,1},{1,3},{2,5},{3,7},{4,9},{5,11},{6,13},{7,15},{8,0},{9,2},{10... | collective-permute-start | bytes 491528 | tf_op jit(solution)/shard_map/ppermute | solution.py:511
  26.7 3.5 %collective-permute-start = (bf16[32,2560]{1,0:T(8,128)(2,1)}, bf16[32,2560]{1,0:T(8,128)(2,1)}, u32[]{:S(2)}, u32[]{:S(2)}) collective-permute-start(bf16[32,2560]{1,0:T(8,128)(2,1)} %get-tuple-element.53), channel_id=1, source_target_pairs={{0,0},{1,2},{2,4},{3,6},{4,8},{5,10},{6,12},{7,14},{8,1},{9,3},{10... | collective-permute-start | bytes 491528 | tf_op jit(solution)/shard_map/ppermute | solution.py:510
  30.2 0.9 dynamic-slice_bitcast_fusion.1
  31.1 2.3 %collective-permute-start.7 = (bf16[384,256]{1,0:T(8,128)(2,1)}, bf16[384,256]{1,0:T(8,128)(2,1)S(1)}, u32[]{:S(2)}, u32[]{:S(2)}) collective-permute-start(bf16[384,256]{1,0:T(8,128)(2,1)} %get-tuple-element.43), channel_id=1, source_target_pairs={{0,12},{1,13},{2,14},{3,15},{4,8},{5,9},{6,10},{7,11},{8,4},{9,5},... | collective-permute-start | bytes 589832 | tf_op jit(solution)/shard_map/ppermute | solution.py:44
  33.3 1.5 collective-permute-start.6
  42.3 0.8 dynamic-slice_bitcast_fusion.9
  43.1 0.9 broadcast_in_dim.38
  44.1 7.0 %all-to-all-start.1 = ((bf16[16,160,128]{2,1,0:T(8,128)(2,1)}), bf16[16,160,128]{2,1,0:T(8,128)(2,1)S(1)}, u32[]{:S(2)}, u32[]{:S(2)}) async-start(bf16[16,160,128]{2,1,0:T(8,128)(2,1)} %broadcast_in_dim.38), calls=%async_computation.1 | async-start | bytes 1310720 | tf_op jit(solution)/shard_map/all_to_all | solution.py:35
  51.1 0.8 slice_convert_fusion
  51.9 1.3 reshape.347
  53.2 1.9 copy.121
  55.0 1.3 reshape.334
  56.6 0.8 fusion.30
  57.4 6.0 %all-to-all-done.1 = bf16[16,160,128]{2,1,0:T(8,128)(2,1)S(1)} async-done(((bf16[16,160,128]{2,1,0:T(8,128)(2,1)}), bf16[16,160,128]{2,1,0:T(8,128)(2,1)S(1)}, u32[]{:S(2)}, u32[]{:S(2)}) %all-to-all-start.1) | async-done | bytes 655392 | tf_op jit(solution)/shard_map/all_to_all | solution.py:35
  63.4 2.1 project.1.p0
  65.5 1.6 collective-permute-start.4
  67.1 2.9 %collective-permute-start.3 = (bf16[224,128]{1,0:T(8,128)(2,1)S(1)}, bf16[224,128]{1,0:T(8,128)(2,1)S(1)}, u32[]{:S(2)}, u32[]{:S(2)}) collective-permute-start(bf16[224,128]{1,0:T(8,128)(2,1)S(1)} %project.1.p0), channel_id=1, source_target_pairs={{0,2},{1,3},{2,0},{3,1},{4,6},{5,7},{6,4},{7,5},{8,10},{9,11},{10,... | collective-permute-start | bytes 172040 | tf_op jit(solution)/shard_map/ppermute | solution.py:44
  70.7 2.2 collective-permute-done.3.p2
  72.9 3.7 %attention.1 = (bf16[32,768]{1,0:T(8,128)(2,1)S(1)}, bf16[32,768]{1,0:T(8,128)(2,1)S(1)}, bf16[32,768]{1,0:T(8,128)(2,1)S(1)}, bf16[32,768]{1,0:T(8,128)(2,1)S(1)}) custom-call(s32[3]{0:T(128)S(1)} %pad_add_fusion.scalars, s32[1,128]{1,0:T(1,128)S(1)} %compare_select_fusion.3.parent, f32[64,128]{1,0:T(8,128)S(1)} %copy.116.cosine, ...), custom_call_target="tpu_custom_call" | custom-call | tf_op jit(solution)/shard_map/attention/pallas_call | solution.py:250
  77.3 1.3 collective-permute-start.9
  78.6 2.0 collective-permute-start.10
  81.8 2.5 %collective-permute-done.10 = bf16[32,768]{1,0:T(8,128)(2,1)S(1)} collective-permute-done((bf16[32,768]{1,0:T(8,128)(2,1)S(1)}, bf16[32,768]{1,0:T(8,128)(2,1)S(1)}, u32[]{:S(2)}, u32[]{:S(2)}) %collective-permute-start.10) | collective-permute-done | bytes 49184 | tf_op jit(solution)/shard_map/ppermute | solution.py:44
  84.8 1.9 collective-permute-start.13
  86.7 2.1 collective-permute-start.12
  89.6 0.7 fusion.21.dispatch
  90.3 1.1 collective-permute-done.12
  91.4 1.4 collective-permute-done.11
  92.9 2.9 %fusion.2 = bf16[32,640]{0,1:T(8,128)(2,1)S(1)} fusion(bf16[2560,640]{0,1:T(8,128)(2,1)} %all-gather.2.cloned.1.call-done, bf16[32,640]{1,0:T(8,128)(2,1)S(1)} %get-tuple-element.57, bf16[32,640]{1,0:T(8,128)(2,1)S(1)} %get-tuple-element.56, bf16[32,640]{1,0:T(8,128)(2,1)S(1)} %get-tuple-element.55, bf16[32,640]{1,0:T(8,128)(2,1)S(1)} %get-tuple-element.54, ...), kind=kOutput, calls=%fused_computation.6 | convolution fusion | flops 105574400 | bytes 3522568 | tf_op jit(solution)/shard_map/dot_general | solution.py:29
  96.0 0.8 broadcast_in_dim.43
  96.8 5.5 %all-to-all-start.2 = ((bf16[16,16,640]{2,1,0:T(8,128)(2,1)}), bf16[16,16,640]{2,1,0:T(8,128)(2,1)S(1)}, u32[]{:S(2)}, u32[]{:S(2)}) async-start(bf16[16,16,640]{2,1,0:T(8,128)(2,1)} %bitcast.34), calls=%async_computation.2 | async-start | bytes 655360 | tf_op jit(solution)/shard_map/all_to_all | solution.py:575
  103.4 8.5 %all-to-all-done.2.pieces = bf16[16,16,640]{2,1,0:T(8,128)(2,1)S(1)} async-done(((bf16[16,16,640]{2,1,0:T(8,128)(2,1)}), bf16[16,16,640]{2,1,0:T(8,128)(2,1)S(1)}, u32[]{:S(2)}, u32[]{:S(2)}) %all-to-all-start.2) | async-done | bytes 327712 | tf_op jit(solution)/shard_map/all_to_all | solution.py:575
  111.9 0.7 copy-done.11
  112.6 2.7 %spread.1 = (bf16[64,2560]{1,0:T(8,128)(2,1)}, bf16[64,2560]{1,0:T(8,128)(2,1)}, bf16[256,2560]{1,0:T(8,128)(2,1)}) custom-call(bf16[16,16,640]{2,1,0:T(8,128)(2,1)} %copy-done.11, f32[1,2560]{1,0:T(1,128)} %broadcast_in_dim.44.gain, bf16[256,64]{1,0:T(8,128)(2,1)} %fusion.21.dispatch), custom_call_target="tpu_custom_call" | custom-call | tf_op jit(solution)/shard_map/spread/pallas_call | solution.py:284
  115.3 7.1 %all-to-all-start.3 = ((bf16[16,16,2560]{2,1,0:T(8,128)(2,1)}), bf16[16,16,2560]{2,1,0:T(8,128)(2,1)S(1)}, u32[]{:S(2)}, u32[]{:S(2)}) async-start(bf16[16,16,2560]{2,1,0:T(8,128)(2,1)} %bitcast.165), calls=%async_computation.3 | async-start | bytes 2621440 | tf_op jit(solution)/shard_map/all_to_all | solution.py:630
  122.4 1.1 collective-permute-start.15
  123.6 1.4 fusion.46
  125.0 1.7 fusion.6
  127.7 1.2 fusion
  128.9 1.4 copy.127
  130.3 0.8 dynamic-slice_bitcast_fusion
  131.3 1.2 fusion.1
  133.0 1.1 fusion.8
  134.1 0.8 dynamic-slice_bitcast_fusion.7
  135.3 1.3 copy.125
  136.6 1.2 collective-permute-start.19
  137.7 1.4 collective-permute-done.17
  139.1 0.8 collective-permute-start.18
  139.9 2.0 collective-permute-done.19
  142.0 0.9 collective-permute-start.14
  142.9 1.3 collective-permute-done.18
  144.2 1.0 fusion.19
  145.2 0.8 collective-permute-start.20
  146.0 4.1 %collective-permute-done.20 = bf16[160,128]{1,0:T(8,128)(2,1)S(1)} collective-permute-done((bf16[160,128]{1,0:T(8,128)(2,1)S(1)}, bf16[160,128]{1,0:T(8,128)(2,1)S(1)}, u32[]{:S(2)}, u32[]{:S(2)}) %collective-permute-start.20) | collective-permute-done | bytes 40992 | tf_op jit(solution)/shard_map/ppermute | solution.py:663
  150.2 2.3 %all-to-all-done.3 = bf16[16,16,2560]{2,1,0:T(8,128)(2,1)S(1)} async-done(((bf16[16,16,2560]{2,1,0:T(8,128)(2,1)}), bf16[16,16,2560]{2,1,0:T(8,128)(2,1)S(1)}, u32[]{:S(2)}, u32[]{:S(2)}) %all-to-all-start.3) | async-done | bytes 1310752 | tf_op jit(solution)/shard_map/all_to_all | solution.py:630
  152.5 8.8 %experts.1 = bf16[2560,256]{1,0:T(8,128)(2,1)S(1)} custom-call(s32[1]{0:T(128)} %bitcast.expert, bf16[256,2560]{1,0:T(8,128)(2,1)S(1)} %bitcast.143, bf16[64,2560]{1,0:T(8,128)(2,1)S(1)} %bitcast.148, f32[256,64]{1,0:T(8,128)S(1)} %fusion.7.named, bf16[2560,384]{1,0:T(8,128)(2,1)} %bitcast.160, bf16[2560,384]{1,0:T(8,128)(2,1)} %bitcast.162, ...), custom_call_target="tpu_custom_call" | custom-call | tf_op jit(solution)/shard_map/experts/pallas_call | solution.py:351
  161.3 28.6 %all_to_all.30.returned = bf16[16,160,256]{2,1,0:T(8,128)(2,1)S(1)} all-to-all(bf16[16,160,256]{2,1,0:T(8,128)(2,1)S(1)} %bitcast.144), channel_id=1, replica_groups=mesh['req'=16,'blk'=16] {'blk'}, dimensions={0} | all-to-all | bytes 2621440 | tf_op jit(solution)/shard_map/all_to_all | solution.py:681
  190.0 2.3 %collect.1 = bf16[16,160,128]{2,1,0:T(8,128)(2,1)S(1)} custom-call(s32[1]{0:T(128)} %dynamic_slice.82.slot, bf16[16,160,256]{2,1,0:T(8,128)(2,1)S(1)} %all_to_all.30.returned, s32[8,1024]{1,0:T(8,128)S(1)} %reshape.339.codes, f32[160,128]{1,0:T(8,128)S(1)} %fusion.22.own), custom_call_target="tpu_custom_call" | custom-call | tf_op jit(solution)/shard_map/collect/pallas_call | solution.py:406
  192.3 24.4 %all_to_all.31 = bf16[16,160,128]{2,1,0:T(8,128)(2,1)S(1)} all-to-all(bf16[16,160,128]{2,1,0:T(8,128)(2,1)S(1)} %collect.1), channel_id=1, replica_groups=mesh['req'=16,'blk'=16] {'req'}, dimensions={0} | all-to-all | bytes 1310720 | tf_op jit(solution)/shard_map/all_to_all | solution.py:696
  216.9 0.7 copy.132
  (129 shorter events, 16.9 us)
Async XLA Ops:
  6.5 121.1 %copy-start = (bf16[192,2560]{1,0:T(8,128)(2,1)S(1)}, bf16[192,2560]{1,0:T(8,128)(2,1)}, u32[]{:S(2)}) copy-start(bf16[192,2560]{1,0:T(8,128)(2,1)} %param.37) | copy-start | bytes 2949124
  6.5 14.4 %copy-start.12 = (bf16[1,3,128,1024]{3,2,1,0:T(8,128)(2,1)S(1)}, bf16[1,3,128,1024]{3,2,1,0:T(8,128)(2,1)}, u32[]{:S(2)}) copy-start(bf16[1,3,128,1024]{3,2,1,0:T(8,128)(2,1)} %param.24) | copy-start | bytes 2359300
  6.5 14.2 %copy-start.16 = (s32[16,1,3]{0,1,2:T(1,128)S(1)}, s32[16,1,3]{0,1,2:T(1,128)}, u32[]{:S(2)}) copy-start(s32[16,1,3]{0,1,2:T(1,128)} %param.25) | copy-start | bytes 580
  6.5 86.4 %all-gather.2.cloned.1.call-start = ((), (), s32[]{:S(2)}) async-start(), calls=%async_computation.6 | async-start | bytes 4096000 | tf_op jit(solution)/shard_map/all_gather | solution.py:482
  7.3 0.8 copy-start.3
  8.1 0.7 copy-start.5
  8.8 0.7 copy-start.6
  10.5 31.8 %all-to-all-start = ((bf16[16,168,128]{2,1,0:T(8,128)(2,1)}), bf16[16,168,128]{2,1,0:T(8,128)(2,1)}, u32[]{:S(2)}, u32[]{:S(2)}) async-start(bf16[16,168,128]{2,1,0:T(8,128)(2,1)} %payload.1), calls=%async_computation | async-start | bytes 1376256 | tf_op jit(solution)/shard_map/all_to_all | solution.py:467
  22.1 1.2 copy-start.13
  22.8 12.1 %copy-start.19 = (s32[16]{0:T(128)S(1)}, s32[16]{0:T(128)}, u32[]{:S(2)}) copy-start(s32[16]{0:T(128)} %param.27) | copy-start | bytes 196
  22.8 14.1 %copy-start.18 = (s32[16]{0:T(128)S(1)}, s32[16]{0:T(128)}, u32[]{:S(2)}) copy-start(s32[16]{0:T(128)} %param.26) | copy-start | bytes 196
  22.8 15.3 %copy-start.14 = (f32[2560]{0:T(1024)S(1)}, f32[2560]{0:T(1024)}, u32[]{:S(2)}) copy-start(f32[2560]{0:T(1024)} %param.30) | copy-start | bytes 30724
  24.1 33.3 %collective-permute-start.1 = (bf16[32,2560]{1,0:T(8,128)(2,1)}, bf16[32,2560]{1,0:T(8,128)(2,1)S(1)}, u32[]{:S(2)}, u32[]{:S(2)}) collective-permute-start(bf16[32,2560]{1,0:T(8,128)(2,1)} %get-tuple-element.52), channel_id=1, source_target_pairs={{0,1},{1,3},{2,5},{3,7},{4,9},{5,11},{6,13},{7,15},{8,0},{9,2},{10... | collective-permute-start | bytes 491528 | tf_op jit(solution)/shard_map/ppermute | solution.py:511
  26.7 30.7 %collective-permute-start = (bf16[32,2560]{1,0:T(8,128)(2,1)}, bf16[32,2560]{1,0:T(8,128)(2,1)}, u32[]{:S(2)}, u32[]{:S(2)}) collective-permute-start(bf16[32,2560]{1,0:T(8,128)(2,1)} %get-tuple-element.53), channel_id=1, source_target_pairs={{0,0},{1,2},{2,4},{3,6},{4,8},{5,10},{6,12},{7,14},{8,1},{9,3},{10... | collective-permute-start | bytes 491528 | tf_op jit(solution)/shard_map/ppermute | solution.py:510
  31.1 38.9 %collective-permute-start.7 = (bf16[384,256]{1,0:T(8,128)(2,1)}, bf16[384,256]{1,0:T(8,128)(2,1)S(1)}, u32[]{:S(2)}, u32[]{:S(2)}) collective-permute-start(bf16[384,256]{1,0:T(8,128)(2,1)} %get-tuple-element.43), channel_id=1, source_target_pairs={{0,12},{1,13},{2,14},{3,15},{4,8},{5,9},{6,10},{7,11},{8,4},{9,5},... | collective-permute-start | bytes 589832 | tf_op jit(solution)/shard_map/ppermute | solution.py:44
  33.3 37.3 %collective-permute-start.6 = (bf16[384,256]{1,0:T(8,128)(2,1)}, bf16[384,256]{1,0:T(8,128)(2,1)S(1)}, u32[]{:S(2)}, u32[]{:S(2)}) collective-permute-start(bf16[384,256]{1,0:T(8,128)(2,1)} %get-tuple-element.44), channel_id=1, source_target_pairs={{0,8},{1,9},{2,10},{3,11},{4,12},{5,13},{6,14},{7,15},{8,0},{9,1},... | collective-permute-start | bytes 589832 | tf_op jit(solution)/shard_map/ppermute | solution.py:44
  34.9 35.8 %collective-permute-start.5 = (bf16[384,256]{1,0:T(8,128)(2,1)}, bf16[384,256]{1,0:T(8,128)(2,1)S(1)}, u32[]{:S(2)}, u32[]{:S(2)}) collective-permute-start(bf16[384,256]{1,0:T(8,128)(2,1)} %get-tuple-element.45), channel_id=1, source_target_pairs={{0,4},{1,5},{2,6},{3,7},{4,0},{5,1},{6,2},{7,3},{8,12},{9,13},{10,... | collective-permute-start | bytes 589832 | tf_op jit(solution)/shard_map/ppermute | solution.py:44
  43.1 20.3 %copy-start.1 = (bf16[2560,160]{0,1:T(8,128)(2,1)S(1)}, bf16[2560,160]{0,1:T(8,128)(2,1)}, u32[]{:S(2)}) copy-start(bf16[2560,160]{0,1:T(8,128)(2,1)} %param.21) | copy-start | bytes 2457604
  43.1 20.3 %copy-start.4 = (f32[2560]{0:T(1024)S(1)}, f32[2560]{0:T(1024)}, u32[]{:S(2)}) copy-start(f32[2560]{0:T(1024)} %param.20) | copy-start | bytes 30724
  44.1 19.3 %all-to-all-start.1 = ((bf16[16,160,128]{2,1,0:T(8,128)(2,1)}), bf16[16,160,128]{2,1,0:T(8,128)(2,1)S(1)}, u32[]{:S(2)}, u32[]{:S(2)}) async-start(bf16[16,160,128]{2,1,0:T(8,128)(2,1)} %broadcast_in_dim.38), calls=%async_computation.1 | async-start | bytes 1310720 | tf_op jit(solution)/shard_map/all_to_all | solution.py:35
  65.5 23.7 %copy-start.9 = (s32[16,6,4,2,16]{4,3,2,0,1:T(2,128)S(1)}, s32[16,6,4,2,16]{4,3,2,0,1:T(2,128)}, u32[]{:S(2)}) copy-start(s32[16,6,4,2,16]{4,3,2,0,1:T(2,128)} %reshape.347) | copy-start | bytes 147460
  65.5 5.2 %collective-permute-start.4 = (bf16[224,128]{1,0:T(8,128)(2,1)S(1)}, bf16[224,128]{1,0:T(8,128)(2,1)S(1)}, u32[]{:S(2)}, u32[]{:S(2)}) collective-permute-start(bf16[224,128]{1,0:T(8,128)(2,1)S(1)} %project.1.p0), channel_id=1, source_target_pairs={{0,3},{1,2},{2,1},{3,0},{4,7},{5,6},{6,5},{7,4},{8,11},{9,10},{10,... | collective-permute-start | bytes 172040 | tf_op jit(solution)/shard_map/ppermute | solution.py:44
  67.1 5.7 %collective-permute-start.3 = (bf16[224,128]{1,0:T(8,128)(2,1)S(1)}, bf16[224,128]{1,0:T(8,128)(2,1)S(1)}, u32[]{:S(2)}, u32[]{:S(2)}) collective-permute-start(bf16[224,128]{1,0:T(8,128)(2,1)S(1)} %project.1.p0), channel_id=1, source_target_pairs={{0,2},{1,3},{2,0},{3,1},{4,6},{5,7},{6,4},{7,5},{8,10},{9,11},{10,... | collective-permute-start | bytes 172040 | tf_op jit(solution)/shard_map/ppermute | solution.py:44
  70.0 2.9 %collective-permute-start.2 = (bf16[224,128]{1,0:T(8,128)(2,1)S(1)}, bf16[224,128]{1,0:T(8,128)(2,1)S(1)}, u32[]{:S(2)}, u32[]{:S(2)}) collective-permute-start(bf16[224,128]{1,0:T(8,128)(2,1)S(1)} %project.1.p0), channel_id=1, source_target_pairs={{0,1},{1,0},{2,3},{3,2},{4,5},{5,4},{6,7},{7,6},{8,9},{9,8},{10,11... | collective-permute-start | bytes 172040 | tf_op jit(solution)/shard_map/ppermute | solution.py:44
  76.6 4.7 %collective-permute-start.8 = (bf16[32,768]{1,0:T(8,128)(2,1)S(1)}, bf16[32,768]{1,0:T(8,128)(2,1)S(1)}, u32[]{:S(2)}, u32[]{:S(2)}) collective-permute-start(bf16[32,768]{1,0:T(8,128)(2,1)S(1)} %get-tuple-element.27), channel_id=1, source_target_pairs={{0,1},{1,0},{2,3},{3,2},{4,5},{5,4},{6,7},{7,6},{8,9},{9,8},{10,11... | collective-permute-start | bytes 147464 | tf_op jit(solution)/shard_map/ppermute | solution.py:44
  77.3 4.5 %collective-permute-start.9 = (bf16[32,768]{1,0:T(8,128)(2,1)S(1)}, bf16[32,768]{1,0:T(8,128)(2,1)S(1)}, u32[]{:S(2)}, u32[]{:S(2)}) collective-permute-start(bf16[32,768]{1,0:T(8,128)(2,1)S(1)} %get-tuple-element.28), channel_id=1, source_target_pairs={{0,2},{1,3},{2,0},{3,1},{4,6},{5,7},{6,4},{7,5},{8,10},{9,11},{10,... | collective-permute-start | bytes 147464 | tf_op jit(solution)/shard_map/ppermute | solution.py:44
  78.6 5.7 %collective-permute-start.10 = (bf16[32,768]{1,0:T(8,128)(2,1)S(1)}, bf16[32,768]{1,0:T(8,128)(2,1)S(1)}, u32[]{:S(2)}, u32[]{:S(2)}) collective-permute-start(bf16[32,768]{1,0:T(8,128)(2,1)S(1)} %get-tuple-element.29), channel_id=1, source_target_pairs={{0,3},{1,2},{2,1},{3,0},{4,7},{5,6},{6,5},{7,4},{8,11},{9,10},{10,... | collective-permute-start | bytes 147464 | tf_op jit(solution)/shard_map/ppermute | solution.py:44
  81.2 8.3 %copy-start.15 = (f32[256]{0:T(256)S(1)}, f32[256]{0:T(256)}, u32[]{:S(2)}) copy-start(f32[256]{0:T(256)} %eq.128) | copy-start | bytes 3076
  84.8 5.5 %collective-permute-start.13 = (bf16[32,640]{1,0:T(8,128)(2,1)S(1)}, bf16[32,640]{1,0:T(8,128)(2,1)S(1)}, u32[]{:S(2)}, u32[]{:S(2)}) collective-permute-start(bf16[32,640]{1,0:T(8,128)(2,1)S(1)} %multiply_reduce_fusion), channel_id=1, source_target_pairs={{0,4},{1,5},{2,6},{3,7},{4,0},{5,1},{6,2},{7,3},{8,12},{9,13},{10,... | collective-permute-start | bytes 122888 | tf_op jit(solution)/shard_map/ppermute | solution.py:44
  86.7 4.7 %collective-permute-start.12 = (bf16[32,640]{1,0:T(8,128)(2,1)S(1)}, bf16[32,640]{1,0:T(8,128)(2,1)S(1)}, u32[]{:S(2)}, u32[]{:S(2)}) collective-permute-start(bf16[32,640]{1,0:T(8,128)(2,1)S(1)} %multiply_reduce_fusion), channel_id=1, source_target_pairs={{0,8},{1,9},{2,10},{3,11},{4,12},{5,13},{6,14},{7,15},{8,0},{9,1},... | collective-permute-start | bytes 122888 | tf_op jit(solution)/shard_map/ppermute | solution.py:44
  88.8 4.1 %collective-permute-start.11 = (bf16[32,640]{1,0:T(8,128)(2,1)S(1)}, bf16[32,640]{1,0:T(8,128)(2,1)S(1)}, u32[]{:S(2)}, u32[]{:S(2)}) collective-permute-start(bf16[32,640]{1,0:T(8,128)(2,1)S(1)} %multiply_reduce_fusion), channel_id=1, source_target_pairs={{0,12},{1,13},{2,14},{3,15},{4,8},{5,9},{6,10},{7,11},{8,4},{9,5},... | collective-permute-start | bytes 122888 | tf_op jit(solution)/shard_map/ppermute | solution.py:44
  92.9 9.4 %copy-start.17 = (s32[4]{0:T(128)S(1)}, s32[4]{0:T(128)}, u32[]{:S(2)}) copy-start(s32[4]{0:T(128)} %iota_add_fusion) | copy-start | bytes 52
  92.9 9.5 %copy-start.20 = (s32[16]{0:T(128)S(1)}, s32[16]{0:T(128)}, u32[]{:S(2)}) copy-start(s32[16]{0:T(128)} %broadcast_multiply_fusion) | copy-start | bytes 196
  96.8 26.8 %copy-start.7 = (bf16[2560,192]{0,1:T(8,128)(2,1)S(1)}, bf16[2560,192]{0,1:T(8,128)(2,1)}, u32[]{:S(2)}) copy-start(bf16[2560,192]{0,1:T(8,128)(2,1)} %param.35) | copy-start | bytes 2949124
  96.8 15.1 %all-to-all-start.2 = ((bf16[16,16,640]{2,1,0:T(8,128)(2,1)}), bf16[16,16,640]{2,1,0:T(8,128)(2,1)S(1)}, u32[]{:S(2)}, u32[]{:S(2)}) async-start(bf16[16,16,640]{2,1,0:T(8,128)(2,1)} %bitcast.34), calls=%async_computation.2 | async-start | bytes 655360 | tf_op jit(solution)/shard_map/all_to_all | solution.py:575
  102.6 49.9 %collective-permute-start.21 = (bf16[2560,384]{1,0:T(8,128)(2,1)}, bf16[2560,384]{1,0:T(8,128)(2,1)}, u32[]{:S(2)}, u32[]{:S(2)}) collective-permute-start(bf16[2560,384]{1,0:T(8,128)(2,1)} %bitcast.159), channel_id=1, source_target_pairs={{0,1},{1,0},{2,3},{3,2},{4,5},{5,4},{6,7},{7,6},{8,9},{9,8},{10,11... | collective-permute-start | bytes 5898248 | tf_op jit(solution)/shard_map/ppermute | solution.py:571
  102.9 49.6 %collective-permute-start.22 = (bf16[2560,384]{1,0:T(8,128)(2,1)}, bf16[2560,384]{1,0:T(8,128)(2,1)}, u32[]{:S(2)}, u32[]{:S(2)}) collective-permute-start(bf16[2560,384]{1,0:T(8,128)(2,1)} %bitcast.161), channel_id=1, source_target_pairs={{0,1},{1,0},{2,3},{3,2},{4,5},{5,4},{6,7},{7,6},{8,9},{9,8},{10,11... | collective-permute-start | bytes 5898248 | tf_op jit(solution)/shard_map/ppermute | solution.py:571
  103.2 49.3 %collective-permute-start.23 = (bf16[384,2560]{1,0:T(8,128)(2,1)}, bf16[384,2560]{1,0:T(8,128)(2,1)}, u32[]{:S(2)}, u32[]{:S(2)}) collective-permute-start(bf16[384,2560]{1,0:T(8,128)(2,1)} %bitcast.163), channel_id=1, source_target_pairs={{0,1},{1,0},{2,3},{3,2},{4,5},{5,4},{6,7},{7,6},{8,9},{9,8},{10,11... | collective-permute-start | bytes 5898248 | tf_op jit(solution)/shard_map/ppermute | solution.py:571
  111.9 0.7 copy-start.11
  115.3 37.2 %all-to-all-start.3 = ((bf16[16,16,2560]{2,1,0:T(8,128)(2,1)}), bf16[16,16,2560]{2,1,0:T(8,128)(2,1)S(1)}, u32[]{:S(2)}, u32[]{:S(2)}) async-start(bf16[16,16,2560]{2,1,0:T(8,128)(2,1)} %bitcast.165), calls=%async_computation.3 | async-start | bytes 2621440 | tf_op jit(solution)/shard_map/all_to_all | solution.py:630
  122.4 4.8 %copy-start.8 = (bf16[2560,192]{0,1:T(8,128)(2,1)S(1)}, bf16[2560,192]{0,1:T(8,128)(2,1)}, u32[]{:S(2)}) copy-start(bf16[2560,192]{0,1:T(8,128)(2,1)} %param.36) | copy-start | bytes 2949124
  122.4 4.3 %collective-permute-start.15 = (bf16[64,2560]{1,0:T(8,128)(2,1)}, bf16[64,2560]{1,0:T(8,128)(2,1)S(1)}, u32[]{:S(2)}, u32[]{:S(2)}) collective-permute-start(bf16[64,2560]{1,0:T(8,128)(2,1)} %get-tuple-element.33), channel_id=1, source_target_pairs={{0,1},{1,0},{2,3},{3,2},{4,5},{5,4},{6,7},{7,6},{8,9},{9,8},{10,11... | collective-permute-start | bytes 983048 | tf_op jit(solution)/shard_map/ppermute | solution.py:634
  131.0 2.0 collective-permute-start.16
  132.4 20.0 %copy-start.2 = (bf16[2560,64]{0,1:T(8,128)(2,1)S(1)}, bf16[2560,64]{0,1:T(8,128)(2,1)}, u32[]{:S(2)}) copy-start(bf16[2560,64]{0,1:T(8,128)(2,1)} %param.31) | copy-start | bytes 983044
  134.1 0.8 copy-start.10
  134.9 4.2 %collective-permute-start.17 = (bf16[2,160,128]{2,1,0:T(8,128)(2,1)}, bf16[2,160,128]{2,1,0:T(8,128)(2,1)}, u32[]{:S(2)}, u32[]{:S(2)}) collective-permute-start(bf16[2,160,128]{2,1,0:T(8,128)(2,1)} %get-tuple-element.49), channel_id=1, source_target_pairs={{0,4},{1,5},{2,6},{3,7},{4,0},{5,1},{6,2},{7,3},{8,12},{9,13},{10,... | collective-permute-start | bytes 245768 | tf_op jit(solution)/shard_map/ppermute | solution.py:44
  136.6 5.4 %collective-permute-start.19 = (bf16[2,160,128]{2,1,0:T(8,128)(2,1)}, bf16[2,160,128]{2,1,0:T(8,128)(2,1)S(1)}, u32[]{:S(2)}, u32[]{:S(2)}) collective-permute-start(bf16[2,160,128]{2,1,0:T(8,128)(2,1)} %get-tuple-element.50), channel_id=1, source_target_pairs={{0,12},{1,13},{2,14},{3,15},{4,8},{5,9},{6,10},{7,11},{8,4},{9,5},... | collective-permute-start | bytes 245768 | tf_op jit(solution)/shard_map/ppermute | solution.py:44
  139.1 5.1 %collective-permute-start.18 = (bf16[2,160,128]{2,1,0:T(8,128)(2,1)S(1)}, bf16[2,160,128]{2,1,0:T(8,128)(2,1)S(1)}, u32[]{:S(2)}, u32[]{:S(2)}) collective-permute-start(bf16[2,160,128]{2,1,0:T(8,128)(2,1)S(1)} %get-tuple-element.51), channel_id=1, source_target_pairs={{0,8},{1,9},{2,10},{3,11},{4,12},{5,13},{6,14},{7,15},{8,0},{9,1},... | collective-permute-start | bytes 245768 | tf_op jit(solution)/shard_map/ppermute | solution.py:44
  142.0 4.0 %collective-permute-start.14 = (bf16[64,160]{0,1:T(8,128)(2,1)S(1)}, bf16[64,160]{0,1:T(8,128)(2,1)S(1)}, u32[]{:S(2)}, u32[]{:S(2)}) collective-permute-start(bf16[64,160]{0,1:T(8,128)(2,1)S(1)} %constant_dynamic-slice_fusion.1), channel_id=1, source_target_pairs={{0,1},{1,0},{2,3},{3,2},{4,5},{5,4},{6,7},{7,6},{8,9},{9,8},{10,11... | collective-permute-start | bytes 61448 | tf_op jit(solution)/shard_map/ppermute | solution.py:675
  145.2 4.9 %collective-permute-start.20 = (bf16[160,128]{1,0:T(8,128)(2,1)S(1)}, bf16[160,128]{1,0:T(8,128)(2,1)S(1)}, u32[]{:S(2)}, u32[]{:S(2)}) collective-permute-start(bf16[160,128]{1,0:T(8,128)(2,1)S(1)} %fusion.28), channel_id=1, source_target_pairs={{0,2},{1,3},{2,0},{3,1},{4,6},{5,7},{6,4},{7,5},{8,10},{9,11},{10,... | collective-permute-start | bytes 122888 | tf_op jit(solution)/shard_map/ppermute | solution.py:663
Sparse Core Ops, SparseCore 0:
  9.2 54.2 all-gather.1

commit v6 on v5

--- a/solution.py
+++ b/solution.py
@@ -129,7 +129,6 @@
         in_specs=[vmem] * 3,
         out_specs=vmem,
         scratch_shapes=[pltpu.VMEM((width + TOPK + 2, total), bf16)],
-        compiler_params=pltpu.CompilerParams(vmem_limit_bytes=4 << 20),
         name="payload",
     )(x, routes, beams)
 
@@ -264,6 +263,37 @@
         compiler_params=pltpu.CompilerParams(vmem_limit_bytes=12 << 20),
         name="attention",
     )(scalars, parent, cosine, sine, *pieces, *caches)
+
+
+def output_kernel(x_index, h0, h1, h2, h3, weights, residual, out):
+    rows, span = h0.shape
+    acc = residual[...].astype(f32)
+    for d, h in enumerate((h0, h1, h2, h3)):
+        place = pl.multiple_of((x_index[0] ^ d) * span, span)
+        acc = acc + lax.dot_general(
+            h[...],
+            weights[:, pl.ds(place, span)],
+            (((1,), (1,)), ((), ())),
+            preferred_element_type=f32,
+        )
+    attended = acc.astype(bf16)
+    part = rows // 2
+    for j in range(out.shape[0]):
+        t = j % 2
+        out[j] = attended[t * part : (t + 1) * part, :]
+
+
+def output_rows(x_index, heads, weights, residual, count):
+    rows, span = residual.shape
+    vmem = pl.BlockSpec(memory_space=pltpu.VMEM)
+    return pl.pallas_call(
+        output_kernel,
+        out_shape=jax.ShapeDtypeStruct((count, rows // 2, span), bf16),
+        in_specs=[pl.BlockSpec(memory_space=pltpu.SMEM)] + [vmem] * (SIDE + 2),
+        out_specs=vmem,
+        compiler_params=pltpu.CompilerParams(vmem_limit_bytes=16 << 20),
+        name="output",
+    )(x_index, *heads, weights, residual)
 
 
 def spread_kernel(pieces, gain, dispatch, attended, normed, sent):
@@ -557,21 +587,21 @@
         .reshape(subset, span)
     )
 
-    all_heads = jnp.concatenate(
-        in_order(group_parts(lambda d: heads, SIDE), x_index), axis=1
-    )
     residual = lax.dynamic_slice(
         inputs, (x_index * span, q_index * subset), (span, subset)
     ).T
-    attended_part = (residual.astype(f32) + dot(all_heads, output_columns)).astype(bf16)
-    gate_here, up_here, down_here, attended_part = lax.optimization_barrier(
-        (expert_gate[0], expert_up[0], expert_down[0], attended_part)
+    to_core = output_rows(
+        x_index[None].astype(jnp.int32),
+        group_parts(lambda d: heads, SIDE),
+        output_columns.T,
+        residual,
+        blk_count,
+    )
+    gate_here, up_here, down_here, to_core = lax.optimization_barrier(
+        (expert_gate[0], expert_up[0], expert_down[0], to_core)
     )
     blocks = [gate_here, up_here, down_here]
     expert_blocks = blocks + [lax.ppermute(b, "blk", partners(1)) for b in blocks]
-    to_core = jnp.broadcast_to(
-        attended_part.reshape(1, steps, part, span), (blk_count // 2, steps, part, span)
-    ).reshape(blk_count, part, span)
     attended_pieces = lax.all_to_all(to_core, "blk", 0, 0, tiled=True)
 
     per_req = E // req_count

time: 226 us -> 224 us (level)
  matrix products: 9.38 us -> 6.44 us
  Pallas kernels: 20.8 us -> 23.4 us
    dot_general x7 -> x6, matrix products: 7.39 us -> 4.47 us  [dot(): return jnp.dot(a, b, preferred_element_type=f32)]
  transfers between devices with their start and end apart: 29 -> 29, of which waited for: 13 -> 12; matrix products, arithmetic and copies ran while one was open for 15% -> 16% of each run, Pallas kernels for 4% -> 5%
where the time goes in v6:
time: 224 us; the launch traced here: 223 us
  starting transfers between devices  58.1 us (26%)
  blocking collectives  53 us (24%)
  waiting for transfers between devices  34 us (15%)
  Pallas kernels  23.4 us (10%)
  local copies, waits for them, and re-layouts  22 us (10%)
  between operations  15.9 us (7%)
  other arithmetic  9.74 us (4%)
  matrix products  6.44 us (3%)
    all_to_all x1, blocking collectives, per_device(): lax.all_to_all(expert_rows((req_index * per_req + x_index)[None].astype(j...  28.6 us
    all_to_all x1, blocking collectives, per_device(): final = lax.all_to_all(outgoing, 'req', 0, 0, tiled=True)  24.5 us
    ppermute x15, starting transfers between devices, group_parts(): lax.ppermute(piece_for(d), 'blk', partners(d * stride))  18.1 us
    ppermute x15, waiting for transfers between devices, group_parts(): lax.ppermute(piece_for(d), 'blk', partners(d * stride))  11.7 us
    all_to_all x1, starting transfers between devices, per_device(): by_slot = lax.all_to_all(payload, 'req', 0, 0, tiled=True)  10.2 us
    pallas_call x1, Pallas kernels, expert_rows(): pl.pallas_call(expert_kernel, out_shape=jax.ShapeDtypeStruct((width, coun...  8.84 us
    all_to_all x1, waiting for transfers between devices, per_device(): attended_pieces = lax.all_to_all(to_core, 'blk', 0, 0, tiled=True)  8.53 us
    all_to_all x1, starting transfers between devices, per_device(): lax.all_to_all(sent.reshape(req_count, CAP, width), 'req', 0, 0, tiled=True)  7.13 us
  transfers between devices with their start and end apart: 29, of which 12 were waited for; matrix products, arithmetic and copies ran while one was open for 16% of the time, Pallas kernels for 5%

profile of v6, /device:TPU:1, one launch (start us, length us, event | category | flops | bytes accessed | tf_op | source)
XLA Modules:
  0.0 222.6 jit_solution(8621958774207962157)
XLA Ops:
  6.5 0.7 all-gather.2.cloned.1.call-update
  7.3 1.9 payload.1
  9.2 10.2 %all-to-all-start = ((bf16[16,168,128]{2,1,0:T(8,128)(2,1)}), bf16[16,168,128]{2,1,0:T(8,128)(2,1)}, u32[]{:S(2)}, u32[]{:S(2)}) async-start(bf16[16,168,128]{2,1,0:T(8,128)(2,1)} %payload.1), calls=%async_computation | async-start | bytes 1376256 | tf_op jit(solution)/shard_map/all_to_all | solution.py:497
  22.0 0.8 broadcast_select_fusion
  22.8 2.6 %collective-permute-start.1 = (bf16[32,2560]{1,0:T(8,128)(2,1)}, bf16[32,2560]{1,0:T(8,128)(2,1)S(1)}, u32[]{:S(2)}, u32[]{:S(2)}) collective-permute-start(bf16[32,2560]{1,0:T(8,128)(2,1)} %get-tuple-element.52), channel_id=1, source_target_pairs={{0,1},{1,3},{2,5},{3,7},{4,9},{5,11},{6,13},{7,15},{8,0},{9,2},{10... | collective-permute-start | bytes 491528 | tf_op jit(solution)/shard_map/ppermute | solution.py:541
  25.4 3.5 %collective-permute-start = (bf16[32,2560]{1,0:T(8,128)(2,1)}, bf16[32,2560]{1,0:T(8,128)(2,1)}, u32[]{:S(2)}, u32[]{:S(2)}) collective-permute-start(bf16[32,2560]{1,0:T(8,128)(2,1)} %get-tuple-element.53), channel_id=1, source_target_pairs={{0,0},{1,2},{2,4},{3,6},{4,8},{5,10},{6,12},{7,14},{8,1},{9,3},{10... | collective-permute-start | bytes 491528 | tf_op jit(solution)/shard_map/ppermute | solution.py:540
  28.9 0.9 dynamic-slice_bitcast_fusion.1
  29.8 2.3 %collective-permute-start.7 = (bf16[384,256]{1,0:T(8,128)(2,1)}, bf16[384,256]{1,0:T(8,128)(2,1)S(1)}, u32[]{:S(2)}, u32[]{:S(2)}) collective-permute-start(bf16[384,256]{1,0:T(8,128)(2,1)} %get-tuple-element.43), channel_id=1, source_target_pairs={{0,12},{1,13},{2,14},{3,15},{4,8},{5,9},{6,10},{7,11},{8,4},{9,5},... | collective-permute-start | bytes 589832 | tf_op jit(solution)/shard_map/ppermute | solution.py:44
  32.0 1.5 collective-permute-start.6
  39.7 0.8 pad_add_fusion.scalars
  41.1 0.8 dynamic-slice_bitcast_fusion.9
  41.9 0.9 broadcast_in_dim.40
  42.9 7.0 %all-to-all-start.1 = ((bf16[16,160,128]{2,1,0:T(8,128)(2,1)}), bf16[16,160,128]{2,1,0:T(8,128)(2,1)S(1)}, u32[]{:S(2)}, u32[]{:S(2)}) async-start(bf16[16,160,128]{2,1,0:T(8,128)(2,1)} %broadcast_in_dim.40), calls=%async_computation.1 | async-start | bytes 1310720 | tf_op jit(solution)/shard_map/all_to_all | solution.py:35
  49.9 0.8 slice_convert_fusion
  50.7 1.3 reshape.341
  52.0 1.9 copy.115
  53.9 1.3 reshape.328
  55.4 0.8 fusion.22
  56.2 6.0 %all-to-all-done.1 = bf16[16,160,128]{2,1,0:T(8,128)(2,1)S(1)} async-done(((bf16[16,160,128]{2,1,0:T(8,128)(2,1)}), bf16[16,160,128]{2,1,0:T(8,128)(2,1)S(1)}, u32[]{:S(2)}, u32[]{:S(2)}) %all-to-all-start.1) | async-done | bytes 655392 | tf_op jit(solution)/shard_map/all_to_all | solution.py:35
  62.2 2.1 project.1.p0
  64.3 1.6 collective-permute-start.4
  66.0 2.9 %collective-permute-start.3 = (bf16[224,128]{1,0:T(8,128)(2,1)S(1)}, bf16[224,128]{1,0:T(8,128)(2,1)S(1)}, u32[]{:S(2)}, u32[]{:S(2)}) collective-permute-start(bf16[224,128]{1,0:T(8,128)(2,1)S(1)} %project.1.p0), channel_id=1, source_target_pairs={{0,2},{1,3},{2,0},{3,1},{4,6},{5,7},{6,4},{7,5},{8,10},{9,11},{10,... | collective-permute-start | bytes 172040 | tf_op jit(solution)/shard_map/ppermute | solution.py:44
  69.5 2.1 collective-permute-done.3.p2
  71.7 3.7 %attention.1 = (bf16[32,768]{1,0:T(8,128)(2,1)S(1)}, bf16[32,768]{1,0:T(8,128)(2,1)S(1)}, bf16[32,768]{1,0:T(8,128)(2,1)S(1)}, bf16[32,768]{1,0:T(8,128)(2,1)S(1)}) custom-call(s32[3]{0:T(128)S(1)} %pad_add_fusion.scalars, s32[1,128]{1,0:T(1,128)S(1)} %compare_select_fusion.3.parent, f32[64,128]{1,0:T(8,128)S(1)} %copy.111.cosine, ...), custom_call_target="tpu_custom_call" | custom-call | tf_op jit(solution)/shard_map/attention/pallas_call | solution.py:249
  75.4 0.7 collective-permute-start.8
  76.1 1.3 collective-permute-start.9
  77.4 2.0 collective-permute-start.10
  80.6 2.5 %collective-permute-done.10 = bf16[32,768]{1,0:T(8,128)(2,1)S(1)} collective-permute-done((bf16[32,768]{1,0:T(8,128)(2,1)S(1)}, bf16[32,768]{1,0:T(8,128)(2,1)S(1)}, u32[]{:S(2)}, u32[]{:S(2)}) %collective-permute-start.10) | collective-permute-done | bytes 49184 | tf_op jit(solution)/shard_map/ppermute | solution.py:44
  83.6 2.8 %collective-permute-start.13 = (bf16[32,640]{1,0:T(8,128)(2,1)S(1)}, bf16[32,640]{1,0:T(8,128)(2,1)S(1)}, u32[]{:S(2)}, u32[]{:S(2)}) collective-permute-start(bf16[32,640]{1,0:T(8,128)(2,1)S(1)} %multiply_reduce_fusion.h0), channel_id=1, source_target_pairs={{0,12},{1,13},{2,14},{3,15},{4,8},{5,9},{6,10},{7,11},{8,4},{9,5},... | collective-permute-start | bytes 122888 | tf_op jit(solution)/shard_map/ppermute | solution.py:44
  86.4 0.9 collective-permute-start.12
  87.7 0.7 fusion.13.dispatch
  88.7 2.1 collective-permute-done.12.h2
  90.8 1.9 copy-done.1
  92.7 1.8 output.1
  94.5 6.0 %all-to-all-start.2 = ((bf16[16,16,640]{2,1,0:T(8,128)(2,1)}), bf16[16,16,640]{2,1,0:T(8,128)(2,1)S(1)}, u32[]{:S(2)}, u32[]{:S(2)}) async-start(bf16[16,16,640]{2,1,0:T(8,128)(2,1)} %output.1), calls=%async_computation.2 | async-start | bytes 655360 | tf_op jit(solution)/shard_map/all_to_all | solution.py:605
  101.6 8.5 %all-to-all-done.2.pieces = bf16[16,16,640]{2,1,0:T(8,128)(2,1)S(1)} async-done(((bf16[16,16,640]{2,1,0:T(8,128)(2,1)}), bf16[16,16,640]{2,1,0:T(8,128)(2,1)S(1)}, u32[]{:S(2)}, u32[]{:S(2)}) %all-to-all-start.2) | async-done | bytes 327712 | tf_op jit(solution)/shard_map/all_to_all | solution.py:605
  110.1 0.7 copy-done.9
  110.8 2.7 %spread.1 = (bf16[64,2560]{1,0:T(8,128)(2,1)}, bf16[64,2560]{1,0:T(8,128)(2,1)}, bf16[256,2560]{1,0:T(8,128)(2,1)}) custom-call(bf16[16,16,640]{2,1,0:T(8,128)(2,1)} %copy-done.9, f32[1,2560]{1,0:T(1,128)} %broadcast_in_dim.41.gain, bf16[256,64]{1,0:T(8,128)(2,1)} %fusion.13.dispatch), custom_call_target="tpu_custom_call" | custom-call | tf_op jit(solution)/shard_map/spread/pallas_call | solution.py:314
  113.5 7.1 %all-to-all-start.3 = ((bf16[16,16,2560]{2,1,0:T(8,128)(2,1)}), bf16[16,16,2560]{2,1,0:T(8,128)(2,1)S(1)}, u32[]{:S(2)}, u32[]{:S(2)}) async-start(bf16[16,16,2560]{2,1,0:T(8,128)(2,1)} %bitcast.162), calls=%async_computation.3 | async-start | bytes 2621440 | tf_op jit(solution)/shard_map/all_to_all | solution.py:660
  120.6 1.1 collective-permute-start.15
  121.7 1.4 fusion.37
  123.1 1.7 fusion.5
  125.8 1.2 fusion
  127.0 1.4 copy.121
  128.4 0.8 dynamic-slice_bitcast_fusion
  129.4 1.2 fusion.1
  131.1 1.1 fusion.7
  132.2 0.8 dynamic-slice_bitcast_fusion.7
  133.4 1.3 copy.119
  134.7 1.3 collective-permute-start.19
  135.9 1.3 collective-permute-done.17
  137.2 0.9 collective-permute-start.18
  138.1 1.9 collective-permute-done.19
  140.1 0.9 collective-permute-start.14
  141.0 1.3 collective-permute-done.18
  142.3 1.0 fusion.11
  143.3 0.8 collective-permute-start.20
  144.2 4.1 %collective-permute-done.20 = bf16[160,128]{1,0:T(8,128)(2,1)S(1)} collective-permute-done((bf16[160,128]{1,0:T(8,128)(2,1)S(1)}, bf16[160,128]{1,0:T(8,128)(2,1)S(1)}, u32[]{:S(2)}, u32[]{:S(2)}) %collective-permute-start.20) | collective-permute-done | bytes 40992 | tf_op jit(solution)/shard_map/ppermute | solution.py:693
  148.3 2.4 %all-to-all-done.3 = bf16[16,16,2560]{2,1,0:T(8,128)(2,1)S(1)} async-done(((bf16[16,16,2560]{2,1,0:T(8,128)(2,1)}), bf16[16,16,2560]{2,1,0:T(8,128)(2,1)S(1)}, u32[]{:S(2)}, u32[]{:S(2)}) %all-to-all-start.3) | async-done | bytes 1310752 | tf_op jit(solution)/shard_map/all_to_all | solution.py:660
  150.7 8.8 %experts.1 = bf16[2560,256]{1,0:T(8,128)(2,1)S(1)} custom-call(s32[1]{0:T(128)} %bitcast.expert, bf16[256,2560]{1,0:T(8,128)(2,1)S(1)} %bitcast.140, bf16[64,2560]{1,0:T(8,128)(2,1)S(1)} %bitcast.146, f32[256,64]{1,0:T(8,128)S(1)} %fusion.6.named, bf16[2560,384]{1,0:T(8,128)(2,1)} %bitcast.157, bf16[2560,384]{1,0:T(8,128)(2,1)} %bitcast.159, ...), custom_call_target="tpu_custom_call" | custom-call | tf_op jit(solution)/shard_map/experts/pallas_call | solution.py:381
  159.6 28.6 %all_to_all.30.returned = bf16[16,160,256]{2,1,0:T(8,128)(2,1)S(1)} all-to-all(bf16[16,160,256]{2,1,0:T(8,128)(2,1)S(1)} %bitcast.141), channel_id=1, replica_groups=mesh['req'=16,'blk'=16] {'blk'}, dimensions={0} | all-to-all | bytes 2621440 | tf_op jit(solution)/shard_map/all_to_all | solution.py:711
  188.1 2.3 %collect.1 = bf16[16,160,128]{2,1,0:T(8,128)(2,1)S(1)} custom-call(s32[1]{0:T(128)} %dynamic_slice.82.slot, bf16[16,160,256]{2,1,0:T(8,128)(2,1)S(1)} %all_to_all.30.returned, s32[8,1024]{1,0:T(8,128)S(1)} %reshape.333.codes, f32[160,128]{1,0:T(8,128)S(1)} %fusion.14.own), custom_call_target="tpu_custom_call" | custom-call | tf_op jit(solution)/shard_map/collect/pallas_call | solution.py:436
  190.4 24.5 %all_to_all.31 = bf16[16,160,128]{2,1,0:T(8,128)(2,1)S(1)} all-to-all(bf16[16,160,128]{2,1,0:T(8,128)(2,1)S(1)} %collect.1), channel_id=1, replica_groups=mesh['req'=16,'blk'=16] {'req'}, dimensions={0} | all-to-all | bytes 1310720 | tf_op jit(solution)/shard_map/all_to_all | solution.py:726
  215.0 0.7 copy.126
  (124 shorter events, 13.9 us)
Async XLA Ops:
  6.5 119.3 %copy-start = (bf16[192,2560]{1,0:T(8,128)(2,1)S(1)}, bf16[192,2560]{1,0:T(8,128)(2,1)}, u32[]{:S(2)}) copy-start(bf16[192,2560]{1,0:T(8,128)(2,1)} %param.37) | copy-start | bytes 2949124
  6.5 13.1 %copy-start.10 = (bf16[1,3,128,1024]{3,2,1,0:T(8,128)(2,1)S(1)}, bf16[1,3,128,1024]{3,2,1,0:T(8,128)(2,1)}, u32[]{:S(2)}) copy-start(bf16[1,3,128,1024]{3,2,1,0:T(8,128)(2,1)} %param.24) | copy-start | bytes 2359300
  6.5 12.8 %copy-start.14 = (s32[16,1,3]{0,1,2:T(1,128)S(1)}, s32[16,1,3]{0,1,2:T(1,128)}, u32[]{:S(2)}) copy-start(s32[16,1,3]{0,1,2:T(1,128)} %param.25) | copy-start | bytes 580
  6.5 84.2 %all-gather.2.cloned.1.call-start = ((), (), s32[]{:S(2)}) async-start(), calls=%async_computation.6 | async-start | bytes 4096000 | tf_op jit(solution)/shard_map/all_gather | solution.py:512
  9.2 32.0 %all-to-all-start = ((bf16[16,168,128]{2,1,0:T(8,128)(2,1)}), bf16[16,168,128]{2,1,0:T(8,128)(2,1)}, u32[]{:S(2)}, u32[]{:S(2)}) async-start(bf16[16,168,128]{2,1,0:T(8,128)(2,1)} %payload.1), calls=%async_computation | async-start | bytes 1376256 | tf_op jit(solution)/shard_map/all_to_all | solution.py:497
  20.8 1.2 copy-start.11
  21.4 12.1 %copy-start.17 = (s32[16]{0:T(128)S(1)}, s32[16]{0:T(128)}, u32[]{:S(2)}) copy-start(s32[16]{0:T(128)} %param.27) | copy-start | bytes 196
  21.4 14.0 %copy-start.16 = (s32[16]{0:T(128)S(1)}, s32[16]{0:T(128)}, u32[]{:S(2)}) copy-start(s32[16]{0:T(128)} %param.26) | copy-start | bytes 196
  21.5 15.3 %copy-start.12 = (f32[2560]{0:T(1024)S(1)}, f32[2560]{0:T(1024)}, u32[]{:S(2)}) copy-start(f32[2560]{0:T(1024)} %param.30) | copy-start | bytes 30724
  22.8 33.4 %collective-permute-start.1 = (bf16[32,2560]{1,0:T(8,128)(2,1)}, bf16[32,2560]{1,0:T(8,128)(2,1)S(1)}, u32[]{:S(2)}, u32[]{:S(2)}) collective-permute-start(bf16[32,2560]{1,0:T(8,128)(2,1)} %get-tuple-element.52), channel_id=1, source_target_pairs={{0,1},{1,3},{2,5},{3,7},{4,9},{5,11},{6,13},{7,15},{8,0},{9,2},{10... | collective-permute-start | bytes 491528 | tf_op jit(solution)/shard_map/ppermute | solution.py:541
  25.4 30.8 %collective-permute-start = (bf16[32,2560]{1,0:T(8,128)(2,1)}, bf16[32,2560]{1,0:T(8,128)(2,1)}, u32[]{:S(2)}, u32[]{:S(2)}) collective-permute-start(bf16[32,2560]{1,0:T(8,128)(2,1)} %get-tuple-element.53), channel_id=1, source_target_pairs={{0,0},{1,2},{2,4},{3,6},{4,8},{5,10},{6,12},{7,14},{8,1},{9,3},{10... | collective-permute-start | bytes 491528 | tf_op jit(solution)/shard_map/ppermute | solution.py:540
  29.8 39.1 %collective-permute-start.7 = (bf16[384,256]{1,0:T(8,128)(2,1)}, bf16[384,256]{1,0:T(8,128)(2,1)S(1)}, u32[]{:S(2)}, u32[]{:S(2)}) collective-permute-start(bf16[384,256]{1,0:T(8,128)(2,1)} %get-tuple-element.43), channel_id=1, source_target_pairs={{0,12},{1,13},{2,14},{3,15},{4,8},{5,9},{6,10},{7,11},{8,4},{9,5},... | collective-permute-start | bytes 589832 | tf_op jit(solution)/shard_map/ppermute | solution.py:44
  32.0 37.5 %collective-permute-start.6 = (bf16[384,256]{1,0:T(8,128)(2,1)}, bf16[384,256]{1,0:T(8,128)(2,1)S(1)}, u32[]{:S(2)}, u32[]{:S(2)}) collective-permute-start(bf16[384,256]{1,0:T(8,128)(2,1)} %get-tuple-element.44), channel_id=1, source_target_pairs={{0,8},{1,9},{2,10},{3,11},{4,12},{5,13},{6,14},{7,15},{8,0},{9,1},... | collective-permute-start | bytes 589832 | tf_op jit(solution)/shard_map/ppermute | solution.py:44
  33.6 36.0 %collective-permute-start.5 = (bf16[384,256]{1,0:T(8,128)(2,1)}, bf16[384,256]{1,0:T(8,128)(2,1)S(1)}, u32[]{:S(2)}, u32[]{:S(2)}) collective-permute-start(bf16[384,256]{1,0:T(8,128)(2,1)} %get-tuple-element.45), channel_id=1, source_target_pairs={{0,4},{1,5},{2,6},{3,7},{4,0},{5,1},{6,2},{7,3},{8,12},{9,13},{10,... | collective-permute-start | bytes 589832 | tf_op jit(solution)/shard_map/ppermute | solution.py:44
  41.9 20.3 %copy-start.2 = (bf16[2560,160]{0,1:T(8,128)(2,1)S(1)}, bf16[2560,160]{0,1:T(8,128)(2,1)}, u32[]{:S(2)}) copy-start(bf16[2560,160]{0,1:T(8,128)(2,1)} %param.21) | copy-start | bytes 2457604
  41.9 20.3 %copy-start.4 = (f32[2560]{0:T(1024)S(1)}, f32[2560]{0:T(1024)}, u32[]{:S(2)}) copy-start(f32[2560]{0:T(1024)} %param.20) | copy-start | bytes 30724
  42.9 19.3 %all-to-all-start.1 = ((bf16[16,160,128]{2,1,0:T(8,128)(2,1)}), bf16[16,160,128]{2,1,0:T(8,128)(2,1)S(1)}, u32[]{:S(2)}, u32[]{:S(2)}) async-start(bf16[16,160,128]{2,1,0:T(8,128)(2,1)} %broadcast_in_dim.40), calls=%async_computation.1 | async-start | bytes 1310720 | tf_op jit(solution)/shard_map/all_to_all | solution.py:35
  64.3 23.0 %copy-start.7 = (s32[16,6,4,2,16]{4,3,2,0,1:T(2,128)S(1)}, s32[16,6,4,2,16]{4,3,2,0,1:T(2,128)}, u32[]{:S(2)}) copy-start(s32[16,6,4,2,16]{4,3,2,0,1:T(2,128)} %reshape.341) | copy-start | bytes 147460
  64.3 5.2 %collective-permute-start.4 = (bf16[224,128]{1,0:T(8,128)(2,1)S(1)}, bf16[224,128]{1,0:T(8,128)(2,1)S(1)}, u32[]{:S(2)}, u32[]{:S(2)}) collective-permute-start(bf16[224,128]{1,0:T(8,128)(2,1)S(1)} %project.1.p0), channel_id=1, source_target_pairs={{0,3},{1,2},{2,1},{3,0},{4,7},{5,6},{6,5},{7,4},{8,11},{9,10},{10,... | collective-permute-start | bytes 172040 | tf_op jit(solution)/shard_map/ppermute | solution.py:44
  66.0 5.7 %collective-permute-start.3 = (bf16[224,128]{1,0:T(8,128)(2,1)S(1)}, bf16[224,128]{1,0:T(8,128)(2,1)S(1)}, u32[]{:S(2)}, u32[]{:S(2)}) collective-permute-start(bf16[224,128]{1,0:T(8,128)(2,1)S(1)} %project.1.p0), channel_id=1, source_target_pairs={{0,2},{1,3},{2,0},{3,1},{4,6},{5,7},{6,4},{7,5},{8,10},{9,11},{10,... | collective-permute-start | bytes 172040 | tf_op jit(solution)/shard_map/ppermute | solution.py:44
  68.8 2.9 %collective-permute-start.2 = (bf16[224,128]{1,0:T(8,128)(2,1)S(1)}, bf16[224,128]{1,0:T(8,128)(2,1)S(1)}, u32[]{:S(2)}, u32[]{:S(2)}) collective-permute-start(bf16[224,128]{1,0:T(8,128)(2,1)S(1)} %project.1.p0), channel_id=1, source_target_pairs={{0,1},{1,0},{2,3},{3,2},{4,5},{5,4},{6,7},{7,6},{8,9},{9,8},{10,11... | collective-permute-start | bytes 172040 | tf_op jit(solution)/shard_map/ppermute | solution.py:44
  75.4 4.7 %collective-permute-start.8 = (bf16[32,768]{1,0:T(8,128)(2,1)S(1)}, bf16[32,768]{1,0:T(8,128)(2,1)S(1)}, u32[]{:S(2)}, u32[]{:S(2)}) collective-permute-start(bf16[32,768]{1,0:T(8,128)(2,1)S(1)} %get-tuple-element.27), channel_id=1, source_target_pairs={{0,1},{1,0},{2,3},{3,2},{4,5},{5,4},{6,7},{7,6},{8,9},{9,8},{10,11... | collective-permute-start | bytes 147464 | tf_op jit(solution)/shard_map/ppermute | solution.py:44
  76.1 4.5 %collective-permute-start.9 = (bf16[32,768]{1,0:T(8,128)(2,1)S(1)}, bf16[32,768]{1,0:T(8,128)(2,1)S(1)}, u32[]{:S(2)}, u32[]{:S(2)}) collective-permute-start(bf16[32,768]{1,0:T(8,128)(2,1)S(1)} %get-tuple-element.28), channel_id=1, source_target_pairs={{0,2},{1,3},{2,0},{3,1},{4,6},{5,7},{6,4},{7,5},{8,10},{9,11},{10,... | collective-permute-start | bytes 147464 | tf_op jit(solution)/shard_map/ppermute | solution.py:44
  77.4 5.7 %collective-permute-start.10 = (bf16[32,768]{1,0:T(8,128)(2,1)S(1)}, bf16[32,768]{1,0:T(8,128)(2,1)S(1)}, u32[]{:S(2)}, u32[]{:S(2)}) collective-permute-start(bf16[32,768]{1,0:T(8,128)(2,1)S(1)} %get-tuple-element.29), channel_id=1, source_target_pairs={{0,3},{1,2},{2,1},{3,0},{4,7},{5,6},{6,5},{7,4},{8,11},{9,10},{10,... | collective-permute-start | bytes 147464 | tf_op jit(solution)/shard_map/ppermute | solution.py:44
  80.1 7.6 %copy-start.13 = (f32[256]{0:T(256)S(1)}, f32[256]{0:T(256)}, u32[]{:S(2)}) copy-start(f32[256]{0:T(256)} %eq.119) | copy-start | bytes 3076
  83.6 5.1 %collective-permute-start.13 = (bf16[32,640]{1,0:T(8,128)(2,1)S(1)}, bf16[32,640]{1,0:T(8,128)(2,1)S(1)}, u32[]{:S(2)}, u32[]{:S(2)}) collective-permute-start(bf16[32,640]{1,0:T(8,128)(2,1)S(1)} %multiply_reduce_fusion.h0), channel_id=1, source_target_pairs={{0,12},{1,13},{2,14},{3,15},{4,8},{5,9},{6,10},{7,11},{8,4},{9,5},... | collective-permute-start | bytes 122888 | tf_op jit(solution)/shard_map/ppermute | solution.py:44
  86.4 4.4 %collective-permute-start.12 = (bf16[32,640]{1,0:T(8,128)(2,1)S(1)}, bf16[32,640]{1,0:T(8,128)(2,1)S(1)}, u32[]{:S(2)}, u32[]{:S(2)}) collective-permute-start(bf16[32,640]{1,0:T(8,128)(2,1)S(1)} %multiply_reduce_fusion.h0), channel_id=1, source_target_pairs={{0,8},{1,9},{2,10},{3,11},{4,12},{5,13},{6,14},{7,15},{8,0},{9,1},... | collective-permute-start | bytes 122888 | tf_op jit(solution)/shard_map/ppermute | solution.py:44
  87.3 3.5 %collective-permute-start.11 = (bf16[32,640]{1,0:T(8,128)(2,1)S(1)}, bf16[32,640]{1,0:T(8,128)(2,1)S(1)}, u32[]{:S(2)}, u32[]{:S(2)}) collective-permute-start(bf16[32,640]{1,0:T(8,128)(2,1)S(1)} %multiply_reduce_fusion.h0), channel_id=1, source_target_pairs={{0,4},{1,5},{2,6},{3,7},{4,0},{5,1},{6,2},{7,3},{8,12},{9,13},{10,... | collective-permute-start | bytes 122888 | tf_op jit(solution)/shard_map/ppermute | solution.py:44
  90.8 1.9 copy-start.1
  92.7 7.8 %copy-start.15 = (s32[4]{0:T(128)S(1)}, s32[4]{0:T(128)}, u32[]{:S(2)}) copy-start(s32[4]{0:T(128)} %iota_add_fusion) | copy-start | bytes 52
  92.7 8.0 %copy-start.18 = (s32[16]{0:T(128)S(1)}, s32[16]{0:T(128)}, u32[]{:S(2)}) copy-start(s32[16]{0:T(128)} %broadcast_multiply_fusion) | copy-start | bytes 196
  94.5 27.2 %copy-start.5 = (bf16[2560,192]{0,1:T(8,128)(2,1)S(1)}, bf16[2560,192]{0,1:T(8,128)(2,1)}, u32[]{:S(2)}) copy-start(bf16[2560,192]{0,1:T(8,128)(2,1)} %param.35) | copy-start | bytes 2949124
  94.5 15.6 %all-to-all-start.2 = ((bf16[16,16,640]{2,1,0:T(8,128)(2,1)}), bf16[16,16,640]{2,1,0:T(8,128)(2,1)S(1)}, u32[]{:S(2)}, u32[]{:S(2)}) async-start(bf16[16,16,640]{2,1,0:T(8,128)(2,1)} %output.1), calls=%async_computation.2 | async-start | bytes 655360 | tf_op jit(solution)/shard_map/all_to_all | solution.py:605
  100.8 49.8 %collective-permute-start.21 = (bf16[2560,384]{1,0:T(8,128)(2,1)}, bf16[2560,384]{1,0:T(8,128)(2,1)}, u32[]{:S(2)}, u32[]{:S(2)}) collective-permute-start(bf16[2560,384]{1,0:T(8,128)(2,1)} %bitcast.156), channel_id=1, source_target_pairs={{0,1},{1,0},{2,3},{3,2},{4,5},{5,4},{6,7},{7,6},{8,9},{9,8},{10,11... | collective-permute-start | bytes 5898248 | tf_op jit(solution)/shard_map/ppermute | solution.py:604
  101.0 49.7 %collective-permute-start.22 = (bf16[2560,384]{1,0:T(8,128)(2,1)}, bf16[2560,384]{1,0:T(8,128)(2,1)}, u32[]{:S(2)}, u32[]{:S(2)}) collective-permute-start(bf16[2560,384]{1,0:T(8,128)(2,1)} %bitcast.158), channel_id=1, source_target_pairs={{0,1},{1,0},{2,3},{3,2},{4,5},{5,4},{6,7},{7,6},{8,9},{9,8},{10,11... | collective-permute-start | bytes 5898248 | tf_op jit(solution)/shard_map/ppermute | solution.py:604
  101.4 49.3 %collective-permute-start.23 = (bf16[384,2560]{1,0:T(8,128)(2,1)}, bf16[384,2560]{1,0:T(8,128)(2,1)}, u32[]{:S(2)}, u32[]{:S(2)}) collective-permute-start(bf16[384,2560]{1,0:T(8,128)(2,1)} %bitcast.160), channel_id=1, source_target_pairs={{0,1},{1,0},{2,3},{3,2},{4,5},{5,4},{6,7},{7,6},{8,9},{9,8},{10,11... | collective-permute-start | bytes 5898248 | tf_op jit(solution)/shard_map/ppermute | solution.py:604
  110.1 0.7 copy-start.9
  113.5 37.2 %all-to-all-start.3 = ((bf16[16,16,2560]{2,1,0:T(8,128)(2,1)}), bf16[16,16,2560]{2,1,0:T(8,128)(2,1)S(1)}, u32[]{:S(2)}, u32[]{:S(2)}) async-start(bf16[16,16,2560]{2,1,0:T(8,128)(2,1)} %bitcast.162), calls=%async_computation.3 | async-start | bytes 2621440 | tf_op jit(solution)/shard_map/all_to_all | solution.py:660
  120.6 4.7 %copy-start.6 = (bf16[2560,192]{0,1:T(8,128)(2,1)S(1)}, bf16[2560,192]{0,1:T(8,128)(2,1)}, u32[]{:S(2)}) copy-start(bf16[2560,192]{0,1:T(8,128)(2,1)} %param.36) | copy-start | bytes 2949124
  120.6 4.2 %collective-permute-start.15 = (bf16[64,2560]{1,0:T(8,128)(2,1)}, bf16[64,2560]{1,0:T(8,128)(2,1)S(1)}, u32[]{:S(2)}, u32[]{:S(2)}) collective-permute-start(bf16[64,2560]{1,0:T(8,128)(2,1)} %get-tuple-element.33), channel_id=1, source_target_pairs={{0,1},{1,0},{2,3},{3,2},{4,5},{5,4},{6,7},{7,6},{8,9},{9,8},{10,11... | collective-permute-start | bytes 983048 | tf_op jit(solution)/shard_map/ppermute | solution.py:664
  129.2 2.0 collective-permute-start.16
  130.6 20.1 %copy-start.3 = (bf16[2560,64]{0,1:T(8,128)(2,1)S(1)}, bf16[2560,64]{0,1:T(8,128)(2,1)}, u32[]{:S(2)}) copy-start(bf16[2560,64]{0,1:T(8,128)(2,1)} %param.31) | copy-start | bytes 983044
  132.2 0.8 copy-start.8
  133.0 4.2 %collective-permute-start.17 = (bf16[2,160,128]{2,1,0:T(8,128)(2,1)}, bf16[2,160,128]{2,1,0:T(8,128)(2,1)}, u32[]{:S(2)}, u32[]{:S(2)}) collective-permute-start(bf16[2,160,128]{2,1,0:T(8,128)(2,1)} %get-tuple-element.49), channel_id=1, source_target_pairs={{0,4},{1,5},{2,6},{3,7},{4,0},{5,1},{6,2},{7,3},{8,12},{9,13},{10,... | collective-permute-start | bytes 245768 | tf_op jit(solution)/shard_map/ppermute | solution.py:44
  134.7 5.4 %collective-permute-start.19 = (bf16[2,160,128]{2,1,0:T(8,128)(2,1)}, bf16[2,160,128]{2,1,0:T(8,128)(2,1)S(1)}, u32[]{:S(2)}, u32[]{:S(2)}) collective-permute-start(bf16[2,160,128]{2,1,0:T(8,128)(2,1)} %get-tuple-element.50), channel_id=1, source_target_pairs={{0,12},{1,13},{2,14},{3,15},{4,8},{5,9},{6,10},{7,11},{8,4},{9,5},... | collective-permute-start | bytes 245768 | tf_op jit(solution)/shard_map/ppermute | solution.py:44
  137.2 5.1 %collective-permute-start.18 = (bf16[2,160,128]{2,1,0:T(8,128)(2,1)S(1)}, bf16[2,160,128]{2,1,0:T(8,128)(2,1)S(1)}, u32[]{:S(2)}, u32[]{:S(2)}) collective-permute-start(bf16[2,160,128]{2,1,0:T(8,128)(2,1)S(1)} %get-tuple-element.51), channel_id=1, source_target_pairs={{0,8},{1,9},{2,10},{3,11},{4,12},{5,13},{6,14},{7,15},{8,0},{9,1},... | collective-permute-start | bytes 245768 | tf_op jit(solution)/shard_map/ppermute | solution.py:44
  140.1 4.1 %collective-permute-start.14 = (bf16[64,160]{0,1:T(8,128)(2,1)S(1)}, bf16[64,160]{0,1:T(8,128)(2,1)S(1)}, u32[]{:S(2)}, u32[]{:S(2)}) collective-permute-start(bf16[64,160]{0,1:T(8,128)(2,1)S(1)} %constant_dynamic-slice_fusion.2), channel_id=1, source_target_pairs={{0,1},{1,0},{2,3},{3,2},{4,5},{5,4},{6,7},{7,6},{8,9},{9,8},{10,11... | collective-permute-start | bytes 61448 | tf_op jit(solution)/shard_map/ppermute | solution.py:705
  143.3 4.9 %collective-permute-start.20 = (bf16[160,128]{1,0:T(8,128)(2,1)S(1)}, bf16[160,128]{1,0:T(8,128)(2,1)S(1)}, u32[]{:S(2)}, u32[]{:S(2)}) collective-permute-start(bf16[160,128]{1,0:T(8,128)(2,1)S(1)} %fusion.20), channel_id=1, source_target_pairs={{0,2},{1,3},{2,0},{3,1},{4,6},{5,7},{6,4},{7,5},{8,10},{9,11},{10,... | collective-permute-start | bytes 122888 | tf_op jit(solution)/shard_map/ppermute | solution.py:693
Sparse Core Ops, SparseCore 0:
  9.2 54.3 all-gather.1

commit v7 on v6

--- a/solution.py
+++ b/solution.py
@@ -265,14 +265,23 @@
     )(scalars, parent, cosine, sine, *pieces, *caches)
 
 
-def output_kernel(x_index, h0, h1, h2, h3, weights, residual, out):
+def output_kernel(x_index, h0, h1, h2, h3, weights, residual, out, blocks, sems):
     rows, span = h0.shape
+    copies = []
+    for d in range(SIDE):
+        place = pl.multiple_of((x_index[0] ^ d) * span, span)
+        copies.append(
+            pltpu.make_async_copy(
+                weights.at[:, pl.ds(place, span)], blocks.at[d], sems.at[d]
+            )
+        )
+        copies[-1].start()
     acc = residual[...].astype(f32)
     for d, h in enumerate((h0, h1, h2, h3)):
-        place = pl.multiple_of((x_index[0] ^ d) * span, span)
+        copies[d].wait()
         acc = acc + lax.dot_general(
             h[...],
-            weights[:, pl.ds(place, span)],
+            blocks[d],
             (((1,), (1,)), ((), ())),
             preferred_element_type=f32,
         )
@@ -289,11 +298,19 @@
     return pl.pallas_call(
         output_kernel,
         out_shape=jax.ShapeDtypeStruct((count, rows // 2, span), bf16),
-        in_specs=[pl.BlockSpec(memory_space=pltpu.SMEM)] + [vmem] * (SIDE + 2),
+        in_specs=[pl.BlockSpec(memory_space=pltpu.SMEM)]
+        + [vmem] * SIDE
+        + [pl.BlockSpec(memory_space=pltpu.HBM), vmem],
         out_specs=vmem,
+        scratch_shapes=[
+            pltpu.VMEM((SIDE, span, span), bf16),
+            pltpu.SemaphoreType.DMA((SIDE,)),
+        ],
         compiler_params=pltpu.CompilerParams(vmem_limit_bytes=16 << 20),
         name="output",
-    )(x_index, *heads, weights, residual)
+    )(
+        x_index, *heads, pltpu.with_memory_space_constraint(weights, pltpu.HBM), residual
+    )
 
 
 def spread_kernel(pieces, gain, dispatch, attended, normed, sent):
@@ -706,7 +723,7 @@
         ).T.astype(f32)
         + shared
     )
-    arrived, own = lax.optimization_barrier((arrived, own))
+    arrived, _ = lax.optimization_barrier((arrived, over_x))
 
     returned = lax.all_to_all(
         expert_rows(

time: 224 us -> 220 us (0.982)
  blocking collectives: 53 us -> 22.1 us
  waiting for transfers between devices: 34 us -> 52.5 us
  starting transfers between devices: 58.1 us -> 68.4 us
  local copies, waits for them, and re-layouts: 22 us -> 18.3 us
    all_to_all x1 -> x0, blocking collectives: 28.6 us -> none  [per_device(): lax.all_to_all(expert_rows((req_index * per_req + x_index)[None].astype(j...]
    all_to_all x0 -> x1, starting transfers between devices: none -> 8.77 us  [per_device(): lax.all_to_all(expert_rows((req_index * per_req + x_index)[None].astype(j...]
    all_to_all x1, waiting for transfers between devices: 2.36 us -> 9.45 us  [per_device(): lax.all_to_all(sent.reshape(req_count, CAP, width), 'req', 0, 0, tiled=True)]
    all_to_all x0 -> x1, waiting for transfers between devices: none -> 6.93 us  [per_device(): lax.all_to_all(expert_rows((req_index * per_req + x_index)[None].astype(j...]
    ppermute x1, waiting for transfers between devices: 4.05 us -> 9.28 us  [per_device(): lax.ppermute(lax.dynamic_index_in_dim(over_x, 1 - q_high, 0, False).astyp...]
    all_to_all x1, blocking collectives: 24.5 us -> 22.1 us  [per_device(): final = lax.all_to_all(outgoing, 'req', 0, 0, tiled=True)]
    ppermute x15, waiting for transfers between devices: 11.7 us -> 14.1 us  [group_parts(): lax.ppermute(piece_for(d), 'blk', partners(d * stride))]
  transfers between devices with their start and end apart: 29 -> 30, of which waited for: 12 -> 14; matrix products, arithmetic and copies ran while one was open for 16% -> 15% of each run, Pallas kernels for 5% -> 5%
where the time goes in v7:
time: 220 us; the launch traced here: 218 us
  starting transfers between devices  68.4 us (31%)
  waiting for transfers between devices  52.5 us (24%)
  Pallas kernels  24.8 us (11%)
  blocking collectives  22.1 us (10%)
  local copies, waits for them, and re-layouts  18.3 us (8%)
  between operations  16.1 us (7%)
  other arithmetic  9.68 us (4%)
  matrix products  6.46 us (3%)
    all_to_all x1, blocking collectives, per_device(): final = lax.all_to_all(outgoing, 'req', 0, 0, tiled=True)  22.1 us
    ppermute x15, starting transfers between devices, group_parts(): lax.ppermute(piece_for(d), 'blk', partners(d * stride))  18.2 us
    ppermute x15, waiting for transfers between devices, group_parts(): lax.ppermute(piece_for(d), 'blk', partners(d * stride))  14.1 us
    all_to_all x1, starting transfers between devices, per_device(): by_slot = lax.all_to_all(payload, 'req', 0, 0, tiled=True)  10.1 us
    all_to_all x1, waiting for transfers between devices, per_device(): lax.all_to_all(sent.reshape(req_count, CAP, width), 'req', 0, 0, tiled=True)  9.45 us
    ppermute x1, waiting for transfers between devices, per_device(): lax.ppermute(lax.dynamic_index_in_dim(over_x, 1 - q_high, 0, False).astyp...  9.28 us
    all_to_all x1, starting transfers between devices, per_device(): lax.all_to_all(expert_rows((req_index * per_req + x_index)[None].astype(j...  8.77 us
    pallas_call x1, Pallas kernels, expert_rows(): pl.pallas_call(expert_kernel, out_shape=jax.ShapeDtypeStruct((width, coun...  8.5 us
  transfers between devices with their start and end apart: 30, of which 14 were waited for; matrix products, arithmetic and copies ran while one was open for 15% of the time, Pallas kernels for 5%

profile of v7, /device:TPU:1, one launch (start us, length us, event | category | flops | bytes accessed | tf_op | source)
XLA Modules:
  0.0 218.3 jit_solution(5316183176903151364)
XLA Ops:
  6.5 0.7 all-gather.2.cloned.1.call-update
  7.3 1.9 payload.1
  9.2 10.1 %all-to-all-start = ((bf16[16,168,128]{2,1,0:T(8,128)(2,1)}), bf16[16,168,128]{2,1,0:T(8,128)(2,1)S(1)}, u32[]{:S(2)}, u32[]{:S(2)}) async-start(bf16[16,168,128]{2,1,0:T(8,128)(2,1)} %payload.1), calls=%async_computation | async-start | bytes 1376256 | tf_op jit(solution)/shard_map/all_to_all | solution.py:514
  21.9 1.8 broadcast_select_fusion
  23.7 2.6 %collective-permute-start.1 = (bf16[32,2560]{1,0:T(8,128)(2,1)}, bf16[32,2560]{1,0:T(8,128)(2,1)S(1)}, u32[]{:S(2)}, u32[]{:S(2)}) collective-permute-start(bf16[32,2560]{1,0:T(8,128)(2,1)} %get-tuple-element.50), channel_id=1, source_target_pairs={{0,1},{1,3},{2,5},{3,7},{4,9},{5,11},{6,13},{7,15},{8,0},{9,2},{10... | collective-permute-start | bytes 491528 | tf_op jit(solution)/shard_map/ppermute | solution.py:558
  26.3 3.5 %collective-permute-start = (bf16[32,2560]{1,0:T(8,128)(2,1)}, bf16[32,2560]{1,0:T(8,128)(2,1)}, u32[]{:S(2)}, u32[]{:S(2)}) collective-permute-start(bf16[32,2560]{1,0:T(8,128)(2,1)} %get-tuple-element.51), channel_id=1, source_target_pairs={{0,0},{1,2},{2,4},{3,6},{4,8},{5,10},{6,12},{7,14},{8,1},{9,3},{10... | collective-permute-start | bytes 491528 | tf_op jit(solution)/shard_map/ppermute | solution.py:557
  29.8 0.9 dynamic-slice_bitcast_fusion.1
  30.6 2.3 %collective-permute-start.7 = (bf16[384,256]{1,0:T(8,128)(2,1)}, bf16[384,256]{1,0:T(8,128)(2,1)S(1)}, u32[]{:S(2)}, u32[]{:S(2)}) collective-permute-start(bf16[384,256]{1,0:T(8,128)(2,1)} %get-tuple-element.41), channel_id=1, source_target_pairs={{0,12},{1,13},{2,14},{3,15},{4,8},{5,9},{6,10},{7,11},{8,4},{9,5},... | collective-permute-start | bytes 589832 | tf_op jit(solution)/shard_map/ppermute | solution.py:44
  32.9 1.5 collective-permute-start.6
  34.5 0.7 dynamic_slice.82.slot
  37.8 0.7 add_convert_fusion
  39.6 0.8 copy-done.8
  40.4 0.9 broadcast_in_dim.40
  41.4 8.4 %all-to-all-start.1 = ((bf16[16,160,128]{2,1,0:T(8,128)(2,1)}), bf16[16,160,128]{2,1,0:T(8,128)(2,1)S(1)}, u32[]{:S(2)}, u32[]{:S(2)}) async-start(bf16[16,160,128]{2,1,0:T(8,128)(2,1)} %broadcast_in_dim.40), calls=%async_computation.1 | async-start | bytes 1310720 | tf_op jit(solution)/shard_map/all_to_all | solution.py:35
  50.3 0.7 eq.119
  51.8 0.7 pad_add_fusion.scalars
  52.5 0.8 slice_convert_fusion
  53.3 1.3 reshape.341
  54.6 1.9 copy.115
  56.5 1.3 reshape.328
  58.1 4.0 %all-to-all-done.1 = bf16[16,160,128]{2,1,0:T(8,128)(2,1)S(1)} async-done(((bf16[16,160,128]{2,1,0:T(8,128)(2,1)}), bf16[16,160,128]{2,1,0:T(8,128)(2,1)S(1)}, u32[]{:S(2)}, u32[]{:S(2)}) %all-to-all-start.1) | async-done | bytes 655392 | tf_op jit(solution)/shard_map/all_to_all | solution.py:35
  62.1 2.1 project.1.p0
  64.2 1.6 collective-permute-start.4
  65.8 2.9 %collective-permute-start.3 = (bf16[224,128]{1,0:T(8,128)(2,1)S(1)}, bf16[224,128]{1,0:T(8,128)(2,1)S(1)}, u32[]{:S(2)}, u32[]{:S(2)}) collective-permute-start(bf16[224,128]{1,0:T(8,128)(2,1)S(1)} %project.1.p0), channel_id=1, source_target_pairs={{0,2},{1,3},{2,0},{3,1},{4,6},{5,7},{6,4},{7,5},{8,10},{9,11},{10,... | collective-permute-start | bytes 172040 | tf_op jit(solution)/shard_map/ppermute | solution.py:44
  68.6 0.7 compare_select_fusion.3.parent
  69.4 2.1 collective-permute-done.3.p2
  71.5 3.7 %attention.1 = (bf16[32,768]{1,0:T(8,128)(2,1)S(1)}, bf16[32,768]{1,0:T(8,128)(2,1)S(1)}, bf16[32,768]{1,0:T(8,128)(2,1)S(1)}, bf16[32,768]{1,0:T(8,128)(2,1)S(1)}) custom-call(s32[3]{0:T(128)S(1)} %pad_add_fusion.scalars, s32[1,128]{1,0:T(1,128)S(1)} %compare_select_fusion.3.parent, f32[64,128]{1,0:T(8,128)S(1)} %copy.111.cosine, ...), custom_call_target="tpu_custom_call" | custom-call | tf_op jit(solution)/shard_map/attention/pallas_call | solution.py:249
  75.2 0.7 collective-permute-start.8
  75.9 1.3 collective-permute-start.9
  77.2 2.0 collective-permute-start.10
  79.2 0.8 fusion.22
  80.4 2.5 %collective-permute-done.10 = bf16[32,768]{1,0:T(8,128)(2,1)S(1)} collective-permute-done((bf16[32,768]{1,0:T(8,128)(2,1)S(1)}, bf16[32,768]{1,0:T(8,128)(2,1)S(1)}, u32[]{:S(2)}, u32[]{:S(2)}) %collective-permute-start.10) | collective-permute-done | bytes 49184 | tf_op jit(solution)/shard_map/ppermute | solution.py:44
  83.4 2.8 %collective-permute-start.13 = (bf16[32,640]{1,0:T(8,128)(2,1)S(1)}, bf16[32,640]{1,0:T(8,128)(2,1)S(1)}, u32[]{:S(2)}, u32[]{:S(2)}) collective-permute-start(bf16[32,640]{1,0:T(8,128)(2,1)S(1)} %multiply_reduce_fusion.h0), channel_id=1, source_target_pairs={{0,12},{1,13},{2,14},{3,15},{4,8},{5,9},{6,10},{7,11},{8,4},{9,5},... | collective-permute-start | bytes 122888 | tf_op jit(solution)/shard_map/ppermute | solution.py:44
  86.3 0.9 collective-permute-start.12
  87.9 2.7 %collective-permute-done.12.h2 = bf16[32,640]{1,0:T(8,128)(2,1)S(1)} collective-permute-done((bf16[32,640]{1,0:T(8,128)(2,1)S(1)}, bf16[32,640]{1,0:T(8,128)(2,1)S(1)}, u32[]{:S(2)}, u32[]{:S(2)}) %collective-permute-start.12) | collective-permute-done | bytes 40992 | tf_op jit(solution)/shard_map/ppermute | solution.py:44
  90.6 3.4 %output.1 = bf16[16,16,640]{2,1,0:T(8,128)(2,1)} custom-call(s32[1]{0:T(128)} %bitcast.4.x_index, bf16[32,640]{1,0:T(8,128)(2,1)S(1)} %multiply_reduce_fusion.h0, bf16[32,640]{1,0:T(8,128)(2,1)S(1)} %collective-permute-done.11.h1, bf16[32,640]{1,0:T(8,128)(2,1)S(1)} %collective-permute-done.12.h2, bf16[32,640]{1,0:T(8,128)(2,1)S(1)} %collective-permute-done.13.h3, ...), custom_call_target="tpu_custom_call" | custom-call | tf_op jit(solution)/shard_map/output/pallas_call | solution.py:298
  94.1 6.0 %all-to-all-start.2 = ((bf16[16,16,640]{2,1,0:T(8,128)(2,1)}), bf16[16,16,640]{2,1,0:T(8,128)(2,1)S(1)}, u32[]{:S(2)}, u32[]{:S(2)}) async-start(bf16[16,16,640]{2,1,0:T(8,128)(2,1)} %output.1), calls=%async_computation.2 | async-start | bytes 655360 | tf_op jit(solution)/shard_map/all_to_all | solution.py:622
  100.1 0.7 dynamic-slice_bitcast_fusion.10
  100.9 0.7 fusion.13.dispatch
  102.4 7.2 %all-to-all-done.2.pieces = bf16[16,16,640]{2,1,0:T(8,128)(2,1)S(1)} async-done(((bf16[16,16,640]{2,1,0:T(8,128)(2,1)}), bf16[16,16,640]{2,1,0:T(8,128)(2,1)S(1)}, u32[]{:S(2)}, u32[]{:S(2)}) %all-to-all-start.2) | async-done | bytes 327712 | tf_op jit(solution)/shard_map/all_to_all | solution.py:622
  109.6 0.7 copy-done.7
  110.3 2.7 %spread.1 = (bf16[64,2560]{1,0:T(8,128)(2,1)}, bf16[64,2560]{1,0:T(8,128)(2,1)}, bf16[256,2560]{1,0:T(8,128)(2,1)}) custom-call(bf16[16,16,640]{2,1,0:T(8,128)(2,1)} %copy-done.7, f32[1,2560]{1,0:T(1,128)} %broadcast_in_dim.41.gain, bf16[256,64]{1,0:T(8,128)(2,1)} %fusion.13.dispatch), custom_call_target="tpu_custom_call" | custom-call | tf_op jit(solution)/shard_map/spread/pallas_call | solution.py:331
  113.1 5.6 %all-to-all-start.3 = ((bf16[16,16,2560]{2,1,0:T(8,128)(2,1)}), bf16[16,16,2560]{2,1,0:T(8,128)(2,1)S(1)}, u32[]{:S(2)}, u32[]{:S(2)}) async-start(bf16[16,16,2560]{2,1,0:T(8,128)(2,1)} %bitcast.161), calls=%async_computation.3 | async-start | bytes 2621440 | tf_op jit(solution)/shard_map/all_to_all | solution.py:677
  118.7 1.1 collective-permute-start.14
  119.8 1.4 fusion.37
  121.2 1.7 fusion.5
  123.9 1.2 fusion
  125.1 1.4 copy.119
  126.6 0.7 dynamic-slice_bitcast_fusion
  127.5 1.2 fusion.1
  129.3 1.1 fusion.7
  130.5 1.2 collective-permute-start.18
  131.8 2.6 %collective-permute-done.16 = bf16[2,160,128]{2,1,0:T(8,128)(2,1)S(1)} collective-permute-done((bf16[2,160,128]{2,1,0:T(8,128)(2,1)S(1)}, bf16[2,160,128]{2,1,0:T(8,128)(2,1)S(1)}, u32[]{:S(2)}, u32[]{:S(2)}) %collective-permute-start.16) | collective-permute-done | bytes 81952 | tf_op jit(solution)/shard_map/ppermute | solution.py:44
  134.4 0.9 collective-permute-start.17
  135.7 3.6 %collective-permute-done.17 = bf16[2,160,128]{2,1,0:T(8,128)(2,1)S(1)} collective-permute-done((bf16[2,160,128]{2,1,0:T(8,128)(2,1)S(1)}, bf16[2,160,128]{2,1,0:T(8,128)(2,1)S(1)}, u32[]{:S(2)}, u32[]{:S(2)}) %collective-permute-start.17) | collective-permute-done | bytes 81952 | tf_op jit(solution)/shard_map/ppermute | solution.py:44
  139.3 9.5 %all-to-all-done.3 = bf16[16,16,2560]{2,1,0:T(8,128)(2,1)S(1)} async-done(((bf16[16,16,2560]{2,1,0:T(8,128)(2,1)}), bf16[16,16,2560]{2,1,0:T(8,128)(2,1)S(1)}, u32[]{:S(2)}, u32[]{:S(2)}) %all-to-all-start.3) | async-done | bytes 1310752 | tf_op jit(solution)/shard_map/all_to_all | solution.py:677
  148.8 8.5 %experts.1 = bf16[2560,256]{1,0:T(8,128)(2,1)} custom-call(s32[1]{0:T(128)} %bitcast.expert, bf16[256,2560]{1,0:T(8,128)(2,1)S(1)} %bitcast.140, bf16[64,2560]{1,0:T(8,128)(2,1)S(1)} %bitcast.144, f32[256,64]{1,0:T(8,128)S(1)} %fusion.6.named, bf16[2560,384]{1,0:T(8,128)(2,1)} %bitcast.156, bf16[2560,384]{1,0:T(8,128)(2,1)} %bitcast.158, ...), custom_call_target="tpu_custom_call" | custom-call | tf_op jit(solution)/shard_map/experts/pallas_call | solution.py:398
  157.3 8.8 %all-to-all-start.4 = ((bf16[16,160,256]{2,1,0:T(8,128)(2,1)}), bf16[16,160,256]{2,1,0:T(8,128)(2,1)S(1)}, u32[]{:S(2)}, u32[]{:S(2)}) async-start(bf16[16,160,256]{2,1,0:T(8,128)(2,1)} %bitcast.62), calls=%async_computation.4 | async-start | bytes 2621440 | tf_op jit(solution)/shard_map/all_to_all | solution.py:728
  166.7 3.0 %collective-permute-start.23 = (bf16[160,128]{1,0:T(8,128)(2,1)S(1)}, bf16[160,128]{1,0:T(8,128)(2,1)S(1)}, u32[]{:S(2)}, u32[]{:S(2)}) collective-permute-start(bf16[160,128]{1,0:T(8,128)(2,1)S(1)} %fusion.20), channel_id=1, source_target_pairs={{0,2},{1,3},{2,0},{3,1},{4,6},{5,7},{6,4},{7,5},{8,10},{9,11},{10,... | collective-permute-start | bytes 122888 | tf_op jit(solution)/shard_map/ppermute | solution.py:710
  169.8 9.3 %collective-permute-done.23 = bf16[160,128]{1,0:T(8,128)(2,1)S(1)} collective-permute-done((bf16[160,128]{1,0:T(8,128)(2,1)S(1)}, bf16[160,128]{1,0:T(8,128)(2,1)S(1)}, u32[]{:S(2)}, u32[]{:S(2)}) %collective-permute-start.23) | collective-permute-done | bytes 40992 | tf_op jit(solution)/shard_map/ppermute | solution.py:710
  179.2 6.9 %all-to-all-done.4.returned = bf16[16,160,256]{2,1,0:T(8,128)(2,1)S(1)} async-done(((bf16[16,160,256]{2,1,0:T(8,128)(2,1)}), bf16[16,160,256]{2,1,0:T(8,128)(2,1)S(1)}, u32[]{:S(2)}, u32[]{:S(2)}) %all-to-all-start.4) | async-done | bytes 1310752 | tf_op jit(solution)/shard_map/all_to_all | solution.py:728
  186.1 2.4 %collect.1 = bf16[16,160,128]{2,1,0:T(8,128)(2,1)S(1)} custom-call(s32[1]{0:T(128)} %dynamic_slice.82.slot, bf16[16,160,256]{2,1,0:T(8,128)(2,1)S(1)} %all-to-all-done.4.returned, s32[8,1024]{1,0:T(8,128)S(1)} %reshape.333.codes, f32[160,128]{1,0:T(8,128)S(1)} %fusion.14.own), custom_call_target="tpu_custom_call" | custom-call | tf_op jit(solution)/shard_map/collect/pallas_call | solution.py:453
  188.5 22.1 %all_to_all.30 = bf16[16,160,128]{2,1,0:T(8,128)(2,1)S(1)} all-to-all(bf16[16,160,128]{2,1,0:T(8,128)(2,1)S(1)} %collect.1), channel_id=1, replica_groups=mesh['req'=16,'blk'=16] {'req'}, dimensions={0} | all-to-all | bytes 1310720 | tf_op jit(solution)/shard_map/all_to_all | solution.py:743
  210.7 0.7 copy.126
  (123 shorter events, 11.6 us)
Async XLA Ops:
  6.5 117.3 %copy-start = (bf16[192,2560]{1,0:T(8,128)(2,1)S(1)}, bf16[192,2560]{1,0:T(8,128)(2,1)}, u32[]{:S(2)}) copy-start(bf16[192,2560]{1,0:T(8,128)(2,1)} %param.37) | copy-start | bytes 2949124
  6.5 13.0 %copy-start.9 = (bf16[1,3,128,1024]{3,2,1,0:T(8,128)(2,1)S(1)}, bf16[1,3,128,1024]{3,2,1,0:T(8,128)(2,1)}, u32[]{:S(2)}) copy-start(bf16[1,3,128,1024]{3,2,1,0:T(8,128)(2,1)} %param.24) | copy-start | bytes 2359300
  6.5 12.8 %copy-start.13 = (s32[16,1,3]{0,1,2:T(1,128)S(1)}, s32[16,1,3]{0,1,2:T(1,128)}, u32[]{:S(2)}) copy-start(s32[16,1,3]{0,1,2:T(1,128)} %param.25) | copy-start | bytes 580
  6.5 84.1 %all-gather.2.cloned.1.call-start = ((), (), s32[]{:S(2)}) async-start(), calls=%async_computation.6 | async-start | bytes 4096000 | tf_op jit(solution)/shard_map/all_gather | solution.py:529
  9.2 30.4 %all-to-all-start = ((bf16[16,168,128]{2,1,0:T(8,128)(2,1)}), bf16[16,168,128]{2,1,0:T(8,128)(2,1)S(1)}, u32[]{:S(2)}, u32[]{:S(2)}) async-start(bf16[16,168,128]{2,1,0:T(8,128)(2,1)} %payload.1), calls=%async_computation | async-start | bytes 1376256 | tf_op jit(solution)/shard_map/all_to_all | solution.py:514
  21.4 13.1 %copy-start.16 = (s32[16]{0:T(128)S(1)}, s32[16]{0:T(128)}, u32[]{:S(2)}) copy-start(s32[16]{0:T(128)} %param.27) | copy-start | bytes 196
  21.4 15.1 %copy-start.15 = (s32[16]{0:T(128)S(1)}, s32[16]{0:T(128)}, u32[]{:S(2)}) copy-start(s32[16]{0:T(128)} %param.26) | copy-start | bytes 196
  23.7 27.3 %copy-start.11 = (f32[2560]{0:T(1024)S(1)}, f32[2560]{0:T(1024)}, u32[]{:S(2)}) copy-start(f32[2560]{0:T(1024)} %param.30) | copy-start | bytes 30724
  23.7 34.4 %collective-permute-start.1 = (bf16[32,2560]{1,0:T(8,128)(2,1)}, bf16[32,2560]{1,0:T(8,128)(2,1)S(1)}, u32[]{:S(2)}, u32[]{:S(2)}) collective-permute-start(bf16[32,2560]{1,0:T(8,128)(2,1)} %get-tuple-element.50), channel_id=1, source_target_pairs={{0,1},{1,3},{2,5},{3,7},{4,9},{5,11},{6,13},{7,15},{8,0},{9,2},{10... | collective-permute-start | bytes 491528 | tf_op jit(solution)/shard_map/ppermute | solution.py:558
  26.3 31.8 %collective-permute-start = (bf16[32,2560]{1,0:T(8,128)(2,1)}, bf16[32,2560]{1,0:T(8,128)(2,1)}, u32[]{:S(2)}, u32[]{:S(2)}) collective-permute-start(bf16[32,2560]{1,0:T(8,128)(2,1)} %get-tuple-element.51), channel_id=1, source_target_pairs={{0,0},{1,2},{2,4},{3,6},{4,8},{5,10},{6,12},{7,14},{8,1},{9,3},{10... | collective-permute-start | bytes 491528 | tf_op jit(solution)/shard_map/ppermute | solution.py:557
  30.6 38.0 %collective-permute-start.7 = (bf16[384,256]{1,0:T(8,128)(2,1)}, bf16[384,256]{1,0:T(8,128)(2,1)S(1)}, u32[]{:S(2)}, u32[]{:S(2)}) collective-permute-start(bf16[384,256]{1,0:T(8,128)(2,1)} %get-tuple-element.41), channel_id=1, source_target_pairs={{0,12},{1,13},{2,14},{3,15},{4,8},{5,9},{6,10},{7,11},{8,4},{9,5},... | collective-permute-start | bytes 589832 | tf_op jit(solution)/shard_map/ppermute | solution.py:44
  32.9 36.4 %collective-permute-start.6 = (bf16[384,256]{1,0:T(8,128)(2,1)}, bf16[384,256]{1,0:T(8,128)(2,1)S(1)}, u32[]{:S(2)}, u32[]{:S(2)}) collective-permute-start(bf16[384,256]{1,0:T(8,128)(2,1)} %get-tuple-element.42), channel_id=1, source_target_pairs={{0,8},{1,9},{2,10},{3,11},{4,12},{5,13},{6,14},{7,15},{8,0},{9,1},... | collective-permute-start | bytes 589832 | tf_op jit(solution)/shard_map/ppermute | solution.py:44
  34.5 34.9 %collective-permute-start.5 = (bf16[384,256]{1,0:T(8,128)(2,1)}, bf16[384,256]{1,0:T(8,128)(2,1)S(1)}, u32[]{:S(2)}, u32[]{:S(2)}) collective-permute-start(bf16[384,256]{1,0:T(8,128)(2,1)} %get-tuple-element.43), channel_id=1, source_target_pairs={{0,4},{1,5},{2,6},{3,7},{4,0},{5,1},{6,2},{7,3},{8,12},{9,13},{10,... | collective-permute-start | bytes 589832 | tf_op jit(solution)/shard_map/ppermute | solution.py:44
  39.6 0.8 copy-start.8
  41.4 20.7 %copy-start.1 = (bf16[2560,160]{0,1:T(8,128)(2,1)S(1)}, bf16[2560,160]{0,1:T(8,128)(2,1)}, u32[]{:S(2)}) copy-start(bf16[2560,160]{0,1:T(8,128)(2,1)} %param.21) | copy-start | bytes 2457604
  41.4 20.7 %copy-start.3 = (f32[2560]{0:T(1024)S(1)}, f32[2560]{0:T(1024)}, u32[]{:S(2)}) copy-start(f32[2560]{0:T(1024)} %param.20) | copy-start | bytes 30724
  41.4 20.7 %all-to-all-start.1 = ((bf16[16,160,128]{2,1,0:T(8,128)(2,1)}), bf16[16,160,128]{2,1,0:T(8,128)(2,1)S(1)}, u32[]{:S(2)}, u32[]{:S(2)}) async-start(bf16[16,160,128]{2,1,0:T(8,128)(2,1)} %broadcast_in_dim.40), calls=%async_computation.1 | async-start | bytes 1310720 | tf_op jit(solution)/shard_map/all_to_all | solution.py:35
  64.1 23.1 %copy-start.6 = (s32[16,6,4,2,16]{4,3,2,0,1:T(2,128)S(1)}, s32[16,6,4,2,16]{4,3,2,0,1:T(2,128)}, u32[]{:S(2)}) copy-start(s32[16,6,4,2,16]{4,3,2,0,1:T(2,128)} %reshape.341) | copy-start | bytes 147460
  64.2 5.2 %collective-permute-start.4 = (bf16[224,128]{1,0:T(8,128)(2,1)S(1)}, bf16[224,128]{1,0:T(8,128)(2,1)S(1)}, u32[]{:S(2)}, u32[]{:S(2)}) collective-permute-start(bf16[224,128]{1,0:T(8,128)(2,1)S(1)} %project.1.p0), channel_id=1, source_target_pairs={{0,3},{1,2},{2,1},{3,0},{4,7},{5,6},{6,5},{7,4},{8,11},{9,10},{10,... | collective-permute-start | bytes 172040 | tf_op jit(solution)/shard_map/ppermute | solution.py:44
  65.8 5.7 %collective-permute-start.3 = (bf16[224,128]{1,0:T(8,128)(2,1)S(1)}, bf16[224,128]{1,0:T(8,128)(2,1)S(1)}, u32[]{:S(2)}, u32[]{:S(2)}) collective-permute-start(bf16[224,128]{1,0:T(8,128)(2,1)S(1)} %project.1.p0), channel_id=1, source_target_pairs={{0,2},{1,3},{2,0},{3,1},{4,6},{5,7},{6,4},{7,5},{8,10},{9,11},{10,... | collective-permute-start | bytes 172040 | tf_op jit(solution)/shard_map/ppermute | solution.py:44
  68.6 2.9 %collective-permute-start.2 = (bf16[224,128]{1,0:T(8,128)(2,1)S(1)}, bf16[224,128]{1,0:T(8,128)(2,1)S(1)}, u32[]{:S(2)}, u32[]{:S(2)}) collective-permute-start(bf16[224,128]{1,0:T(8,128)(2,1)S(1)} %project.1.p0), channel_id=1, source_target_pairs={{0,1},{1,0},{2,3},{3,2},{4,5},{5,4},{6,7},{7,6},{8,9},{9,8},{10,11... | collective-permute-start | bytes 172040 | tf_op jit(solution)/shard_map/ppermute | solution.py:44
  75.2 4.7 %collective-permute-start.8 = (bf16[32,768]{1,0:T(8,128)(2,1)S(1)}, bf16[32,768]{1,0:T(8,128)(2,1)S(1)}, u32[]{:S(2)}, u32[]{:S(2)}) collective-permute-start(bf16[32,768]{1,0:T(8,128)(2,1)S(1)} %get-tuple-element.26), channel_id=1, source_target_pairs={{0,1},{1,0},{2,3},{3,2},{4,5},{5,4},{6,7},{7,6},{8,9},{9,8},{10,11... | collective-permute-start | bytes 147464 | tf_op jit(solution)/shard_map/ppermute | solution.py:44
  75.9 4.5 %collective-permute-start.9 = (bf16[32,768]{1,0:T(8,128)(2,1)S(1)}, bf16[32,768]{1,0:T(8,128)(2,1)S(1)}, u32[]{:S(2)}, u32[]{:S(2)}) collective-permute-start(bf16[32,768]{1,0:T(8,128)(2,1)S(1)} %get-tuple-element.27), channel_id=1, source_target_pairs={{0,2},{1,3},{2,0},{3,1},{4,6},{5,7},{6,4},{7,5},{8,10},{9,11},{10,... | collective-permute-start | bytes 147464 | tf_op jit(solution)/shard_map/ppermute | solution.py:44
  77.2 5.7 %collective-permute-start.10 = (bf16[32,768]{1,0:T(8,128)(2,1)S(1)}, bf16[32,768]{1,0:T(8,128)(2,1)S(1)}, u32[]{:S(2)}, u32[]{:S(2)}) collective-permute-start(bf16[32,768]{1,0:T(8,128)(2,1)S(1)} %get-tuple-element.28), channel_id=1, source_target_pairs={{0,3},{1,2},{2,1},{3,0},{4,7},{5,6},{6,5},{7,4},{8,11},{9,10},{10,... | collective-permute-start | bytes 147464 | tf_op jit(solution)/shard_map/ppermute | solution.py:44
  83.4 4.5 %collective-permute-start.13 = (bf16[32,640]{1,0:T(8,128)(2,1)S(1)}, bf16[32,640]{1,0:T(8,128)(2,1)S(1)}, u32[]{:S(2)}, u32[]{:S(2)}) collective-permute-start(bf16[32,640]{1,0:T(8,128)(2,1)S(1)} %multiply_reduce_fusion.h0), channel_id=1, source_target_pairs={{0,12},{1,13},{2,14},{3,15},{4,8},{5,9},{6,10},{7,11},{8,4},{9,5},... | collective-permute-start | bytes 122888 | tf_op jit(solution)/shard_map/ppermute | solution.py:44
  86.3 4.4 %collective-permute-start.12 = (bf16[32,640]{1,0:T(8,128)(2,1)S(1)}, bf16[32,640]{1,0:T(8,128)(2,1)S(1)}, u32[]{:S(2)}, u32[]{:S(2)}) collective-permute-start(bf16[32,640]{1,0:T(8,128)(2,1)S(1)} %multiply_reduce_fusion.h0), channel_id=1, source_target_pairs={{0,8},{1,9},{2,10},{3,11},{4,12},{5,13},{6,14},{7,15},{8,0},{9,1},... | collective-permute-start | bytes 122888 | tf_op jit(solution)/shard_map/ppermute | solution.py:44
  87.1 3.5 %collective-permute-start.11 = (bf16[32,640]{1,0:T(8,128)(2,1)S(1)}, bf16[32,640]{1,0:T(8,128)(2,1)S(1)}, u32[]{:S(2)}, u32[]{:S(2)}) collective-permute-start(bf16[32,640]{1,0:T(8,128)(2,1)S(1)} %multiply_reduce_fusion.h0), channel_id=1, source_target_pairs={{0,4},{1,5},{2,6},{3,7},{4,0},{5,1},{6,2},{7,3},{8,12},{9,13},{10,... | collective-permute-start | bytes 122888 | tf_op jit(solution)/shard_map/ppermute | solution.py:44
  90.6 10.2 %copy-start.12 = (f32[256]{0:T(256)S(1)}, f32[256]{0:T(256)}, u32[]{:S(2)}) copy-start(f32[256]{0:T(256)} %eq.119) | copy-start | bytes 3076
  90.6 11.0 %copy-start.14 = (s32[4]{0:T(128)S(1)}, s32[4]{0:T(128)}, u32[]{:S(2)}) copy-start(s32[4]{0:T(128)} %iota_add_fusion) | copy-start | bytes 52
  94.1 25.8 %copy-start.4 = (bf16[2560,192]{0,1:T(8,128)(2,1)S(1)}, bf16[2560,192]{0,1:T(8,128)(2,1)}, u32[]{:S(2)}) copy-start(bf16[2560,192]{0,1:T(8,128)(2,1)} %param.35) | copy-start | bytes 2949124
  94.1 15.5 %all-to-all-start.2 = ((bf16[16,16,640]{2,1,0:T(8,128)(2,1)}), bf16[16,16,640]{2,1,0:T(8,128)(2,1)S(1)}, u32[]{:S(2)}, u32[]{:S(2)}) async-start(bf16[16,16,640]{2,1,0:T(8,128)(2,1)} %output.1), calls=%async_computation.2 | async-start | bytes 655360 | tf_op jit(solution)/shard_map/all_to_all | solution.py:622
  101.7 47.1 %collective-permute-start.19 = (bf16[2560,384]{1,0:T(8,128)(2,1)}, bf16[2560,384]{1,0:T(8,128)(2,1)}, u32[]{:S(2)}, u32[]{:S(2)}) collective-permute-start(bf16[2560,384]{1,0:T(8,128)(2,1)} %bitcast.155), channel_id=1, source_target_pairs={{0,1},{1,0},{2,3},{3,2},{4,5},{5,4},{6,7},{7,6},{8,9},{9,8},{10,11... | collective-permute-start | bytes 5898248 | tf_op jit(solution)/shard_map/ppermute | solution.py:621
  101.9 46.9 %collective-permute-start.20 = (bf16[2560,384]{1,0:T(8,128)(2,1)}, bf16[2560,384]{1,0:T(8,128)(2,1)}, u32[]{:S(2)}, u32[]{:S(2)}) collective-permute-start(bf16[2560,384]{1,0:T(8,128)(2,1)} %bitcast.157), channel_id=1, source_target_pairs={{0,1},{1,0},{2,3},{3,2},{4,5},{5,4},{6,7},{7,6},{8,9},{9,8},{10,11... | collective-permute-start | bytes 5898248 | tf_op jit(solution)/shard_map/ppermute | solution.py:621
  102.3 46.5 %collective-permute-start.21 = (bf16[384,2560]{1,0:T(8,128)(2,1)}, bf16[384,2560]{1,0:T(8,128)(2,1)}, u32[]{:S(2)}, u32[]{:S(2)}) collective-permute-start(bf16[384,2560]{1,0:T(8,128)(2,1)} %bitcast.159), channel_id=1, source_target_pairs={{0,1},{1,0},{2,3},{3,2},{4,5},{5,4},{6,7},{7,6},{8,9},{9,8},{10,11... | collective-permute-start | bytes 5898248 | tf_op jit(solution)/shard_map/ppermute | solution.py:621
  109.6 0.7 copy-start.7
  113.1 35.7 %all-to-all-start.3 = ((bf16[16,16,2560]{2,1,0:T(8,128)(2,1)}), bf16[16,16,2560]{2,1,0:T(8,128)(2,1)S(1)}, u32[]{:S(2)}, u32[]{:S(2)}) async-start(bf16[16,16,2560]{2,1,0:T(8,128)(2,1)} %bitcast.161), calls=%async_computation.3 | async-start | bytes 2621440 | tf_op jit(solution)/shard_map/all_to_all | solution.py:677
  118.7 4.7 %copy-start.5 = (bf16[2560,192]{0,1:T(8,128)(2,1)S(1)}, bf16[2560,192]{0,1:T(8,128)(2,1)}, u32[]{:S(2)}) copy-start(bf16[2560,192]{0,1:T(8,128)(2,1)} %param.36) | copy-start | bytes 2949124
  118.7 4.2 %collective-permute-start.14 = (bf16[64,2560]{1,0:T(8,128)(2,1)}, bf16[64,2560]{1,0:T(8,128)(2,1)S(1)}, u32[]{:S(2)}, u32[]{:S(2)}) collective-permute-start(bf16[64,2560]{1,0:T(8,128)(2,1)} %get-tuple-element.31), channel_id=1, source_target_pairs={{0,1},{1,0},{2,3},{3,2},{4,5},{5,4},{6,7},{7,6},{8,9},{9,8},{10,11... | collective-permute-start | bytes 983048 | tf_op jit(solution)/shard_map/ppermute | solution.py:681
  123.9 3.5 %copy-start.17 = (s32[16]{0:T(128)S(1)}, s32[16]{0:T(128)}, u32[]{:S(2)}) copy-start(s32[16]{0:T(128)} %broadcast_multiply_fusion) | copy-start | bytes 196
  126.5 22.2 %copy-start.2 = (bf16[2560,64]{0,1:T(8,128)(2,1)S(1)}, bf16[2560,64]{0,1:T(8,128)(2,1)}, u32[]{:S(2)}) copy-start(bf16[2560,64]{0,1:T(8,128)(2,1)} %param.31) | copy-start | bytes 983044
  127.3 2.0 collective-permute-start.15
  130.4 4.0 %collective-permute-start.16 = (bf16[2,160,128]{2,1,0:T(8,128)(2,1)S(1)}, bf16[2,160,128]{2,1,0:T(8,128)(2,1)S(1)}, u32[]{:S(2)}, u32[]{:S(2)}) collective-permute-start(bf16[2,160,128]{2,1,0:T(8,128)(2,1)S(1)} %get-tuple-element.47), channel_id=1, source_target_pairs={{0,4},{1,5},{2,6},{3,7},{4,0},{5,1},{6,2},{7,3},{8,12},{9,13},{10,... | collective-permute-start | bytes 245768 | tf_op jit(solution)/shard_map/ppermute | solution.py:44
  130.5 5.2 %collective-permute-start.18 = (bf16[2,160,128]{2,1,0:T(8,128)(2,1)S(1)}, bf16[2,160,128]{2,1,0:T(8,128)(2,1)S(1)}, u32[]{:S(2)}, u32[]{:S(2)}) collective-permute-start(bf16[2,160,128]{2,1,0:T(8,128)(2,1)S(1)} %get-tuple-element.48), channel_id=1, source_target_pairs={{0,12},{1,13},{2,14},{3,15},{4,8},{5,9},{6,10},{7,11},{8,4},{9,5},... | collective-permute-start | bytes 245768 | tf_op jit(solution)/shard_map/ppermute | solution.py:44
  134.4 4.9 %collective-permute-start.17 = (bf16[2,160,128]{2,1,0:T(8,128)(2,1)S(1)}, bf16[2,160,128]{2,1,0:T(8,128)(2,1)S(1)}, u32[]{:S(2)}, u32[]{:S(2)}) collective-permute-start(bf16[2,160,128]{2,1,0:T(8,128)(2,1)S(1)} %get-tuple-element.49), channel_id=1, source_target_pairs={{0,8},{1,9},{2,10},{3,11},{4,12},{5,13},{6,14},{7,15},{8,0},{9,1},... | collective-permute-start | bytes 245768 | tf_op jit(solution)/shard_map/ppermute | solution.py:44
  157.3 8.8 %copy-start.10 = (bf16[64,2560]{1,0:T(8,128)(2,1)S(1)}, bf16[64,2560]{1,0:T(8,128)(2,1)}, u32[]{:S(2)}) copy-start(bf16[64,2560]{1,0:T(8,128)(2,1)} %get-tuple-element.36) | copy-start | bytes 983044
  157.3 28.8 %all-to-all-start.4 = ((bf16[16,160,256]{2,1,0:T(8,128)(2,1)}), bf16[16,160,256]{2,1,0:T(8,128)(2,1)S(1)}, u32[]{:S(2)}, u32[]{:S(2)}) async-start(bf16[16,160,256]{2,1,0:T(8,128)(2,1)} %bitcast.62), calls=%async_computation.4 | async-start | bytes 2621440 | tf_op jit(solution)/shard_map/all_to_all | solution.py:728
  166.4 3.3 %collective-permute-start.22 = (bf16[64,160]{0,1:T(8,128)(2,1)S(1)}, bf16[64,160]{0,1:T(8,128)(2,1)S(1)}, u32[]{:S(2)}, u32[]{:S(2)}) collective-permute-start(bf16[64,160]{0,1:T(8,128)(2,1)S(1)} %constant_dynamic-slice_fusion.1), channel_id=1, source_target_pairs={{0,1},{1,0},{2,3},{3,2},{4,5},{5,4},{6,7},{7,6},{8,9},{9,8},{10,11... | collective-permute-start | bytes 61448 | tf_op jit(solution)/shard_map/ppermute | solution.py:722
  166.7 12.4 %collective-permute-start.23 = (bf16[160,128]{1,0:T(8,128)(2,1)S(1)}, bf16[160,128]{1,0:T(8,128)(2,1)S(1)}, u32[]{:S(2)}, u32[]{:S(2)}) collective-permute-start(bf16[160,128]{1,0:T(8,128)(2,1)S(1)} %fusion.20), channel_id=1, source_target_pairs={{0,2},{1,3},{2,0},{3,1},{4,6},{5,7},{6,4},{7,5},{8,10},{9,11},{10,... | collective-permute-start | bytes 122888 | tf_op jit(solution)/shard_map/ppermute | solution.py:710
Sparse Core Ops, SparseCore 0:
  9.2 54.1 all-gather.1

commit v8 on v7

--- a/solution.py
+++ b/solution.py
@@ -564,7 +564,8 @@
         first,
         second,
     )
-    length = cache_lengths[req_index]
+    lengths, _ = lax.optimization_barrier((cache_lengths, by_slot))
+    length = lengths[req_index]
     frequency = rope_base ** (
         -2.0 * jnp.arange(HEAD_WIDTH // 2, dtype=f32) / HEAD_WIDTH
     )
@@ -587,6 +588,7 @@
         group_parts(lambda d: projected, 1),
         caches,
     )
+    migration_late, _ = lax.optimization_barrier((migration, parts[0]))
     met = jnp.stack(group_parts(lambda d: parts[d], 1))
     levels = sum(
         met[:, :, span + i * heads_here : span + (i + 1) * heads_here].astype(f32)
@@ -624,7 +626,7 @@
     per_req = E // req_count
     slot_ids = jnp.arange(req_count, dtype=jnp.int32)
     holder = jnp.sum(
-        jnp.where(migration[None, :] == slot_ids[:, None], slot_ids[None, :], 0), axis=1
+        jnp.where(migration_late[None, :] == slot_ids[:, None], slot_ids[None, :], 0), axis=1
     )
     owned = jnp.arange(per_req, dtype=jnp.int32) + req_index * per_req
     named_all = jnp.any(

time: 220 us -> 225 us (1.023)
  waiting for transfers between devices: 52.5 us -> 59.1 us
    all_to_all x1, waiting for transfers between devices: 3.99 us -> 9.07 us  [to_all(): return lax.all_to_all(copies, axis, 0, 0, tiled=True)]
  transfers between devices with their start and end apart: 30 -> 30, of which waited for: 14 -> 14; matrix products, arithmetic and copies ran while one was open for 15% -> 14% of each run, Pallas kernels for 5% -> 5%
where the time goes in v8:
time: 225 us; the launch traced here: 224 us
  starting transfers between devices  68.8 us (31%)
  waiting for transfers between devices  59.1 us (26%)
  Pallas kernels  24.8 us (11%)
  blocking collectives  22.1 us (10%)
  local copies, waits for them, and re-layouts  18.3 us (8%)
  between operations  16.1 us (7%)
  other arithmetic  8.2 us (4%)
  matrix products  6.43 us (3%)
    all_to_all x1, blocking collectives, per_device(): final = lax.all_to_all(outgoing, 'req', 0, 0, tiled=True)  22.1 us
    ppermute x15, starting transfers between devices, group_parts(): lax.ppermute(piece_for(d), 'blk', partners(d * stride))  17.8 us
    ppermute x15, waiting for transfers between devices, group_parts(): lax.ppermute(piece_for(d), 'blk', partners(d * stride))  13.1 us
    all_to_all x1, starting transfers between devices, per_device(): by_slot = lax.all_to_all(payload, 'req', 0, 0, tiled=True)  10.2 us
    all_to_all x1, waiting for transfers between devices, per_device(): lax.all_to_all(sent.reshape(req_count, CAP, width), 'req', 0, 0, tiled=True)  9.46 us
    ppermute x1, waiting for transfers between devices, per_device(): lax.ppermute(lax.dynamic_index_in_dim(over_x, 1 - q_high, 0, False).astyp...  9.28 us
    all_to_all x1, waiting for transfers between devices, to_all(): return lax.all_to_all(copies, axis, 0, 0, tiled=True)  9.07 us
    all_to_all x1, starting transfers between devices, per_device(): lax.all_to_all(expert_rows((req_index * per_req + x_index)[None].astype(j...  8.76 us
  transfers between devices with their start and end apart: 30, of which 14 were waited for; matrix products, arithmetic and copies ran while one was open for 14% of the time, Pallas kernels for 5%

profile of v8, /device:TPU:1, one launch (start us, length us, event | category | flops | bytes accessed | tf_op | source)
XLA Modules:
  0.0 223.9 jit_solution(17219289949899031769)
XLA Ops:
  6.5 0.7 all-gather.2.cloned.1.call-update
  7.3 1.9 payload.1
  9.2 10.2 %all-to-all-start = ((bf16[16,168,128]{2,1,0:T(8,128)(2,1)}), bf16[16,168,128]{2,1,0:T(8,128)(2,1)}, u32[]{:S(2)}, u32[]{:S(2)}) async-start(bf16[16,168,128]{2,1,0:T(8,128)(2,1)} %payload.1), calls=%async_computation | async-start | bytes 1376256 | tf_op jit(solution)/shard_map/all_to_all | solution.py:514
  22.0 0.7 broadcast_select_fusion
  22.7 2.6 %collective-permute-start.1 = (bf16[32,2560]{1,0:T(8,128)(2,1)}, bf16[32,2560]{1,0:T(8,128)(2,1)S(1)}, u32[]{:S(2)}, u32[]{:S(2)}) collective-permute-start(bf16[32,2560]{1,0:T(8,128)(2,1)} %get-tuple-element.54), channel_id=1, source_target_pairs={{0,1},{1,3},{2,5},{3,7},{4,9},{5,11},{6,13},{7,15},{8,0},{9,2},{10... | collective-permute-start | bytes 491528 | tf_op jit(solution)/shard_map/ppermute | solution.py:558
  25.4 3.5 %collective-permute-start = (bf16[32,2560]{1,0:T(8,128)(2,1)}, bf16[32,2560]{1,0:T(8,128)(2,1)}, u32[]{:S(2)}, u32[]{:S(2)}) collective-permute-start(bf16[32,2560]{1,0:T(8,128)(2,1)} %get-tuple-element.55), channel_id=1, source_target_pairs={{0,0},{1,2},{2,4},{3,6},{4,8},{5,10},{6,12},{7,14},{8,1},{9,3},{10... | collective-permute-start | bytes 491528 | tf_op jit(solution)/shard_map/ppermute | solution.py:557
  28.9 0.9 dynamic-slice_bitcast_fusion.1
  29.7 2.3 %collective-permute-start.7 = (bf16[384,256]{1,0:T(8,128)(2,1)}, bf16[384,256]{1,0:T(8,128)(2,1)S(1)}, u32[]{:S(2)}, u32[]{:S(2)}) collective-permute-start(bf16[384,256]{1,0:T(8,128)(2,1)} %get-tuple-element.45), channel_id=1, source_target_pairs={{0,12},{1,13},{2,14},{3,15},{4,8},{5,9},{6,10},{7,11},{8,4},{9,5},... | collective-permute-start | bytes 589832 | tf_op jit(solution)/shard_map/ppermute | solution.py:44
  32.0 1.5 collective-permute-start.6
  37.1 2.1 all-to-all-done
  39.2 0.8 slice_convert_fusion
  40.5 0.8 copy.121
  41.4 0.8 copy.115
  42.9 1.2 eq.123
  44.1 1.3 reshape.328
  46.3 0.8 dynamic-slice_bitcast_fusion.9
  47.0 0.9 broadcast_in_dim.40
  48.0 8.7 %all-to-all-start.1 = ((bf16[16,160,128]{2,1,0:T(8,128)(2,1)}), bf16[16,160,128]{2,1,0:T(8,128)(2,1)S(1)}, u32[]{:S(2)}, u32[]{:S(2)}) async-start(bf16[16,160,128]{2,1,0:T(8,128)(2,1)} %broadcast_in_dim.40), calls=%async_computation.1 | async-start | bytes 1310720 | tf_op jit(solution)/shard_map/all_to_all | solution.py:35
  57.5 0.7 fusion.22
  58.3 0.7 compare_reduce_fusion
  59.2 0.8 pad_add_fusion.scalars
  60.0 9.1 %all-to-all-done.1 = bf16[16,160,128]{2,1,0:T(8,128)(2,1)S(1)} async-done(((bf16[16,160,128]{2,1,0:T(8,128)(2,1)}), bf16[16,160,128]{2,1,0:T(8,128)(2,1)S(1)}, u32[]{:S(2)}, u32[]{:S(2)}) %all-to-all-start.1) | async-done | bytes 655392 | tf_op jit(solution)/shard_map/all_to_all | solution.py:35
  69.0 2.1 project.1.p0
  71.2 1.6 collective-permute-start.4
  72.8 2.9 %collective-permute-start.3 = (bf16[224,128]{1,0:T(8,128)(2,1)S(1)}, bf16[224,128]{1,0:T(8,128)(2,1)S(1)}, u32[]{:S(2)}, u32[]{:S(2)}) collective-permute-start(bf16[224,128]{1,0:T(8,128)(2,1)S(1)} %project.1.p0), channel_id=1, source_target_pairs={{0,2},{1,3},{2,0},{3,1},{4,6},{5,7},{6,4},{7,5},{8,10},{9,11},{10,... | collective-permute-start | bytes 172040 | tf_op jit(solution)/shard_map/ppermute | solution.py:44
  76.4 2.1 collective-permute-done.3.p2
  78.5 3.7 %attention.1 = (bf16[32,768]{1,0:T(8,128)(2,1)S(1)}, bf16[32,768]{1,0:T(8,128)(2,1)S(1)}, bf16[32,768]{1,0:T(8,128)(2,1)S(1)}, bf16[32,768]{1,0:T(8,128)(2,1)S(1)}) custom-call(s32[3]{0:T(128)S(1)} %pad_add_fusion.scalars, s32[1,128]{1,0:T(1,128)S(1)} %compare_select_fusion.3.parent, f32[64,128]{1,0:T(8,128)S(1)} %copy.111.cosine, ...), custom_call_target="tpu_custom_call" | custom-call | tf_op jit(solution)/shard_map/attention/pallas_call | solution.py:249
  82.9 1.3 collective-permute-start.9
  84.2 2.0 collective-permute-start.10
  86.3 1.1 collective-permute-done.9
  87.4 2.5 %collective-permute-done.10 = bf16[32,768]{1,0:T(8,128)(2,1)S(1)} collective-permute-done((bf16[32,768]{1,0:T(8,128)(2,1)S(1)}, bf16[32,768]{1,0:T(8,128)(2,1)S(1)}, u32[]{:S(2)}, u32[]{:S(2)}) %collective-permute-start.10) | collective-permute-done | bytes 49184 | tf_op jit(solution)/shard_map/ppermute | solution.py:44
  90.4 1.0 collective-permute-start.13
  91.4 0.8 collective-permute-start.12
  92.1 1.6 collective-permute-start.11
  94.8 1.0 collective-permute-done.12.h2
  95.9 3.5 %output.1 = bf16[16,16,640]{2,1,0:T(8,128)(2,1)} custom-call(s32[1]{0:T(128)} %bitcast.4.x_index, bf16[32,640]{1,0:T(8,128)(2,1)S(1)} %multiply_reduce_fusion.h0, bf16[32,640]{1,0:T(8,128)(2,1)S(1)} %collective-permute-done.11.h1, bf16[32,640]{1,0:T(8,128)(2,1)S(1)} %collective-permute-done.12.h2, bf16[32,640]{1,0:T(8,128)(2,1)S(1)} %collective-permute-done.13.h3, ...), custom_call_target="tpu_custom_call" | custom-call | tf_op jit(solution)/shard_map/output/pallas_call | solution.py:298
  99.3 6.1 %all-to-all-start.2 = ((bf16[16,16,640]{2,1,0:T(8,128)(2,1)}), bf16[16,16,640]{2,1,0:T(8,128)(2,1)S(1)}, u32[]{:S(2)}, u32[]{:S(2)}) async-start(bf16[16,16,640]{2,1,0:T(8,128)(2,1)} %output.1), calls=%async_computation.2 | async-start | bytes 655360 | tf_op jit(solution)/shard_map/all_to_all | solution.py:624
  105.5 0.7 fusion.13.dispatch
  106.3 1.2 fusion.1
  108.3 6.7 %all-to-all-done.2.pieces = bf16[16,16,640]{2,1,0:T(8,128)(2,1)S(1)} async-done(((bf16[16,16,640]{2,1,0:T(8,128)(2,1)}), bf16[16,16,640]{2,1,0:T(8,128)(2,1)S(1)}, u32[]{:S(2)}, u32[]{:S(2)}) %all-to-all-start.2) | async-done | bytes 327712 | tf_op jit(solution)/shard_map/all_to_all | solution.py:624
  115.0 0.7 copy-done.6
  115.7 2.7 %spread.1 = (bf16[64,2560]{1,0:T(8,128)(2,1)}, bf16[64,2560]{1,0:T(8,128)(2,1)}, bf16[256,2560]{1,0:T(8,128)(2,1)}) custom-call(bf16[16,16,640]{2,1,0:T(8,128)(2,1)} %copy-done.6, f32[1,2560]{1,0:T(1,128)} %broadcast_in_dim.41.gain, bf16[256,64]{1,0:T(8,128)(2,1)} %fusion.13.dispatch), custom_call_target="tpu_custom_call" | custom-call | tf_op jit(solution)/shard_map/spread/pallas_call | solution.py:331
  118.4 5.9 %all-to-all-start.3 = ((bf16[16,16,2560]{2,1,0:T(8,128)(2,1)}), bf16[16,16,2560]{2,1,0:T(8,128)(2,1)S(1)}, u32[]{:S(2)}, u32[]{:S(2)}) async-start(bf16[16,16,2560]{2,1,0:T(8,128)(2,1)} %bitcast.161), calls=%async_computation.3 | async-start | bytes 2621440 | tf_op jit(solution)/shard_map/all_to_all | solution.py:679
  124.3 1.1 collective-permute-start.14
  125.4 1.4 fusion.37
  126.8 1.7 fusion.5
  129.5 1.2 fusion
  130.7 1.4 copy.119
  132.1 0.8 dynamic-slice_bitcast_fusion
  133.1 1.7 collective-permute-done.15
  134.8 1.1 fusion.7
  136.1 1.3 collective-permute-start.18
  137.3 2.6 %collective-permute-done.16 = bf16[2,160,128]{2,1,0:T(8,128)(2,1)S(1)} collective-permute-done((bf16[2,160,128]{2,1,0:T(8,128)(2,1)S(1)}, bf16[2,160,128]{2,1,0:T(8,128)(2,1)S(1)}, u32[]{:S(2)}, u32[]{:S(2)}) %collective-permute-start.16) | collective-permute-done | bytes 81952 | tf_op jit(solution)/shard_map/ppermute | solution.py:44
  139.9 0.9 collective-permute-start.17
  141.3 3.6 %collective-permute-done.17 = bf16[2,160,128]{2,1,0:T(8,128)(2,1)S(1)} collective-permute-done((bf16[2,160,128]{2,1,0:T(8,128)(2,1)S(1)}, bf16[2,160,128]{2,1,0:T(8,128)(2,1)S(1)}, u32[]{:S(2)}, u32[]{:S(2)}) %collective-permute-start.17) | collective-permute-done | bytes 81952 | tf_op jit(solution)/shard_map/ppermute | solution.py:44
  144.9 9.5 %all-to-all-done.3 = bf16[16,16,2560]{2,1,0:T(8,128)(2,1)S(1)} async-done(((bf16[16,16,2560]{2,1,0:T(8,128)(2,1)}), bf16[16,16,2560]{2,1,0:T(8,128)(2,1)S(1)}, u32[]{:S(2)}, u32[]{:S(2)}) %all-to-all-start.3) | async-done | bytes 1310752 | tf_op jit(solution)/shard_map/all_to_all | solution.py:679
  154.4 8.5 %experts.1 = bf16[2560,256]{1,0:T(8,128)(2,1)} custom-call(s32[1]{0:T(128)} %bitcast.expert, bf16[256,2560]{1,0:T(8,128)(2,1)S(1)} %bitcast.140, bf16[64,2560]{1,0:T(8,128)(2,1)S(1)} %bitcast.144, f32[256,64]{1,0:T(8,128)S(1)} %fusion.6.named, bf16[2560,384]{1,0:T(8,128)(2,1)} %bitcast.156, bf16[2560,384]{1,0:T(8,128)(2,1)} %bitcast.158, ...), custom_call_target="tpu_custom_call" | custom-call | tf_op jit(solution)/shard_map/experts/pallas_call | solution.py:398
  162.9 8.8 %all-to-all-start.4 = ((bf16[16,160,256]{2,1,0:T(8,128)(2,1)}), bf16[16,160,256]{2,1,0:T(8,128)(2,1)S(1)}, u32[]{:S(2)}, u32[]{:S(2)}) async-start(bf16[16,160,256]{2,1,0:T(8,128)(2,1)} %bitcast.62), calls=%async_computation.4 | async-start | bytes 2621440 | tf_op jit(solution)/shard_map/all_to_all | solution.py:730
  172.3 3.0 %collective-permute-start.23 = (bf16[160,128]{1,0:T(8,128)(2,1)S(1)}, bf16[160,128]{1,0:T(8,128)(2,1)S(1)}, u32[]{:S(2)}, u32[]{:S(2)}) collective-permute-start(bf16[160,128]{1,0:T(8,128)(2,1)S(1)} %fusion.20), channel_id=1, source_target_pairs={{0,2},{1,3},{2,0},{3,1},{4,6},{5,7},{6,4},{7,5},{8,10},{9,11},{10,... | collective-permute-start | bytes 122888 | tf_op jit(solution)/shard_map/ppermute | solution.py:712
  175.4 9.3 %collective-permute-done.23 = bf16[160,128]{1,0:T(8,128)(2,1)S(1)} collective-permute-done((bf16[160,128]{1,0:T(8,128)(2,1)S(1)}, bf16[160,128]{1,0:T(8,128)(2,1)S(1)}, u32[]{:S(2)}, u32[]{:S(2)}) %collective-permute-start.23) | collective-permute-done | bytes 40992 | tf_op jit(solution)/shard_map/ppermute | solution.py:712
  184.8 6.9 %all-to-all-done.4.returned = bf16[16,160,256]{2,1,0:T(8,128)(2,1)S(1)} async-done(((bf16[16,160,256]{2,1,0:T(8,128)(2,1)}), bf16[16,160,256]{2,1,0:T(8,128)(2,1)S(1)}, u32[]{:S(2)}, u32[]{:S(2)}) %all-to-all-start.4) | async-done | bytes 1310752 | tf_op jit(solution)/shard_map/all_to_all | solution.py:730
  191.7 2.4 %collect.1 = bf16[16,160,128]{2,1,0:T(8,128)(2,1)S(1)} custom-call(s32[1]{0:T(128)} %dynamic_slice.82.slot, bf16[16,160,256]{2,1,0:T(8,128)(2,1)S(1)} %all-to-all-done.4.returned, s32[8,1024]{1,0:T(8,128)S(1)} %reshape.333.codes, f32[160,128]{1,0:T(8,128)S(1)} %fusion.14.own), custom_call_target="tpu_custom_call" | custom-call | tf_op jit(solution)/shard_map/collect/pallas_call | solution.py:453
  194.1 22.1 %all_to_all.30 = bf16[16,160,128]{2,1,0:T(8,128)(2,1)S(1)} all-to-all(bf16[16,160,128]{2,1,0:T(8,128)(2,1)S(1)} %collect.1), channel_id=1, replica_groups=mesh['req'=16,'blk'=16] {'req'}, dimensions={0} | all-to-all | bytes 1310720 | tf_op jit(solution)/shard_map/all_to_all | solution.py:745
  216.3 0.7 copy.126
  (127 shorter events, 13.5 us)
Async XLA Ops:
  6.5 122.9 %copy-start = (bf16[192,2560]{1,0:T(8,128)(2,1)S(1)}, bf16[192,2560]{1,0:T(8,128)(2,1)}, u32[]{:S(2)}) copy-start(bf16[192,2560]{1,0:T(8,128)(2,1)} %param.37) | copy-start | bytes 2949124
  6.5 13.1 %copy-start.7 = (bf16[1,3,128,1024]{3,2,1,0:T(8,128)(2,1)S(1)}, bf16[1,3,128,1024]{3,2,1,0:T(8,128)(2,1)}, u32[]{:S(2)}) copy-start(bf16[1,3,128,1024]{3,2,1,0:T(8,128)(2,1)} %param.24) | copy-start | bytes 2359300
  6.5 12.8 %copy-start.16 = (s32[16,1,3]{0,1,2:T(1,128)S(1)}, s32[16,1,3]{0,1,2:T(1,128)}, u32[]{:S(2)}) copy-start(s32[16,1,3]{0,1,2:T(1,128)} %param.25) | copy-start | bytes 580
  6.5 89.3 %all-gather.2.cloned.1.call-start = ((), (), s32[]{:S(2)}) async-start(), calls=%async_computation.6 | async-start | bytes 4096000 | tf_op jit(solution)/shard_map/all_gather | solution.py:529
  9.2 30.0 %all-to-all-start = ((bf16[16,168,128]{2,1,0:T(8,128)(2,1)}), bf16[16,168,128]{2,1,0:T(8,128)(2,1)}, u32[]{:S(2)}, u32[]{:S(2)}) async-start(bf16[16,168,128]{2,1,0:T(8,128)(2,1)} %payload.1), calls=%async_computation | async-start | bytes 1376256 | tf_op jit(solution)/shard_map/all_to_all | solution.py:514
  20.8 1.2 copy-start.8
  21.4 12.1 %copy-start.18 = (s32[16]{0:T(128)S(1)}, s32[16]{0:T(128)}, u32[]{:S(2)}) copy-start(s32[16]{0:T(128)} %param.27) | copy-start | bytes 196
  21.5 14.3 %copy-start.15 = (f32[2560]{0:T(1024)S(1)}, f32[2560]{0:T(1024)}, u32[]{:S(2)}) copy-start(f32[2560]{0:T(1024)} %param.30) | copy-start | bytes 30724
  22.7 37.2 %collective-permute-start.1 = (bf16[32,2560]{1,0:T(8,128)(2,1)}, bf16[32,2560]{1,0:T(8,128)(2,1)S(1)}, u32[]{:S(2)}, u32[]{:S(2)}) collective-permute-start(bf16[32,2560]{1,0:T(8,128)(2,1)} %get-tuple-element.54), channel_id=1, source_target_pairs={{0,1},{1,3},{2,5},{3,7},{4,9},{5,11},{6,13},{7,15},{8,0},{9,2},{10... | collective-permute-start | bytes 491528 | tf_op jit(solution)/shard_map/ppermute | solution.py:558
  25.4 34.6 %collective-permute-start = (bf16[32,2560]{1,0:T(8,128)(2,1)}, bf16[32,2560]{1,0:T(8,128)(2,1)}, u32[]{:S(2)}, u32[]{:S(2)}) collective-permute-start(bf16[32,2560]{1,0:T(8,128)(2,1)} %get-tuple-element.55), channel_id=1, source_target_pairs={{0,0},{1,2},{2,4},{3,6},{4,8},{5,10},{6,12},{7,14},{8,1},{9,3},{10... | collective-permute-start | bytes 491528 | tf_op jit(solution)/shard_map/ppermute | solution.py:557
  28.9 13.4 %copy-start.17 = (s32[16]{0:T(128)S(1)}, s32[16]{0:T(128)}, u32[]{:S(2)}) copy-start(s32[16]{0:T(128)} %param.26) | copy-start | bytes 196
  29.7 45.9 %collective-permute-start.7 = (bf16[384,256]{1,0:T(8,128)(2,1)}, bf16[384,256]{1,0:T(8,128)(2,1)S(1)}, u32[]{:S(2)}, u32[]{:S(2)}) collective-permute-start(bf16[384,256]{1,0:T(8,128)(2,1)} %get-tuple-element.45), channel_id=1, source_target_pairs={{0,12},{1,13},{2,14},{3,15},{4,8},{5,9},{6,10},{7,11},{8,4},{9,5},... | collective-permute-start | bytes 589832 | tf_op jit(solution)/shard_map/ppermute | solution.py:44
  32.0 44.3 %collective-permute-start.6 = (bf16[384,256]{1,0:T(8,128)(2,1)}, bf16[384,256]{1,0:T(8,128)(2,1)S(1)}, u32[]{:S(2)}, u32[]{:S(2)}) collective-permute-start(bf16[384,256]{1,0:T(8,128)(2,1)} %get-tuple-element.46), channel_id=1, source_target_pairs={{0,8},{1,9},{2,10},{3,11},{4,12},{5,13},{6,14},{7,15},{8,0},{9,1},... | collective-permute-start | bytes 589832 | tf_op jit(solution)/shard_map/ppermute | solution.py:44
  33.6 42.8 %collective-permute-start.5 = (bf16[384,256]{1,0:T(8,128)(2,1)}, bf16[384,256]{1,0:T(8,128)(2,1)S(1)}, u32[]{:S(2)}, u32[]{:S(2)}) collective-permute-start(bf16[384,256]{1,0:T(8,128)(2,1)} %get-tuple-element.47), channel_id=1, source_target_pairs={{0,4},{1,5},{2,6},{3,7},{4,0},{5,1},{6,2},{7,3},{8,12},{9,13},{10,... | collective-permute-start | bytes 589832 | tf_op jit(solution)/shard_map/ppermute | solution.py:44
  42.2 26.8 %copy-start.1 = (bf16[2560,160]{0,1:T(8,128)(2,1)S(1)}, bf16[2560,160]{0,1:T(8,128)(2,1)}, u32[]{:S(2)}) copy-start(bf16[2560,160]{0,1:T(8,128)(2,1)} %param.21) | copy-start | bytes 2457604
  42.2 26.8 %copy-start.3 = (f32[2560]{0:T(1024)S(1)}, f32[2560]{0:T(1024)}, u32[]{:S(2)}) copy-start(f32[2560]{0:T(1024)} %param.20) | copy-start | bytes 30724
  45.3 2.6 %copy-start.10 = (s32[16,6,128]{2,0,1:T(8,128)}, s32[16,6,128]{2,0,1:T(8,128)S(1)}, u32[]{:S(2)}) copy-start(s32[16,6,128]{2,0,1:T(8,128)S(1)} %reshape.328) | copy-start | bytes 147460
  45.6 0.6 copy-start.12
  48.0 21.1 %all-to-all-start.1 = ((bf16[16,160,128]{2,1,0:T(8,128)(2,1)}), bf16[16,160,128]{2,1,0:T(8,128)(2,1)S(1)}, u32[]{:S(2)}, u32[]{:S(2)}) async-start(bf16[16,160,128]{2,1,0:T(8,128)(2,1)} %broadcast_in_dim.40), calls=%async_computation.1 | async-start | bytes 1310720 | tf_op jit(solution)/shard_map/all_to_all | solution.py:35
  59.2 27.0 %copy-start.11 = (s32[16,6,128]{2,0,1:T(8,128)S(1)}, s32[16,6,128]{2,0,1:T(8,128)}, u32[]{:S(2)}) copy-start(s32[16,6,128]{2,0,1:T(8,128)} %copy-done.10) | copy-start | bytes 147460
  71.1 23.3 %copy-start.13 = (pred[64,64]{1,0:T(8,128)(4,1)S(1)}, pred[64,64]{1,0:T(8,128)(4,1)}, u32[]{:S(2)}) copy-start(pred[64,64]{1,0:T(8,128)(4,1)} %copy-done.12) | copy-start | bytes 12292
  71.2 5.2 %collective-permute-start.4 = (bf16[224,128]{1,0:T(8,128)(2,1)S(1)}, bf16[224,128]{1,0:T(8,128)(2,1)S(1)}, u32[]{:S(2)}, u32[]{:S(2)}) collective-permute-start(bf16[224,128]{1,0:T(8,128)(2,1)S(1)} %project.1.p0), channel_id=1, source_target_pairs={{0,3},{1,2},{2,1},{3,0},{4,7},{5,6},{6,5},{7,4},{8,11},{9,10},{10,... | collective-permute-start | bytes 172040 | tf_op jit(solution)/shard_map/ppermute | solution.py:44
  72.8 5.7 %collective-permute-start.3 = (bf16[224,128]{1,0:T(8,128)(2,1)S(1)}, bf16[224,128]{1,0:T(8,128)(2,1)S(1)}, u32[]{:S(2)}, u32[]{:S(2)}) collective-permute-start(bf16[224,128]{1,0:T(8,128)(2,1)S(1)} %project.1.p0), channel_id=1, source_target_pairs={{0,2},{1,3},{2,0},{3,1},{4,6},{5,7},{6,4},{7,5},{8,10},{9,11},{10,... | collective-permute-start | bytes 172040 | tf_op jit(solution)/shard_map/ppermute | solution.py:44
  75.6 2.9 %collective-permute-start.2 = (bf16[224,128]{1,0:T(8,128)(2,1)S(1)}, bf16[224,128]{1,0:T(8,128)(2,1)S(1)}, u32[]{:S(2)}, u32[]{:S(2)}) collective-permute-start(bf16[224,128]{1,0:T(8,128)(2,1)S(1)} %project.1.p0), channel_id=1, source_target_pairs={{0,1},{1,0},{2,3},{3,2},{4,5},{5,4},{6,7},{7,6},{8,9},{9,8},{10,11... | collective-permute-start | bytes 172040 | tf_op jit(solution)/shard_map/ppermute | solution.py:44
  82.2 4.0 %collective-permute-start.8 = (bf16[32,768]{1,0:T(8,128)(2,1)S(1)}, bf16[32,768]{1,0:T(8,128)(2,1)S(1)}, u32[]{:S(2)}, u32[]{:S(2)}) collective-permute-start(bf16[32,768]{1,0:T(8,128)(2,1)S(1)} %get-tuple-element.29), channel_id=1, source_target_pairs={{0,1},{1,0},{2,3},{3,2},{4,5},{5,4},{6,7},{7,6},{8,9},{9,8},{10,11... | collective-permute-start | bytes 147464 | tf_op jit(solution)/shard_map/ppermute | solution.py:44
  82.9 4.5 %collective-permute-start.9 = (bf16[32,768]{1,0:T(8,128)(2,1)S(1)}, bf16[32,768]{1,0:T(8,128)(2,1)S(1)}, u32[]{:S(2)}, u32[]{:S(2)}) collective-permute-start(bf16[32,768]{1,0:T(8,128)(2,1)S(1)} %get-tuple-element.30), channel_id=1, source_target_pairs={{0,2},{1,3},{2,0},{3,1},{4,6},{5,7},{6,4},{7,5},{8,10},{9,11},{10,... | collective-permute-start | bytes 147464 | tf_op jit(solution)/shard_map/ppermute | solution.py:44
  84.2 5.7 %collective-permute-start.10 = (bf16[32,768]{1,0:T(8,128)(2,1)S(1)}, bf16[32,768]{1,0:T(8,128)(2,1)S(1)}, u32[]{:S(2)}, u32[]{:S(2)}) collective-permute-start(bf16[32,768]{1,0:T(8,128)(2,1)S(1)} %get-tuple-element.31), channel_id=1, source_target_pairs={{0,3},{1,2},{2,1},{3,0},{4,7},{5,6},{6,5},{7,4},{8,11},{9,10},{10,... | collective-permute-start | bytes 147464 | tf_op jit(solution)/shard_map/ppermute | solution.py:44
  90.4 4.4 %collective-permute-start.13 = (bf16[32,640]{1,0:T(8,128)(2,1)S(1)}, bf16[32,640]{1,0:T(8,128)(2,1)S(1)}, u32[]{:S(2)}, u32[]{:S(2)}) collective-permute-start(bf16[32,640]{1,0:T(8,128)(2,1)S(1)} %multiply_reduce_fusion.h0), channel_id=1, source_target_pairs={{0,12},{1,13},{2,14},{3,15},{4,8},{5,9},{6,10},{7,11},{8,4},{9,5},... | collective-permute-start | bytes 122888 | tf_op jit(solution)/shard_map/ppermute | solution.py:44
  91.4 4.5 %collective-permute-start.12 = (bf16[32,640]{1,0:T(8,128)(2,1)S(1)}, bf16[32,640]{1,0:T(8,128)(2,1)S(1)}, u32[]{:S(2)}, u32[]{:S(2)}) collective-permute-start(bf16[32,640]{1,0:T(8,128)(2,1)S(1)} %multiply_reduce_fusion.h0), channel_id=1, source_target_pairs={{0,8},{1,9},{2,10},{3,11},{4,12},{5,13},{6,14},{7,15},{8,0},{9,1},... | collective-permute-start | bytes 122888 | tf_op jit(solution)/shard_map/ppermute | solution.py:44
  92.1 3.7 %collective-permute-start.11 = (bf16[32,640]{1,0:T(8,128)(2,1)S(1)}, bf16[32,640]{1,0:T(8,128)(2,1)S(1)}, u32[]{:S(2)}, u32[]{:S(2)}) collective-permute-start(bf16[32,640]{1,0:T(8,128)(2,1)S(1)} %multiply_reduce_fusion.h0), channel_id=1, source_target_pairs={{0,4},{1,5},{2,6},{3,7},{4,0},{5,1},{6,2},{7,3},{8,12},{9,13},{10,... | collective-permute-start | bytes 122888 | tf_op jit(solution)/shard_map/ppermute | solution.py:44
  95.9 11.6 %copy-start.19 = (s32[16]{0:T(128)S(1)}, s32[16]{0:T(128)}, u32[]{:S(2)}) copy-start(s32[16]{0:T(128)} %param.27) | copy-start | bytes 196
  99.3 26.1 %copy-start.4 = (bf16[2560,192]{0,1:T(8,128)(2,1)S(1)}, bf16[2560,192]{0,1:T(8,128)(2,1)}, u32[]{:S(2)}) copy-start(bf16[2560,192]{0,1:T(8,128)(2,1)} %param.35) | copy-start | bytes 2949124
  99.3 15.6 %all-to-all-start.2 = ((bf16[16,16,640]{2,1,0:T(8,128)(2,1)}), bf16[16,16,640]{2,1,0:T(8,128)(2,1)S(1)}, u32[]{:S(2)}, u32[]{:S(2)}) async-start(bf16[16,16,640]{2,1,0:T(8,128)(2,1)} %output.1), calls=%async_computation.2 | async-start | bytes 655360 | tf_op jit(solution)/shard_map/all_to_all | solution.py:624
  107.6 46.8 %collective-permute-start.19 = (bf16[2560,384]{1,0:T(8,128)(2,1)}, bf16[2560,384]{1,0:T(8,128)(2,1)}, u32[]{:S(2)}, u32[]{:S(2)}) collective-permute-start(bf16[2560,384]{1,0:T(8,128)(2,1)} %bitcast.155), channel_id=1, source_target_pairs={{0,1},{1,0},{2,3},{3,2},{4,5},{5,4},{6,7},{7,6},{8,9},{9,8},{10,11... | collective-permute-start | bytes 5898248 | tf_op jit(solution)/shard_map/ppermute | solution.py:623
  107.8 46.6 %collective-permute-start.20 = (bf16[2560,384]{1,0:T(8,128)(2,1)}, bf16[2560,384]{1,0:T(8,128)(2,1)}, u32[]{:S(2)}, u32[]{:S(2)}) collective-permute-start(bf16[2560,384]{1,0:T(8,128)(2,1)} %bitcast.157), channel_id=1, source_target_pairs={{0,1},{1,0},{2,3},{3,2},{4,5},{5,4},{6,7},{7,6},{8,9},{9,8},{10,11... | collective-permute-start | bytes 5898248 | tf_op jit(solution)/shard_map/ppermute | solution.py:623
  108.2 46.2 %collective-permute-start.21 = (bf16[384,2560]{1,0:T(8,128)(2,1)}, bf16[384,2560]{1,0:T(8,128)(2,1)}, u32[]{:S(2)}, u32[]{:S(2)}) collective-permute-start(bf16[384,2560]{1,0:T(8,128)(2,1)} %bitcast.159), channel_id=1, source_target_pairs={{0,1},{1,0},{2,3},{3,2},{4,5},{5,4},{6,7},{7,6},{8,9},{9,8},{10,11... | collective-permute-start | bytes 5898248 | tf_op jit(solution)/shard_map/ppermute | solution.py:623
  115.0 0.7 copy-start.6
  118.4 36.0 %all-to-all-start.3 = ((bf16[16,16,2560]{2,1,0:T(8,128)(2,1)}), bf16[16,16,2560]{2,1,0:T(8,128)(2,1)S(1)}, u32[]{:S(2)}, u32[]{:S(2)}) async-start(bf16[16,16,2560]{2,1,0:T(8,128)(2,1)} %bitcast.161), calls=%async_computation.3 | async-start | bytes 2621440 | tf_op jit(solution)/shard_map/all_to_all | solution.py:679
  124.3 4.7 %copy-start.5 = (bf16[2560,192]{0,1:T(8,128)(2,1)S(1)}, bf16[2560,192]{0,1:T(8,128)(2,1)}, u32[]{:S(2)}) copy-start(bf16[2560,192]{0,1:T(8,128)(2,1)} %param.36) | copy-start | bytes 2949124
  124.3 4.2 %collective-permute-start.14 = (bf16[64,2560]{1,0:T(8,128)(2,1)}, bf16[64,2560]{1,0:T(8,128)(2,1)S(1)}, u32[]{:S(2)}, u32[]{:S(2)}) collective-permute-start(bf16[64,2560]{1,0:T(8,128)(2,1)} %get-tuple-element.34), channel_id=1, source_target_pairs={{0,1},{1,0},{2,3},{3,2},{4,5},{5,4},{6,7},{7,6},{8,9},{9,8},{10,11... | collective-permute-start | bytes 983048 | tf_op jit(solution)/shard_map/ppermute | solution.py:683
  129.4 3.5 %copy-start.14 = (pred[4,16,2,64]{3,1,2,0:T(8,128)(4,1)S(1)}, pred[4,16,2,64]{3,1,2,0:T(8,128)(4,1)}, u32[]{:S(2)}) copy-start(pred[4,16,2,64]{3,1,2,0:T(8,128)(4,1)} %compare_reduce_fusion) | copy-start | bytes 24580
  132.1 22.3 %copy-start.2 = (bf16[2560,64]{0,1:T(8,128)(2,1)S(1)}, bf16[2560,64]{0,1:T(8,128)(2,1)}, u32[]{:S(2)}) copy-start(bf16[2560,64]{0,1:T(8,128)(2,1)} %param.31) | copy-start | bytes 983044
  132.9 2.0 collective-permute-start.15
  135.9 4.0 %collective-permute-start.16 = (bf16[2,160,128]{2,1,0:T(8,128)(2,1)S(1)}, bf16[2,160,128]{2,1,0:T(8,128)(2,1)S(1)}, u32[]{:S(2)}, u32[]{:S(2)}) collective-permute-start(bf16[2,160,128]{2,1,0:T(8,128)(2,1)S(1)} %get-tuple-element.51), channel_id=1, source_target_pairs={{0,4},{1,5},{2,6},{3,7},{4,0},{5,1},{6,2},{7,3},{8,12},{9,13},{10,... | collective-permute-start | bytes 245768 | tf_op jit(solution)/shard_map/ppermute | solution.py:44
  136.1 5.2 %collective-permute-start.18 = (bf16[2,160,128]{2,1,0:T(8,128)(2,1)S(1)}, bf16[2,160,128]{2,1,0:T(8,128)(2,1)S(1)}, u32[]{:S(2)}, u32[]{:S(2)}) collective-permute-start(bf16[2,160,128]{2,1,0:T(8,128)(2,1)S(1)} %get-tuple-element.52), channel_id=1, source_target_pairs={{0,12},{1,13},{2,14},{3,15},{4,8},{5,9},{6,10},{7,11},{8,4},{9,5},... | collective-permute-start | bytes 245768 | tf_op jit(solution)/shard_map/ppermute | solution.py:44
  139.9 4.9 %collective-permute-start.17 = (bf16[2,160,128]{2,1,0:T(8,128)(2,1)S(1)}, bf16[2,160,128]{2,1,0:T(8,128)(2,1)S(1)}, u32[]{:S(2)}, u32[]{:S(2)}) collective-permute-start(bf16[2,160,128]{2,1,0:T(8,128)(2,1)S(1)} %get-tuple-element.53), channel_id=1, source_target_pairs={{0,8},{1,9},{2,10},{3,11},{4,12},{5,13},{6,14},{7,15},{8,0},{9,1},... | collective-permute-start | bytes 245768 | tf_op jit(solution)/shard_map/ppermute | solution.py:44
  162.9 8.8 %copy-start.9 = (bf16[64,2560]{1,0:T(8,128)(2,1)S(1)}, bf16[64,2560]{1,0:T(8,128)(2,1)}, u32[]{:S(2)}) copy-start(bf16[64,2560]{1,0:T(8,128)(2,1)} %get-tuple-element.40) | copy-start | bytes 983044
  162.9 28.8 %all-to-all-start.4 = ((bf16[16,160,256]{2,1,0:T(8,128)(2,1)}), bf16[16,160,256]{2,1,0:T(8,128)(2,1)S(1)}, u32[]{:S(2)}, u32[]{:S(2)}) async-start(bf16[16,160,256]{2,1,0:T(8,128)(2,1)} %bitcast.62), calls=%async_computation.4 | async-start | bytes 2621440 | tf_op jit(solution)/shard_map/all_to_all | solution.py:730
  172.0 3.3 %collective-permute-start.22 = (bf16[64,160]{0,1:T(8,128)(2,1)S(1)}, bf16[64,160]{0,1:T(8,128)(2,1)S(1)}, u32[]{:S(2)}, u32[]{:S(2)}) collective-permute-start(bf16[64,160]{0,1:T(8,128)(2,1)S(1)} %constant_dynamic-slice_fusion.1), channel_id=1, source_target_pairs={{0,1},{1,0},{2,3},{3,2},{4,5},{5,4},{6,7},{7,6},{8,9},{9,8},{10,11... | collective-permute-start | bytes 61448 | tf_op jit(solution)/shard_map/ppermute | solution.py:724
  172.3 12.4 %collective-permute-start.23 = (bf16[160,128]{1,0:T(8,128)(2,1)S(1)}, bf16[160,128]{1,0:T(8,128)(2,1)S(1)}, u32[]{:S(2)}, u32[]{:S(2)}) collective-permute-start(bf16[160,128]{1,0:T(8,128)(2,1)S(1)} %fusion.20), channel_id=1, source_target_pairs={{0,2},{1,3},{2,0},{3,1},{4,6},{5,7},{6,4},{7,5},{8,10},{9,11},{10,... | collective-permute-start | bytes 122888 | tf_op jit(solution)/shard_map/ppermute | solution.py:712
Sparse Core Ops, SparseCore 0:
  9.2 47.2 all-gather.1
